TPU v7x, 32 devices: a whole 2x2x4 slice. The times are simulated.
32 devices in a mesh: batch: 8 (over z, y), head: 4 (over x, core).
Axes of the slice: x: 2, y: 2, z: 4, core: 2. Of those that a mesh axis runs over, the one named last changes fastest.
Arguments:
- inputs: bfloat16 [8192, 768], P(('batch', 'head')), may hold values from -6 to 6
- bucket: int32 [16], P('batch'), may hold values from 0 to 1, as said below
- lengths: int32 [16, 4], P('batch'), may hold values from 0 to 512, as said below
- qkv_weight: bfloat16 [768, 2304], P(None, ('batch', 'head')), may hold values from -0.21875 to 0.21875
- query_bias: bfloat16 [768], P(('batch', 'head')), may hold values from -3 to 3
- value_bias: bfloat16 [768], P(('batch', 'head')), may hold values from -3 to 3
- proj_weight: bfloat16 [768, 768], P(None, ('batch', 'head')), may hold values from -1.75 to 1.75
- proj_bias: bfloat16 [768], P(('batch', 'head')), may hold values from -3 to 3
- first_gain: bfloat16 [768], P(('batch', 'head')), may hold values from 0.099609375 to 1.8984375
- first_shift: bfloat16 [768], P(('batch', 'head')), may hold values from -2 to 2
- up_weight: bfloat16 [768, 3072], P(None, ('batch', 'head')), may hold values from -0.21875 to 0.21875
- up_bias: bfloat16 [3072], P(('batch', 'head')), may hold values from -3 to 3
- down_weight: bfloat16 [3072, 768], P(('batch', 'head')), may hold values from -0.109375 to 0.109375
- down_bias: bfloat16 [768], P(('batch', 'head')), may hold values from -3 to 3
- second_gain: bfloat16 [768], P(('batch', 'head')), may hold values from 0.099609375 to 1.8984375
- second_shift: bfloat16 [768], P(('batch', 'head')), may hold values from -2 to 2
- cotangent: bfloat16 [8192, 768], P(('batch', 'head')), may hold values from -6 to 6
Outputs:
- layer_out: bfloat16 [8192, 768], P(('batch', 'head'))
- inputs_grad: bfloat16 [8192, 768], P(('batch', 'head'))
- qkv_grad: float32 [768, 2304], P('batch', 'head')
- qbias_grad: float32 [768], P(('batch', 'head'))
- vbias_grad: float32 [768], P(('batch', 'head'))
- proj_grad: float32 [768, 768], P('head', 'batch')
- pbias_grad: float32 [768], P(('batch', 'head'))
- fgain_grad: float32 [768], P(('batch', 'head'))
- fshift_grad: float32 [768], P(('batch', 'head'))
- up_grad: float32 [768, 3072], P(None, ('batch', 'head'))
- ubias_grad: float32 [3072], P(('batch', 'head'))
- down_grad: float32 [3072, 768], P(('batch', 'head'))
- dbias_grad: float32 [768], P(('batch', 'head'))
- sgain_grad: float32 [768], P(('batch', 'head'))
- sshift_grad: float32 [768], P(('batch', 'head'))
Inputs may be any that keep to these rules, and one draw needn't show every extreme that they name: `bucket`: 1 marks a block holding one sequence of up to 512 tokens, 0 a block holding 4 sequences, one in each aligned block of 128 rows. For a block marked 1, entry 0 is its sequence's length, over 128, and the other entries are 0; for a block marked 0, entry u is the length of the sequence starting at row u * 128, 1 to 128; lengths 512 and 128 occur.
All inputs are finite; a program needn't handle non-finite values.
Results may differ from a plain program's by a relative error of at most 0.017.
Values may be sent and summed in bfloat16 or wider, within the bound.
No kernel may reach another device: no remote copies, remote signals or barrier semaphores. Data moves between devices by JAX's collectives and lax.ppermute only.
A program may use at most 128 MiB of HBM per device.

v0:
```python
import functools

import jax
import jax.numpy as jnp
from jax import lax
from jax.experimental import pallas as pl
from jax.experimental.pallas import tpu as pltpu
from jax.sharding import PartitionSpec as P

D = 768
HEADS = 12
HEAD_DIM = 64
FF = 3072
BIG = 512
SMALL = 128
UNITS = 4
NORM_EPS = 1e-12
F32 = jnp.float32
BF16 = jnp.bfloat16

CORE = [(i, i ^ 1) for i in range(4)]
XPAIR = [(i, i ^ 2) for i in range(4)]
YPAIR = [(i, i ^ 1) for i in range(8)]
ZPAIR = [[(i, i ^ (2 * k)) for i in range(8)] for k in range(4)]


def core_swap(v):
    return lax.ppermute(v, "head", CORE)


def x_swap(v):
    return lax.ppermute(v, "head", XPAIR)


def y_swap(v):
    return lax.ppermute(v, "batch", YPAIR)


def z_swap(v, k):
    return lax.ppermute(v, "batch", ZPAIR[k])


def after(value, other):
    return lax.optimization_barrier((value, other))[0]


def nt(a, b, out=F32):
    return lax.dot_general(a, b, (((1,), (1,)), ((), ())), preferred_element_type=F32).astype(out)


def nn(a, b, out=F32):
    return lax.dot_general(a, b, (((1,), (0,)), ((), ())), preferred_element_type=F32).astype(out)


def tn(a, b, out=F32):
    return lax.dot_general(a, b, (((0,), (0,)), ((), ())), preferred_element_type=F32).astype(out)


def gather_z(shard):
    got = [shard] + [z_swap(shard, k) for k in (1, 2, 3)]
    return jnp.stack(got[:2]), jnp.stack(got[2:])


def gather_xy(lo, hi):
    y_lo, x_hi = y_swap(lo), x_swap(hi)
    x_lo, y_hi = x_swap(lo), y_swap(hi)
    return [(lo, hi), (x_lo, x_hi), (y_lo, y_hi), (x_swap(y_lo), y_swap(x_hi))]


def gather_any(shard):
    whole = lax.all_gather(shard, "batch", axis=0)
    return [whole, x_swap(whole)]


def scatter_xy(parts):
    (g_lo, g_hi), (x_lo, x_hi), (y_lo, y_hi), (d_lo, d_hi) = parts
    from_x, from_y = x_swap(d_lo), y_swap(d_hi)
    y_hi, x_lo = y_swap(y_hi), x_swap(x_lo)
    y_lo, x_hi = y_swap(add_low(y_lo, from_x)), x_swap(add_low(x_hi, from_y))
    return combine(g_lo, g_hi, x_lo, x_hi, y_lo, y_hi)


def scatter_z(mine, others):
    return (mine,) + tuple(z_swap(others[k - 1], k) for k in (1, 2, 3))


def scatter_any(parts):
    total = parts[0].astype(F32) + x_swap(parts[1]).astype(F32)
    return lax.psum_scatter(total, "batch", scatter_dimension=0, tiled=False)


def est(flops, moved, trans=0):
    return pl.CostEstimate(flops=int(flops), bytes_accessed=int(moved), transcendentals=int(trans))


def call(kernel, out_shape, operands, scratch=(), cost=None, limit=16):
    vmem = pl.BlockSpec(memory_space=pltpu.VMEM)
    single = not isinstance(out_shape, (tuple, list))
    return pl.pallas_call(
        kernel,
        out_shape=out_shape,
        in_specs=[pl.BlockSpec(memory_space=pltpu.SMEM)] + [vmem] * (len(operands) - 1),
        out_specs=vmem if single else [vmem] * len(out_shape),
        scratch_shapes=list(scratch),
        compiler_params=pltpu.CompilerParams(vmem_limit_bytes=limit << 20),
        cost_estimate=cost,
    )(*operands)


def add_low(a, b):
    return (a.astype(F32) + b.astype(F32)).astype(BF16)


def shape(dims, dtype=BF16):
    return jax.ShapeDtypeStruct(dims, dtype)


def combine_kernel(_, g_lo, g_hi, x_lo, x_hi, y_lo, y_hi, mine, one, two, three):
    outs = (mine, one, two, three)
    for k in range(4):
        g, xx, yy = (g_lo, x_lo, y_lo) if k < 2 else (g_hi, x_hi, y_hi)
        total = g[k % 2].astype(F32) + xx[k % 2].astype(F32) + yy[k % 2].astype(F32)
        outs[k][...] = total.astype(outs[k].dtype)


def combine(*parts):
    rows = parts[0].shape[1]
    mine, *others = call(
        combine_kernel,
        (shape((rows, D), F32),) + (shape((rows, D)),) * 3,
        (jnp.zeros((1,), jnp.int32), *parts),
        cost=est(8 * rows * D, 24 * rows * D),
    )
    return mine, others


def total_of(refs):
    return refs[0][...] + refs[1][...].astype(F32) + refs[2][...].astype(F32) + refs[3][...].astype(F32)


def finish_attend_kernel(_, mine, one, two, three, qkv, proj):
    total = total_of((mine, one, two, three))
    for hh in range(3):
        for t in range(3):
            at, to = 192 * t + 64 * hh, 192 * hh + 64 * t
            qkv[:, to : to + 64] = total[:, at : at + 64]
    proj[...] = total[:, 576:].T


def finish_attend(parts):
    rows = parts[0].shape[0]
    return call(
        finish_attend_kernel,
        (shape((rows, 576), F32), shape((192, rows), F32)),
        (jnp.zeros((1,), jnp.int32), *parts),
        cost=est(8 * rows * D, 16 * rows * D),
    )


def finish_ffn_kernel(_, mine, one, two, three, up, down):
    half = mine.shape[0] // 2
    total = total_of((mine, one, two, three))
    up[...] = total[:half].T
    down[...] = total[half:]


def finish_ffn(parts):
    half = parts[0].shape[0] // 2
    return call(
        finish_ffn_kernel,
        (shape((D, half), F32), shape((half, D), F32)),
        (jnp.zeros((1,), jnp.int32), *parts),
        cost=est(8 * half * D, 32 * half * D),
    )


def flip(a, bit):
    return a + bit - 2 * a * bit


def order_kernel(rows_q, rows_p, place, *refs):
    sources, (wq, wp, small) = refs[:16], refs[16:]
    z, y, x, c = place[0], place[1], place[2], place[3]
    zl, zh = lax.rem(z, 2), lax.div(z, 2)
    p = flip(c, zl)
    total = jnp.zeros(small.shape, F32)
    for swapped in range(2):
        cc = c if swapped == 0 else 1 - c
        for spot in range(4):
            kx, ky = spot % 2, spot // 2
            pair = sources[8 * swapped + 2 * spot : 8 * swapped + 2 * spot + 2]
            j = flip(y, ky) * 4 + flip(x, kx) * 2 + cc
            for i in range(2):
                wq[flip(zh, i) * 8 + j] = pair[i][p, 0:rows_q]
            for kz in range(4):
                zi = flip(zl, kz % 2) + 2 * flip(zh, kz // 2)
                src = pair[kz // 2]
                wp[zi * 8 + j] = src[kz % 2, rows_q : rows_q + rows_p]
                total = total + src[kz % 2, rows_q + rows_p :].astype(F32)
    small[...] = total


def order_weights(own, swapped, place, rows_q, rows_p, rows_s):
    return call(
        functools.partial(order_kernel, rows_q, rows_p),
        (
            shape((16, rows_q, D)),
            shape((32, rows_p, D)),
            shape((rows_s, D), F32),
        ),
        (place, *own, *swapped),
        cost=est(1e6, 9e6),
    )


def live_units(meta):
    c, kind = meta[0], meta[1]
    first = meta[2]
    units = []
    for u in range(UNITS):
        far = jnp.clip(first - SMALL * u, 0, SMALL)
        units.append(jnp.where(kind == 1, far, meta[2 + u]))
    return c, kind, units


def place_of(index, c):
    return jnp.bitwise_xor(index, c * (BIG // 2))


def live_of(place, units):
    unit = lax.shift_right_logical(place, 7)
    inner = jnp.bitwise_and(place, SMALL - 1)
    count = jnp.where(
        unit < 2, jnp.where(unit == 0, units[0], units[1]), jnp.where(unit == 2, units[2], units[3])
    )
    return inner < count


def heads_of(row, c):
    parts = []
    for g in range(2):
        lo = row[:, 384 * g : 384 * g + 192]
        hi = row[:, 384 * g + 192 : 384 * g + 384]
        parts.append(jnp.where(c == 0, lo, hi))
    return jnp.concatenate(parts, 1)


def attend_kernel(meta, x0, x1, w, small, q, k, v, ctx0, ctx1, probs, wr, mask):
    c, kind, units = live_units(meta)
    half = x0.shape[0]
    for t in range(3):
        for hd in range(6):
            src = ((hd // 3) * 9 + (hd % 3) * 3 + t) * HEAD_DIM
            dst = (t * 6 + hd) * HEAD_DIM
            wr[dst : dst + HEAD_DIM] = w[src : src + HEAD_DIM]
    biases = (heads_of(small[0:1], c), None, heads_of(small[1:2], c))
    for t, ref in enumerate((q, k, v)):
        for i, xr in enumerate((x0, x1)):
            val = nt(xr[...], wr[384 * t : 384 * t + 384])
            if biases[t] is not None:
                val = val + biases[t]
            ref[half * i : half * i + half] = val.astype(BF16)
    rows = lax.broadcasted_iota(jnp.int32, (BIG, BIG), 0)
    cols = lax.broadcasted_iota(jnp.int32, (BIG, BIG), 1)
    prow, pcol = place_of(rows, c), place_of(cols, c)
    same = jnp.logical_or(
        kind == 1, lax.shift_right_logical(prow, 7) == lax.shift_right_logical(pcol, 7)
    )
    mask[...] = jnp.where(jnp.logical_and(same, live_of(pcol, units)), 0.0, -1e30)
    lane = lax.broadcasted_iota(jnp.int32, (half, 128), 1)
    for pair in range(3):
        lanes = slice(128 * pair, 128 * pair + 128)
        kp, vp = k[:, lanes], v[:, lanes]
        for i, ctx in enumerate((ctx0, ctx1)):
            rws = slice(half * i, half * i + half)
            qp = q[rws, lanes] * jnp.asarray(HEAD_DIM**-0.5, BF16)
            outs = []
            for e in range(2):
                mine = (lane < HEAD_DIM) if e == 0 else (lane >= HEAD_DIM)
                s = nt(jnp.where(mine, qp, jnp.zeros_like(qp)), kp) + mask[rws]
                ex = jnp.exp(s - jnp.max(s, -1, keepdims=True))
                pr = (ex * (1.0 / jnp.sum(ex, -1, keepdims=True))).astype(BF16)
                probs[2 * pair + e, rws] = pr
                outs.append(nn(pr, vp))
            ctx[:, lanes] = jnp.where(lane < HEAD_DIM, outs[0], outs[1]).astype(BF16)


def attend(meta, x0, x1, w, small):
    half = x0.shape[0]
    n = 2 * half
    return call(
        attend_kernel,
        (
            shape((n, 384)),
            shape((n, 384)),
            shape((n, 384)),
            shape((half, 384)),
            shape((half, 384)),
            shape((6, n, n)),
            shape((1152, D)),
        ),
        (meta, x0, x1, w, small),
        scratch=[pltpu.VMEM((n, n), F32)],
        cost=est(2 * n * D * 1152 + 8 * n * n * 384, 9e6, 6 * n * n),
    )


def norm(values):
    center = values - jnp.mean(values, -1, keepdims=True)
    spread = jnp.mean(center * center, -1, keepdims=True)
    scale = lax.rsqrt(spread + NORM_EPS)
    return center * scale, scale


def norm_back(cot, normal, scale, gain):
    w = cot * gain
    return scale * (
        w - jnp.mean(w, -1, keepdims=True) - normal * jnp.mean(w * normal, -1, keepdims=True)
    )


def first_kernel(meta, x, ctx_own, ctx_in, wp, small, first, low, normal, scale):
    c = meta[0]
    mine = pl.multiple_of(c * 384, 128)
    theirs = pl.multiple_of((1 - c) * 384, 128)
    attn = nt(ctx_own[...], wp[:, pl.ds(mine, 384)]) + nt(ctx_in[...], wp[:, pl.ds(theirs, 384)])
    n, r = norm(x[...].astype(F32) + attn + small[2:3])
    out = n * small[3:4] + small[4:5]
    first[...] = out
    low[...] = out.astype(BF16)
    normal[...] = n
    scale[...] = jnp.broadcast_to(r, scale.shape)


def first_norm(meta, x, ctx_own, ctx_in, wp, small):
    n = x.shape[0]
    return call(
        first_kernel,
        (shape((n, D), F32), shape((n, D)), shape((n, D), F32), shape((n, 128), F32)),
        (meta, x, ctx_own, ctx_in, wp, small),
        cost=est(2 * n * D * D, 5e6),
    )


def ffn_weights(refs):
    if len(refs[0].shape) == 2:
        return refs[0][...], refs[1][...]
    half = refs[0].shape[1] // 2
    blocks = [(r, i) for r in refs for i in range(r.shape[0])]
    up = jnp.concatenate([r[i, 0:half] for r, i in blocks])
    down = jnp.concatenate([r[i, half : 2 * half] for r, i in blocks])
    return up, down


def ffn_kernel(first, meta, x0, x1, ub, w0, w1, *refs):
    if first:
        in0 = in1 = None
    else:
        (in0, in1), refs = refs[:2], refs[2:]
    hid, slope, out0, out1 = refs
    half = x0.shape[0]
    uw, dw = ffn_weights((w0, w1))
    for i, (xr, before, out) in enumerate(((x0, in0, out0), (x1, in1, out1))):
        rws = slice(half * i, half * i + half)
        up = nt(xr[...], uw) + ub[...]
        phi = 0.5 + 0.5 * lax.erf(up * (2.0**-0.5))
        hd = (up * phi).astype(BF16)
        hid[rws] = hd
        slope[rws] = (phi + up * jnp.exp(-0.5 * up * up) * 0.3989422804014327).astype(BF16)
        part = nn(hd, dw)
        out[...] = part if before is None else before[...] + part


def ffn(meta, x0, x1, ub, weights, sums):
    half, width = x0.shape[0], ub.shape[1]
    n = 2 * half
    return call(
        functools.partial(ffn_kernel, not sums),
        (shape((n, width)), shape((n, width)), shape((half, D), F32), shape((half, D), F32)),
        (meta, x0, x1, ub, *weights, *sums),
        cost=est(4 * n * D * width, 4 * D * width + 5e6, 2 * n * width),
    )


def second_kernel(meta, first, part, got, small, cot, out, sum_two, low, sums):
    c, _, units = live_units(meta)
    n, r = norm(first[...] + (part[...] + got[...] + small[5:6]))
    out[...] = (n * small[6:7] + small[7:8]).astype(BF16)
    index = lax.broadcasted_iota(jnp.int32, (first.shape[0], 1), 0)
    live = live_of(place_of(index, c), units)
    oc = jnp.where(live, cot[...].astype(F32), 0.0)
    st = norm_back(oc, n, r, small[6:7])
    sum_two[...] = st
    lo = st.astype(BF16)
    low[...] = lo
    sums[0:1] = jnp.sum(lo.astype(F32), 0, keepdims=True)
    sums[1:2] = jnp.sum(oc * n, 0, keepdims=True)
    sums[2:3] = jnp.sum(oc, 0, keepdims=True)


def second_norm(meta, first, part, got, small, cot):
    n = first.shape[0]
    return call(
        second_kernel,
        (shape((n, D)), shape((n, D), F32), shape((n, D)), shape((3, D), F32)),
        (meta, first, part, got, small, cot),
        cost=est(40 * n * D, 5e6),
    )


def ffn_back_kernel(first, meta, d0, d1, x0, x1, w0, w1, hid, slope, *refs):
    if first:
        in0 = in1 = None
    else:
        (in0, in1), refs = refs[:2], refs[2:]
    g0, g1, ub, out0, out1 = refs
    half = x0.shape[0]
    uw, dw = ffn_weights((w0, w1))
    cots = []
    for i, (d, before, out) in enumerate(((d0, in0, out0), (d1, in1, out1))):
        rws = slice(half * i, half * i + half)
        uc = (nt(d[...], dw) * slope[rws].astype(F32)).astype(BF16)
        cots.append(uc)
        part = nn(uc, uw)
        out[...] = part if before is None else before[...] + part
    ub[...] = jnp.sum(cots[0].astype(F32), 0, keepdims=True) + jnp.sum(
        cots[1].astype(F32), 0, keepdims=True
    )
    dg = (tn(hid[0:half], d0[...]) + tn(hid[half : 2 * half], d1[...])).astype(BF16)
    ug = (tn(cots[0], x0[...]) + tn(cots[1], x1[...])).astype(BF16)
    if len(g0.shape) == 2:
        g0[...], g1[...] = ug, dg
    else:
        rows = g0.shape[1] // 2
        at = 0
        for g in (g0, g1):
            for i in range(g.shape[0]):
                g[i, 0:rows] = ug[at : at + rows]
                g[i, rows : 2 * rows] = dg[at : at + rows]
                at += rows


def ffn_back(meta, d0, d1, x0, x1, weights, hid, slope, sums):
    half, width = x0.shape[0], hid.shape[1]
    return call(
        functools.partial(ffn_back_kernel, not sums),
        (
            shape(weights[0].shape),
            shape(weights[1].shape),
            shape((1, width), F32),
            shape((half, D), F32),
            shape((half, D), F32),
        ),
        (meta, d0, d1, x0, x1, *weights, hid, slope, *sums),
        cost=est(16 * half * D * width, 8 * D * width + 5e6),
    )


def first_back_kernel(meta, sum_two, part, got, normal, scale, small, sum_one, low, sums):
    fc = sum_two[...] + part[...] + got[...]
    n = normal[...]
    so = norm_back(fc, n, scale[:, 0:1], small[3:4])
    sum_one[...] = so
    lo = so.astype(BF16)
    low[...] = lo
    sums[0:1] = jnp.sum(lo.astype(F32), 0, keepdims=True)
    sums[1:2] = jnp.sum(fc * n, 0, keepdims=True)
    sums[2:3] = jnp.sum(fc, 0, keepdims=True)


def first_back(meta, sum_two, part, got, normal, scale, small):
    n = sum_two.shape[0]
    return call(
        first_back_kernel,
        (shape((n, D), F32), shape((n, D)), shape((3, D), F32)),
        (meta, sum_two, part, got, normal, scale, small),
        cost=est(30 * n * D, 5e6),
    )


def attend_back_kernel(
    sets, meta, a0, a1, x0, x1, wp, wr, q, k, v, ctx0, ctx1, probs, *refs
):
    outs, (in0, in1, sums, dctx, cots, grads) = refs[:sets], refs[sets:]
    c = meta[0]
    half = a0.shape[0]
    n = 2 * half
    wpo = wp[:, pl.ds(pl.multiple_of(c * 384, 128), 384)]
    dctx[0:half] = nn(a0[...], wpo).astype(BF16)
    dctx[half:n] = nn(a1[...], wpo).astype(BF16)
    lane = lax.broadcasted_iota(jnp.int32, (n, 128), 1)
    zero = jnp.zeros((n, 128), BF16)
    scale = HEAD_DIM**-0.5
    heads = [[], [], []]
    for pair in range(3):
        lanes = slice(128 * pair, 128 * pair + 128)
        qp, kp, vp, dp = q[:, lanes], k[:, lanes], v[:, lanes], dctx[:, lanes]
        dq = dk = dv = 0.0
        for e in range(2):
            mine = (lane < HEAD_DIM) if e == 0 else (lane >= HEAD_DIM)
            dh, kh, qh = jnp.where(mine, dp, zero), jnp.where(mine, kp, zero), jnp.where(mine, qp, zero)
            pr = probs[2 * pair + e]
            dv = dv + tn(pr, dh)
            pf = pr.astype(F32)
            t = pf * nt(dh, vp)
            ds = (t - pf * jnp.sum(t, -1, keepdims=True)).astype(BF16)
            dq = dq + nn(ds, kh)
            dk = dk + tn(ds, qh)
        for t, val in enumerate((dq * scale, dk * scale, dv)):
            val = val.astype(BF16)
            for e in range(2):
                hd = 2 * pair + e
                g, hh = hd // 3, hd % 3
                at = 640 * g + 192 * t + 64 * hh
                cots[:, at : at + 64] = val[:, 64 * e : 64 * e + 64]
            heads[t].append(val)
    for g in range(2):
        cots[:, 640 * g + 576 : 640 * g + 640] = jnp.zeros((n, 64), BF16)
    parts = [jnp.concatenate(heads[t], 1) for t in range(3)]
    for i, out in enumerate((in0, in1)):
        rws = slice(half * i, half * i + half)
        total = 0.0
        for t in range(3):
            total = total + nn(parts[t][rws], wr[384 * t : 384 * t + 384])
        out[...] = total
    for row, t in ((0, 0), (1, 2)):
        s = jnp.sum(parts[t].astype(F32), 0, keepdims=True)
        for g in range(2):
            sg = s[:, 192 * g : 192 * g + 192]
            sums[row : row + 1, 384 * g : 384 * g + 192] = jnp.where(c == 0, sg, 0.0)
            sums[row : row + 1, 384 * g + 192 : 384 * g + 384] = jnp.where(c == 1, sg, 0.0)
    for d in range(3):
        at = slice(256 * d, 256 * d + 256)
        full = tn(x0[:, at], cots[0:half]) + tn(x1[:, at], cots[half:n])
        pg = tn(a0[:, at], ctx0[...]) + tn(a1[:, at], ctx1[...])
        for g in range(2):
            grads[g, at, 0:576] = full[:, 640 * g : 640 * g + 576].astype(BF16)
            grads[g, at, 576:768] = pg[:, 192 * g : 192 * g + 192].astype(BF16)
    if sets == 1:
        outs[0][...] = grads[...]
    else:
        z, y, x = meta[6], meta[7], meta[8]
        rows = outs[0].shape[1]
        for spot in range(4):
            g, yi = flip(x, spot % 2), flip(y, spot // 2)
            for kz in range(4):
                zi = flip(lax.rem(z, 2), kz % 2) + 2 * flip(lax.div(z, 2), kz // 2)
                at = pl.multiple_of((2 * zi + yi) * rows, rows)
                outs[2 * spot + kz // 2][kz % 2] = grads[g, pl.ds(at, rows), :]


def attend_back(direct, meta, a0, a1, x0, x1, wp, wr, q, k, v, ctx0, ctx1, probs):
    half = a0.shape[0]
    n = 2 * half
    sets = (shape((2, 96, D)),) * 8 if direct else (shape((2, D, D)),)
    return call(
        functools.partial(attend_back_kernel, len(sets)),
        (*sets, shape((half, D), F32), shape((half, D), F32), shape((2, D), F32)),
        (meta, a0, a1, x0, x1, wp, wr, q, k, v, ctx0, ctx1, probs),
        scratch=[
            pltpu.VMEM((n, 384), BF16),
            pltpu.VMEM((n, 1280), BF16),
            pltpu.VMEM((2, D, D), BF16),
        ],
        cost=est(2 * n * D * 3500 + 14 * n * n * 384, 14e6),
    )


def local(
    inputs,
    bucket,
    lengths,
    qkv_weight,
    query_bias,
    value_bias,
    proj_weight,
    proj_bias,
    first_gain,
    first_shift,
    up_weight,
    up_bias,
    down_weight,
    down_bias,
    second_gain,
    second_shift,
    cotangent,
):
    head_count = lax.axis_size("head")
    batch_count = lax.axis_size("batch")
    devices = head_count * batch_count
    direct = batch_count == 8
    b = lax.axis_index("batch")
    h = lax.axis_index("head")
    me = b * head_count + h
    x, c = h // 2, h % 2
    z, y = b // 2, b % 2
    wq, wp, wf = 3 * D // devices, D // devices, FF // devices

    vectors = jnp.stack(
        [
            query_bias,
            value_bias,
            proj_bias,
            first_gain,
            first_shift,
            down_bias,
            second_gain,
            second_shift,
        ]
    )
    small = lax.dynamic_update_slice(jnp.zeros((16, D), BF16), vectors, (0, me * wp))
    per_row = D // wf
    small = lax.dynamic_update_slice(
        small, up_bias[None, :], (8 + me // per_row, (me % per_row) * wf)
    )
    proj_t = proj_weight.T.reshape(wp, 2, 2, 192).transpose(0, 2, 1, 3).reshape(wp, D)
    a_shard = jnp.concatenate([qkv_weight.T, proj_t, small])
    f_shard = jnp.concatenate([up_weight.T, down_weight])
    other_in = core_swap(inputs)
    meta = jnp.concatenate(
        [
            jnp.stack([c, lax.dynamic_index_in_dim(bucket, x, 0, keepdims=False)]),
            lax.dynamic_index_in_dim(lengths, x, 0, keepdims=False),
            jnp.stack([z, y, x]),
        ]
    ).astype(jnp.int32)

    k = jnp.arange(batch_count * 2)
    if direct:
        a_lo, a_hi = gather_z(a_shard)
        f_lo, f_hi = gather_z(after(f_shard, a_lo))
        a_own = [v for pair in gather_xy(a_lo, a_hi) for v in pair]
        f_lo, f_hi, _ = lax.optimization_barrier((f_lo, f_hi, a_own))
        f_all = gather_xy(f_lo, f_hi)
        a_swapped = [core_swap(v) for v in a_own]
        place = jnp.stack([z, y, x, c]).astype(jnp.int32)
        qkv_w, proj_w, small_all = order_weights(a_own, a_swapped, place, wq, wp, 16)
        qkv_w = qkv_w.reshape(2 * 576, D)
        proj_w = proj_w.reshape(D, D)
        kz = jnp.array([0, 1, 2, 3] * 4)
        ky = jnp.array([0] * 8 + [1] * 8)
        kx = jnp.array([0] * 4 + [1] * 4 + [0] * 4 + [1] * 4)
        owner = (z ^ kz) * 8 + (y ^ ky) * 4 + (x ^ kx) * 2 + c
    else:
        a_all = lax.all_gather(a_shard, ("batch", "head"), axis=0)
        qkv_all = a_all[:, :wq].reshape(2, 2, 576, D)
        qkv_w = lax.dynamic_index_in_dim(qkv_all, c, 1, keepdims=False).reshape(2 * 576, D)
        proj_w = a_all[:, wq : wq + wp].reshape(D, D)
        small_all = jnp.sum(a_all[:, wq + wp :].astype(F32), 0)
        f_all = [
            (v[:, :wf].reshape(-1, D), v[:, wf:].reshape(-1, D)) for v in gather_any(f_shard)
        ]
        owner = (k % batch_count) * 4 + (x ^ (k // batch_count)) * 2 + c
    spread = (owner[None, :] == jnp.arange(devices)[:, None]).astype(F32)
    ub_all = tn(spread, small_all[8:12].reshape(devices, wf)).reshape(1, FF // 2)

    q, kk, v, ctx_own, ctx_other, probs, wr = attend(meta, inputs, other_in, qkv_w, small_all)
    ctx_in = core_swap(ctx_other)
    first, first_low, first_n, first_r = first_norm(meta, inputs, ctx_own, ctx_in, proj_w, small_all)
    first_in = core_swap(first_low)
    sums = ()
    kept = []
    width = FF // 2 // len(f_all)
    for i, weights in enumerate(f_all):
        ub = ub_all[:, i * width : i * width + width]
        hid, slope, *sums = ffn(meta, first_low, first_in, ub, weights, sums)
        kept.append((weights, hid, slope))
    layer_out, sum_two, down_low, sums_two = second_norm(
        meta, first, sums[0], core_swap(sums[1]), small_all, cotangent
    )
    down_in = core_swap(down_low)

    sums = ()
    f_parts, ub_parts = [], []
    for weights, hid, slope in reversed(kept):
        g0, g1, ub, *sums = ffn_back(
            meta, down_low, down_in, first_low, first_in, weights, hid, slope, sums
        )
        f_parts.insert(0, (g0, g1))
        ub_parts.insert(0, ub)
    sum_one, attn_low, sums_one = first_back(
        meta, sum_two, sums[0], core_swap(sums[1]), first_n, first_r, small_all
    )
    attn_in = core_swap(attn_low)
    *a_grads, in_own, in_other, sums_zero = attend_back(
        direct,
        meta,
        attn_low,
        attn_in,
        inputs,
        other_in,
        proj_w,
        wr,
        q,
        kk,
        v,
        ctx_own,
        ctx_other,
        probs,
    )
    inputs_grad = (sum_one + in_own + core_swap(in_other)).astype(BF16)

    if direct:
        f_sums = scatter_z(*scatter_xy(f_parts))
        up_grad, down_grad = finish_ffn(f_sums)
        a_parts = [tuple(a_grads[2 * i : 2 * i + 2]) for i in range(4)]
        qkv_grad, proj_grad = finish_attend(scatter_z(*scatter_xy(a_parts)))
    else:
        wb = D // batch_count
        a_grads = a_grads[0].reshape(2, batch_count, wb, D)
        a_mine = scatter_any(
            [
                lax.dynamic_index_in_dim(a_grads, x, 0, keepdims=False),
                lax.dynamic_index_in_dim(a_grads, 1 - x, 0, keepdims=False),
            ]
        )
        f_mine = scatter_any(
            [
                jnp.concatenate(
                    [ug.reshape(batch_count, wf, D), dg.reshape(batch_count, wf, D)], 1
                )
                for ug, dg in f_parts
            ]
        )
        qkv_grad = a_mine[:, :576].reshape(wb, 3, 3, HEAD_DIM).transpose(0, 2, 1, 3)
        qkv_grad = qkv_grad.reshape(wb, 576)
        proj_grad = a_mine[:, 576:].T
        up_grad, down_grad = f_mine[:wf].T, f_mine[wf:]

    vecs = jnp.concatenate([sums_zero, sums_one, sums_two])
    vecs = vecs.reshape(8, devices, wp).transpose(1, 0, 2).reshape(devices, 8 * wp)
    ubias = jnp.concatenate(ub_parts, 1).reshape(batch_count * 2, wf)
    ubias = lax.dot_general(
        spread, ubias, (((1,), (0,)), ((), ())), precision=lax.Precision.HIGHEST
    )
    packed = jnp.concatenate([vecs, ubias], 1)
    packed = lax.all_to_all(packed, ("batch", "head"), split_axis=0, concat_axis=0, tiled=True)
    packed = jnp.sum(packed, 0)
    qb_g, vb_g, pb_g, fg_g, fs_g, db_g, sg_g, ss_g = [
        packed[i * wp : (i + 1) * wp] for i in range(8)
    ]
    return (
        layer_out,
        inputs_grad,
        qkv_grad,
        qb_g,
        vb_g,
        proj_grad,
        pb_g,
        fg_g,
        fs_g,
        up_grad,
        packed[8 * wp :],
        down_grad,
        db_g,
        sg_g,
        ss_g,
    )


def solution(mesh):
    both = ("batch", "head")
    in_specs = (
        P(both, None),
        P("batch"),
        P("batch", None),
        P(None, both),
        P(both),
        P(both),
        P(None, both),
        P(both),
        P(both),
        P(both),
        P(None, both),
        P(both),
        P(both, None),
        P(both),
        P(both),
        P(both),
        P(both, None),
    )
    out_specs = (
        P(both, None),
        P(both, None),
        P("batch", "head"),
        P(both),
        P(both),
        P("head", "batch"),
        P(both),
        P(both),
        P(both),
        P(None, both),
        P(both),
        P(both, None),
        P(both),
        P(both),
        P(both),
    )
    return jax.shard_map(local, mesh=mesh, in_specs=in_specs, out_specs=out_specs, check_vma=False)
```

profile of v0, /device:TPU:0, one launch (start us, length us, event | category | flops | bytes accessed | tf_op | source)
XLA Modules:
  0.0 249.3 jit_solution(2906574965136376785)
XLA Ops:
  4.6 3.3 %collective-permute-start.1 = (bf16[112,768]{1,0:T(8,128)(2,1)S(1)}, bf16[112,768]{1,0:T(8,128)(2,1)S(1)}, u32[]{:S(2)}, u32[]{:S(2)}) collective-permute-start(bf16[112,768]{1,0:T(8,128)(2,1)S(1)} %get-tuple-element.227), channel_id=1, source_target_pairs={{0,8},{4,12},{8,0},{12,4},{16,24},{20,28},{24,16},{28,20},{1,9},{5... | collective-permute-start | bytes 516104 | tf_op jit(solution)/shard_map/ppermute | solution.py:40
  8.0 2.6 %collective-permute-start.2 = (bf16[112,768]{1,0:T(8,128)(2,1)S(1)}, bf16[112,768]{1,0:T(8,128)(2,1)S(1)}, u32[]{:S(2)}, u32[]{:S(2)}) collective-permute-start(bf16[112,768]{1,0:T(8,128)(2,1)S(1)} %get-tuple-element.227), channel_id=1, source_target_pairs={{0,16},{4,20},{8,24},{12,28},{16,0},{20,4},{24,8},{28,12},{1,17},{... | collective-permute-start | bytes 516104 | tf_op jit(solution)/shard_map/ppermute | solution.py:40
  11.6 3.8 %collective-permute-done.1 = bf16[112,768]{1,0:T(8,128)(2,1)S(1)} collective-permute-done((bf16[112,768]{1,0:T(8,128)(2,1)S(1)}, bf16[112,768]{1,0:T(8,128)(2,1)S(1)}, u32[]{:S(2)}, u32[]{:S(2)}) %collective-permute-start.1) | collective-permute-done | bytes 172064 | tf_op jit(solution)/shard_map/ppermute | solution.py:40
  15.4 3.4 %collective-permute-start.22 = (bf16[192,768]{1,0:T(8,128)(2,1)S(1)}, bf16[192,768]{1,0:T(8,128)(2,1)S(1)}, u32[]{:S(2)}, u32[]{:S(2)}) collective-permute-start(bf16[192,768]{1,0:T(8,128)(2,1)S(1)} %pad_maximum_fusion.4), channel_id=1, source_target_pairs={{0,24},{4,28},{8,16},{12,20},{16,8},{20,12},{24,0},{28,4},{1,25},{... | collective-permute-start | bytes 884744 | tf_op jit(solution)/shard_map/ppermute | solution.py:40
  19.8 16.4 %collective-permute-done.2 = bf16[112,768]{1,0:T(8,128)(2,1)S(1)} collective-permute-done((bf16[112,768]{1,0:T(8,128)(2,1)S(1)}, bf16[112,768]{1,0:T(8,128)(2,1)S(1)}, u32[]{:S(2)}, u32[]{:S(2)}) %collective-permute-start.2) | collective-permute-done | bytes 172064 | tf_op jit(solution)/shard_map/ppermute | solution.py:40
  36.3 1.6 collective-permute-start.7
  37.9 1.6 collective-permute-start.5
  39.5 11.7 %collective-permute-done.21 = bf16[192,768]{1,0:T(8,128)(2,1)S(1)} collective-permute-done((bf16[192,768]{1,0:T(8,128)(2,1)S(1)}, bf16[192,768]{1,0:T(8,128)(2,1)S(1)}, u32[]{:S(2)}, u32[]{:S(2)}) %collective-permute-start.21) | collective-permute-done | bytes 294944 | tf_op jit(solution)/shard_map/ppermute | solution.py:40
  51.2 1.6 collective-permute-start.6
  57.5 4.6 %collective-permute-done.6.refs_4_ = bf16[2,112,768]{2,1,0:T(8,128)(2,1)S(1)} collective-permute-done((bf16[2,112,768]{2,1,0:T(8,128)(2,1)S(1)}, bf16[2,112,768]{2,1,0:T(8,128)(2,1)S(1)}, u32[]{:S(2)}, u32[]{:S(2)}) %collective-permute-start.6) | collective-permute-done | bytes 344096 | tf_op jit(solution)/shard_map/ppermute | solution.py:36
  66.8 2.4 collective-permute-done.9.refs_7_
  69.2 2.3 collective-permute-done.8.refs_6_
  85.5 1.8 shard_map.307
  88.3 7.8 %shard_map.308 = (bf16[512,384]{1,0:T(8,128)(2,1)S(1)}, bf16[512,384]{1,0:T(8,128)(2,1)S(1)}, bf16[512,384]{1,0:T(8,128)(2,1)S(1)}, bf16[256,384]{1,0:T(8,128)(2...) custom-call(s32[9]{0:T(128)S(1)} %concatenate.18.meta, ...), custom_call_target="tpu_custom_call" | custom-call | flops 1711276032 | bytes 9000000 | tf_op jit(solution)/shard_map/pallas_call | solution.py:99
  96.2 1.7 copy-done.52
  104.1 1.9 shard_map.309
  110.5 1.8 shard_map.310
  112.4 2.3 shard_map.311
  114.7 3.0 %collective-permute-done.27.w1 = bf16[2,192,768]{2,1,0:T(8,128)(2,1)} collective-permute-done((bf16[2,192,768]{2,1,0:T(8,128)(2,1)S(1)}, bf16[2,192,768]{2,1,0:T(8,128)(2,1)}, u32[]{:S(2)}, u32[]{:S(2)}) %collective-permute-start.27) | collective-permute-done | bytes 589856 | tf_op jit(solution)/shard_map/ppermute | solution.py:36
  117.7 2.5 %shard_map.312 = (bf16[512,384]{1,0:T(8,128)(2,1)S(1)}, bf16[512,384]{1,0:T(8,128)(2,1)S(1)}, f32[256,768]{1,0:T(8,128)S(1)}, f32[256,768]{1,0:T(8,128)S(1)}) custom-call(s32[9]{0:T(128)S(1)} %concatenate.18.meta, bf16[256,768]{1,0:T(8,128)(2,1)S(1)} %get-tuple-element.104.x0, bf16[256,768]{1,0:T(8,128)(2,1)S(1)} %collective-permute-done.19.x1, ...), custom_call_target="tpu_custom_call" | custom-call | flops 603979776 | bytes 6179648 | tf_op jit(solution)/shard_map/pallas_call | solution.py:99
  120.2 3.4 %collective-permute-done.24.w0 = bf16[2,192,768]{2,1,0:T(8,128)(2,1)} collective-permute-done((bf16[2,192,768]{2,1,0:T(8,128)(2,1)S(1)}, bf16[2,192,768]{2,1,0:T(8,128)(2,1)}, u32[]{:S(2)}, u32[]{:S(2)}) %collective-permute-start.24) | collective-permute-done | bytes 589856 | tf_op jit(solution)/shard_map/ppermute | solution.py:32
  123.6 6.3 %collective-permute-done.26.w1 = bf16[2,192,768]{2,1,0:T(8,128)(2,1)} collective-permute-done((bf16[2,192,768]{2,1,0:T(8,128)(2,1)S(1)}, bf16[2,192,768]{2,1,0:T(8,128)(2,1)}, u32[]{:S(2)}, u32[]{:S(2)}) %collective-permute-start.26) | collective-permute-done | bytes 589856 | tf_op jit(solution)/shard_map/ppermute | solution.py:36
  130.0 2.6 %shard_map.313 = (bf16[512,384]{1,0:T(8,128)(2,1)S(1)}, bf16[512,384]{1,0:T(8,128)(2,1)S(1)}, f32[256,768]{1,0:T(8,128)S(1)}, f32[256,768]{1,0:T(8,128)S(1)}) custom-call(s32[9]{0:T(128)S(1)} %concatenate.18.meta, bf16[256,768]{1,0:T(8,128)(2,1)S(1)} %get-tuple-element.104.x0, bf16[256,768]{1,0:T(8,128)(2,1)S(1)} %collective-permute-done.19.x1, ...), custom_call_target="tpu_custom_call" | custom-call | flops 603979776 | bytes 6179648 | tf_op jit(solution)/shard_map/pallas_call | solution.py:99
  132.7 2.3 collective-permute-done.29.got
  134.9 1.9 shard_map.314
  137.0 1.6 collective-permute-done.30.d1
  138.6 3.1 %shard_map.315 = (bf16[2,192,768]{2,1,0:T(8,128)(2,1)S(1)}, bf16[2,192,768]{2,1,0:T(8,128)(2,1)S(1)}, f32[1,384]{1,0:T(1,128)S(1)}, f32[256,768]{1,0:T(8,128)S(1)}, f32[256,768]{1,0:T(8,128)S(1)}) custom-call(s32[9]{0:T(128)S(1)} %concatenate.18.meta, bf16[256,768]{1,0:T(8,128)(2,1)S(1)} %get-tuple-element.118.d0, ...), custom_call_target="tpu_custom_call" | custom-call | flops 1207959552 | bytes 7359296 | tf_op jit(solution)/shard_map/pallas_call | solution.py:99
  141.7 3.8 %shard_map.316 = (bf16[2,192,768]{2,1,0:T(8,128)(2,1)S(1)}, bf16[2,192,768]{2,1,0:T(8,128)(2,1)}, f32[1,384]{1,0:T(1,128)S(1)}, f32[256,768]{1,0:T(8,128)S(1)}, f32[256,768]{1,0:T(8,128)S(1)}) custom-call(s32[9]{0:T(128)S(1)} %concatenate.18.meta, bf16[256,768]{1,0:T(8,128)(2,1)S(1)} %get-tuple-element.118.d0, ...), custom_call_target="tpu_custom_call" | custom-call | flops 1207959552 | bytes 7359296 | tf_op jit(solution)/shard_map/pallas_call | solution.py:99
  145.4 3.7 %shard_map.317 = (bf16[2,192,768]{2,1,0:T(8,128)(2,1)}, bf16[2,192,768]{2,1,0:T(8,128)(2,1)S(1)}, f32[1,384]{1,0:T(1,128)S(1)}, f32[256,768]{1,0:T(8,128)S(1)}, f32[256,768]{1,0:T(8,128)S(1)}) custom-call(s32[9]{0:T(128)S(1)} %concatenate.18.meta, bf16[256,768]{1,0:T(8,128)(2,1)S(1)} %get-tuple-element.118.d0, ...), custom_call_target="tpu_custom_call" | custom-call | flops 1207959552 | bytes 7359296 | tf_op jit(solution)/shard_map/pallas_call | solution.py:99
  149.2 2.4 shard_map.318
  157.1 10.8 %collective-permute-done.44 = bf16[2,192,768]{2,1,0:T(8,128)(2,1)S(1)} collective-permute-done((bf16[2,192,768]{2,1,0:T(8,128)(2,1)S(1)}, bf16[2,192,768]{2,1,0:T(8,128)(2,1)S(1)}, u32[]{:S(2)}, u32[]{:S(2)}) %collective-permute-start.44) | collective-permute-done | bytes 589856 | tf_op jit(solution)/shard_map/ppermute | solution.py:36
  172.0 10.1 %shard_map.320 = (bf16[2,96,768]{2,1,0:T(8,128)(2,1)S(1)}, bf16[2,96,768]{2,1,0:T(8,128)(2,1)S(1)}, bf16[2,96,768]{2,1,0:T(8,128)(2,1)S(1)}, bf16[2,96,768]{2,1,...) custom-call(s32[9]{0:T(128)S(1)} %concatenate.18.meta, ...), custom_call_target="tpu_custom_call" | custom-call | flops 4161798144 | bytes 14000000 | tf_op jit(solution)/shard_map/pallas_call | solution.py:99
  190.2 3.7 %collective-permute-done.45.x_hi = bf16[2,192,768]{2,1,0:T(8,128)(2,1)} collective-permute-done((bf16[2,192,768]{2,1,0:T(8,128)(2,1)}, bf16[2,192,768]{2,1,0:T(8,128)(2,1)}, u32[]{:S(2)}, u32[]{:S(2)}) %collective-permute-start.45) | collective-permute-done | bytes 589856 | tf_op jit(solution)/shard_map/ppermute | solution.py:32
  195.0 2.5 %shard_map.323 = (f32[192,768]{1,0:T(8,128)S(1)}, bf16[192,768]{1,0:T(8,128)(2,1)}, bf16[192,768]{1,0:T(8,128)(2,1)}, bf16[192,768]{1,0:T(8,128)(2,1)S(1)}) custom-call(s32[1]{0:T(128)} %constant.95.clone.1._, bf16[2,192,768]{2,1,0:T(8,128)(2,1)S(1)} %get-tuple-element.167.g_lo, bf16[2,192,768]{2,1,0:T(8,128)(2,1)S(1)} %get-tuple-element.168.g_hi, ...), custom_call_target="tpu_custom_call" | custom-call | flops 1179648 | bytes 3538944 | tf_op jit(solution)/shard_map/pallas_call | solution.py:99
  197.5 1.6 collective-permute-start.34
  200.6 1.8 add_convert_fusion.4
  203.8 1.7 collective-permute-done.34.x_lo
  205.5 2.1 collective-permute-start.50
  210.6 1.6 copy.41
  214.0 4.0 %all-to-all-start = ((f32[32,1,288]{2,1,0:T(1,128)}), f32[32,1,288]{2,1,0:T(1,128)S(1)}, u32[]{:S(2)}, u32[]{:S(2)}) async-start(f32[32,1,288]{2,1,0:T(1,128)} %copy.42), calls=%async_computation | async-start | bytes 98304 | tf_op jit(solution)/shard_map/all_to_all | solution.py:737
  218.0 3.7 %collective-permute-start.51 = (bf16[192,768]{1,0:T(8,128)(2,1)}, bf16[192,768]{1,0:T(8,128)(2,1)}, u32[]{:S(2)}, u32[]{:S(2)}) collective-permute-start(bf16[192,768]{1,0:T(8,128)(2,1)} %copy-done.44), channel_id=1, source_target_pairs={{0,24},{4,28},{8,16},{12,20},{16,8},{20,12},{24,0},{28,4},{1,25},{... | collective-permute-start | bytes 884744 | tf_op jit(solution)/shard_map/ppermute | solution.py:40
  221.7 3.8 %all-to-all-done = f32[32,1,288]{2,1,0:T(1,128)S(1)} async-done(((f32[32,1,288]{2,1,0:T(1,128)}), f32[32,1,288]{2,1,0:T(1,128)S(1)}, u32[]{:S(2)}, u32[]{:S(2)}) %all-to-all-start) | async-done | bytes 36896 | tf_op jit(solution)/shard_map/all_to_all | solution.py:737
  228.1 1.9 shard_map.321
  231.0 3.3 %collective-permute-start.42 = (bf16[96,768]{1,0:T(8,128)(2,1)}, bf16[96,768]{1,0:T(8,128)(2,1)}, u32[]{:S(2)}, u32[]{:S(2)}) collective-permute-start(bf16[96,768]{1,0:T(8,128)(2,1)} %get-tuple-element.157), channel_id=1, source_target_pairs={{0,24},{4,28},{8,16},{12,20},{16,8},{20,12},{24,0},{28,4},{1,25},{... | collective-permute-start | bytes 442376 | tf_op jit(solution)/shard_map/ppermute | solution.py:40
  235.0 2.0 shard_map.324
  237.8 7.7 %collective-permute-done.41.two = bf16[96,768]{1,0:T(8,128)(2,1)S(1)} collective-permute-done((bf16[96,768]{1,0:T(8,128)(2,1)}, bf16[96,768]{1,0:T(8,128)(2,1)S(1)}, u32[]{:S(2)}, u32[]{:S(2)}) %collective-permute-start.41) | collective-permute-done | bytes 147488 | tf_op jit(solution)/shard_map/ppermute | solution.py:40
  245.5 1.8 shard_map.322
  247.3 2.0 add_convert_fusion.2
  (265 shorter events, 72.8 us)
Async XLA Ops:
  4.6 10.7 %collective-permute-start.1 = (bf16[112,768]{1,0:T(8,128)(2,1)S(1)}, bf16[112,768]{1,0:T(8,128)(2,1)S(1)}, u32[]{:S(2)}, u32[]{:S(2)}) collective-permute-start(bf16[112,768]{1,0:T(8,128)(2,1)S(1)} %get-tuple-element.227), channel_id=1, source_target_pairs={{0,8},{4,12},{8,0},{12,4},{16,24},{20,28},{24,16},{28,20},{1,9},{5... | collective-permute-start | bytes 516104 | tf_op jit(solution)/shard_map/ppermute | solution.py:40
  8.0 28.2 %collective-permute-start.2 = (bf16[112,768]{1,0:T(8,128)(2,1)S(1)}, bf16[112,768]{1,0:T(8,128)(2,1)S(1)}, u32[]{:S(2)}, u32[]{:S(2)}) collective-permute-start(bf16[112,768]{1,0:T(8,128)(2,1)S(1)} %get-tuple-element.227), channel_id=1, source_target_pairs={{0,16},{4,20},{8,24},{12,28},{16,0},{20,4},{24,8},{28,12},{1,17},{... | collective-permute-start | bytes 516104 | tf_op jit(solution)/shard_map/ppermute | solution.py:40
  10.5 25.7 %collective-permute-start.3 = (bf16[112,768]{1,0:T(8,128)(2,1)S(1)}, bf16[112,768]{1,0:T(8,128)(2,1)S(1)}, u32[]{:S(2)}, u32[]{:S(2)}) collective-permute-start(bf16[112,768]{1,0:T(8,128)(2,1)S(1)} %get-tuple-element.227), channel_id=1, source_target_pairs={{0,24},{4,28},{8,16},{12,20},{16,8},{20,12},{24,0},{28,4},{1,25},{... | collective-permute-start | bytes 516104 | tf_op jit(solution)/shard_map/ppermute | solution.py:40
  15.4 22.5 %collective-permute-start.22 = (bf16[192,768]{1,0:T(8,128)(2,1)S(1)}, bf16[192,768]{1,0:T(8,128)(2,1)S(1)}, u32[]{:S(2)}, u32[]{:S(2)}) collective-permute-start(bf16[192,768]{1,0:T(8,128)(2,1)S(1)} %pad_maximum_fusion.4), channel_id=1, source_target_pairs={{0,24},{4,28},{8,16},{12,20},{16,8},{20,12},{24,0},{28,4},{1,25},{... | collective-permute-start | bytes 884744 | tf_op jit(solution)/shard_map/ppermute | solution.py:40
  18.7 32.5 %collective-permute-start.21 = (bf16[192,768]{1,0:T(8,128)(2,1)S(1)}, bf16[192,768]{1,0:T(8,128)(2,1)S(1)}, u32[]{:S(2)}, u32[]{:S(2)}) collective-permute-start(bf16[192,768]{1,0:T(8,128)(2,1)S(1)} %pad_maximum_fusion.4), channel_id=1, source_target_pairs={{0,16},{4,20},{8,24},{12,28},{16,0},{20,4},{24,8},{28,12},{1,17},{... | collective-permute-start | bytes 884744 | tf_op jit(solution)/shard_map/ppermute | solution.py:40
  18.7 32.5 %collective-permute-start.20 = (bf16[192,768]{1,0:T(8,128)(2,1)S(1)}, bf16[192,768]{1,0:T(8,128)(2,1)S(1)}, u32[]{:S(2)}, u32[]{:S(2)}) collective-permute-start(bf16[192,768]{1,0:T(8,128)(2,1)S(1)} %pad_maximum_fusion.4), channel_id=1, source_target_pairs={{0,8},{4,12},{8,0},{12,4},{16,24},{20,28},{24,16},{28,20},{1,9},{5... | collective-permute-start | bytes 884744 | tf_op jit(solution)/shard_map/ppermute | solution.py:40
  36.2 16.6 %collective-permute-start.11 = (bf16[2,112,768]{2,1,0:T(8,128)(2,1)S(1)}, bf16[2,112,768]{2,1,0:T(8,128)(2,1)S(1)}, u32[]{:S(2)}, u32[]{:S(2)}) collective-permute-start(bf16[2,112,768]{2,1,0:T(8,128)(2,1)S(1)} %pad_maximum_fusion.3.refs_1_), channel_id=1, source_target_pairs={{0,1},{1,0},{2,3},{3,2},{4,5},{5,4},{6,7},{7,6},{8,9},{9,8},{10,11... | collective-permute-start | bytes 1032200 | tf_op jit(solution)/shard_map/ppermute | solution.py:28
  36.3 18.7 %collective-permute-start.7 = (bf16[2,112,768]{2,1,0:T(8,128)(2,1)S(1)}, bf16[2,112,768]{2,1,0:T(8,128)(2,1)S(1)}, u32[]{:S(2)}, u32[]{:S(2)}) collective-permute-start(bf16[2,112,768]{2,1,0:T(8,128)(2,1)S(1)} %pad_maximum_fusion.3.refs_1_), channel_id=1, source_target_pairs={{0,4},{4,0},{8,12},{12,8},{16,20},{20,16},{24,28},{28,24},{1,5},{5... | collective-permute-start | bytes 1032200 | tf_op jit(solution)/shard_map/ppermute | solution.py:36
  37.9 17.8 %collective-permute-start.5 = (bf16[2,112,768]{2,1,0:T(8,128)(2,1)S(1)}, bf16[2,112,768]{2,1,0:T(8,128)(2,1)S(1)}, u32[]{:S(2)}, u32[]{:S(2)}) collective-permute-start(bf16[2,112,768]{2,1,0:T(8,128)(2,1)S(1)} %pad_maximum_fusion.3.refs_1_), channel_id=1, source_target_pairs={{0,2},{1,3},{2,0},{3,1},{4,6},{5,7},{6,4},{7,5},{8,10},{9,11},{10,... | collective-permute-start | bytes 1032200 | tf_op jit(solution)/shard_map/ppermute | solution.py:32
  51.2 5.1 %collective-permute-start.10 = (bf16[2,112,768]{2,1,0:T(8,128)(2,1)S(1)}, bf16[2,112,768]{2,1,0:T(8,128)(2,1)S(1)}, u32[]{:S(2)}, u32[]{:S(2)}) collective-permute-start(bf16[2,112,768]{2,1,0:T(8,128)(2,1)S(1)} %pad_maximum_fusion.2.refs_0_), channel_id=1, source_target_pairs={{0,1},{1,0},{2,3},{3,2},{4,5},{5,4},{6,7},{7,6},{8,9},{9,8},{10,11... | collective-permute-start | bytes 1032200 | tf_op jit(solution)/shard_map/ppermute | solution.py:28
  51.2 10.9 %collective-permute-start.6 = (bf16[2,112,768]{2,1,0:T(8,128)(2,1)S(1)}, bf16[2,112,768]{2,1,0:T(8,128)(2,1)S(1)}, u32[]{:S(2)}, u32[]{:S(2)}) collective-permute-start(bf16[2,112,768]{2,1,0:T(8,128)(2,1)S(1)} %pad_maximum_fusion.2.refs_0_), channel_id=1, source_target_pairs={{0,4},{4,0},{8,12},{12,8},{16,20},{20,16},{24,28},{28,24},{1,5},{5... | collective-permute-start | bytes 1032200 | tf_op jit(solution)/shard_map/ppermute | solution.py:36
  53.6 10.1 %collective-permute-start.4 = (bf16[2,112,768]{2,1,0:T(8,128)(2,1)S(1)}, bf16[2,112,768]{2,1,0:T(8,128)(2,1)S(1)}, u32[]{:S(2)}, u32[]{:S(2)}) collective-permute-start(bf16[2,112,768]{2,1,0:T(8,128)(2,1)S(1)} %pad_maximum_fusion.2.refs_0_), channel_id=1, source_target_pairs={{0,2},{1,3},{2,0},{3,1},{4,6},{5,7},{6,4},{7,5},{8,10},{9,11},{10,... | collective-permute-start | bytes 1032200 | tf_op jit(solution)/shard_map/ppermute | solution.py:32
  55.0 8.7 %collective-permute-start.15 = (bf16[2,112,768]{2,1,0:T(8,128)(2,1)S(1)}, bf16[2,112,768]{2,1,0:T(8,128)(2,1)S(1)}, u32[]{:S(2)}, u32[]{:S(2)}) collective-permute-start(bf16[2,112,768]{2,1,0:T(8,128)(2,1)S(1)} %collective-permute-done.7.refs_5_), channel_id=1, source_target_pairs={{0,1},{1,0},{2,3},{3,2},{4,5},{5,4},{6,7},{7,6},{8,9},{9,8},{10,11... | collective-permute-start | bytes 1032200 | tf_op jit(solution)/shard_map/ppermute | solution.py:28
  55.8 9.8 %collective-permute-start.13 = (bf16[2,112,768]{2,1,0:T(8,128)(2,1)S(1)}, bf16[2,112,768]{2,1,0:T(8,128)(2,1)S(1)}, u32[]{:S(2)}, u32[]{:S(2)}) collective-permute-start(bf16[2,112,768]{2,1,0:T(8,128)(2,1)S(1)} %collective-permute-done.5.refs_3_), channel_id=1, source_target_pairs={{0,1},{1,0},{2,3},{3,2},{4,5},{5,4},{6,7},{7,6},{8,9},{9,8},{10,11... | collective-permute-start | bytes 1032200 | tf_op jit(solution)/shard_map/ppermute | solution.py:28
  57.0 12.2 %collective-permute-start.9 = (bf16[2,112,768]{2,1,0:T(8,128)(2,1)S(1)}, bf16[2,112,768]{2,1,0:T(8,128)(2,1)}, u32[]{:S(2)}, u32[]{:S(2)}) collective-permute-start(bf16[2,112,768]{2,1,0:T(8,128)(2,1)S(1)} %collective-permute-done.5.refs_3_), channel_id=1, source_target_pairs={{0,4},{4,0},{8,12},{12,8},{16,20},{20,16},{24,28},{28,24},{1,5},{5... | collective-permute-start | bytes 1032200 | tf_op jit(solution)/shard_map/ppermute | solution.py:36
  62.2 9.3 %collective-permute-start.8 = (bf16[2,112,768]{2,1,0:T(8,128)(2,1)S(1)}, bf16[2,112,768]{2,1,0:T(8,128)(2,1)}, u32[]{:S(2)}, u32[]{:S(2)}) collective-permute-start(bf16[2,112,768]{2,1,0:T(8,128)(2,1)S(1)} %collective-permute-done.6.refs_4_), channel_id=1, source_target_pairs={{0,2},{1,3},{2,0},{3,1},{4,6},{5,7},{6,4},{7,5},{8,10},{9,11},{10,... | collective-permute-start | bytes 1032200 | tf_op jit(solution)/shard_map/ppermute | solution.py:32
  63.7 7.9 %collective-permute-start.14 = (bf16[2,112,768]{2,1,0:T(8,128)(2,1)S(1)}, bf16[2,112,768]{2,1,0:T(8,128)(2,1)S(1)}, u32[]{:S(2)}, u32[]{:S(2)}) collective-permute-start(bf16[2,112,768]{2,1,0:T(8,128)(2,1)S(1)} %collective-permute-done.6.refs_4_), channel_id=1, source_target_pairs={{0,1},{1,0},{2,3},{3,2},{4,5},{5,4},{6,7},{7,6},{8,9},{9,8},{10,11... | collective-permute-start | bytes 1032200 | tf_op jit(solution)/shard_map/ppermute | solution.py:28
  64.5 9.3 %collective-permute-start.12 = (bf16[2,112,768]{2,1,0:T(8,128)(2,1)S(1)}, bf16[2,112,768]{2,1,0:T(8,128)(2,1)}, u32[]{:S(2)}, u32[]{:S(2)}) collective-permute-start(bf16[2,112,768]{2,1,0:T(8,128)(2,1)S(1)} %collective-permute-done.4.refs_2_), channel_id=1, source_target_pairs={{0,1},{1,0},{2,3},{3,2},{4,5},{5,4},{6,7},{7,6},{8,9},{9,8},{10,11... | collective-permute-start | bytes 1032200 | tf_op jit(solution)/shard_map/ppermute | solution.py:28
  65.5 22.8 %collective-permute-start = (bf16[256,768]{1,0:T(8,128)(2,1)}, bf16[256,768]{1,0:T(8,128)(2,1)}, u32[]{:S(2)}, u32[]{:S(2)}) collective-permute-start(bf16[256,768]{1,0:T(8,128)(2,1)} %x0.3), channel_id=1, source_target_pairs={{0,1},{1,0},{2,3},{3,2},{4,5},{5,4},{6,7},{7,6},{8,9},{9,8},{10,11... | collective-permute-start | bytes 1179656 | tf_op jit(solution)/shard_map/ppermute | solution.py:28
  69.2 6.9 %collective-permute-start.17 = (bf16[2,112,768]{2,1,0:T(8,128)(2,1)}, bf16[2,112,768]{2,1,0:T(8,128)(2,1)}, u32[]{:S(2)}, u32[]{:S(2)}) collective-permute-start(bf16[2,112,768]{2,1,0:T(8,128)(2,1)} %collective-permute-done.9.refs_7_), channel_id=1, source_target_pairs={{0,1},{1,0},{2,3},{3,2},{4,5},{5,4},{6,7},{7,6},{8,9},{9,8},{10,11... | collective-permute-start | bytes 1032200 | tf_op jit(solution)/shard_map/ppermute | solution.py:28
  71.5 5.2 %collective-permute-start.16 = (bf16[2,112,768]{2,1,0:T(8,128)(2,1)}, bf16[2,112,768]{2,1,0:T(8,128)(2,1)}, u32[]{:S(2)}, u32[]{:S(2)}) collective-permute-start(bf16[2,112,768]{2,1,0:T(8,128)(2,1)} %collective-permute-done.8.refs_6_), channel_id=1, source_target_pairs={{0,1},{1,0},{2,3},{3,2},{4,5},{5,4},{6,7},{7,6},{8,9},{9,8},{10,11... | collective-permute-start | bytes 1032200 | tf_op jit(solution)/shard_map/ppermute | solution.py:28
  72.3 35.6 %collective-permute-start.23 = (bf16[2,192,768]{2,1,0:T(8,128)(2,1)S(1)}, bf16[2,192,768]{2,1,0:T(8,128)(2,1)S(1)}, u32[]{:S(2)}, u32[]{:S(2)}) collective-permute-start(bf16[2,192,768]{2,1,0:T(8,128)(2,1)S(1)} %pad_maximum_fusion.w0), channel_id=1, source_target_pairs={{0,4},{4,0},{8,12},{12,8},{16,20},{20,16},{24,28},{28,24},{1,5},{5... | collective-permute-start | bytes 1769480 | tf_op jit(solution)/shard_map/ppermute | solution.py:36
  73.8 35.6 %collective-permute-start.25 = (bf16[2,192,768]{2,1,0:T(8,128)(2,1)S(1)}, bf16[2,192,768]{2,1,0:T(8,128)(2,1)S(1)}, u32[]{:S(2)}, u32[]{:S(2)}) collective-permute-start(bf16[2,192,768]{2,1,0:T(8,128)(2,1)S(1)} %pad_maximum_fusion.1.w1), channel_id=1, source_target_pairs={{0,2},{1,3},{2,0},{3,1},{4,6},{5,7},{6,4},{7,5},{8,10},{9,11},{10,... | collective-permute-start | bytes 1769480 | tf_op jit(solution)/shard_map/ppermute | solution.py:32
  76.1 36.3 %collective-permute-start.28 = (bf16[2,192,768]{2,1,0:T(8,128)(2,1)S(1)}, bf16[2,192,768]{2,1,0:T(8,128)(2,1)}, u32[]{:S(2)}, u32[]{:S(2)}) collective-permute-start(bf16[2,192,768]{2,1,0:T(8,128)(2,1)S(1)} %pad_maximum_fusion.w0), channel_id=1, source_target_pairs={{0,2},{1,3},{2,0},{3,1},{4,6},{5,7},{6,4},{7,5},{8,10},{9,11},{10,... | collective-permute-start | bytes 1769480 | tf_op jit(solution)/shard_map/ppermute | solution.py:32
  101.4 16.3 %collective-permute-start.27 = (bf16[2,192,768]{2,1,0:T(8,128)(2,1)S(1)}, bf16[2,192,768]{2,1,0:T(8,128)(2,1)}, u32[]{:S(2)}, u32[]{:S(2)}) collective-permute-start(bf16[2,192,768]{2,1,0:T(8,128)(2,1)S(1)} %pad_maximum_fusion.1.w1), channel_id=1, source_target_pairs={{0,4},{4,0},{8,12},{12,8},{16,20},{20,16},{24,28},{28,24},{1,5},{5... | collective-permute-start | bytes 1769480 | tf_op jit(solution)/shard_map/ppermute | solution.py:36
  107.9 15.7 %collective-permute-start.24 = (bf16[2,192,768]{2,1,0:T(8,128)(2,1)S(1)}, bf16[2,192,768]{2,1,0:T(8,128)(2,1)}, u32[]{:S(2)}, u32[]{:S(2)}) collective-permute-start(bf16[2,192,768]{2,1,0:T(8,128)(2,1)S(1)} %collective-permute-done.23.w0), channel_id=1, source_target_pairs={{0,2},{1,3},{2,0},{3,1},{4,6},{5,7},{6,4},{7,5},{8,10},{9,11},{10,... | collective-permute-start | bytes 1769480 | tf_op jit(solution)/shard_map/ppermute | solution.py:32
  109.4 20.6 %collective-permute-start.26 = (bf16[2,192,768]{2,1,0:T(8,128)(2,1)S(1)}, bf16[2,192,768]{2,1,0:T(8,128)(2,1)}, u32[]{:S(2)}, u32[]{:S(2)}) collective-permute-start(bf16[2,192,768]{2,1,0:T(8,128)(2,1)S(1)} %collective-permute-done.25.w1), channel_id=1, source_target_pairs={{0,4},{4,0},{8,12},{12,8},{16,20},{20,16},{24,28},{28,24},{1,5},{5... | collective-permute-start | bytes 1769480 | tf_op jit(solution)/shard_map/ppermute | solution.py:36
  151.8 16.2 %collective-permute-start.44 = (bf16[2,192,768]{2,1,0:T(8,128)(2,1)S(1)}, bf16[2,192,768]{2,1,0:T(8,128)(2,1)S(1)}, u32[]{:S(2)}, u32[]{:S(2)}) collective-permute-start(bf16[2,192,768]{2,1,0:T(8,128)(2,1)S(1)} %get-tuple-element.171), channel_id=1, source_target_pairs={{0,4},{4,0},{8,12},{12,8},{16,20},{20,16},{24,28},{28,24},{1,5},{5... | collective-permute-start | bytes 1769480 | tf_op jit(solution)/shard_map/ppermute | solution.py:36
  152.3 18.1 %collective-permute-start.46 = (bf16[2,192,768]{2,1,0:T(8,128)(2,1)S(1)}, bf16[2,192,768]{2,1,0:T(8,128)(2,1)S(1)}, u32[]{:S(2)}, u32[]{:S(2)}) collective-permute-start(bf16[2,192,768]{2,1,0:T(8,128)(2,1)S(1)} %get-tuple-element.173), channel_id=1, source_target_pairs={{0,2},{1,3},{2,0},{3,1},{4,6},{5,7},{6,4},{7,5},{8,10},{9,11},{10,... | collective-permute-start | bytes 1769480 | tf_op jit(solution)/shard_map/ppermute | solution.py:32
  153.8 34.9 %collective-permute-start.43 = (bf16[2,192,768]{2,1,0:T(8,128)(2,1)}, bf16[2,192,768]{2,1,0:T(8,128)(2,1)S(1)}, u32[]{:S(2)}, u32[]{:S(2)}) collective-permute-start(bf16[2,192,768]{2,1,0:T(8,128)(2,1)} %get-tuple-element.169), channel_id=1, source_target_pairs={{0,2},{1,3},{2,0},{3,1},{4,6},{5,7},{6,4},{7,5},{8,10},{9,11},{10,... | collective-permute-start | bytes 1769480 | tf_op jit(solution)/shard_map/ppermute | solution.py:32
  154.3 35.9 %collective-permute-start.48 = (bf16[2,192,768]{2,1,0:T(8,128)(2,1)}, bf16[2,192,768]{2,1,0:T(8,128)(2,1)}, u32[]{:S(2)}, u32[]{:S(2)}) collective-permute-start(bf16[2,192,768]{2,1,0:T(8,128)(2,1)} %get-tuple-element.174), channel_id=1, source_target_pairs={{0,4},{4,0},{8,12},{12,8},{16,20},{20,16},{24,28},{28,24},{1,5},{5... | collective-permute-start | bytes 1769480 | tf_op jit(solution)/shard_map/ppermute | solution.py:36
  157.0 14.9 %collective-permute-start.32 = (bf16[256,768]{1,0:T(8,128)(2,1)S(1)}, bf16[256,768]{1,0:T(8,128)(2,1)S(1)}, u32[]{:S(2)}, u32[]{:S(2)}) collective-permute-start(bf16[256,768]{1,0:T(8,128)(2,1)S(1)} %get-tuple-element.138.a0), channel_id=1, source_target_pairs={{0,1},{1,0},{2,3},{3,2},{4,5},{5,4},{6,7},{7,6},{8,9},{9,8},{10,11... | collective-permute-start | bytes 1179656 | tf_op jit(solution)/shard_map/ppermute | solution.py:28
  168.9 24.9 %collective-permute-start.45 = (bf16[2,192,768]{2,1,0:T(8,128)(2,1)}, bf16[2,192,768]{2,1,0:T(8,128)(2,1)}, u32[]{:S(2)}, u32[]{:S(2)}) collective-permute-start(bf16[2,192,768]{2,1,0:T(8,128)(2,1)} %add_convert_fusion.1), channel_id=1, source_target_pairs={{0,2},{1,3},{2,0},{3,1},{4,6},{5,7},{6,4},{7,5},{8,10},{9,11},{10,... | collective-permute-start | bytes 1769480 | tf_op jit(solution)/shard_map/ppermute | solution.py:32
  171.4 22.5 %collective-permute-start.47 = (bf16[2,192,768]{2,1,0:T(8,128)(2,1)}, bf16[2,192,768]{2,1,0:T(8,128)(2,1)}, u32[]{:S(2)}, u32[]{:S(2)}) collective-permute-start(bf16[2,192,768]{2,1,0:T(8,128)(2,1)} %add_convert_fusion), channel_id=1, source_target_pairs={{0,4},{4,0},{8,12},{12,8},{16,20},{20,16},{24,28},{28,24},{1,5},{5... | collective-permute-start | bytes 1769480 | tf_op jit(solution)/shard_map/ppermute | solution.py:36
  187.1 13.5 %collective-permute-start.35 = (bf16[2,96,768]{2,1,0:T(8,128)(2,1)}, bf16[2,96,768]{2,1,0:T(8,128)(2,1)}, u32[]{:S(2)}, u32[]{:S(2)}) collective-permute-start(bf16[2,96,768]{2,1,0:T(8,128)(2,1)} %get-tuple-element.150), channel_id=1, source_target_pairs={{0,4},{4,0},{8,12},{12,8},{16,20},{20,16},{24,28},{28,24},{1,5},{5... | collective-permute-start | bytes 884744 | tf_op jit(solution)/shard_map/ppermute | solution.py:36
  189.5 12.9 %collective-permute-start.37 = (bf16[2,96,768]{2,1,0:T(8,128)(2,1)}, bf16[2,96,768]{2,1,0:T(8,128)(2,1)S(1)}, u32[]{:S(2)}, u32[]{:S(2)}) collective-permute-start(bf16[2,96,768]{2,1,0:T(8,128)(2,1)} %copy-done.49), channel_id=1, source_target_pairs={{0,2},{1,3},{2,0},{3,1},{4,6},{5,7},{6,4},{7,5},{8,10},{9,11},{10,... | collective-permute-start | bytes 884744 | tf_op jit(solution)/shard_map/ppermute | solution.py:32
  197.5 33.1 %collective-permute-start.49 = (bf16[192,768]{1,0:T(8,128)(2,1)}, bf16[192,768]{1,0:T(8,128)(2,1)S(1)}, u32[]{:S(2)}, u32[]{:S(2)}) collective-permute-start(bf16[192,768]{1,0:T(8,128)(2,1)} %get-tuple-element.176), channel_id=1, source_target_pairs={{0,8},{4,12},{8,0},{12,4},{16,24},{20,28},{24,16},{28,20},{1,9},{5... | collective-permute-start | bytes 884744 | tf_op jit(solution)/shard_map/ppermute | solution.py:40
  197.5 8.0 %collective-permute-start.34 = (bf16[2,96,768]{2,1,0:T(8,128)(2,1)S(1)}, bf16[2,96,768]{2,1,0:T(8,128)(2,1)S(1)}, u32[]{:S(2)}, u32[]{:S(2)}) collective-permute-start(bf16[2,96,768]{2,1,0:T(8,128)(2,1)S(1)} %copy-done.48), channel_id=1, source_target_pairs={{0,2},{1,3},{2,0},{3,1},{4,6},{5,7},{6,4},{7,5},{8,10},{9,11},{10,... | collective-permute-start | bytes 884744 | tf_op jit(solution)/shard_map/ppermute | solution.py:32
  199.1 8.6 %collective-permute-start.39 = (bf16[2,96,768]{2,1,0:T(8,128)(2,1)S(1)}, bf16[2,96,768]{2,1,0:T(8,128)(2,1)S(1)}, u32[]{:S(2)}, u32[]{:S(2)}) collective-permute-start(bf16[2,96,768]{2,1,0:T(8,128)(2,1)S(1)} %copy-done.46), channel_id=1, source_target_pairs={{0,4},{4,0},{8,12},{12,8},{16,20},{20,16},{24,28},{28,24},{1,5},{5... | collective-permute-start | bytes 884744 | tf_op jit(solution)/shard_map/ppermute | solution.py:36
  200.6 46.7 %collective-permute-start.33 = (f32[256,768]{1,0:T(8,128)}, f32[256,768]{1,0:T(8,128)}, u32[]{:S(2)}, u32[]{:S(2)}) collective-permute-start(f32[256,768]{1,0:T(8,128)} %get-tuple-element.145), channel_id=1, source_target_pairs={{0,1},{1,0},{2,3},{3,2},{4,5},{5,4},{6,7},{7,6},{8,9},{9,8},{10,11... | collective-permute-start | bytes 2359304 | tf_op jit(solution)/shard_map/ppermute | solution.py:28
  202.4 15.5 %collective-permute-start.36 = (bf16[2,96,768]{2,1,0:T(8,128)(2,1)}, bf16[2,96,768]{2,1,0:T(8,128)(2,1)}, u32[]{:S(2)}, u32[]{:S(2)}) collective-permute-start(bf16[2,96,768]{2,1,0:T(8,128)(2,1)} %add_convert_fusion.4), channel_id=1, source_target_pairs={{0,2},{1,3},{2,0},{3,1},{4,6},{5,7},{6,4},{7,5},{8,10},{9,11},{10,... | collective-permute-start | bytes 884744 | tf_op jit(solution)/shard_map/ppermute | solution.py:32
  205.5 25.5 %collective-permute-start.50 = (bf16[192,768]{1,0:T(8,128)(2,1)}, bf16[192,768]{1,0:T(8,128)(2,1)}, u32[]{:S(2)}, u32[]{:S(2)}) collective-permute-start(bf16[192,768]{1,0:T(8,128)(2,1)} %get-tuple-element.177), channel_id=1, source_target_pairs={{0,16},{4,20},{8,24},{12,28},{16,0},{20,4},{24,8},{28,12},{1,17},{... | collective-permute-start | bytes 884744 | tf_op jit(solution)/shard_map/ppermute | solution.py:40
  208.4 17.8 %collective-permute-start.38 = (bf16[2,96,768]{2,1,0:T(8,128)(2,1)}, bf16[2,96,768]{2,1,0:T(8,128)(2,1)}, u32[]{:S(2)}, u32[]{:S(2)}) collective-permute-start(bf16[2,96,768]{2,1,0:T(8,128)(2,1)} %add_convert_fusion.3), channel_id=1, source_target_pairs={{0,4},{4,0},{8,12},{12,8},{16,20},{20,16},{24,28},{28,24},{1,5},{5... | collective-permute-start | bytes 884744 | tf_op jit(solution)/shard_map/ppermute | solution.py:36
  214.0 11.5 %all-to-all-start = ((f32[32,1,288]{2,1,0:T(1,128)}), f32[32,1,288]{2,1,0:T(1,128)S(1)}, u32[]{:S(2)}, u32[]{:S(2)}) async-start(f32[32,1,288]{2,1,0:T(1,128)} %copy.42), calls=%async_computation | async-start | bytes 98304 | tf_op jit(solution)/shard_map/all_to_all | solution.py:737
  218.0 17.0 %collective-permute-start.51 = (bf16[192,768]{1,0:T(8,128)(2,1)}, bf16[192,768]{1,0:T(8,128)(2,1)}, u32[]{:S(2)}, u32[]{:S(2)}) collective-permute-start(bf16[192,768]{1,0:T(8,128)(2,1)} %copy-done.44), channel_id=1, source_target_pairs={{0,24},{4,28},{8,16},{12,20},{16,8},{20,12},{24,0},{28,4},{1,25},{... | collective-permute-start | bytes 884744 | tf_op jit(solution)/shard_map/ppermute | solution.py:40
  229.9 7.9 %collective-permute-start.40 = (bf16[96,768]{1,0:T(8,128)(2,1)}, bf16[96,768]{1,0:T(8,128)(2,1)S(1)}, u32[]{:S(2)}, u32[]{:S(2)}) collective-permute-start(bf16[96,768]{1,0:T(8,128)(2,1)} %get-tuple-element.155), channel_id=1, source_target_pairs={{0,8},{4,12},{8,0},{12,4},{16,24},{20,28},{24,16},{28,20},{1,9},{5... | collective-permute-start | bytes 442376 | tf_op jit(solution)/shard_map/ppermute | solution.py:40
  230.6 14.9 %collective-permute-start.41 = (bf16[96,768]{1,0:T(8,128)(2,1)}, bf16[96,768]{1,0:T(8,128)(2,1)S(1)}, u32[]{:S(2)}, u32[]{:S(2)}) collective-permute-start(bf16[96,768]{1,0:T(8,128)(2,1)} %get-tuple-element.156), channel_id=1, source_target_pairs={{0,16},{4,20},{8,24},{12,28},{16,0},{20,4},{24,8},{28,12},{1,17},{... | collective-permute-start | bytes 442376 | tf_op jit(solution)/shard_map/ppermute | solution.py:40
  231.0 14.4 %collective-permute-start.42 = (bf16[96,768]{1,0:T(8,128)(2,1)}, bf16[96,768]{1,0:T(8,128)(2,1)}, u32[]{:S(2)}, u32[]{:S(2)}) collective-permute-start(bf16[96,768]{1,0:T(8,128)(2,1)} %get-tuple-element.157), channel_id=1, source_target_pairs={{0,24},{4,28},{8,16},{12,20},{16,8},{20,12},{24,0},{28,4},{1,25},{... | collective-permute-start | bytes 442376 | tf_op jit(solution)/shard_map/ppermute | solution.py:40
  (79 other events, 611.9 us)
where the time goes:
time: 251 us; the launch traced here: 249 us
  waiting for transfers between devices  86.3 us (34%)
  Pallas kernels  55 us (22%)
  starting transfers between devices  54.1 us (22%)
  local copies, waits for them, and re-layouts  42.1 us (17%)
  other arithmetic  10.2 us (4%)
    pallas_call x18, Pallas kernels, call(): pl.pallas_call(kernel, out_shape=out_shape, in_specs=[pl.BlockSpec(memory...  55 us
    ppermute x12, waiting for transfers between devices, z_swap(): return lax.ppermute(v, 'batch', ZPAIR[k])  39.5 us
    unnamed x149, local copies, waits for them, and re-layouts  32.3 us
    ppermute x12, waiting for transfers between devices, y_swap(): return lax.ppermute(v, 'batch', YPAIR)  27.2 us
    ppermute x12, starting transfers between devices, z_swap(): return lax.ppermute(v, 'batch', ZPAIR[k])  20.5 us
    ppermute x12, starting transfers between devices, x_swap(): return lax.ppermute(v, 'head', XPAIR)  14.2 us
    ppermute x12, starting transfers between devices, y_swap(): return lax.ppermute(v, 'batch', YPAIR)  13.6 us
    ppermute x12, waiting for transfers between devices, x_swap(): return lax.ppermute(v, 'head', XPAIR)  11.1 us
  transfers between devices with their start and end apart: 53, of which 17 were waited for; matrix products, arithmetic and copies ran while one was open for 6% of the time, Pallas kernels for 15%

commit v1 on v0

--- a/solution.py
+++ b/solution.py
@@ -56,9 +56,13 @@
     return lax.dot_general(a, b, (((0,), (0,)), ((), ())), preferred_element_type=F32).astype(out)
 
 
-def gather_z(shard):
-    got = [shard] + [z_swap(shard, k) for k in (1, 2, 3)]
-    return jnp.stack(got[:2]), jnp.stack(got[2:])
+def z_line(shard):
+    return [shard] + [z_swap(shard, k) for k in (1, 2, 3)]
+
+
+def gather_four(z):
+    x, y = x_swap(z), y_swap(z)
+    return [z, x, y, x_swap(y[:2]), y_swap(x[2:])]
 
 
 def gather_xy(lo, hi):
@@ -72,11 +76,16 @@
     return [whole, x_swap(whole)]
 
 
-def scatter_xy(parts):
+def scatter_first(parts):
     (g_lo, g_hi), (x_lo, x_hi), (y_lo, y_hi), (d_lo, d_hi) = parts
     from_x, from_y = x_swap(d_lo), y_swap(d_hi)
+    y_lo, x_hi = add_low(y_lo, from_x), add_low(x_hi, from_y)
+    return (g_lo, g_hi, x_lo, x_hi, y_lo, y_hi), (y_lo, x_hi)
+
+
+def scatter_xy(g_lo, g_hi, x_lo, x_hi, y_lo, y_hi):
     y_hi, x_lo = y_swap(y_hi), x_swap(x_lo)
-    y_lo, x_hi = y_swap(add_low(y_lo, from_x)), x_swap(add_low(x_hi, from_y))
+    y_lo, x_hi = y_swap(y_lo), x_swap(x_hi)
     return combine(g_lo, g_hi, x_lo, x_hi, y_lo, y_hi)
 
 
@@ -93,18 +102,46 @@
     return pl.CostEstimate(flops=int(flops), bytes_accessed=int(moved), transcendentals=int(trans))
 
 
-def call(kernel, out_shape, operands, scratch=(), cost=None, limit=16):
+def call(kernel, out_shape, operands, scratch=(), cost=None, limit=16, far_in=(), far_out=(), sems=0):
     vmem = pl.BlockSpec(memory_space=pltpu.VMEM)
-    single = not isinstance(out_shape, (tuple, list))
+    hbm = pl.BlockSpec(memory_space=pltpu.HBM)
+    smem = pl.BlockSpec(memory_space=pltpu.SMEM)
+    ins = [smem] + [hbm if i in far_in else vmem for i in range(1, len(operands))]
+    outs = [hbm if i in far_out else vmem for i in range(len(out_shape))]
+    scratch = list(scratch) + ([pltpu.SemaphoreType.DMA((sems,))] if sems else [])
+    operands = [
+        pltpu.with_memory_space_constraint(v, pltpu.HBM) if i in far_in else v
+        for i, v in enumerate(operands)
+    ]
+    out_shape = [
+        pltpu.HBM(v.shape, v.dtype) if i in far_out else v for i, v in enumerate(out_shape)
+    ]
     return pl.pallas_call(
         kernel,
         out_shape=out_shape,
-        in_specs=[pl.BlockSpec(memory_space=pltpu.SMEM)] + [vmem] * (len(operands) - 1),
-        out_specs=vmem if single else [vmem] * len(out_shape),
-        scratch_shapes=list(scratch),
+        in_specs=ins,
+        out_specs=outs,
+        scratch_shapes=scratch,
         compiler_params=pltpu.CompilerParams(vmem_limit_bytes=limit << 20),
         cost_estimate=cost,
     )(*operands)
+
+
+class Copies:
+    def __init__(self, sems):
+        self.sems, self.used, self.open = sems, 0, []
+
+    def start(self, src, dst):
+        copy = pltpu.make_async_copy(src, dst, self.sems.at[self.used])
+        self.used += 1
+        copy.start()
+        self.open.append(copy)
+        return copy
+
+    def wait(self, *copies):
+        for copy in copies or list(self.open):
+            copy.wait()
+            self.open.remove(copy)
 
 
 def add_low(a, b):
@@ -176,41 +213,6 @@
 
 def flip(a, bit):
     return a + bit - 2 * a * bit
-
-
-def order_kernel(rows_q, rows_p, place, *refs):
-    sources, (wq, wp, small) = refs[:16], refs[16:]
-    z, y, x, c = place[0], place[1], place[2], place[3]
-    zl, zh = lax.rem(z, 2), lax.div(z, 2)
-    p = flip(c, zl)
-    total = jnp.zeros(small.shape, F32)
-    for swapped in range(2):
-        cc = c if swapped == 0 else 1 - c
-        for spot in range(4):
-            kx, ky = spot % 2, spot // 2
-            pair = sources[8 * swapped + 2 * spot : 8 * swapped + 2 * spot + 2]
-            j = flip(y, ky) * 4 + flip(x, kx) * 2 + cc
-            for i in range(2):
-                wq[flip(zh, i) * 8 + j] = pair[i][p, 0:rows_q]
-            for kz in range(4):
-                zi = flip(zl, kz % 2) + 2 * flip(zh, kz // 2)
-                src = pair[kz // 2]
-                wp[zi * 8 + j] = src[kz % 2, rows_q : rows_q + rows_p]
-                total = total + src[kz % 2, rows_q + rows_p :].astype(F32)
-    small[...] = total
-
-
-def order_weights(own, swapped, place, rows_q, rows_p, rows_s):
-    return call(
-        functools.partial(order_kernel, rows_q, rows_p),
-        (
-            shape((16, rows_q, D)),
-            shape((32, rows_p, D)),
-            shape((rows_s, D), F32),
-        ),
-        (place, *own, *swapped),
-        cost=est(1e6, 9e6),
-    )
 
 
 def live_units(meta):
@@ -245,21 +247,39 @@
     return jnp.concatenate(parts, 1)
 
 
-def attend_kernel(meta, x0, x1, w, small, q, k, v, ctx0, ctx1, probs, wr, mask):
+def fetch_shards(meta, copies, sources, slots):
+    c, z, y, x = meta[0], meta[6], meta[7], meta[8]
+    zl, zh = lax.rem(z, 2), lax.div(z, 2)
+    for swapped in range(2):
+        cc = c if swapped == 0 else 1 - c
+        zs, xs, ys, xa, xb = sources[5 * swapped : 5 * swapped + 5]
+        for kx, ky, pair in ((0, 0, (zs,)), (1, 0, (xs,)), (0, 1, (ys,)), (1, 1, (xa, xb))):
+            j = flip(y, ky) * 4 + flip(x, kx) * 2 + cc
+            for kz in range(4):
+                src = pair[0].at[kz] if len(pair) == 1 else pair[kz // 2].at[kz % 2]
+                zi = flip(zl, kz % 2) + 2 * flip(zh, kz // 2)
+                copies.start(src, slots.at[zi * 8 + j])
+
+
+def attend_kernel(rows_q, rows_p, meta, x0, x1, *refs):
+    sources = 10 if rows_q else 2
+    weights, refs = refs[:sources], refs[sources:]
+    (ctx0, ctx1, q_out, k_out, v_out, ctx_out, probs_out, wr_out), refs = refs[:8], refs[8:]
+    if rows_q:
+        (wp_out, small_out), refs = refs[:2], refs[2:]
+        (q, k, v, ctx, probs, wr, mask, xs, slots, wp, small, sems) = refs
+    else:
+        (q, k, v, ctx, probs, wr, mask, xs, w, small, sems) = refs
+    copies = Copies(sems)
     c, kind, units = live_units(meta)
     half = x0.shape[0]
-    for t in range(3):
-        for hd in range(6):
-            src = ((hd // 3) * 9 + (hd % 3) * 3 + t) * HEAD_DIM
-            dst = (t * 6 + hd) * HEAD_DIM
-            wr[dst : dst + HEAD_DIM] = w[src : src + HEAD_DIM]
-    biases = (heads_of(small[0:1], c), None, heads_of(small[1:2], c))
-    for t, ref in enumerate((q, k, v)):
-        for i, xr in enumerate((x0, x1)):
-            val = nt(xr[...], wr[384 * t : 384 * t + 384])
-            if biases[t] is not None:
-                val = val + biases[t]
-            ref[half * i : half * i + half] = val.astype(BF16)
+    copies.start(x0, xs.at[0:half])
+    copies.start(x1, xs.at[half : 2 * half])
+    if rows_q:
+        fetch_shards(meta, copies, weights, slots)
+    else:
+        copies.start(weights[0], w)
+        copies.start(weights[1], small)
     rows = lax.broadcasted_iota(jnp.int32, (BIG, BIG), 0)
     cols = lax.broadcasted_iota(jnp.int32, (BIG, BIG), 1)
     prow, pcol = place_of(rows, c), place_of(cols, c)
@@ -267,11 +287,39 @@
         kind == 1, lax.shift_right_logical(prow, 7) == lax.shift_right_logical(pcol, 7)
     )
     mask[...] = jnp.where(jnp.logical_and(same, live_of(pcol, units)), 0.0, -1e30)
+    copies.wait()
+    if rows_q:
+        for g in range(2):
+            cuts = jnp.concatenate([slots[16 * g + 8 * c + j, 0:rows_q] for j in range(8)])
+            for t in range(3):
+                for hh in range(3):
+                    src, dst = (hh * 3 + t) * HEAD_DIM, (t * 6 + g * 3 + hh) * HEAD_DIM
+                    wr[dst : dst + HEAD_DIM] = cuts[src : src + HEAD_DIM]
+        small[...] = sum(slots[i, rows_q + rows_p :].astype(F32) for i in range(32))
+    else:
+        for t in range(3):
+            for hd in range(6):
+                src = ((hd // 3) * 9 + (hd % 3) * 3 + t) * HEAD_DIM
+                dst = (t * 6 + hd) * HEAD_DIM
+                wr[dst : dst + HEAD_DIM] = w[src : src + HEAD_DIM]
+    copies.start(wr, wr_out)
+    biases = (heads_of(small[0:1], c), None, heads_of(small[1:2], c))
+    for t, (ref, out) in enumerate(((q, q_out), (k, k_out), (v, v_out))):
+        val = nt(xs[...], wr[384 * t : 384 * t + 384])
+        if biases[t] is not None:
+            val = val + biases[t]
+        ref[...] = val.astype(BF16)
+        copies.start(ref, out)
+    if rows_q:
+        for i in range(32):
+            wp[rows_p * i : rows_p * i + rows_p] = slots[i, rows_q : rows_q + rows_p]
+        copies.start(wp, wp_out)
+        copies.start(small, small_out)
     lane = lax.broadcasted_iota(jnp.int32, (half, 128), 1)
     for pair in range(3):
         lanes = slice(128 * pair, 128 * pair + 128)
         kp, vp = k[:, lanes], v[:, lanes]
-        for i, ctx in enumerate((ctx0, ctx1)):
+        for i, near in enumerate((ctx0, ctx1)):
             rws = slice(half * i, half * i + half)
             qp = q[rws, lanes] * jnp.asarray(HEAD_DIM**-0.5, BF16)
             outs = []
@@ -282,26 +330,55 @@
                 pr = (ex * (1.0 / jnp.sum(ex, -1, keepdims=True))).astype(BF16)
                 probs[2 * pair + e, rws] = pr
                 outs.append(nn(pr, vp))
-            ctx[:, lanes] = jnp.where(lane < HEAD_DIM, outs[0], outs[1]).astype(BF16)
-
-
-def attend(meta, x0, x1, w, small):
+            val = jnp.where(lane < HEAD_DIM, outs[0], outs[1]).astype(BF16)
+            ctx[rws, lanes] = val
+            near[:, lanes] = val
+        for e in range(2):
+            copies.start(probs.at[2 * pair + e], probs_out.at[2 * pair + e])
+    copies.start(ctx, ctx_out)
+    copies.wait()
+
+
+def attend(meta, x0, x1, weights, rows_q=0, rows_p=0, rows_s=16):
     half = x0.shape[0]
     n = 2 * half
+    direct = rows_q > 0
+    outs = [
+        shape((half, 384)),
+        shape((half, 384)),
+        shape((n, 384)),
+        shape((n, 384)),
+        shape((n, 384)),
+        shape((n, 384)),
+        shape((6, n, n)),
+        shape((1152, D)),
+    ]
+    scratch = [pltpu.VMEM((n, 384), BF16)] * 4 + [
+        pltpu.VMEM((6, n, n), BF16),
+        pltpu.VMEM((1152, D), BF16),
+        pltpu.VMEM((n, n), F32),
+        pltpu.VMEM((n, D), BF16),
+    ]
+    if direct:
+        outs += [shape((D, D)), shape((rows_s, D), F32)]
+        scratch += [
+            pltpu.VMEM((32, rows_q + rows_p + rows_s, D), BF16),
+            pltpu.VMEM((D, D), BF16),
+            pltpu.VMEM((rows_s, D), F32),
+        ]
+    else:
+        scratch += [pltpu.VMEM((1152, D), BF16), pltpu.VMEM((rows_s, D), F32)]
+    operands = (meta, x0, x1, *weights)
     return call(
-        attend_kernel,
-        (
-            shape((n, 384)),
-            shape((n, 384)),
-            shape((n, 384)),
-            shape((half, 384)),
-            shape((half, 384)),
-            shape((6, n, n)),
-            shape((1152, D)),
-        ),
-        (meta, x0, x1, w, small),
-        scratch=[pltpu.VMEM((n, n), F32)],
-        cost=est(2 * n * D * 1152 + 8 * n * n * 384, 9e6, 6 * n * n),
+        functools.partial(attend_kernel, rows_q, rows_p),
+        outs,
+        operands,
+        scratch=scratch,
+        cost=est(2 * n * D * 1152 + 8 * n * n * 384, 12e6, 6 * n * n),
+        limit=32,
+        far_in=range(1, len(operands)),
+        far_out=range(2, len(outs)),
+        sems=50,
     )
 
 
@@ -319,26 +396,45 @@
     )
 
 
-def first_kernel(meta, x, ctx_own, ctx_in, wp, small, first, low, normal, scale):
+def first_kernel(
+    meta, x_in, ctx_own, ctx_in, wp_in, small_in, low, first_out, normal_out, scale, x, wp, small, first, normal, sems
+):
+    copies = Copies(sems)
+    for src, dst in ((wp_in, wp), (x_in, x), (small_in, small)):
+        copies.start(src, dst)
     c = meta[0]
+    copies.wait()
     mine = pl.multiple_of(c * 384, 128)
     theirs = pl.multiple_of((1 - c) * 384, 128)
     attn = nt(ctx_own[...], wp[:, pl.ds(mine, 384)]) + nt(ctx_in[...], wp[:, pl.ds(theirs, 384)])
     n, r = norm(x[...].astype(F32) + attn + small[2:3])
+    normal[...] = n
+    copies.start(normal, normal_out)
     out = n * small[3:4] + small[4:5]
     first[...] = out
+    copies.start(first, first_out)
     low[...] = out.astype(BF16)
-    normal[...] = n
     scale[...] = jnp.broadcast_to(r, scale.shape)
+    copies.wait()
 
 
 def first_norm(meta, x, ctx_own, ctx_in, wp, small):
     n = x.shape[0]
     return call(
         first_kernel,
-        (shape((n, D), F32), shape((n, D)), shape((n, D), F32), shape((n, 128), F32)),
+        (shape((n, D)), shape((n, D), F32), shape((n, D), F32), shape((n, 128), F32)),
         (meta, x, ctx_own, ctx_in, wp, small),
+        scratch=[
+            pltpu.VMEM((n, D), BF16),
+            pltpu.VMEM((D, D), BF16),
+            pltpu.VMEM((16, D), F32),
+            pltpu.VMEM((n, D), F32),
+            pltpu.VMEM((n, D), F32),
+        ],
         cost=est(2 * n * D * D, 5e6),
+        far_in=(1, 4, 5),
+        far_out=(1, 2),
+        sems=5,
     )
 
 
@@ -352,12 +448,16 @@
     return up, down
 
 
-def ffn_kernel(first, meta, x0, x1, ub, w0, w1, *refs):
+def ffn_kernel(first, meta, x0, x1, ub, w0_in, w1_in, *refs):
     if first:
         in0 = in1 = None
     else:
         (in0, in1), refs = refs[:2], refs[2:]
-    hid, slope, out0, out1 = refs
+    hid_out, slope_out, out0, out1, w0, w1, hid, slope, sems = refs
+    copies = Copies(sems)
+    copies.start(w0_in, w0)
+    copies.start(w1_in, w1)
+    copies.wait()
     half = x0.shape[0]
     uw, dw = ffn_weights((w0, w1))
     for i, (xr, before, out) in enumerate(((x0, in0, out0), (x1, in1, out1))):
@@ -367,8 +467,11 @@
         hd = (up * phi).astype(BF16)
         hid[rws] = hd
         slope[rws] = (phi + up * jnp.exp(-0.5 * up * up) * 0.3989422804014327).astype(BF16)
+        copies.start(hid.at[rws], hid_out.at[rws])
+        copies.start(slope.at[rws], slope_out.at[rws])
         part = nn(hd, dw)
         out[...] = part if before is None else before[...] + part
+    copies.wait()
 
 
 def ffn(meta, x0, x1, ub, weights, sums):
@@ -378,12 +481,22 @@
         functools.partial(ffn_kernel, not sums),
         (shape((n, width)), shape((n, width)), shape((half, D), F32), shape((half, D), F32)),
         (meta, x0, x1, ub, *weights, *sums),
+        scratch=[pltpu.VMEM(w.shape, BF16) for w in weights] + [pltpu.VMEM((n, width), BF16)] * 2,
         cost=est(4 * n * D * width, 4 * D * width + 5e6, 2 * n * width),
-    )
-
-
-def second_kernel(meta, first, part, got, small, cot, out, sum_two, low, sums):
+        far_in=(4, 5),
+        far_out=(0, 1),
+        sems=6,
+    )
+
+
+def second_kernel(
+    meta, first_in, part, got, small_in, cot_in, out, sum_two, low, sums, first, small, cot, sems
+):
+    copies = Copies(sems)
+    for src, dst in ((first_in, first), (small_in, small), (cot_in, cot)):
+        copies.start(src, dst)
     c, _, units = live_units(meta)
+    copies.wait()
     n, r = norm(first[...] + (part[...] + got[...] + small[5:6]))
     out[...] = (n * small[6:7] + small[7:8]).astype(BF16)
     index = lax.broadcasted_iota(jnp.int32, (first.shape[0], 1), 0)
@@ -404,16 +517,23 @@
         second_kernel,
         (shape((n, D)), shape((n, D), F32), shape((n, D)), shape((3, D), F32)),
         (meta, first, part, got, small, cot),
+        scratch=[pltpu.VMEM((n, D), F32), pltpu.VMEM((16, D), F32), pltpu.VMEM((n, D), BF16)],
         cost=est(40 * n * D, 5e6),
-    )
-
-
-def ffn_back_kernel(first, meta, d0, d1, x0, x1, w0, w1, hid, slope, *refs):
+        far_in=(1, 4, 5),
+        sems=3,
+    )
+
+
+def ffn_back_kernel(first, meta, d0, d1, x0, x1, w0_in, w1_in, hid_in, slope_in, *refs):
     if first:
         in0 = in1 = None
     else:
         (in0, in1), refs = refs[:2], refs[2:]
-    g0, g1, ub, out0, out1 = refs
+    g0, g1, ub, out0, out1, w0, w1, hid, slope, sems = refs
+    copies = Copies(sems)
+    for src, dst in ((w0_in, w0), (w1_in, w1), (slope_in, slope), (hid_in, hid)):
+        copies.start(src, dst)
+    copies.wait()
     half = x0.shape[0]
     uw, dw = ffn_weights((w0, w1))
     cots = []
@@ -452,11 +572,20 @@
             shape((half, D), F32),
         ),
         (meta, d0, d1, x0, x1, *weights, hid, slope, *sums),
-        cost=est(16 * half * D * width, 8 * D * width + 5e6),
-    )
-
-
-def first_back_kernel(meta, sum_two, part, got, normal, scale, small, sum_one, low, sums):
+        scratch=[pltpu.VMEM(v.shape, BF16) for v in (*weights, hid, slope)],
+        cost=est(1000, 1000),
+        far_in=(5, 6, 7, 8),
+        sems=4,
+    )
+
+
+def first_back_kernel(
+    meta, sum_two, part, got, normal_in, scale, small_in, sum_one, low, sums, normal, small, sems
+):
+    copies = Copies(sems)
+    copies.start(normal_in, normal)
+    copies.start(small_in, small)
+    copies.wait()
     fc = sum_two[...] + part[...] + got[...]
     n = normal[...]
     so = norm_back(fc, n, scale[:, 0:1], small[3:4])
@@ -474,20 +603,27 @@
         first_back_kernel,
         (shape((n, D), F32), shape((n, D)), shape((3, D), F32)),
         (meta, sum_two, part, got, normal, scale, small),
+        scratch=[pltpu.VMEM((n, D), F32), pltpu.VMEM((16, D), F32)],
         cost=est(30 * n * D, 5e6),
-    )
-
-
-def attend_back_kernel(
-    sets, meta, a0, a1, x0, x1, wp, wr, q, k, v, ctx0, ctx1, probs, *refs
-):
-    outs, (in0, in1, sums, dctx, cots, grads) = refs[:sets], refs[sets:]
+        far_in=(4, 6),
+        sems=2,
+    )
+
+
+def attend_back_kernel(sets, meta, a0, a1, *refs):
+    far, outs, (in0, in1, sums), refs = refs[:9], refs[9 : 9 + sets], refs[9 + sets : 12 + sets], refs[12 + sets :]
+    wp, v, probs, k, q, wr, x0, x1, ctx, dctx, cots, grads, sems = refs
+    copies = Copies(sems)
+    near = (wp, v, probs, k, q, wr, x0, x1, ctx)
+    got = [copies.start(src, dst) for src, dst in zip(far, near)]
     c = meta[0]
     half = a0.shape[0]
     n = 2 * half
+    copies.wait(got[0])
     wpo = wp[:, pl.ds(pl.multiple_of(c * 384, 128), 384)]
     dctx[0:half] = nn(a0[...], wpo).astype(BF16)
     dctx[half:n] = nn(a1[...], wpo).astype(BF16)
+    copies.wait()
     lane = lax.broadcasted_iota(jnp.int32, (n, 128), 1)
     zero = jnp.zeros((n, 128), BF16)
     scale = HEAD_DIM**-0.5
@@ -532,37 +668,40 @@
     for d in range(3):
         at = slice(256 * d, 256 * d + 256)
         full = tn(x0[:, at], cots[0:half]) + tn(x1[:, at], cots[half:n])
-        pg = tn(a0[:, at], ctx0[...]) + tn(a1[:, at], ctx1[...])
+        pg = tn(a0[:, at], ctx[0:half]) + tn(a1[:, at], ctx[half:n])
         for g in range(2):
             grads[g, at, 0:576] = full[:, 640 * g : 640 * g + 576].astype(BF16)
             grads[g, at, 576:768] = pg[:, 192 * g : 192 * g + 192].astype(BF16)
     if sets == 1:
-        outs[0][...] = grads[...]
+        copies.start(grads, outs[0])
     else:
         z, y, x = meta[6], meta[7], meta[8]
         rows = outs[0].shape[1]
-        for spot in range(4):
+        for spot in (3, 2, 1, 0):
             g, yi = flip(x, spot % 2), flip(y, spot // 2)
             for kz in range(4):
                 zi = flip(lax.rem(z, 2), kz % 2) + 2 * flip(lax.div(z, 2), kz // 2)
                 at = pl.multiple_of((2 * zi + yi) * rows, rows)
-                outs[2 * spot + kz // 2][kz % 2] = grads[g, pl.ds(at, rows), :]
-
-
-def attend_back(direct, meta, a0, a1, x0, x1, wp, wr, q, k, v, ctx0, ctx1, probs):
+                copies.start(grads.at[g, pl.ds(at, rows)], outs[2 * spot + kz // 2].at[kz % 2])
+    copies.wait()
+
+
+def attend_back(direct, meta, a0, a1, x0, x1, wp, wr, q, k, v, ctx, probs):
     half = a0.shape[0]
     n = 2 * half
     sets = (shape((2, 96, D)),) * 8 if direct else (shape((2, D, D)),)
+    far = (wp, v, probs, k, q, wr, x0, x1, ctx)
     return call(
         functools.partial(attend_back_kernel, len(sets)),
         (*sets, shape((half, D), F32), shape((half, D), F32), shape((2, D), F32)),
-        (meta, a0, a1, x0, x1, wp, wr, q, k, v, ctx0, ctx1, probs),
-        scratch=[
-            pltpu.VMEM((n, 384), BF16),
-            pltpu.VMEM((n, 1280), BF16),
-            pltpu.VMEM((2, D, D), BF16),
-        ],
+        (meta, a0, a1, *far),
+        scratch=[pltpu.VMEM(f.shape, BF16) for f in far]
+        + [pltpu.VMEM((n, 384), BF16), pltpu.VMEM((n, 1280), BF16), pltpu.VMEM((2, D, D), BF16)],
         cost=est(2 * n * D * 3500 + 14 * n * n * 384, 14e6),
+        limit=32,
+        far_in=range(3, 12),
+        far_out=range(len(sets)),
+        sems=26,
     )
 
 
@@ -627,16 +766,16 @@
 
     k = jnp.arange(batch_count * 2)
     if direct:
-        a_lo, a_hi = gather_z(a_shard)
-        f_lo, f_hi = gather_z(after(f_shard, a_lo))
-        a_own = [v for pair in gather_xy(a_lo, a_hi) for v in pair]
+        a_z = jnp.stack(z_line(a_shard))
+        f_z = z_line(after(f_shard, a_z))
+        f_lo, f_hi = jnp.stack(f_z[:2]), jnp.stack(f_z[2:])
+        a_own = gather_four(a_z)
         f_lo, f_hi, _ = lax.optimization_barrier((f_lo, f_hi, a_own))
         f_all = gather_xy(f_lo, f_hi)
         a_swapped = [core_swap(v) for v in a_own]
-        place = jnp.stack([z, y, x, c]).astype(jnp.int32)
-        qkv_w, proj_w, small_all = order_weights(a_own, a_swapped, place, wq, wp, 16)
-        qkv_w = qkv_w.reshape(2 * 576, D)
-        proj_w = proj_w.reshape(D, D)
+        ctx_own, ctx_other, q, kk, v, ctx, probs, wr, proj_w, small_all = attend(
+            meta, inputs, other_in, (*a_own, *a_swapped), wq, wp
+        )
         kz = jnp.array([0, 1, 2, 3] * 4)
         ky = jnp.array([0] * 8 + [1] * 8)
         kx = jnp.array([0] * 4 + [1] * 4 + [0] * 4 + [1] * 4)
@@ -647,6 +786,9 @@
         qkv_w = lax.dynamic_index_in_dim(qkv_all, c, 1, keepdims=False).reshape(2 * 576, D)
         proj_w = a_all[:, wq : wq + wp].reshape(D, D)
         small_all = jnp.sum(a_all[:, wq + wp :].astype(F32), 0)
+        ctx_own, ctx_other, q, kk, v, ctx, probs, wr = attend(
+            meta, inputs, other_in, (qkv_w, small_all)
+        )
         f_all = [
             (v[:, :wf].reshape(-1, D), v[:, wf:].reshape(-1, D)) for v in gather_any(f_shard)
         ]
@@ -654,9 +796,8 @@
     spread = (owner[None, :] == jnp.arange(devices)[:, None]).astype(F32)
     ub_all = tn(spread, small_all[8:12].reshape(devices, wf)).reshape(1, FF // 2)
 
-    q, kk, v, ctx_own, ctx_other, probs, wr = attend(meta, inputs, other_in, qkv_w, small_all)
     ctx_in = core_swap(ctx_other)
-    first, first_low, first_n, first_r = first_norm(meta, inputs, ctx_own, ctx_in, proj_w, small_all)
+    first_low, first, first_n, first_r = first_norm(meta, inputs, ctx_own, ctx_in, proj_w, small_all)
     first_in = core_swap(first_low)
     sums = ()
     kept = []
@@ -678,8 +819,12 @@
         )
         f_parts.insert(0, (g0, g1))
         ub_parts.insert(0, ub)
+    part_own, part_other = sums
+    if direct:
+        f_parts, f_moved = scatter_first(f_parts)
+        part_other = lax.optimization_barrier((part_other, f_moved))[0]
     sum_one, attn_low, sums_one = first_back(
-        meta, sum_two, sums[0], core_swap(sums[1]), first_n, first_r, small_all
+        meta, sum_two, part_own, core_swap(part_other), first_n, first_r, small_all
     )
     attn_in = core_swap(attn_low)
     *a_grads, in_own, in_other, sums_zero = attend_back(
@@ -694,17 +839,17 @@
         q,
         kk,
         v,
-        ctx_own,
-        ctx_other,
+        ctx,
         probs,
     )
     inputs_grad = (sum_one + in_own + core_swap(in_other)).astype(BF16)
 
     if direct:
-        f_sums = scatter_z(*scatter_xy(f_parts))
+        f_sums = scatter_z(*scatter_xy(*f_parts))
         up_grad, down_grad = finish_ffn(f_sums)
         a_parts = [tuple(a_grads[2 * i : 2 * i + 2]) for i in range(4)]
-        qkv_grad, proj_grad = finish_attend(scatter_z(*scatter_xy(a_parts)))
+        a_parts, _ = scatter_first(a_parts)
+        qkv_grad, proj_grad = finish_attend(scatter_z(*scatter_xy(*a_parts)))
     else:
         wb = D // batch_count
         a_grads = a_grads[0].reshape(2, batch_count, wb, D)

time: 251 us -> 236 us (0.940)
  local copies, waits for them, and re-layouts: 42.1 us -> 16.6 us
  Pallas kernels: 55 us -> 71.9 us
  waiting for transfers between devices: 86.3 us -> 79.4 us
  starting transfers between devices: 54.1 us -> 57.4 us
    unnamed x149 -> x59, local copies, waits for them, and re-layouts: 32.3 us -> 7.15 us
    pallas_call x18 -> x17, Pallas kernels: 55 us -> 71.9 us  [call(): pl.pallas_call(kernel, out_shape=out_shape, in_specs=ins, out_specs=outs,...]
    ppermute x12 -> x11, waiting for transfers between devices: 27.2 us -> 20.8 us  [y_swap(): return lax.ppermute(v, 'batch', YPAIR)]
    ppermute x12 -> x11, waiting for transfers between devices: 11.1 us -> 5.68 us  [x_swap(): return lax.ppermute(v, 'head', XPAIR)]
    ppermute x12, waiting for transfers between devices: 39.5 us -> 43.9 us  [z_swap(): return lax.ppermute(v, 'batch', ZPAIR[k])]
    ppermute x12, starting transfers between devices: 20.5 us -> 24.6 us  [z_swap(): return lax.ppermute(v, 'batch', ZPAIR[k])]
    ppermute x16 -> x13, waiting for transfers between devices: 4.62 us -> 6.35 us  [core_swap(): return lax.ppermute(v, 'head', CORE)]
    ppermute x12 -> x11, starting transfers between devices: 13.6 us -> 12.8 us  [y_swap(): return lax.ppermute(v, 'batch', YPAIR)]
  transfers between devices with their start and end apart: 53 -> 48, of which waited for: 17 -> 18; matrix products, arithmetic and copies ran while one was open for 6% -> 5% of each run, Pallas kernels for 15% -> 25%
where the time goes in v1:
time: 236 us; the launch traced here: 235 us
  waiting for transfers between devices  79.4 us (34%)
  Pallas kernels  71.9 us (30%)
  starting transfers between devices  57.4 us (24%)
  local copies, waits for them, and re-layouts  16.6 us (7%)
  other arithmetic  7.86 us (3%)
    pallas_call x17, Pallas kernels, call(): pl.pallas_call(kernel, out_shape=out_shape, in_specs=ins, out_specs=outs,...  71.9 us
    ppermute x12, waiting for transfers between devices, z_swap(): return lax.ppermute(v, 'batch', ZPAIR[k])  43.9 us
    ppermute x12, starting transfers between devices, z_swap(): return lax.ppermute(v, 'batch', ZPAIR[k])  24.6 us
    ppermute x11, waiting for transfers between devices, y_swap(): return lax.ppermute(v, 'batch', YPAIR)  20.8 us
    ppermute x11, starting transfers between devices, x_swap(): return lax.ppermute(v, 'head', XPAIR)  13.5 us
    ppermute x11, starting transfers between devices, y_swap(): return lax.ppermute(v, 'batch', YPAIR)  12.8 us
    unnamed x59, local copies, waits for them, and re-layouts  7.15 us
    ppermute x13, waiting for transfers between devices, core_swap(): return lax.ppermute(v, 'head', CORE)  6.35 us
  transfers between devices with their start and end apart: 48, of which 18 were waited for; matrix products, arithmetic and copies ran while one was open for 5% of the time, Pallas kernels for 25%

profile of v1, /device:TPU:0, one launch (start us, length us, event | category | flops | bytes accessed | tf_op | source)
XLA Modules:
  0.0 234.7 jit_solution(1211870391631272715)
XLA Ops:
  4.7 4.1 %collective-permute-start.2 = (bf16[112,768]{1,0:T(8,128)(2,1)S(1)}, bf16[112,768]{1,0:T(8,128)(2,1)S(1)}, u32[]{:S(2)}, u32[]{:S(2)}) collective-permute-start(bf16[112,768]{1,0:T(8,128)(2,1)S(1)} %get-tuple-element.229), channel_id=1, source_target_pairs={{0,16},{4,20},{8,24},{12,28},{16,0},{20,4},{24,8},{28,12},{1,17},{... | collective-permute-start | bytes 516104 | tf_op jit(solution)/shard_map/ppermute | solution.py:40
  8.8 1.8 collective-permute-start.1
  10.6 7.4 %collective-permute-done.2 = bf16[112,768]{1,0:T(8,128)(2,1)S(1)} collective-permute-done((bf16[112,768]{1,0:T(8,128)(2,1)S(1)}, bf16[112,768]{1,0:T(8,128)(2,1)S(1)}, u32[]{:S(2)}, u32[]{:S(2)}) %collective-permute-start.2) | collective-permute-done | bytes 172064 | tf_op jit(solution)/shard_map/ppermute | solution.py:40
  18.1 4.0 %collective-permute-done.3 = bf16[112,768]{1,0:T(8,128)(2,1)S(1)} collective-permute-done((bf16[112,768]{1,0:T(8,128)(2,1)S(1)}, bf16[112,768]{1,0:T(8,128)(2,1)S(1)}, u32[]{:S(2)}, u32[]{:S(2)}) %collective-permute-start.3) | collective-permute-done | bytes 172064 | tf_op jit(solution)/shard_map/ppermute | solution.py:40
  22.2 1.6 collective-permute-start.5
  25.3 2.5 %collective-permute-start.17 = (bf16[192,768]{1,0:T(8,128)(2,1)S(1)}, bf16[192,768]{1,0:T(8,128)(2,1)S(1)}, u32[]{:S(2)}, u32[]{:S(2)}) collective-permute-start(bf16[192,768]{1,0:T(8,128)(2,1)S(1)} %pad_maximum_fusion.3), channel_id=1, source_target_pairs={{0,24},{4,28},{8,16},{12,20},{16,8},{20,12},{24,0},{28,4},{1,25},{... | collective-permute-start | bytes 884744 | tf_op jit(solution)/shard_map/ppermute | solution.py:40
  27.8 2.7 %collective-permute-start.16 = (bf16[192,768]{1,0:T(8,128)(2,1)S(1)}, bf16[192,768]{1,0:T(8,128)(2,1)S(1)}, u32[]{:S(2)}, u32[]{:S(2)}) collective-permute-start(bf16[192,768]{1,0:T(8,128)(2,1)S(1)} %pad_maximum_fusion.3), channel_id=1, source_target_pairs={{0,16},{4,20},{8,24},{12,28},{16,0},{20,4},{24,8},{28,12},{1,17},{... | collective-permute-start | bytes 884744 | tf_op jit(solution)/shard_map/ppermute | solution.py:40
  30.6 8.2 %collective-permute-done.5.refs_2_ = bf16[4,112,768]{2,1,0:T(8,128)(2,1)} collective-permute-done((bf16[4,112,768]{2,1,0:T(8,128)(2,1)S(1)}, bf16[4,112,768]{2,1,0:T(8,128)(2,1)}, u32[]{:S(2)}, u32[]{:S(2)}) %collective-permute-start.5) | collective-permute-done | bytes 688160 | tf_op jit(solution)/shard_map/ppermute | solution.py:36
  38.8 4.2 %collective-permute-start.15 = (bf16[192,768]{1,0:T(8,128)(2,1)S(1)}, bf16[192,768]{1,0:T(8,128)(2,1)S(1)}, u32[]{:S(2)}, u32[]{:S(2)}) collective-permute-start(bf16[192,768]{1,0:T(8,128)(2,1)S(1)} %pad_maximum_fusion.3), channel_id=1, source_target_pairs={{0,8},{4,12},{8,0},{12,4},{16,24},{20,28},{24,16},{28,20},{1,9},{5... | collective-permute-start | bytes 884744 | tf_op jit(solution)/shard_map/ppermute | solution.py:40
  44.7 1.5 collective-permute-start.6
  47.2 1.6 collective-permute-start.7
  48.8 6.8 %collective-permute-done.16 = bf16[192,768]{1,0:T(8,128)(2,1)S(1)} collective-permute-done((bf16[192,768]{1,0:T(8,128)(2,1)S(1)}, bf16[192,768]{1,0:T(8,128)(2,1)S(1)}, u32[]{:S(2)}, u32[]{:S(2)}) %collective-permute-start.16) | collective-permute-done | bytes 294944 | tf_op jit(solution)/shard_map/ppermute | solution.py:40
  57.1 1.6 collective-permute-start.18
  62.3 11.8 %shard_map.307 = (bf16[256,384]{1,0:T(8,128)(2,1)S(1)}, bf16[256,384]{1,0:T(8,128)(2,1)S(1)}, bf16[512,384]{1,0:T(8,128)(2,1)}, bf16[512,384]{1,0:T(8,128)(2,1)}...) custom-call(s32[9]{0:T(128)S(1)} %concatenate.18.meta, ...), custom_call_target="tpu_custom_call" | custom-call | flops 1711276032 | bytes 12000000 | tf_op jit(solution)/shard_map/pallas_call | solution.py:119
  76.2 4.0 %shard_map.308 = (bf16[256,768]{1,0:T(8,128)(2,1)S(1)}, f32[256,768]{1,0:T(8,128)}, f32[256,768]{1,0:T(8,128)}, f32[256,128]{1,0:T(8,128)S(1)}) custom-call(s32[9]{0:T(128)S(1)} %concatenate.18.meta, bf16[256,768]{1,0:T(8,128)(2,1)} %refs_6_.1, bf16[256,384]{1,0:T(8,128)(2,1)S(1)} %get-tuple-element.99.ctx_own, ...), custom_call_target="tpu_custom_call" | custom-call | flops 301989888 | bytes 5000000 | tf_op jit(solution)/shard_map/pallas_call | solution.py:119
  80.5 1.7 collective-permute-start.19
  83.0 3.6 %shard_map.309 = (bf16[512,384]{1,0:T(8,128)(2,1)}, bf16[512,384]{1,0:T(8,128)(2,1)}, f32[256,768]{1,0:T(8,128)S(1)}, f32[256,768]{1,0:T(8,128)S(1)}) custom-call(s32[9]{0:T(128)S(1)} %concatenate.18.meta, bf16[256,768]{1,0:T(8,128)(2,1)S(1)} %get-tuple-element.104.x0, bf16[256,768]{1,0:T(8,128)(2,1)S(1)} %collective-permute-done.14.x1, ...), custom_call_target="tpu_custom_call" | custom-call | flops 603979776 | bytes 6179648 | tf_op jit(solution)/shard_map/pallas_call | solution.py:119
  87.8 3.7 %shard_map.310 = (bf16[512,384]{1,0:T(8,128)(2,1)}, bf16[512,384]{1,0:T(8,128)(2,1)}, f32[256,768]{1,0:T(8,128)S(1)}, f32[256,768]{1,0:T(8,128)S(1)}) custom-call(s32[9]{0:T(128)S(1)} %concatenate.18.meta, bf16[256,768]{1,0:T(8,128)(2,1)S(1)} %get-tuple-element.104.x0, bf16[256,768]{1,0:T(8,128)(2,1)S(1)} %collective-permute-done.14.x1, ...), custom_call_target="tpu_custom_call" | custom-call | flops 603979776 | bytes 6179648 | tf_op jit(solution)/shard_map/pallas_call | solution.py:119
  91.4 3.6 %shard_map.311 = (bf16[512,384]{1,0:T(8,128)(2,1)}, bf16[512,384]{1,0:T(8,128)(2,1)}, f32[256,768]{1,0:T(8,128)S(1)}, f32[256,768]{1,0:T(8,128)S(1)}) custom-call(s32[9]{0:T(128)S(1)} %concatenate.18.meta, bf16[256,768]{1,0:T(8,128)(2,1)S(1)} %get-tuple-element.104.x0, bf16[256,768]{1,0:T(8,128)(2,1)S(1)} %collective-permute-done.14.x1, ...), custom_call_target="tpu_custom_call" | custom-call | flops 603979776 | bytes 6179648 | tf_op jit(solution)/shard_map/pallas_call | solution.py:119
  95.1 4.5 %collective-permute-done.19.w0_in = bf16[2,192,768]{2,1,0:T(8,128)(2,1)} collective-permute-done((bf16[2,192,768]{2,1,0:T(8,128)(2,1)S(1)}, bf16[2,192,768]{2,1,0:T(8,128)(2,1)}, u32[]{:S(2)}, u32[]{:S(2)}) %collective-permute-start.19) | collective-permute-done | bytes 589856 | tf_op jit(solution)/shard_map/ppermute | solution.py:32
  99.6 3.1 %collective-permute-done.21.w1_in = bf16[2,192,768]{2,1,0:T(8,128)(2,1)} collective-permute-done((bf16[2,192,768]{2,1,0:T(8,128)(2,1)S(1)}, bf16[2,192,768]{2,1,0:T(8,128)(2,1)}, u32[]{:S(2)}, u32[]{:S(2)}) %collective-permute-start.21) | collective-permute-done | bytes 589856 | tf_op jit(solution)/shard_map/ppermute | solution.py:36
  102.7 3.8 %shard_map.312 = (bf16[512,384]{1,0:T(8,128)(2,1)}, bf16[512,384]{1,0:T(8,128)(2,1)}, f32[256,768]{1,0:T(8,128)S(1)}, f32[256,768]{1,0:T(8,128)S(1)}) custom-call(s32[9]{0:T(128)S(1)} %concatenate.18.meta, bf16[256,768]{1,0:T(8,128)(2,1)S(1)} %get-tuple-element.104.x0, bf16[256,768]{1,0:T(8,128)(2,1)S(1)} %collective-permute-done.14.x1, ...), custom_call_target="tpu_custom_call" | custom-call | flops 603979776 | bytes 6179648 | tf_op jit(solution)/shard_map/pallas_call | solution.py:119
  106.6 2.3 collective-permute-done.24.got
  108.9 3.2 %shard_map.313 = (bf16[256,768]{1,0:T(8,128)(2,1)}, f32[256,768]{1,0:T(8,128)S(1)}, bf16[256,768]{1,0:T(8,128)(2,1)S(1)}, f32[3,768]{1,0:T(4,128)S(1)}) custom-call(s32[9]{0:T(128)S(1)} %concatenate.18.meta, f32[256,768]{1,0:T(8,128)} %get-tuple-element.103.first_in, f32[256,768]{1,0:T(8,128)S(1)} %get-tuple-element.114.part, ...), custom_call_target="tpu_custom_call" | custom-call | flops 7864320 | bytes 5000000 | tf_op jit(solution)/shard_map/pallas_call | solution.py:119
  112.3 1.6 collective-permute-done.25.d1
  113.9 3.9 %shard_map.314 = (bf16[2,192,768]{2,1,0:T(8,128)(2,1)S(1)}, bf16[2,192,768]{2,1,0:T(8,128)(2,1)S(1)}, f32[1,384]{1,0:T(1,128)S(1)}, f32[256,768]{1,0:T(8,128)S(1)}, f32[256,768]{1,0:T(8,128)S(1)}) custom-call(s32[9]{0:T(128)S(1)} %concatenate.18.meta, bf16[256,768]{1,0:T(8,128)(2,1)S(1)} %get-tuple-element.118.d0, ...), custom_call_target="tpu_custom_call" | custom-call | flops 1000 | bytes 1000 | tf_op jit(solution)/shard_map/pallas_call | solution.py:119
  119.1 1.5 collective-permute-start.27
  120.6 4.8 %shard_map.315 = (bf16[2,192,768]{2,1,0:T(8,128)(2,1)S(1)}, bf16[2,192,768]{2,1,0:T(8,128)(2,1)}, f32[1,384]{1,0:T(1,128)S(1)}, f32[256,768]{1,0:T(8,128)S(1)}, f32[256,768]{1,0:T(8,128)S(1)}) custom-call(s32[9]{0:T(128)S(1)} %concatenate.18.meta, bf16[256,768]{1,0:T(8,128)(2,1)S(1)} %get-tuple-element.118.d0, ...), custom_call_target="tpu_custom_call" | custom-call | flops 1000 | bytes 1000 | tf_op jit(solution)/shard_map/pallas_call | solution.py:119
  125.4 4.7 %shard_map.316 = (bf16[2,192,768]{2,1,0:T(8,128)(2,1)}, bf16[2,192,768]{2,1,0:T(8,128)(2,1)S(1)}, f32[1,384]{1,0:T(1,128)S(1)}, f32[256,768]{1,0:T(8,128)S(1)}, f32[256,768]{1,0:T(8,128)S(1)}) custom-call(s32[9]{0:T(128)S(1)} %concatenate.18.meta, bf16[256,768]{1,0:T(8,128)(2,1)S(1)} %get-tuple-element.118.d0, ...), custom_call_target="tpu_custom_call" | custom-call | flops 1000 | bytes 1000 | tf_op jit(solution)/shard_map/pallas_call | solution.py:119
  130.1 3.9 %shard_map.317 = (bf16[2,192,768]{2,1,0:T(8,128)(2,1)S(1)}, bf16[2,192,768]{2,1,0:T(8,128)(2,1)S(1)}, f32[1,384]{1,0:T(1,128)S(1)}, f32[256,768]{1,0:T(8,128)S(1)}, f32[256,768]{1,0:T(8,128)S(1)}) custom-call(s32[9]{0:T(128)S(1)} %concatenate.18.meta, bf16[256,768]{1,0:T(8,128)(2,1)S(1)} %get-tuple-element.118.d0, ...), custom_call_target="tpu_custom_call" | custom-call | flops 1000 | bytes 1000 | tf_op jit(solution)/shard_map/pallas_call | solution.py:119
  136.0 2.3 collective-permute-done.28.got
  138.3 2.3 shard_map.318
  141.2 1.5 collective-permute-start.43
  143.2 1.6 collective-permute-start.41
  144.8 13.6 %shard_map.319 = (bf16[2,96,768]{2,1,0:T(8,128)(2,1)}, bf16[2,96,768]{2,1,0:T(8,128)(2,1)}, bf16[2,96,768]{2,1,0:T(8,128)(2,1)}, bf16[2,96,768]{2,1,0:T(8,128)(2...) custom-call(s32[9]{0:T(128)S(1)} %concatenate.18.meta, ...), custom_call_target="tpu_custom_call" | custom-call | flops 4161798144 | bytes 14000000 | tf_op jit(solution)/shard_map/pallas_call | solution.py:119
  161.6 8.8 %collective-permute-done.42.y_lo = bf16[2,192,768]{2,1,0:T(8,128)(2,1)} collective-permute-done((bf16[2,192,768]{2,1,0:T(8,128)(2,1)}, bf16[2,192,768]{2,1,0:T(8,128)(2,1)}, u32[]{:S(2)}, u32[]{:S(2)}) %collective-permute-start.42) | collective-permute-done | bytes 589856 | tf_op jit(solution)/shard_map/ppermute | solution.py:36
  171.4 1.9 shard_map.322
  173.3 2.3 collective-permute-start.44
  175.6 1.7 collective-permute-start.45
  178.1 1.7 add_convert_fusion.4
  181.9 3.9 %collective-permute-done.44.one = bf16[192,768]{1,0:T(8,128)(2,1)S(1)} collective-permute-done((bf16[192,768]{1,0:T(8,128)(2,1)S(1)}, bf16[192,768]{1,0:T(8,128)(2,1)S(1)}, u32[]{:S(2)}, u32[]{:S(2)}) %collective-permute-start.44) | collective-permute-done | bytes 294944 | tf_op jit(solution)/shard_map/ppermute | solution.py:40
  186.9 12.2 %collective-permute-done.45.two = bf16[192,768]{1,0:T(8,128)(2,1)S(1)} collective-permute-done((bf16[192,768]{1,0:T(8,128)(2,1)S(1)}, bf16[192,768]{1,0:T(8,128)(2,1)S(1)}, u32[]{:S(2)}, u32[]{:S(2)}) %collective-permute-start.45) | collective-permute-done | bytes 294944 | tf_op jit(solution)/shard_map/ppermute | solution.py:40
  202.8 5.1 %all-to-all-start = ((f32[32,1,288]{2,1,0:T(1,128)}), f32[32,1,288]{2,1,0:T(1,128)S(1)}, u32[]{:S(2)}, u32[]{:S(2)}) async-start(f32[32,1,288]{2,1,0:T(1,128)} %copy.42), calls=%async_computation | async-start | bytes 98304 | tf_op jit(solution)/shard_map/all_to_all | solution.py:882
  212.6 2.6 %all-to-all-done = f32[32,1,288]{2,1,0:T(1,128)S(1)} async-done(((f32[32,1,288]{2,1,0:T(1,128)}), f32[32,1,288]{2,1,0:T(1,128)S(1)}, u32[]{:S(2)}, u32[]{:S(2)}) %all-to-all-start) | async-done | bytes 36896 | tf_op jit(solution)/shard_map/all_to_all | solution.py:882
  218.9 2.8 %collective-permute-start.39 = (bf16[96,768]{1,0:T(8,128)(2,1)S(1)}, bf16[96,768]{1,0:T(8,128)(2,1)S(1)}, u32[]{:S(2)}, u32[]{:S(2)}) collective-permute-start(bf16[96,768]{1,0:T(8,128)(2,1)S(1)} %get-tuple-element.163), channel_id=1, source_target_pairs={{0,24},{4,28},{8,16},{12,20},{16,8},{20,12},{24,0},{28,4},{1,25},{... | collective-permute-start | bytes 442376 | tf_op jit(solution)/shard_map/ppermute | solution.py:40
  222.3 2.6 %collective-permute-done.37.one = bf16[96,768]{1,0:T(8,128)(2,1)S(1)} collective-permute-done((bf16[96,768]{1,0:T(8,128)(2,1)S(1)}, bf16[96,768]{1,0:T(8,128)(2,1)S(1)}, u32[]{:S(2)}, u32[]{:S(2)}) %collective-permute-start.37) | collective-permute-done | bytes 147488 | tf_op jit(solution)/shard_map/ppermute | solution.py:40
  225.0 6.8 %collective-permute-done.38.two = bf16[96,768]{1,0:T(8,128)(2,1)S(1)} collective-permute-done((bf16[96,768]{1,0:T(8,128)(2,1)S(1)}, bf16[96,768]{1,0:T(8,128)(2,1)S(1)}, u32[]{:S(2)}, u32[]{:S(2)}) %collective-permute-start.38) | collective-permute-done | bytes 147488 | tf_op jit(solution)/shard_map/ppermute | solution.py:40
  232.7 2.0 add_convert_fusion.2
  (164 shorter events, 43.9 us)
Async XLA Ops:
  4.7 13.4 %collective-permute-start.2 = (bf16[112,768]{1,0:T(8,128)(2,1)S(1)}, bf16[112,768]{1,0:T(8,128)(2,1)S(1)}, u32[]{:S(2)}, u32[]{:S(2)}) collective-permute-start(bf16[112,768]{1,0:T(8,128)(2,1)S(1)} %get-tuple-element.229), channel_id=1, source_target_pairs={{0,16},{4,20},{8,24},{12,28},{16,0},{20,4},{24,8},{28,12},{1,17},{... | collective-permute-start | bytes 516104 | tf_op jit(solution)/shard_map/ppermute | solution.py:40
  8.8 9.3 %collective-permute-start.1 = (bf16[112,768]{1,0:T(8,128)(2,1)S(1)}, bf16[112,768]{1,0:T(8,128)(2,1)S(1)}, u32[]{:S(2)}, u32[]{:S(2)}) collective-permute-start(bf16[112,768]{1,0:T(8,128)(2,1)S(1)} %get-tuple-element.229), channel_id=1, source_target_pairs={{0,8},{4,12},{8,0},{12,4},{16,24},{20,28},{24,16},{28,20},{1,9},{5... | collective-permute-start | bytes 516104 | tf_op jit(solution)/shard_map/ppermute | solution.py:40
  10.6 11.5 %collective-permute-start.3 = (bf16[112,768]{1,0:T(8,128)(2,1)S(1)}, bf16[112,768]{1,0:T(8,128)(2,1)S(1)}, u32[]{:S(2)}, u32[]{:S(2)}) collective-permute-start(bf16[112,768]{1,0:T(8,128)(2,1)S(1)} %get-tuple-element.229), channel_id=1, source_target_pairs={{0,24},{4,28},{8,16},{12,20},{16,8},{20,12},{24,0},{28,4},{1,25},{... | collective-permute-start | bytes 516104 | tf_op jit(solution)/shard_map/ppermute | solution.py:40
  22.2 16.6 %collective-permute-start.5 = (bf16[4,112,768]{2,1,0:T(8,128)(2,1)S(1)}, bf16[4,112,768]{2,1,0:T(8,128)(2,1)}, u32[]{:S(2)}, u32[]{:S(2)}) collective-permute-start(bf16[4,112,768]{2,1,0:T(8,128)(2,1)S(1)} %pad_maximum_fusion.refs_0_), channel_id=1, source_target_pairs={{0,4},{4,0},{8,12},{12,8},{16,20},{20,16},{24,28},{28,24},{1,5},{5... | collective-permute-start | bytes 2064392 | tf_op jit(solution)/shard_map/ppermute | solution.py:36
  23.8 20.2 %collective-permute-start.4 = (bf16[4,112,768]{2,1,0:T(8,128)(2,1)S(1)}, bf16[4,112,768]{2,1,0:T(8,128)(2,1)}, u32[]{:S(2)}, u32[]{:S(2)}) collective-permute-start(bf16[4,112,768]{2,1,0:T(8,128)(2,1)S(1)} %pad_maximum_fusion.refs_0_), channel_id=1, source_target_pairs={{0,2},{1,3},{2,0},{3,1},{4,6},{5,7},{6,4},{7,5},{8,10},{9,11},{10,... | collective-permute-start | bytes 2064392 | tf_op jit(solution)/shard_map/ppermute | solution.py:32
  25.3 18.7 %collective-permute-start = (bf16[256,768]{1,0:T(8,128)(2,1)S(1)}, bf16[256,768]{1,0:T(8,128)(2,1)S(1)}, u32[]{:S(2)}, u32[]{:S(2)}) collective-permute-start(bf16[256,768]{1,0:T(8,128)(2,1)S(1)} %copy-done.17), channel_id=1, source_target_pairs={{0,1},{1,0},{2,3},{3,2},{4,5},{5,4},{6,7},{7,6},{8,9},{9,8},{10,11... | collective-permute-start | bytes 1179656 | tf_op jit(solution)/shard_map/ppermute | solution.py:28
  25.3 21.9 %collective-permute-start.17 = (bf16[192,768]{1,0:T(8,128)(2,1)S(1)}, bf16[192,768]{1,0:T(8,128)(2,1)S(1)}, u32[]{:S(2)}, u32[]{:S(2)}) collective-permute-start(bf16[192,768]{1,0:T(8,128)(2,1)S(1)} %pad_maximum_fusion.3), channel_id=1, source_target_pairs={{0,24},{4,28},{8,16},{12,20},{16,8},{20,12},{24,0},{28,4},{1,25},{... | collective-permute-start | bytes 884744 | tf_op jit(solution)/shard_map/ppermute | solution.py:40
  27.8 27.7 %collective-permute-start.16 = (bf16[192,768]{1,0:T(8,128)(2,1)S(1)}, bf16[192,768]{1,0:T(8,128)(2,1)S(1)}, u32[]{:S(2)}, u32[]{:S(2)}) collective-permute-start(bf16[192,768]{1,0:T(8,128)(2,1)S(1)} %pad_maximum_fusion.3), channel_id=1, source_target_pairs={{0,16},{4,20},{8,24},{12,28},{16,0},{20,4},{24,8},{28,12},{1,17},{... | collective-permute-start | bytes 884744 | tf_op jit(solution)/shard_map/ppermute | solution.py:40
  38.8 16.9 %collective-permute-start.15 = (bf16[192,768]{1,0:T(8,128)(2,1)S(1)}, bf16[192,768]{1,0:T(8,128)(2,1)S(1)}, u32[]{:S(2)}, u32[]{:S(2)}) collective-permute-start(bf16[192,768]{1,0:T(8,128)(2,1)S(1)} %pad_maximum_fusion.3), channel_id=1, source_target_pairs={{0,8},{4,12},{8,0},{12,4},{16,24},{20,28},{24,16},{28,20},{1,9},{5... | collective-permute-start | bytes 884744 | tf_op jit(solution)/shard_map/ppermute | solution.py:40
  43.9 13.1 %collective-permute-start.8 = (bf16[4,112,768]{2,1,0:T(8,128)(2,1)S(1)}, bf16[4,112,768]{2,1,0:T(8,128)(2,1)S(1)}, u32[]{:S(2)}, u32[]{:S(2)}) collective-permute-start(bf16[4,112,768]{2,1,0:T(8,128)(2,1)S(1)} %pad_maximum_fusion.refs_0_), channel_id=1, source_target_pairs={{0,1},{1,0},{2,3},{3,2},{4,5},{5,4},{6,7},{7,6},{8,9},{9,8},{10,11... | collective-permute-start | bytes 2064392 | tf_op jit(solution)/shard_map/ppermute | solution.py:28
  44.7 11.4 %collective-permute-start.6 = (bf16[2,112,768]{2,1,0:T(8,128)(2,1)S(1)}, bf16[2,112,768]{2,1,0:T(8,128)(2,1)S(1)}, u32[]{:S(2)}, u32[]{:S(2)}) collective-permute-start(bf16[2,112,768]{2,1,0:T(8,128)(2,1)S(1)} %slice.64), channel_id=1, source_target_pairs={{0,2},{1,3},{2,0},{3,1},{4,6},{5,7},{6,4},{7,5},{8,10},{9,11},{10,... | collective-permute-start | bytes 1032200 | tf_op jit(solution)/shard_map/ppermute | solution.py:32
  47.2 9.7 %collective-permute-start.7 = (bf16[2,112,768]{2,1,0:T(8,128)(2,1)S(1)}, bf16[2,112,768]{2,1,0:T(8,128)(2,1)}, u32[]{:S(2)}, u32[]{:S(2)}) collective-permute-start(bf16[2,112,768]{2,1,0:T(8,128)(2,1)S(1)} %slice.65), channel_id=1, source_target_pairs={{0,4},{4,0},{8,12},{12,8},{16,20},{20,16},{24,28},{28,24},{1,5},{5... | collective-permute-start | bytes 1032200 | tf_op jit(solution)/shard_map/ppermute | solution.py:36
  55.6 5.9 %collective-permute-start.10 = (bf16[4,112,768]{2,1,0:T(8,128)(2,1)}, bf16[4,112,768]{2,1,0:T(8,128)(2,1)}, u32[]{:S(2)}, u32[]{:S(2)}) collective-permute-start(bf16[4,112,768]{2,1,0:T(8,128)(2,1)} %collective-permute-done.5.refs_2_), channel_id=1, source_target_pairs={{0,1},{1,0},{2,3},{3,2},{4,5},{5,4},{6,7},{7,6},{8,9},{9,8},{10,11... | collective-permute-start | bytes 2064392 | tf_op jit(solution)/shard_map/ppermute | solution.py:28
  55.6 6.6 %collective-permute-start.9 = (bf16[4,112,768]{2,1,0:T(8,128)(2,1)}, bf16[4,112,768]{2,1,0:T(8,128)(2,1)}, u32[]{:S(2)}, u32[]{:S(2)}) collective-permute-start(bf16[4,112,768]{2,1,0:T(8,128)(2,1)} %collective-permute-done.4.refs_1_), channel_id=1, source_target_pairs={{0,1},{1,0},{2,3},{3,2},{4,5},{5,4},{6,7},{7,6},{8,9},{9,8},{10,11... | collective-permute-start | bytes 2064392 | tf_op jit(solution)/shard_map/ppermute | solution.py:28
  56.1 2.7 %collective-permute-start.11 = (bf16[2,112,768]{2,1,0:T(8,128)(2,1)S(1)}, bf16[2,112,768]{2,1,0:T(8,128)(2,1)}, u32[]{:S(2)}, u32[]{:S(2)}) collective-permute-start(bf16[2,112,768]{2,1,0:T(8,128)(2,1)S(1)} %collective-permute-done.6.refs_3_), channel_id=1, source_target_pairs={{0,1},{1,0},{2,3},{3,2},{4,5},{5,4},{6,7},{7,6},{8,9},{9,8},{10,11... | collective-permute-start | bytes 1032200 | tf_op jit(solution)/shard_map/ppermute | solution.py:28
  56.9 5.4 %collective-permute-start.12 = (bf16[2,112,768]{2,1,0:T(8,128)(2,1)}, bf16[2,112,768]{2,1,0:T(8,128)(2,1)}, u32[]{:S(2)}, u32[]{:S(2)}) collective-permute-start(bf16[2,112,768]{2,1,0:T(8,128)(2,1)} %collective-permute-done.7.refs_4_), channel_id=1, source_target_pairs={{0,1},{1,0},{2,3},{3,2},{4,5},{5,4},{6,7},{7,6},{8,9},{9,8},{10,11... | collective-permute-start | bytes 1032200 | tf_op jit(solution)/shard_map/ppermute | solution.py:28
  57.1 23.4 %collective-permute-start.18 = (bf16[2,192,768]{2,1,0:T(8,128)(2,1)S(1)}, bf16[2,192,768]{2,1,0:T(8,128)(2,1)S(1)}, u32[]{:S(2)}, u32[]{:S(2)}) collective-permute-start(bf16[2,192,768]{2,1,0:T(8,128)(2,1)S(1)} %pad_maximum_fusion.1.w0_in), channel_id=1, source_target_pairs={{0,4},{4,0},{8,12},{12,8},{16,20},{20,16},{24,28},{28,24},{1,5},{5... | collective-permute-start | bytes 1769480 | tf_op jit(solution)/shard_map/ppermute | solution.py:36
  58.8 23.3 %collective-permute-start.20 = (bf16[2,192,768]{2,1,0:T(8,128)(2,1)S(1)}, bf16[2,192,768]{2,1,0:T(8,128)(2,1)S(1)}, u32[]{:S(2)}, u32[]{:S(2)}) collective-permute-start(bf16[2,192,768]{2,1,0:T(8,128)(2,1)S(1)} %pad_maximum_fusion.2.w1_in), channel_id=1, source_target_pairs={{0,2},{1,3},{2,0},{3,1},{4,6},{5,7},{6,4},{7,5},{8,10},{9,11},{10,... | collective-permute-start | bytes 1769480 | tf_op jit(solution)/shard_map/ppermute | solution.py:32
  61.5 26.3 %collective-permute-start.23 = (bf16[2,192,768]{2,1,0:T(8,128)(2,1)S(1)}, bf16[2,192,768]{2,1,0:T(8,128)(2,1)}, u32[]{:S(2)}, u32[]{:S(2)}) collective-permute-start(bf16[2,192,768]{2,1,0:T(8,128)(2,1)S(1)} %pad_maximum_fusion.1.w0_in), channel_id=1, source_target_pairs={{0,2},{1,3},{2,0},{3,1},{4,6},{5,7},{6,4},{7,5},{8,10},{9,11},{10,... | collective-permute-start | bytes 1769480 | tf_op jit(solution)/shard_map/ppermute | solution.py:32
  74.1 2.1 collective-permute-start.13
  74.2 17.2 %collective-permute-start.22 = (bf16[2,192,768]{2,1,0:T(8,128)(2,1)S(1)}, bf16[2,192,768]{2,1,0:T(8,128)(2,1)}, u32[]{:S(2)}, u32[]{:S(2)}) collective-permute-start(bf16[2,192,768]{2,1,0:T(8,128)(2,1)S(1)} %pad_maximum_fusion.2.w1_in), channel_id=1, source_target_pairs={{0,4},{4,0},{8,12},{12,8},{16,20},{20,16},{24,28},{28,24},{1,5},{5... | collective-permute-start | bytes 1769480 | tf_op jit(solution)/shard_map/ppermute | solution.py:36
  80.2 2.8 %collective-permute-start.14 = (bf16[256,768]{1,0:T(8,128)(2,1)S(1)}, bf16[256,768]{1,0:T(8,128)(2,1)S(1)}, u32[]{:S(2)}, u32[]{:S(2)}) collective-permute-start(bf16[256,768]{1,0:T(8,128)(2,1)S(1)} %get-tuple-element.104.x0), channel_id=1, source_target_pairs={{0,1},{1,0},{2,3},{3,2},{4,5},{5,4},{6,7},{7,6},{8,9},{9,8},{10,11... | collective-permute-start | bytes 1179656 | tf_op jit(solution)/shard_map/ppermute | solution.py:28
  80.5 19.1 %collective-permute-start.19 = (bf16[2,192,768]{2,1,0:T(8,128)(2,1)S(1)}, bf16[2,192,768]{2,1,0:T(8,128)(2,1)}, u32[]{:S(2)}, u32[]{:S(2)}) collective-permute-start(bf16[2,192,768]{2,1,0:T(8,128)(2,1)S(1)} %collective-permute-done.18.w0_in), channel_id=1, source_target_pairs={{0,2},{1,3},{2,0},{3,1},{4,6},{5,7},{6,4},{7,5},{8,10},{9,11},{10,... | collective-permute-start | bytes 1769480 | tf_op jit(solution)/shard_map/ppermute | solution.py:32
  82.2 20.5 %collective-permute-start.21 = (bf16[2,192,768]{2,1,0:T(8,128)(2,1)S(1)}, bf16[2,192,768]{2,1,0:T(8,128)(2,1)}, u32[]{:S(2)}, u32[]{:S(2)}) collective-permute-start(bf16[2,192,768]{2,1,0:T(8,128)(2,1)S(1)} %collective-permute-done.20.w1_in), channel_id=1, source_target_pairs={{0,4},{4,0},{8,12},{12,8},{16,20},{20,16},{24,28},{28,24},{1,5},{5... | collective-permute-start | bytes 1769480 | tf_op jit(solution)/shard_map/ppermute | solution.py:36
  106.5 2.4 %collective-permute-start.24 = (f32[256,768]{1,0:T(8,128)S(1)}, f32[256,768]{1,0:T(8,128)S(1)}, u32[]{:S(2)}, u32[]{:S(2)}) collective-permute-start(f32[256,768]{1,0:T(8,128)S(1)} %get-tuple-element.115), channel_id=1, source_target_pairs={{0,1},{1,0},{2,3},{3,2},{4,5},{5,4},{6,7},{7,6},{8,9},{9,8},{10,11... | collective-permute-start | bytes 2359304 | tf_op jit(solution)/shard_map/ppermute | solution.py:28
  112.1 1.8 collective-permute-start.25
  117.8 16.3 %collective-permute-start.26 = (bf16[2,192,768]{2,1,0:T(8,128)(2,1)S(1)}, bf16[2,192,768]{2,1,0:T(8,128)(2,1)S(1)}, u32[]{:S(2)}, u32[]{:S(2)}) collective-permute-start(bf16[2,192,768]{2,1,0:T(8,128)(2,1)S(1)} %get-tuple-element.136), channel_id=1, source_target_pairs={{0,2},{1,3},{2,0},{3,1},{4,6},{5,7},{6,4},{7,5},{8,10},{9,11},{10,... | collective-permute-start | bytes 1769480 | tf_op jit(solution)/shard_map/ppermute | solution.py:32
  119.1 15.9 %collective-permute-start.27 = (bf16[2,192,768]{2,1,0:T(8,128)(2,1)S(1)}, bf16[2,192,768]{2,1,0:T(8,128)(2,1)S(1)}, u32[]{:S(2)}, u32[]{:S(2)}) collective-permute-start(bf16[2,192,768]{2,1,0:T(8,128)(2,1)S(1)} %get-tuple-element.138), channel_id=1, source_target_pairs={{0,4},{4,0},{8,12},{12,8},{16,20},{20,16},{24,28},{28,24},{1,5},{5... | collective-permute-start | bytes 1769480 | tf_op jit(solution)/shard_map/ppermute | solution.py:36
  136.0 2.3 collective-permute-start.28
  140.6 4.3 %collective-permute-start.29 = (bf16[256,768]{1,0:T(8,128)(2,1)S(1)}, bf16[256,768]{1,0:T(8,128)(2,1)S(1)}, u32[]{:S(2)}, u32[]{:S(2)}) collective-permute-start(bf16[256,768]{1,0:T(8,128)(2,1)S(1)} %get-tuple-element.143.a0), channel_id=1, source_target_pairs={{0,1},{1,0},{2,3},{3,2},{4,5},{5,4},{6,7},{7,6},{8,9},{9,8},{10,11... | collective-permute-start | bytes 1179656 | tf_op jit(solution)/shard_map/ppermute | solution.py:28
  140.8 18.5 %collective-permute-start.40 = (bf16[2,192,768]{2,1,0:T(8,128)(2,1)}, bf16[2,192,768]{2,1,0:T(8,128)(2,1)S(1)}, u32[]{:S(2)}, u32[]{:S(2)}) collective-permute-start(bf16[2,192,768]{2,1,0:T(8,128)(2,1)} %get-tuple-element.175), channel_id=1, source_target_pairs={{0,2},{1,3},{2,0},{3,1},{4,6},{5,7},{6,4},{7,5},{8,10},{9,11},{10,... | collective-permute-start | bytes 1769480 | tf_op jit(solution)/shard_map/ppermute | solution.py:32
  141.2 20.4 %collective-permute-start.43 = (bf16[2,192,768]{2,1,0:T(8,128)(2,1)}, bf16[2,192,768]{2,1,0:T(8,128)(2,1)}, u32[]{:S(2)}, u32[]{:S(2)}) collective-permute-start(bf16[2,192,768]{2,1,0:T(8,128)(2,1)} %get-tuple-element.176), channel_id=1, source_target_pairs={{0,4},{4,0},{8,12},{12,8},{16,20},{20,16},{24,28},{28,24},{1,5},{5... | collective-permute-start | bytes 1769480 | tf_op jit(solution)/shard_map/ppermute | solution.py:36
  142.7 27.6 %collective-permute-start.42 = (bf16[2,192,768]{2,1,0:T(8,128)(2,1)}, bf16[2,192,768]{2,1,0:T(8,128)(2,1)}, u32[]{:S(2)}, u32[]{:S(2)}) collective-permute-start(bf16[2,192,768]{2,1,0:T(8,128)(2,1)} %add_convert_fusion.1), channel_id=1, source_target_pairs={{0,4},{4,0},{8,12},{12,8},{16,20},{20,16},{24,28},{28,24},{1,5},{5... | collective-permute-start | bytes 1769480 | tf_op jit(solution)/shard_map/ppermute | solution.py:36
  143.2 27.1 %collective-permute-start.41 = (bf16[2,192,768]{2,1,0:T(8,128)(2,1)}, bf16[2,192,768]{2,1,0:T(8,128)(2,1)}, u32[]{:S(2)}, u32[]{:S(2)}) collective-permute-start(bf16[2,192,768]{2,1,0:T(8,128)(2,1)} %add_convert_fusion), channel_id=1, source_target_pairs={{0,2},{1,3},{2,0},{3,1},{4,6},{5,7},{6,4},{7,5},{8,10},{9,11},{10,... | collective-permute-start | bytes 1769480 | tf_op jit(solution)/shard_map/ppermute | solution.py:32
  158.5 19.6 %collective-permute-start.32 = (bf16[2,96,768]{2,1,0:T(8,128)(2,1)}, bf16[2,96,768]{2,1,0:T(8,128)(2,1)}, u32[]{:S(2)}, u32[]{:S(2)}) collective-permute-start(bf16[2,96,768]{2,1,0:T(8,128)(2,1)} %get-tuple-element.156), channel_id=1, source_target_pairs={{0,4},{4,0},{8,12},{12,8},{16,20},{20,16},{24,28},{28,24},{1,5},{5... | collective-permute-start | bytes 884744 | tf_op jit(solution)/shard_map/ppermute | solution.py:36
  160.2 19.7 %collective-permute-start.34 = (bf16[2,96,768]{2,1,0:T(8,128)(2,1)}, bf16[2,96,768]{2,1,0:T(8,128)(2,1)S(1)}, u32[]{:S(2)}, u32[]{:S(2)}) collective-permute-start(bf16[2,96,768]{2,1,0:T(8,128)(2,1)} %get-tuple-element.158), channel_id=1, source_target_pairs={{0,2},{1,3},{2,0},{3,1},{4,6},{5,7},{6,4},{7,5},{8,10},{9,11},{10,... | collective-permute-start | bytes 884744 | tf_op jit(solution)/shard_map/ppermute | solution.py:32
  173.3 12.6 %collective-permute-start.44 = (bf16[192,768]{1,0:T(8,128)(2,1)S(1)}, bf16[192,768]{1,0:T(8,128)(2,1)S(1)}, u32[]{:S(2)}, u32[]{:S(2)}) collective-permute-start(bf16[192,768]{1,0:T(8,128)(2,1)S(1)} %get-tuple-element.178), channel_id=1, source_target_pairs={{0,8},{4,12},{8,0},{12,4},{16,24},{20,28},{24,16},{28,20},{1,9},{5... | collective-permute-start | bytes 884744 | tf_op jit(solution)/shard_map/ppermute | solution.py:40
  175.6 23.5 %collective-permute-start.45 = (bf16[192,768]{1,0:T(8,128)(2,1)S(1)}, bf16[192,768]{1,0:T(8,128)(2,1)S(1)}, u32[]{:S(2)}, u32[]{:S(2)}) collective-permute-start(bf16[192,768]{1,0:T(8,128)(2,1)S(1)} %get-tuple-element.179), channel_id=1, source_target_pairs={{0,16},{4,20},{8,24},{12,28},{16,0},{20,4},{24,8},{28,12},{1,17},{... | collective-permute-start | bytes 884744 | tf_op jit(solution)/shard_map/ppermute | solution.py:40
  177.3 22.6 %collective-permute-start.46 = (bf16[192,768]{1,0:T(8,128)(2,1)S(1)}, bf16[192,768]{1,0:T(8,128)(2,1)S(1)}, u32[]{:S(2)}, u32[]{:S(2)}) collective-permute-start(bf16[192,768]{1,0:T(8,128)(2,1)S(1)} %get-tuple-element.180), channel_id=1, source_target_pairs={{0,24},{4,28},{8,16},{12,20},{16,8},{20,12},{24,0},{28,4},{1,25},{... | collective-permute-start | bytes 884744 | tf_op jit(solution)/shard_map/ppermute | solution.py:40
  178.1 54.6 %collective-permute-start.30 = (f32[256,768]{1,0:T(8,128)}, f32[256,768]{1,0:T(8,128)}, u32[]{:S(2)}, u32[]{:S(2)}) collective-permute-start(f32[256,768]{1,0:T(8,128)} %get-tuple-element.151), channel_id=1, source_target_pairs={{0,1},{1,0},{2,3},{3,2},{4,5},{5,4},{6,7},{7,6},{8,9},{9,8},{10,11... | collective-permute-start | bytes 2359304 | tf_op jit(solution)/shard_map/ppermute | solution.py:28
  179.8 36.1 %collective-permute-start.31 = (bf16[2,96,768]{2,1,0:T(8,128)(2,1)}, bf16[2,96,768]{2,1,0:T(8,128)(2,1)S(1)}, u32[]{:S(2)}, u32[]{:S(2)}) collective-permute-start(bf16[2,96,768]{2,1,0:T(8,128)(2,1)} %get-tuple-element.154), channel_id=1, source_target_pairs={{0,2},{1,3},{2,0},{3,1},{4,6},{5,7},{6,4},{7,5},{8,10},{9,11},{10,... | collective-permute-start | bytes 884744 | tf_op jit(solution)/shard_map/ppermute | solution.py:32
  185.9 30.0 %collective-permute-start.36 = (bf16[2,96,768]{2,1,0:T(8,128)(2,1)}, bf16[2,96,768]{2,1,0:T(8,128)(2,1)}, u32[]{:S(2)}, u32[]{:S(2)}) collective-permute-start(bf16[2,96,768]{2,1,0:T(8,128)(2,1)} %get-tuple-element.159), channel_id=1, source_target_pairs={{0,4},{4,0},{8,12},{12,8},{16,20},{20,16},{24,28},{28,24},{1,5},{5... | collective-permute-start | bytes 884744 | tf_op jit(solution)/shard_map/ppermute | solution.py:36
  199.1 16.8 %collective-permute-start.33 = (bf16[2,96,768]{2,1,0:T(8,128)(2,1)}, bf16[2,96,768]{2,1,0:T(8,128)(2,1)}, u32[]{:S(2)}, u32[]{:S(2)}) collective-permute-start(bf16[2,96,768]{2,1,0:T(8,128)(2,1)} %add_convert_fusion.4), channel_id=1, source_target_pairs={{0,2},{1,3},{2,0},{3,1},{4,6},{5,7},{6,4},{7,5},{8,10},{9,11},{10,... | collective-permute-start | bytes 884744 | tf_op jit(solution)/shard_map/ppermute | solution.py:32
  200.6 15.3 %collective-permute-start.35 = (bf16[2,96,768]{2,1,0:T(8,128)(2,1)}, bf16[2,96,768]{2,1,0:T(8,128)(2,1)}, u32[]{:S(2)}, u32[]{:S(2)}) collective-permute-start(bf16[2,96,768]{2,1,0:T(8,128)(2,1)} %add_convert_fusion.3), channel_id=1, source_target_pairs={{0,4},{4,0},{8,12},{12,8},{16,20},{20,16},{24,28},{28,24},{1,5},{5... | collective-permute-start | bytes 884744 | tf_op jit(solution)/shard_map/ppermute | solution.py:36
  202.8 12.4 %all-to-all-start = ((f32[32,1,288]{2,1,0:T(1,128)}), f32[32,1,288]{2,1,0:T(1,128)S(1)}, u32[]{:S(2)}, u32[]{:S(2)}) async-start(f32[32,1,288]{2,1,0:T(1,128)} %copy.42), calls=%async_computation | async-start | bytes 98304 | tf_op jit(solution)/shard_map/all_to_all | solution.py:882
  217.3 7.7 %collective-permute-start.37 = (bf16[96,768]{1,0:T(8,128)(2,1)S(1)}, bf16[96,768]{1,0:T(8,128)(2,1)S(1)}, u32[]{:S(2)}, u32[]{:S(2)}) collective-permute-start(bf16[96,768]{1,0:T(8,128)(2,1)S(1)} %get-tuple-element.161), channel_id=1, source_target_pairs={{0,8},{4,12},{8,0},{12,4},{16,24},{20,28},{24,16},{28,20},{1,9},{5... | collective-permute-start | bytes 442376 | tf_op jit(solution)/shard_map/ppermute | solution.py:40
  217.9 13.9 %collective-permute-start.38 = (bf16[96,768]{1,0:T(8,128)(2,1)S(1)}, bf16[96,768]{1,0:T(8,128)(2,1)S(1)}, u32[]{:S(2)}, u32[]{:S(2)}) collective-permute-start(bf16[96,768]{1,0:T(8,128)(2,1)S(1)} %get-tuple-element.162), channel_id=1, source_target_pairs={{0,16},{4,20},{8,24},{12,28},{16,0},{20,4},{24,8},{28,12},{1,17},{... | collective-permute-start | bytes 442376 | tf_op jit(solution)/shard_map/ppermute | solution.py:40
  218.9 12.9 %collective-permute-start.39 = (bf16[96,768]{1,0:T(8,128)(2,1)S(1)}, bf16[96,768]{1,0:T(8,128)(2,1)S(1)}, u32[]{:S(2)}, u32[]{:S(2)}) collective-permute-start(bf16[96,768]{1,0:T(8,128)(2,1)S(1)} %get-tuple-element.163), channel_id=1, source_target_pairs={{0,24},{4,28},{8,16},{12,20},{16,8},{20,12},{24,0},{28,4},{1,25},{... | collective-permute-start | bytes 442376 | tf_op jit(solution)/shard_map/ppermute | solution.py:40
  (29 other events, 339.3 us)

commit v2 on v1

--- a/solution.py
+++ b/solution.py
@@ -65,32 +65,17 @@
     return [z, x, y, x_swap(y[:2]), y_swap(x[2:])]
 
 
-def gather_xy(lo, hi):
-    y_lo, x_hi = y_swap(lo), x_swap(hi)
-    x_lo, y_hi = x_swap(lo), y_swap(hi)
-    return [(lo, hi), (x_lo, x_hi), (y_lo, y_hi), (x_swap(y_lo), y_swap(x_hi))]
-
-
 def gather_any(shard):
     whole = lax.all_gather(shard, "batch", axis=0)
     return [whole, x_swap(whole)]
 
 
-def scatter_first(parts):
-    (g_lo, g_hi), (x_lo, x_hi), (y_lo, y_hi), (d_lo, d_hi) = parts
-    from_x, from_y = x_swap(d_lo), y_swap(d_hi)
-    y_lo, x_hi = add_low(y_lo, from_x), add_low(x_hi, from_y)
-    return (g_lo, g_hi, x_lo, x_hi, y_lo, y_hi), (y_lo, x_hi)
-
-
-def scatter_xy(g_lo, g_hi, x_lo, x_hi, y_lo, y_hi):
-    y_hi, x_lo = y_swap(y_hi), x_swap(x_lo)
-    y_lo, x_hi = y_swap(y_lo), x_swap(x_hi)
-    return combine(g_lo, g_hi, x_lo, x_hi, y_lo, y_hi)
-
-
-def scatter_z(mine, others):
-    return (mine,) + tuple(z_swap(others[k - 1], k) for k in (1, 2, 3))
+def scatter_xy(z, x, y):
+    return z, x_swap(x), y_swap(y)
+
+
+def scatter_z(others):
+    return [z_swap(others[k - 1], k) for k in (1, 2, 3)]
 
 
 def scatter_any(parts):
@@ -106,7 +91,8 @@
     vmem = pl.BlockSpec(memory_space=pltpu.VMEM)
     hbm = pl.BlockSpec(memory_space=pltpu.HBM)
     smem = pl.BlockSpec(memory_space=pltpu.SMEM)
-    ins = [smem] + [hbm if i in far_in else vmem for i in range(1, len(operands))]
+    ins = [hbm if i in far_in else vmem for i in range(len(operands))]
+    ins = [smem if v.dtype == jnp.int32 else spec for spec, v in zip(ins, operands)]
     outs = [hbm if i in far_out else vmem for i in range(len(out_shape))]
     scratch = list(scratch) + ([pltpu.SemaphoreType.DMA((sems,))] if sems else [])
     operands = [
@@ -152,77 +138,180 @@
     return jax.ShapeDtypeStruct(dims, dtype)
 
 
-def combine_kernel(_, g_lo, g_hi, x_lo, x_hi, y_lo, y_hi, mine, one, two, three):
-    outs = (mine, one, two, three)
-    for k in range(4):
-        g, xx, yy = (g_lo, x_lo, y_lo) if k < 2 else (g_hi, x_hi, y_hi)
-        total = g[k % 2].astype(F32) + xx[k % 2].astype(F32) + yy[k % 2].astype(F32)
-        outs[k][...] = total.astype(outs[k].dtype)
-
-
-def combine(*parts):
-    rows = parts[0].shape[1]
+def add_moved_kernel(x, for_x, y, for_y, x_out, y_out):
+    y_out[0:2] = add_low(y[0:2], for_y[...])
+    y_out[2:4] = y[2:4]
+    x_out[0:2] = x[0:2]
+    x_out[2:4] = add_low(x[2:4], for_x[...])
+
+
+def add_moved(x, for_x, y, for_y):
+    return call(
+        add_moved_kernel,
+        (shape(x.shape), shape(y.shape)),
+        (x, for_x, y, for_y),
+        cost=est(1000, 1000),
+        limit=8,
+    )
+
+
+def combine_kernel(parts, z, x, y, *refs):
+    outs, (mine, low, sems) = refs[: 1 + 3 * parts], refs[1 + 3 * parts :]
+    copies = Copies(sems)
+    rows = z.shape[1] // parts
+    for k in (1, 2, 3, 0):
+        total = z[k].astype(F32) + x[k].astype(F32) + y[k].astype(F32)
+        if k == 0:
+            mine[...] = total
+            copies.start(mine, outs[0])
+        else:
+            low[k - 1] = total.astype(BF16)
+            for i in range(parts):
+                copies.start(low.at[k - 1, pl.ds(rows * i, rows)], outs[1 + 3 * i + k - 1])
+    copies.wait()
+
+
+def combine(z, x, y, parts):
+    rows = z.shape[1]
     mine, *others = call(
-        combine_kernel,
-        (shape((rows, D), F32),) + (shape((rows, D)),) * 3,
-        (jnp.zeros((1,), jnp.int32), *parts),
-        cost=est(8 * rows * D, 24 * rows * D),
-    )
-    return mine, others
+        functools.partial(combine_kernel, parts),
+        (shape((rows, D), F32),) + (shape((rows // parts, D)),) * (3 * parts),
+        (z, x, y),
+        scratch=[pltpu.VMEM((rows, D), F32), pltpu.VMEM((3, rows, D), BF16)],
+        cost=est(1000, 1000),
+        limit=8,
+        far_out=range(1 + 3 * parts),
+        sems=1 + 3 * parts,
+    )
+    return mine, [others[3 * i : 3 * i + 3] for i in range(parts)]
 
 
 def total_of(refs):
     return refs[0][...] + refs[1][...].astype(F32) + refs[2][...].astype(F32) + refs[3][...].astype(F32)
 
 
-def finish_attend_kernel(_, mine, one, two, three, qkv, proj):
+def finish_attend_kernel(mine, one, two, three, qkv, proj):
     total = total_of((mine, one, two, three))
     for hh in range(3):
         for t in range(3):
             at, to = 192 * t + 64 * hh, 192 * hh + 64 * t
             qkv[:, to : to + 64] = total[:, at : at + 64]
-    proj[...] = total[:, 576:].T
+    proj[...] = total[:, 576:]
 
 
 def finish_attend(parts):
     rows = parts[0].shape[0]
     return call(
         finish_attend_kernel,
-        (shape((rows, 576), F32), shape((192, rows), F32)),
-        (jnp.zeros((1,), jnp.int32), *parts),
+        (shape((rows, 576), F32), shape((rows, 192), F32)),
+        tuple(parts),
         cost=est(8 * rows * D, 16 * rows * D),
     )
 
 
-def finish_ffn_kernel(_, mine, one, two, three, up, down):
+def finish_ffn_kernel(mine, *refs):
+    ups, downs, (up, down) = refs[:3], refs[3:6], refs[6:]
     half = mine.shape[0] // 2
-    total = total_of((mine, one, two, three))
-    up[...] = total[:half].T
-    down[...] = total[half:]
-
-
-def finish_ffn(parts):
-    half = parts[0].shape[0] // 2
+    up[...] = mine[0:half] + sum(r[...].astype(F32) for r in ups)
+    down[...] = mine[half:] + sum(r[...].astype(F32) for r in downs)
+
+
+def finish_ffn(mine, ups, downs):
+    half = mine.shape[0] // 2
     return call(
         finish_ffn_kernel,
-        (shape((D, half), F32), shape((half, D), F32)),
-        (jnp.zeros((1,), jnp.int32), *parts),
-        cost=est(8 * half * D, 32 * half * D),
-    )
+        (shape((half, D), F32), shape((half, D), F32)),
+        (mine, *ups, *downs),
+        cost=est(1000, 1000),
+        limit=8,
+    )
+
+
+def exchange_kernel(zero, one, two, *refs):
+    ubs, out = refs[:4], refs[4]
+    vecs = jnp.concatenate([zero[...], one[...], two[...]])
+    width = D // out.shape[0]
+    out[...] = jnp.zeros(out.shape, F32)
+    for i in range(out.shape[0]):
+        out[i, 0:8, 0:width] = vecs[:, width * i : width * i + width]
+    for spot in range(4):
+        for kz in range(4):
+            out[slot_of(spot, kz), 0:1, 24:120] = ubs[spot][:, 96 * kz : 96 * kz + 96]
+
+
+def exchange_terms(zero, one, two, ubs, devices):
+    return call(
+        exchange_kernel,
+        (shape((devices, 8, 128), F32),),
+        (zero, one, two, *ubs),
+        cost=est(1000, 1000),
+        limit=8,
+    )[0]
 
 
 def flip(a, bit):
     return a + bit - 2 * a * bit
 
 
-def live_units(meta):
-    c, kind = meta[0], meta[1]
-    first = meta[2]
+def pack_kernel(qkv_in, proj_in, up_in, down_in, bias, vectors, a_out, fa_out, fb_out, a, p, f, sems):
+    rows_q, rows_p, half = qkv_in.shape[0], proj_in.shape[0], down_in.shape[0]
+    copies = Copies(sems)
+    copies.start(qkv_in, a.at[pl.ds(0, rows_q)])
+    copies.start(proj_in, p)
+    copies.start(up_in, f.at[pl.ds(0, half)])
+    copies.start(down_in, f.at[pl.ds(half, half)])
+    width = vectors.shape[1]
+    b, h = lax.axis_index("batch"), lax.axis_index("head")
+    me = b * lax.axis_size("head") + h
+    v = vectors[...].astype(F32)
+    v = jnp.concatenate([v] * (D // width), 1)
+    lane = lax.broadcasted_iota(jnp.int32, (8, D), 1)
+    mine = jnp.logical_and(lane >= me * width, lane < me * width + width)
+    v = jnp.where(mine, v, 0.0)
+    extra = jnp.concatenate([bias[...].astype(F32), jnp.zeros((1, D - half), F32)], 1)
+    v = jnp.concatenate([v, extra, jnp.zeros((7, D), F32)])
+    copies.wait()
+    a_out[0:rows_q] = a[0:rows_q]
+    q = p[...]
+    a_out[rows_q : rows_q + rows_p] = jnp.concatenate(
+        [q[:, 192 * i : 192 * i + 192] for i in (0, 2, 1, 3)], 1
+    )
+    a_out[rows_q + rows_p :] = v.astype(BF16)
+    fa_out[...] = f[0 : fa_out.shape[0]]
+    fb_out[...] = f[fa_out.shape[0] :]
+
+
+def pack(qkv, proj, up, down, bias, vectors):
+    rows, half = qkv.shape[0] + proj.shape[0] + 16, down.shape[0]
+    return call(
+        pack_kernel,
+        (shape((rows, D)), shape((rows, D)), shape((2 * half - rows, D))),
+        (qkv, proj, up, down, bias[None], jnp.stack(vectors)),
+        scratch=[
+            pltpu.VMEM((rows, D), BF16),
+            pltpu.VMEM(proj.shape, BF16),
+            pltpu.VMEM((2 * half, D), BF16),
+        ],
+        cost=est(1000, 1000),
+        limit=8,
+        far_in=(0, 1, 2, 3),
+        sems=4,
+    )
+
+
+def place_here():
+    b, h = lax.axis_index("batch"), lax.axis_index("head")
+    return lax.rem(h, 2), lax.div(b, 2), lax.rem(b, 2), lax.div(h, 2)
+
+
+def live_units(bucket, lengths):
+    x = place_here()[3]
+    kind, first = bucket[x], lengths[x, 0]
     units = []
     for u in range(UNITS):
         far = jnp.clip(first - SMALL * u, 0, SMALL)
-        units.append(jnp.where(kind == 1, far, meta[2 + u]))
-    return c, kind, units
+        units.append(jnp.where(kind == 1, far, lengths[x, u]))
+    return kind, units
 
 
 def place_of(index, c):
@@ -247,8 +336,8 @@
     return jnp.concatenate(parts, 1)
 
 
-def fetch_shards(meta, copies, sources, slots):
-    c, z, y, x = meta[0], meta[6], meta[7], meta[8]
+def fetch_shards(copies, sources, slots):
+    c, z, y, x = place_here()
     zl, zh = lax.rem(z, 2), lax.div(z, 2)
     for swapped in range(2):
         cc = c if swapped == 0 else 1 - c
@@ -261,22 +350,37 @@
                 copies.start(src, slots.at[zi * 8 + j])
 
 
-def attend_kernel(rows_q, rows_p, meta, x0, x1, *refs):
+def slot_of(spot, kz):
+    c, z, y, x = place_here()
+    zi = flip(lax.rem(z, 2), kz % 2) + 2 * flip(lax.div(z, 2), kz // 2)
+    return zi * 8 + flip(y, spot // 2) * 4 + flip(x, spot % 2) * 2 + c
+
+
+def bias_order(slots, row, out):
+    for spot in range(4):
+        for kz in range(4):
+            b = slots[slot_of(spot, kz), row : row + 1, 0:128].astype(F32)
+            at = 384 * spot + 96 * kz
+            out[:, at : at + 96] = b[:, 0:96]
+
+
+def attend_kernel(rows_q, rows_p, bucket, lengths, x0, x1, *refs):
     sources = 10 if rows_q else 2
     weights, refs = refs[:sources], refs[sources:]
     (ctx0, ctx1, q_out, k_out, v_out, ctx_out, probs_out, wr_out), refs = refs[:8], refs[8:]
     if rows_q:
-        (wp_out, small_out), refs = refs[:2], refs[2:]
+        (ub_out, wp_out, small_out), refs = refs[:3], refs[3:]
         (q, k, v, ctx, probs, wr, mask, xs, slots, wp, small, sems) = refs
     else:
         (q, k, v, ctx, probs, wr, mask, xs, w, small, sems) = refs
     copies = Copies(sems)
-    c, kind, units = live_units(meta)
+    c = place_here()[0]
+    kind, units = live_units(bucket, lengths)
     half = x0.shape[0]
     copies.start(x0, xs.at[0:half])
     copies.start(x1, xs.at[half : 2 * half])
     if rows_q:
-        fetch_shards(meta, copies, weights, slots)
+        fetch_shards(copies, weights, slots)
     else:
         copies.start(weights[0], w)
         copies.start(weights[1], small)
@@ -315,6 +419,7 @@
             wp[rows_p * i : rows_p * i + rows_p] = slots[i, rows_q : rows_q + rows_p]
         copies.start(wp, wp_out)
         copies.start(small, small_out)
+        bias_order(slots, rows_q + rows_p + 8, ub_out)
     lane = lax.broadcasted_iota(jnp.int32, (half, 128), 1)
     for pair in range(3):
         lanes = slice(128 * pair, 128 * pair + 128)
@@ -339,7 +444,7 @@
     copies.wait()
 
 
-def attend(meta, x0, x1, weights, rows_q=0, rows_p=0, rows_s=16):
+def attend(bucket, lengths, x0, x1, weights, rows_q=0, rows_p=0, rows_s=16):
     half = x0.shape[0]
     n = 2 * half
     direct = rows_q > 0
@@ -360,7 +465,7 @@
         pltpu.VMEM((n, D), BF16),
     ]
     if direct:
-        outs += [shape((D, D)), shape((rows_s, D), F32)]
+        outs += [shape((1, FF // 2), F32), shape((D, D)), shape((rows_s, D), F32)]
         scratch += [
             pltpu.VMEM((32, rows_q + rows_p + rows_s, D), BF16),
             pltpu.VMEM((D, D), BF16),
@@ -368,7 +473,7 @@
         ]
     else:
         scratch += [pltpu.VMEM((1152, D), BF16), pltpu.VMEM((rows_s, D), F32)]
-    operands = (meta, x0, x1, *weights)
+    operands = (bucket, lengths, x0, x1, *weights)
     return call(
         functools.partial(attend_kernel, rows_q, rows_p),
         outs,
@@ -376,8 +481,8 @@
         scratch=scratch,
         cost=est(2 * n * D * 1152 + 8 * n * n * 384, 12e6, 6 * n * n),
         limit=32,
-        far_in=range(1, len(operands)),
-        far_out=range(2, len(outs)),
+        far_in=range(2, len(operands)),
+        far_out=[i for i in range(2, len(outs)) if i != 8],
         sems=50,
     )
 
@@ -397,12 +502,12 @@
 
 
 def first_kernel(
-    meta, x_in, ctx_own, ctx_in, wp_in, small_in, low, first_out, normal_out, scale, x, wp, small, first, normal, sems
+    x_in, ctx_own, ctx_in, wp_in, small_in, low, first_out, normal_out, scale, x, wp, small, first, normal, sems
 ):
     copies = Copies(sems)
     for src, dst in ((wp_in, wp), (x_in, x), (small_in, small)):
         copies.start(src, dst)
-    c = meta[0]
+    c = place_here()[0]
     copies.wait()
     mine = pl.multiple_of(c * 384, 128)
     theirs = pl.multiple_of((1 - c) * 384, 128)
@@ -418,12 +523,12 @@
     copies.wait()
 
 
-def first_norm(meta, x, ctx_own, ctx_in, wp, small):
+def first_norm(x, ctx_own, ctx_in, wp, small):
     n = x.shape[0]
     return call(
         first_kernel,
         (shape((n, D)), shape((n, D), F32), shape((n, D), F32), shape((n, 128), F32)),
-        (meta, x, ctx_own, ctx_in, wp, small),
+        (x, ctx_own, ctx_in, wp, small),
         scratch=[
             pltpu.VMEM((n, D), BF16),
             pltpu.VMEM((D, D), BF16),
@@ -432,7 +537,7 @@
             pltpu.VMEM((n, D), F32),
         ],
         cost=est(2 * n * D * D, 5e6),
-        far_in=(1, 4, 5),
+        far_in=(0, 3, 4),
         far_out=(1, 2),
         sems=5,
     )
@@ -448,18 +553,20 @@
     return up, down
 
 
-def ffn_kernel(first, meta, x0, x1, ub, w0_in, w1_in, *refs):
+def ffn_kernel(first, count, x0, x1, ub, *refs):
+    far, refs = refs[:count], refs[count:]
     if first:
         in0 = in1 = None
     else:
         (in0, in1), refs = refs[:2], refs[2:]
-    hid_out, slope_out, out0, out1, w0, w1, hid, slope, sems = refs
+    (hid_out, slope_out, out0, out1), refs = refs[:4], refs[4:]
+    near, (hid, slope, sems) = refs[:count], refs[count:]
     copies = Copies(sems)
-    copies.start(w0_in, w0)
-    copies.start(w1_in, w1)
+    for src, dst in zip(far, near):
+        copies.start(src, dst)
     copies.wait()
     half = x0.shape[0]
-    uw, dw = ffn_weights((w0, w1))
+    uw, dw = ffn_weights(near)
     for i, (xr, before, out) in enumerate(((x0, in0, out0), (x1, in1, out1))):
         rws = slice(half * i, half * i + half)
         up = nt(xr[...], uw) + ub[...]
@@ -470,34 +577,41 @@
         copies.start(hid.at[rws], hid_out.at[rws])
         copies.start(slope.at[rws], slope_out.at[rws])
         part = nn(hd, dw)
-        out[...] = part if before is None else before[...] + part
-    copies.wait()
-
-
-def ffn(meta, x0, x1, ub, weights, sums):
-    half, width = x0.shape[0], ub.shape[1]
+        part = part if before is None else before[...] + part
+        out[...] = part.astype(out.dtype)
+    copies.wait()
+
+
+def ffn(x0, x1, ub, weights, sums, last):
+    half, width, count = x0.shape[0], ub.shape[1], len(weights)
     n = 2 * half
     return call(
-        functools.partial(ffn_kernel, not sums),
-        (shape((n, width)), shape((n, width)), shape((half, D), F32), shape((half, D), F32)),
-        (meta, x0, x1, ub, *weights, *sums),
+        functools.partial(ffn_kernel, not sums, count),
+        (
+            shape((n, width)),
+            shape((n, width)),
+            shape((half, D), F32),
+            shape((half, D), BF16 if last else F32),
+        ),
+        (x0, x1, ub, *weights, *sums),
         scratch=[pltpu.VMEM(w.shape, BF16) for w in weights] + [pltpu.VMEM((n, width), BF16)] * 2,
         cost=est(4 * n * D * width, 4 * D * width + 5e6, 2 * n * width),
-        far_in=(4, 5),
+        far_in=range(3, 3 + count),
         far_out=(0, 1),
-        sems=6,
+        sems=4 + count,
     )
 
 
 def second_kernel(
-    meta, first_in, part, got, small_in, cot_in, out, sum_two, low, sums, first, small, cot, sems
+    bucket, lengths, first_in, part, got, small_in, cot_in, out, sum_two, low, sums, first, small, cot, sems
 ):
     copies = Copies(sems)
     for src, dst in ((first_in, first), (small_in, small), (cot_in, cot)):
         copies.start(src, dst)
-    c, _, units = live_units(meta)
-    copies.wait()
-    n, r = norm(first[...] + (part[...] + got[...] + small[5:6]))
+    c = place_here()[0]
+    _, units = live_units(bucket, lengths)
+    copies.wait()
+    n, r = norm(first[...] + (part[...] + got[...].astype(F32) + small[5:6]))
     out[...] = (n * small[6:7] + small[7:8]).astype(BF16)
     index = lax.broadcasted_iota(jnp.int32, (first.shape[0], 1), 0)
     live = live_of(place_of(index, c), units)
@@ -511,82 +625,95 @@
     sums[2:3] = jnp.sum(oc, 0, keepdims=True)
 
 
-def second_norm(meta, first, part, got, small, cot):
+def second_norm(bucket, lengths, first, part, got, small, cot):
     n = first.shape[0]
     return call(
         second_kernel,
         (shape((n, D)), shape((n, D), F32), shape((n, D)), shape((3, D), F32)),
-        (meta, first, part, got, small, cot),
+        (bucket, lengths, first, part, got, small, cot),
         scratch=[pltpu.VMEM((n, D), F32), pltpu.VMEM((16, D), F32), pltpu.VMEM((n, D), BF16)],
         cost=est(40 * n * D, 5e6),
-        far_in=(1, 4, 5),
+        far_in=(2, 5, 6),
         sems=3,
     )
 
 
-def ffn_back_kernel(first, meta, d0, d1, x0, x1, w0_in, w1_in, hid_in, slope_in, *refs):
+def ffn_back_kernel(first, lead, count, d0, d1, x0, x1, *refs):
+    far, hid_in, slope_in, refs = refs[:count], refs[count], refs[count + 1], refs[count + 2 :]
     if first:
         in0 = in1 = None
     else:
         (in0, in1), refs = refs[:2], refs[2:]
-    g0, g1, ub, out0, out1, w0, w1, hid, slope, sems = refs
+    outs, (ub, out0, out1), near, (hid, slope, sems) = (
+        refs[:count],
+        refs[count : count + 3],
+        refs[count + 3 : 2 * count + 3],
+        refs[2 * count + 3 :],
+    )
     copies = Copies(sems)
-    for src, dst in ((w0_in, w0), (w1_in, w1), (slope_in, slope), (hid_in, hid)):
+    half, width = x0.shape[0], hid.shape[1]
+    for src, dst in zip(far, near):
         copies.start(src, dst)
-    copies.wait()
-    half = x0.shape[0]
-    uw, dw = ffn_weights((w0, w1))
+    copies.start(slope_in.at[:, pl.ds(lead, width)], slope)
+    copies.start(hid_in.at[:, pl.ds(lead, width)], hid)
+    copies.wait()
+    uw, dw = ffn_weights(near)
     cots = []
     for i, (d, before, out) in enumerate(((d0, in0, out0), (d1, in1, out1))):
         rws = slice(half * i, half * i + half)
         uc = (nt(d[...], dw) * slope[rws].astype(F32)).astype(BF16)
         cots.append(uc)
         part = nn(uc, uw)
-        out[...] = part if before is None else before[...] + part
+        part = part if before is None else before[...] + part
+        out[...] = part.astype(out.dtype)
     ub[...] = jnp.sum(cots[0].astype(F32), 0, keepdims=True) + jnp.sum(
         cots[1].astype(F32), 0, keepdims=True
     )
     dg = (tn(hid[0:half], d0[...]) + tn(hid[half : 2 * half], d1[...])).astype(BF16)
     ug = (tn(cots[0], x0[...]) + tn(cots[1], x1[...])).astype(BF16)
-    if len(g0.shape) == 2:
-        g0[...], g1[...] = ug, dg
+    if len(outs[0].shape) == 2:
+        outs[0][...], outs[1][...] = ug, dg
     else:
-        rows = g0.shape[1] // 2
+        rows = outs[0].shape[1] // 2
         at = 0
-        for g in (g0, g1):
+        for g in outs:
             for i in range(g.shape[0]):
                 g[i, 0:rows] = ug[at : at + rows]
                 g[i, rows : 2 * rows] = dg[at : at + rows]
                 at += rows
 
 
-def ffn_back(meta, d0, d1, x0, x1, weights, hid, slope, sums):
-    half, width = x0.shape[0], hid.shape[1]
-    return call(
-        functools.partial(ffn_back_kernel, not sums),
+def ffn_back(d0, d1, x0, x1, weights, kept, lead, sums, last):
+    half, count = x0.shape[0], len(weights)
+    flat = len(weights[0].shape) == 2
+    width = weights[0].shape[0] if flat else sum(w.shape[0] * w.shape[1] // 2 for w in weights)
+    near = [pltpu.VMEM(w.shape, BF16) for w in weights]
+    *grads, ub, s0, s1 = call(
+        functools.partial(ffn_back_kernel, not sums, lead, count),
         (
-            shape(weights[0].shape),
-            shape(weights[1].shape),
+            *[shape(w.shape) for w in weights],
             shape((1, width), F32),
             shape((half, D), F32),
-            shape((half, D), F32),
+            shape((half, D), BF16 if last else F32),
         ),
-        (meta, d0, d1, x0, x1, *weights, hid, slope, *sums),
-        scratch=[pltpu.VMEM(v.shape, BF16) for v in (*weights, hid, slope)],
+        (d0, d1, x0, x1, *weights, *kept, *sums),
+        scratch=near + [pltpu.VMEM((2 * half, width), BF16)] * 2,
         cost=est(1000, 1000),
-        far_in=(5, 6, 7, 8),
-        sems=4,
-    )
+        far_in=range(4, 6 + count),
+        sems=2 + count,
+    )
+    return grads, ub, (s0, s1)
 
 
 def first_back_kernel(
-    meta, sum_two, part, got, normal_in, scale, small_in, sum_one, low, sums, normal, small, sems
+    sum_two, part, got, normal_in, scale, small_in, *refs
 ):
+    *refs, sum_one, low, sums, normal, small, sems = refs
     copies = Copies(sems)
     copies.start(normal_in, normal)
     copies.start(small_in, small)
     copies.wait()
-    fc = sum_two[...] + part[...] + got[...]
+    fc = sum_two[...] + part[...] + got[...].astype(F32)
     n = normal[...]
     so = norm_back(fc, n, scale[:, 0:1], small[3:4])
     sum_one[...] = so
@@ -595,28 +722,32 @@
     sums[0:1] = jnp.sum(lo.astype(F32), 0, keepdims=True)
     sums[1:2] = jnp.sum(fc * n, 0, keepdims=True)
     sums[2:3] = jnp.sum(fc, 0, keepdims=True)
-
-
-def first_back(meta, sum_two, part, got, normal, scale, small):
+    if refs:
+        add_moved_kernel(*refs)
+
+
+def first_back(sum_two, part, got, normal, scale, small, moved=()):
     n = sum_two.shape[0]
-    return call(
+    outs = [shape(moved[0].shape), shape(moved[2].shape)] if moved else []
+    *added, sum_one, low, sums = call(
         first_back_kernel,
-        (shape((n, D), F32), shape((n, D)), shape((3, D), F32)),
-        (meta, sum_two, part, got, normal, scale, small),
+        (*outs, shape((n, D), F32), shape((n, D)), shape((3, D), F32)),
+        (sum_two, part, got, normal, scale, small, *moved),
         scratch=[pltpu.VMEM((n, D), F32), pltpu.VMEM((16, D), F32)],
-        cost=est(30 * n * D, 5e6),
-        far_in=(4, 6),
+        cost=est(1000, 1000),
+        far_in=(3, 5),
         sems=2,
     )
-
-
-def attend_back_kernel(sets, meta, a0, a1, *refs):
+    return added, sum_one, low, sums
+
+
+def attend_back_kernel(sets, a0, a1, *refs):
     far, outs, (in0, in1, sums), refs = refs[:9], refs[9 : 9 + sets], refs[9 + sets : 12 + sets], refs[12 + sets :]
     wp, v, probs, k, q, wr, x0, x1, ctx, dctx, cots, grads, sems = refs
     copies = Copies(sems)
     near = (wp, v, probs, k, q, wr, x0, x1, ctx)
     got = [copies.start(src, dst) for src, dst in zip(far, near)]
-    c = meta[0]
+    c, z, y, x = place_here()
     half = a0.shape[0]
     n = 2 * half
     copies.wait(got[0])
@@ -675,31 +806,33 @@
     if sets == 1:
         copies.start(grads, outs[0])
     else:
-        z, y, x = meta[6], meta[7], meta[8]
         rows = outs[0].shape[1]
         for spot in (3, 2, 1, 0):
             g, yi = flip(x, spot % 2), flip(y, spot // 2)
             for kz in range(4):
                 zi = flip(lax.rem(z, 2), kz % 2) + 2 * flip(lax.div(z, 2), kz // 2)
                 at = pl.multiple_of((2 * zi + yi) * rows, rows)
-                copies.start(grads.at[g, pl.ds(at, rows)], outs[2 * spot + kz // 2].at[kz % 2])
-    copies.wait()
-
-
-def attend_back(direct, meta, a0, a1, x0, x1, wp, wr, q, k, v, ctx, probs):
+                dst = outs[spot].at[kz] if spot < 3 else outs[3 + kz // 2].at[kz % 2]
+                copies.start(grads.at[g, pl.ds(at, rows)], dst)
+    copies.wait()
+
+
+def attend_back(direct, a0, a1, x0, x1, wp, wr, q, k, v, ctx, probs):
     half = a0.shape[0]
     n = 2 * half
-    sets = (shape((2, 96, D)),) * 8 if direct else (shape((2, D, D)),)
+    sets = (shape((2, D, D)),)
+    if direct:
+        sets = (shape((4, 96, D)),) * 3 + (shape((2, 96, D)),) * 2
     far = (wp, v, probs, k, q, wr, x0, x1, ctx)
     return call(
         functools.partial(attend_back_kernel, len(sets)),
         (*sets, shape((half, D), F32), shape((half, D), F32), shape((2, D), F32)),
-        (meta, a0, a1, *far),
+        (a0, a1, *far),
         scratch=[pltpu.VMEM(f.shape, BF16) for f in far]
         + [pltpu.VMEM((n, 384), BF16), pltpu.VMEM((n, 1280), BF16), pltpu.VMEM((2, D, D), BF16)],
-        cost=est(2 * n * D * 3500 + 14 * n * n * 384, 14e6),
+        cost=est(1000, 1000),
         limit=32,
-        far_in=range(3, 12),
+        far_in=range(2, 11),
         far_out=range(len(sets)),
         sems=26,
     )
@@ -735,51 +868,49 @@
     z, y = b // 2, b % 2
     wq, wp, wf = 3 * D // devices, D // devices, FF // devices
 
-    vectors = jnp.stack(
-        [
-            query_bias,
-            value_bias,
-            proj_bias,
-            first_gain,
-            first_shift,
-            down_bias,
-            second_gain,
-            second_shift,
-        ]
-    )
-    small = lax.dynamic_update_slice(jnp.zeros((16, D), BF16), vectors, (0, me * wp))
-    per_row = D // wf
-    small = lax.dynamic_update_slice(
-        small, up_bias[None, :], (8 + me // per_row, (me % per_row) * wf)
-    )
-    proj_t = proj_weight.T.reshape(wp, 2, 2, 192).transpose(0, 2, 1, 3).reshape(wp, D)
-    a_shard = jnp.concatenate([qkv_weight.T, proj_t, small])
-    f_shard = jnp.concatenate([up_weight.T, down_weight])
+    vectors = [
+        query_bias,
+        value_bias,
+        proj_bias,
+        first_gain,
+        first_shift,
+        down_bias,
+        second_gain,
+        second_shift,
+    ]
+    if direct:
+        a_shard, fa_shard, fb_shard = pack(
+            qkv_weight.T, proj_weight.T, up_weight.T, down_weight, up_bias, vectors
+        )
+    else:
+        small = lax.dynamic_update_slice(
+            jnp.zeros((16, D), BF16), jnp.stack(vectors), (0, me * wp)
+        )
+        per_row = D // wf
+        small = lax.dynamic_update_slice(
+            small, up_bias[None, :], (8 + me // per_row, (me % per_row) * wf)
+        )
+        proj_t = proj_weight.T.reshape(wp, 2, 2, 192).transpose(0, 2, 1, 3).reshape(wp, D)
+        a_shard = jnp.concatenate([qkv_weight.T, proj_t, small])
     other_in = core_swap(inputs)
-    meta = jnp.concatenate(
-        [
-            jnp.stack([c, lax.dynamic_index_in_dim(bucket, x, 0, keepdims=False)]),
-            lax.dynamic_index_in_dim(lengths, x, 0, keepdims=False),
-            jnp.stack([z, y, x]),
-        ]
-    ).astype(jnp.int32)
-
     k = jnp.arange(batch_count * 2)
     if direct:
         a_z = jnp.stack(z_line(a_shard))
-        f_z = z_line(after(f_shard, a_z))
-        f_lo, f_hi = jnp.stack(f_z[:2]), jnp.stack(f_z[2:])
-        a_own = gather_four(a_z)
-        f_lo, f_hi, _ = lax.optimization_barrier((f_lo, f_hi, a_own))
-        f_all = gather_xy(f_lo, f_hi)
-        a_swapped = [core_swap(v) for v in a_own]
-        ctx_own, ctx_other, q, kk, v, ctx, probs, wr, proj_w, small_all = attend(
-            meta, inputs, other_in, (*a_own, *a_swapped), wq, wp
+        a_z, other_in = lax.optimization_barrier((a_z, other_in))
+        fa_z = z_line(after(fa_shard, a_z))
+        a_x, a_y = x_swap(a_z), y_swap(a_z)
+        a_x, a_y, fa_z = lax.optimization_barrier((a_x, a_y, fa_z))
+        fb_z = z_line(after(fb_shard, fa_z))
+        a_d = [x_swap(a_y[:2]), y_swap(a_x[2:])]
+        a_d, fb_z = lax.optimization_barrier((a_d, fb_z))
+        a_own = [a_z, a_x, a_y, *a_d]
+        a_swapped = [core_swap(v) for v in after(a_own, fb_z)]
+        f_z = jnp.stack([jnp.concatenate(pair) for pair in zip(fa_z, fb_z)])
+        f_x, f_y, *f_d = gather_four(f_z)[1:]
+        ctx_own, ctx_other, q, kk, v, ctx, probs, wr, ub_all, proj_w, small_all = attend(
+            bucket, lengths, inputs, other_in, (*a_own, *a_swapped), wq, wp
         )
-        kz = jnp.array([0, 1, 2, 3] * 4)
-        ky = jnp.array([0] * 8 + [1] * 8)
-        kx = jnp.array([0] * 4 + [1] * 4 + [0] * 4 + [1] * 4)
-        owner = (z ^ kz) * 8 + (y ^ ky) * 4 + (x ^ kx) * 2 + c
+        f_all = [[f_z], [f_x, f_y], f_d]
     else:
         a_all = lax.all_gather(a_shard, ("batch", "head"), axis=0)
         qkv_all = a_all[:, :wq].reshape(2, 2, 576, D)
@@ -787,49 +918,68 @@
         proj_w = a_all[:, wq : wq + wp].reshape(D, D)
         small_all = jnp.sum(a_all[:, wq + wp :].astype(F32), 0)
         ctx_own, ctx_other, q, kk, v, ctx, probs, wr = attend(
-            meta, inputs, other_in, (qkv_w, small_all)
+            bucket, lengths, inputs, other_in, (qkv_w, small_all)
         )
+        f_shard = jnp.concatenate([up_weight.T, down_weight])
         f_all = [
             (v[:, :wf].reshape(-1, D), v[:, wf:].reshape(-1, D)) for v in gather_any(f_shard)
         ]
         owner = (k % batch_count) * 4 + (x ^ (k // batch_count)) * 2 + c
-    spread = (owner[None, :] == jnp.arange(devices)[:, None]).astype(F32)
-    ub_all = tn(spread, small_all[8:12].reshape(devices, wf)).reshape(1, FF // 2)
+    if not direct:
+        spread = (owner[None, :] == jnp.arange(devices)[:, None]).astype(F32)
+        ub_all = tn(spread, small_all[8:12].reshape(devices, wf)).reshape(1, FF // 2)
 
     ctx_in = core_swap(ctx_other)
-    first_low, first, first_n, first_r = first_norm(meta, inputs, ctx_own, ctx_in, proj_w, small_all)
+    first_low, first, first_n, first_r = first_norm(inputs, ctx_own, ctx_in, proj_w, small_all)
     first_in = core_swap(first_low)
     sums = ()
     kept = []
-    width = FF // 2 // len(f_all)
-    for i, weights in enumerate(f_all):
-        ub = ub_all[:, i * width : i * width + width]
-        hid, slope, *sums = ffn(meta, first_low, first_in, ub, weights, sums)
-        kept.append((weights, hid, slope))
+    at = 0
+    for weights in f_all:
+        width = (384, 768, 384)[len(kept)] if direct else FF // 4
+        hid, slope, *sums = ffn(
+            first_low,
+            first_in,
+            ub_all[:, at : at + width],
+            weights,
+            sums,
+            len(kept) == len(f_all) - 1,
+        )
+        kept.append((hid, slope))
+        at += width
     layer_out, sum_two, down_low, sums_two = second_norm(
-        meta, first, sums[0], core_swap(sums[1]), small_all, cotangent
+        bucket, lengths, first, sums[0], core_swap(sums[1]), small_all, cotangent
     )
     down_in = core_swap(down_low)
 
     sums = ()
     f_parts, ub_parts = [], []
-    for weights, hid, slope in reversed(kept):
-        g0, g1, ub, *sums = ffn_back(
-            meta, down_low, down_in, first_low, first_in, weights, hid, slope, sums
-        )
-        f_parts.insert(0, (g0, g1))
-        ub_parts.insert(0, ub)
+    if direct:
+        sets = (([f_z], 0, 0), ([f_x], 1, 0), ([f_y], 1, 384), (f_d, 2, 0))
+        for weights, which, lead in reversed(sets):
+            grads, ub, sums = ffn_back(
+                down_low, down_in, first_low, first_in, weights, kept[which], lead, sums, which + lead == 0
+            )
+            f_parts = grads + f_parts
+            ub_parts.insert(0, ub)
+    else:
+        for weights, pair in zip(f_all, kept):
+            grads, ub, sums = ffn_back(
+                down_low, down_in, first_low, first_in, weights, pair, 0, sums, len(f_parts) == len(f_all) - 1
+            )
+            f_parts.append(grads)
+            ub_parts.append(ub)
     part_own, part_other = sums
+    moved = ()
     if direct:
-        f_parts, f_moved = scatter_first(f_parts)
-        part_other = lax.optimization_barrier((part_other, f_moved))[0]
-    sum_one, attn_low, sums_one = first_back(
-        meta, sum_two, part_own, core_swap(part_other), first_n, first_r, small_all
+        moved = (f_parts[1], y_swap(f_parts[4]), f_parts[2], x_swap(f_parts[3]))
+        part_other = after(part_other, moved)
+    added, sum_one, attn_low, sums_one = first_back(
+        sum_two, part_own, core_swap(part_other), first_n, first_r, small_all, moved
     )
     attn_in = core_swap(attn_low)
     *a_grads, in_own, in_other, sums_zero = attend_back(
         direct,
-        meta,
         attn_low,
         attn_in,
         inputs,
@@ -845,12 +995,37 @@
     inputs_grad = (sum_one + in_own + core_swap(in_other)).astype(BF16)
 
     if direct:
-        f_sums = scatter_z(*scatter_xy(*f_parts))
-        up_grad, down_grad = finish_ffn(f_sums)
-        a_parts = [tuple(a_grads[2 * i : 2 * i + 2]) for i in range(4)]
-        a_parts, _ = scatter_first(a_parts)
-        qkv_grad, proj_grad = finish_attend(scatter_z(*scatter_xy(*a_parts)))
+        f_mine, (f_ups, f_downs) = combine(*scatter_xy(f_parts[0], *added), 2)
+        terms = exchange_terms(sums_zero, sums_one, sums_two, ub_parts, devices)
+        terms = lax.all_to_all(terms, ("batch", "head"), split_axis=0, concat_axis=0, tiled=True)
+        a_zz, a_xx, a_yy, d_lo, d_hi = a_grads
+        d_lo, d_hi = after((d_lo, d_hi), (f_ups, inputs_grad, terms))
+        d_lo, d_hi = x_swap(d_lo), y_swap(d_hi)
+        f_ups = scatter_z(f_ups)
+        d_lo, d_hi, f_ups = lax.optimization_barrier((d_lo, d_hi, f_ups))
+        a_xx, a_yy = add_moved(a_xx, d_hi, a_yy, d_lo)
+        a_sets = scatter_xy(a_zz, a_xx, a_yy)
+        f_downs = scatter_z(after(f_downs, f_ups))
+        a_sets, f_downs = lax.optimization_barrier((a_sets, f_downs))
+        a_mine, (a_others,) = combine(*a_sets, 1)
+        up_grad, down_grad = finish_ffn(f_mine, f_ups, f_downs)
+        up_grad = up_grad.T
+        terms = jnp.sum(terms, 0)
+        packed = jnp.concatenate([terms[:, :wp].reshape(-1), terms[0, wp : wp + wf]])
+        qkv_grad, proj_grad = finish_attend((a_mine, *scatter_z(a_others)))
+        proj_grad = proj_grad.T
     else:
+        vecs = jnp.concatenate([sums_zero, sums_one, sums_two])
+        vecs = vecs.reshape(8, devices, wp).transpose(1, 0, 2).reshape(devices, 8 * wp)
+        ubias = jnp.concatenate(ub_parts).reshape(batch_count * 2, wf)
+        ubias = lax.dot_general(
+            spread, ubias, (((1,), (0,)), ((), ())), precision=lax.Precision.HIGHEST
+        )
+        packed = jnp.concatenate([vecs, ubias], 1)
+        packed = lax.all_to_all(
+            packed, ("batch", "head"), split_axis=0, concat_axis=0, tiled=True
+        )
+        packed = jnp.sum(packed, 0)
         wb = D // batch_count
         a_grads = a_grads[0].reshape(2, batch_count, wb, D)
         a_mine = scatter_any(
@@ -871,16 +1046,6 @@
         qkv_grad = qkv_grad.reshape(wb, 576)
         proj_grad = a_mine[:, 576:].T
         up_grad, down_grad = f_mine[:wf].T, f_mine[wf:]
-
-    vecs = jnp.concatenate([sums_zero, sums_one, sums_two])
-    vecs = vecs.reshape(8, devices, wp).transpose(1, 0, 2).reshape(devices, 8 * wp)
-    ubias = jnp.concatenate(ub_parts, 1).reshape(batch_count * 2, wf)
-    ubias = lax.dot_general(
-        spread, ubias, (((1,), (0,)), ((), ())), precision=lax.Precision.HIGHEST
-    )
-    packed = jnp.concatenate([vecs, ubias], 1)
-    packed = lax.all_to_all(packed, ("batch", "head"), split_axis=0, concat_axis=0, tiled=True)
-    packed = jnp.sum(packed, 0)
     qb_g, vb_g, pb_g, fg_g, fs_g, db_g, sg_g, ss_g = [
         packed[i * wp : (i + 1) * wp] for i in range(8)
     ]

time: 236 us -> 224 us (0.949)
  waiting for transfers between devices: 79.4 us -> 93.6 us
  local copies, waits for them, and re-layouts: 16.6 us -> 8.41 us
  Pallas kernels: 71.9 us -> 64.5 us
  starting transfers between devices: 57.4 us -> 52.3 us
  other arithmetic: 7.86 us -> 3.41 us
    ppermute x11 -> x8, waiting for transfers between devices: 20.8 us -> 4.14 us  [y_swap(): return lax.ppermute(v, 'batch', YPAIR)]
    ppermute x12 -> x18, waiting for transfers between devices: 43.9 us -> 59.9 us  [z_swap(): return lax.ppermute(v, 'batch', ZPAIR[k])]
    ppermute x11 -> x8, waiting for transfers between devices: 5.68 us -> 19.4 us  [x_swap(): return lax.ppermute(v, 'head', XPAIR)]
    pallas_call x17 -> x19, Pallas kernels: 71.9 us -> 64.5 us  [call(): pl.pallas_call(kernel, out_shape=out_shape, in_specs=ins, out_specs=outs,...]
    convert_element_type x4 -> x0, other arithmetic: 4.49 us -> none  [add_low(): return (a.astype(F32) + b.astype(F32)).astype(BF16)]
    ppermute x11 -> x8, starting transfers between devices: 13.5 us -> 9.48 us  [x_swap(): return lax.ppermute(v, 'head', XPAIR)]
    ppermute x13, waiting for transfers between devices: 6.35 us -> 10.1 us  [core_swap(): return lax.ppermute(v, 'head', CORE)]
    ppermute x11 -> x8, starting transfers between devices: 12.8 us -> 9.31 us  [y_swap(): return lax.ppermute(v, 'batch', YPAIR)]
  transfers between devices with their start and end apart: 48 -> 48, of which waited for: 18 -> 25; matrix products, arithmetic and copies ran while one was open for 5% -> 2% of each run, Pallas kernels for 25% -> 22%
where the time goes in v2:
time: 224 us; the launch traced here: 223 us
  waiting for transfers between devices  93.6 us (42%)
  Pallas kernels  64.5 us (29%)
  starting transfers between devices  52.3 us (23%)
  local copies, waits for them, and re-layouts  8.41 us (4%)
  other arithmetic  3.41 us (2%)
    pallas_call x19, Pallas kernels, call(): pl.pallas_call(kernel, out_shape=out_shape, in_specs=ins, out_specs=outs,...  64.5 us
    ppermute x18, waiting for transfers between devices, z_swap(): return lax.ppermute(v, 'batch', ZPAIR[k])  59.9 us
    ppermute x18, starting transfers between devices, z_swap(): return lax.ppermute(v, 'batch', ZPAIR[k])  27.7 us
    ppermute x8, waiting for transfers between devices, x_swap(): return lax.ppermute(v, 'head', XPAIR)  19.4 us
    ppermute x13, waiting for transfers between devices, core_swap(): return lax.ppermute(v, 'head', CORE)  10.1 us
    ppermute x8, starting transfers between devices, x_swap(): return lax.ppermute(v, 'head', XPAIR)  9.48 us
    ppermute x8, starting transfers between devices, y_swap(): return lax.ppermute(v, 'batch', YPAIR)  9.31 us
    unnamed x71, local copies, waits for them, and re-layouts  6.36 us
  transfers between devices with their start and end apart: 48, of which 25 were waited for; matrix products, arithmetic and copies ran while one was open for 2% of the time, Pallas kernels for 22%

profile of v2, /device:TPU:0, one launch (start us, length us, event | category | flops | bytes accessed | tf_op | source)
XLA Modules:
  0.0 223.3 jit_solution(15242681306144656401)
XLA Ops:
  3.8 4.7 %collective-permute-start.2 = (bf16[112,768]{1,0:T(8,128)(2,1)S(1)}, bf16[112,768]{1,0:T(8,128)(2,1)S(1)}, u32[]{:S(2)}, u32[]{:S(2)}) collective-permute-start(bf16[112,768]{1,0:T(8,128)(2,1)S(1)} %get-tuple-element.134), channel_id=1, source_target_pairs={{0,24},{4,28},{8,16},{12,20},{16,8},{20,12},{24,0},{28,4},{1,25},{... | collective-permute-start | bytes 516104 | tf_op jit(solution)/shard_map/ppermute | solution.py:40
  9.1 4.7 %collective-permute-done.2 = bf16[112,768]{1,0:T(8,128)(2,1)S(1)} collective-permute-done((bf16[112,768]{1,0:T(8,128)(2,1)S(1)}, bf16[112,768]{1,0:T(8,128)(2,1)S(1)}, u32[]{:S(2)}, u32[]{:S(2)}) %collective-permute-start.2) | collective-permute-done | bytes 172064 | tf_op jit(solution)/shard_map/ppermute | solution.py:40
  13.9 9.9 %collective-permute-done.1 = bf16[112,768]{1,0:T(8,128)(2,1)S(1)} collective-permute-done((bf16[112,768]{1,0:T(8,128)(2,1)S(1)}, bf16[112,768]{1,0:T(8,128)(2,1)S(1)}, u32[]{:S(2)}, u32[]{:S(2)}) %collective-permute-start.1) | collective-permute-done | bytes 172064 | tf_op jit(solution)/shard_map/ppermute | solution.py:40
  23.9 1.6 collective-permute-start.5
  25.5 1.5 collective-permute-start.4
  26.9 2.5 %collective-permute-start.8 = (bf16[112,768]{1,0:T(8,128)(2,1)S(1)}, bf16[112,768]{1,0:T(8,128)(2,1)S(1)}, u32[]{:S(2)}, u32[]{:S(2)}) collective-permute-start(bf16[112,768]{1,0:T(8,128)(2,1)S(1)} %get-tuple-element.142), channel_id=1, source_target_pairs={{0,24},{4,28},{8,16},{12,20},{16,8},{20,12},{24,0},{28,4},{1,25},{... | collective-permute-start | bytes 516104 | tf_op jit(solution)/shard_map/ppermute | solution.py:40
  29.4 1.9 collective-permute-start.6
  31.3 4.8 %collective-permute-done.8 = bf16[112,768]{1,0:T(8,128)(2,1)S(1)} collective-permute-done((bf16[112,768]{1,0:T(8,128)(2,1)S(1)}, bf16[112,768]{1,0:T(8,128)(2,1)S(1)}, u32[]{:S(2)}, u32[]{:S(2)}) %collective-permute-start.8) | collective-permute-done | bytes 172064 | tf_op jit(solution)/shard_map/ppermute | solution.py:40
  36.1 6.4 %collective-permute-done.7 = bf16[112,768]{1,0:T(8,128)(2,1)S(1)} collective-permute-done((bf16[112,768]{1,0:T(8,128)(2,1)S(1)}, bf16[112,768]{1,0:T(8,128)(2,1)S(1)}, u32[]{:S(2)}, u32[]{:S(2)}) %collective-permute-start.7) | collective-permute-done | bytes 172064 | tf_op jit(solution)/shard_map/ppermute | solution.py:40
  44.4 2.5 %collective-permute-start.13 = (bf16[80,768]{1,0:T(8,128)(2,1)S(1)}, bf16[80,768]{1,0:T(8,128)(2,1)S(1)}, u32[]{:S(2)}, u32[]{:S(2)}) collective-permute-start(bf16[80,768]{1,0:T(8,128)(2,1)S(1)} %get-tuple-element.149), channel_id=1, source_target_pairs={{0,24},{4,28},{8,16},{12,20},{16,8},{20,12},{24,0},{28,4},{1,25},{... | collective-permute-start | bytes 368648 | tf_op jit(solution)/shard_map/ppermute | solution.py:40
  46.8 1.9 collective-permute-start.11
  48.7 3.5 %collective-permute-done.13 = bf16[80,768]{1,0:T(8,128)(2,1)S(1)} collective-permute-done((bf16[80,768]{1,0:T(8,128)(2,1)S(1)}, bf16[80,768]{1,0:T(8,128)(2,1)S(1)}, u32[]{:S(2)}, u32[]{:S(2)}) %collective-permute-start.13) | collective-permute-done | bytes 122912 | tf_op jit(solution)/shard_map/ppermute | solution.py:40
  52.2 3.9 %collective-permute-done.12 = bf16[80,768]{1,0:T(8,128)(2,1)S(1)} collective-permute-done((bf16[80,768]{1,0:T(8,128)(2,1)S(1)}, bf16[80,768]{1,0:T(8,128)(2,1)S(1)}, u32[]{:S(2)}, u32[]{:S(2)}) %collective-permute-start.12) | collective-permute-done | bytes 122912 | tf_op jit(solution)/shard_map/ppermute | solution.py:40
  58.3 1.5 collective-permute-start.21
  60.5 1.5 collective-permute-done.14.refs_5_
  64.8 11.5 %shard_map.281 = (bf16[256,384]{1,0:T(8,128)(2,1)S(1)}, bf16[256,384]{1,0:T(8,128)(2,1)S(1)}, bf16[512,384]{1,0:T(8,128)(2,1)}, bf16[512,384]{1,0:T(8,128)(2,1)}...) custom-call(s32[2]{0:T(128)S(1)} %copy-done.11, ...), custom_call_target="tpu_custom_call" | custom-call | flops 1711276032 | bytes 12000000 | tf_op jit(solution)/shard_map/pallas_call | solution.py:105
  76.6 8.5 %collective-permute-done.23.refs_0_ = bf16[4,192,768]{2,1,0:T(8,128)(2,1)S(1)} collective-permute-done((bf16[4,192,768]{2,1,0:T(8,128)(2,1)S(1)}, bf16[4,192,768]{2,1,0:T(8,128)(2,1)S(1)}, u32[]{:S(2)}, u32[]{:S(2)}) %collective-permute-start.23) | collective-permute-done | bytes 1179680 | tf_op jit(solution)/shard_map/ppermute | solution.py:32
  85.1 1.6 collective-permute-start.24
  87.9 3.4 %shard_map.282 = (bf16[256,768]{1,0:T(8,128)(2,1)S(1)}, f32[256,768]{1,0:T(8,128)}, f32[256,768]{1,0:T(8,128)}, f32[256,128]{1,0:T(8,128)S(1)}) custom-call(bf16[256,768]{1,0:T(8,128)(2,1)} %refs_6_.1, bf16[256,384]{1,0:T(8,128)(2,1)S(1)} %get-tuple-element.158.ctx_own, bf16[256,384]{1,0:T(8,128)(2,1)S(1)} %collective-permute-done.19.ctx_in, ...), custom_call_target="tpu_custom_call" | custom-call | flops 301989888 | bytes 5000000 | tf_op jit(solution)/shard_map/pallas_call | solution.py:105
  91.4 1.7 collective-permute-done.20.x1
  93.1 3.1 %shard_map.283 = (bf16[512,384]{1,0:T(8,128)(2,1)}, bf16[512,384]{1,0:T(8,128)(2,1)}, f32[256,768]{1,0:T(8,128)S(1)}, f32[256,768]{1,0:T(8,128)S(1)}) custom-call(bf16[256,768]{1,0:T(8,128)(2,1)S(1)} %get-tuple-element.163.x0, bf16[256,768]{1,0:T(8,128)(2,1)S(1)} %collective-permute-done.20.x1, f32[1,384]{1,0:T(1,128)S(1)} %get-tuple-element.268.ub, ...), custom_call_target="tpu_custom_call" | custom-call | flops 603979776 | bytes 6179648 | tf_op jit(solution)/shard_map/pallas_call | solution.py:105
  96.2 4.1 %shard_map.284 = (bf16[512,768]{1,0:T(8,128)(2,1)}, bf16[512,768]{1,0:T(8,128)(2,1)}, f32[256,768]{1,0:T(8,128)S(1)}, f32[256,768]{1,0:T(8,128)S(1)}) custom-call(bf16[256,768]{1,0:T(8,128)(2,1)S(1)} %get-tuple-element.163.x0, bf16[256,768]{1,0:T(8,128)(2,1)S(1)} %collective-permute-done.20.x1, f32[1,768]{1,0:T(1,128)S(1)} %slice.86.ub, ...), custom_call_target="tpu_custom_call" | custom-call | flops 1207959552 | bytes 7359296 | tf_op jit(solution)/shard_map/pallas_call | solution.py:105
  101.7 3.3 %shard_map.285 = (bf16[512,384]{1,0:T(8,128)(2,1)}, bf16[512,384]{1,0:T(8,128)(2,1)}, f32[256,768]{1,0:T(8,128)S(1)}, bf16[256,768]{1,0:T(8,128)(2,1)S(1)}) custom-call(bf16[256,768]{1,0:T(8,128)(2,1)S(1)} %get-tuple-element.163.x0, bf16[256,768]{1,0:T(8,128)(2,1)S(1)} %collective-permute-done.20.x1, f32[1,384]{1,0:T(1,128)S(1)} %get-tuple-element.269.ub, ...), custom_call_target="tpu_custom_call" | custom-call | flops 603979776 | bytes 6179648 | tf_op jit(solution)/shard_map/pallas_call | solution.py:105
  105.0 1.7 collective-permute-done.25.got
  106.7 3.2 %shard_map.286 = (bf16[256,768]{1,0:T(8,128)(2,1)}, f32[256,768]{1,0:T(8,128)S(1)}, bf16[256,768]{1,0:T(8,128)(2,1)S(1)}, f32[3,768]{1,0:T(4,128)S(1)}) custom-call(s32[2]{0:T(128)S(1)} %copy-done.11, s32[2,4]{1,0:T(2,128)S(1)} %copy-done.10, f32[256,768]{1,0:T(8,128)} %get-tuple-element.162.first_in, f32[256,768]{1,0:T(8,128)S(1)} %get-tuple-element.169.part, ...), custom_call_target="tpu_custom_call" | custom-call | flops 7864320 | bytes 5000000 | tf_op jit(solution)/shard_map/pallas_call | solution.py:105
  110.1 1.6 collective-permute-done.26.d1
  111.7 3.3 %shard_map.287 = (bf16[2,192,768]{2,1,0:T(8,128)(2,1)S(1)}, bf16[2,192,768]{2,1,0:T(8,128)(2,1)S(1)}, f32[1,384]{1,0:T(1,128)S(1)}, f32[256,768]{1,0:T(8,128)S(1)}, f32[256,768]{1,0:T(8,128)S(1)}) custom-call(bf16[256,768]{1,0:T(8,128)(2,1)S(1)} %get-tuple-element.173.d0, bf16[256,768]{1,0:T(8,128)(2,1)S(1)} %collective-permute-done.26.d1, ...), custom_call_target="tpu_custom_call" | custom-call | flops 1000 | bytes 1000 | tf_op jit(solution)/shard_map/pallas_call | solution.py:105
  117.3 3.3 %shard_map.288 = (bf16[4,192,768]{2,1,0:T(8,128)(2,1)S(1)}, f32[1,384]{1,0:T(1,128)S(1)}, f32[256,768]{1,0:T(8,128)S(1)}, f32[256,768]{1,0:T(8,128)S(1)}) custom-call(bf16[256,768]{1,0:T(8,128)(2,1)S(1)} %get-tuple-element.173.d0, bf16[256,768]{1,0:T(8,128)(2,1)S(1)} %collective-permute-done.26.d1, bf16[256,768]{1,0:T(8,128)(2,1)S(1)} %get-tuple-element.163.x0, ...), custom_call_target="tpu_custom_call" | custom-call | flops 1000 | bytes 1000 | tf_op jit(solution)/shard_map/pallas_call | solution.py:105
  120.6 3.3 %shard_map.289 = (bf16[4,192,768]{2,1,0:T(8,128)(2,1)S(1)}, f32[1,384]{1,0:T(1,128)S(1)}, f32[256,768]{1,0:T(8,128)S(1)}, f32[256,768]{1,0:T(8,128)S(1)}) custom-call(bf16[256,768]{1,0:T(8,128)(2,1)S(1)} %get-tuple-element.173.d0, bf16[256,768]{1,0:T(8,128)(2,1)S(1)} %collective-permute-done.26.d1, bf16[256,768]{1,0:T(8,128)(2,1)S(1)} %get-tuple-element.163.x0, ...), custom_call_target="tpu_custom_call" | custom-call | flops 1000 | bytes 1000 | tf_op jit(solution)/shard_map/pallas_call | solution.py:105
  124.0 3.3 %shard_map.290 = (bf16[4,192,768]{2,1,0:T(8,128)(2,1)S(1)}, f32[1,384]{1,0:T(1,128)S(1)}, f32[256,768]{1,0:T(8,128)S(1)}, bf16[256,768]{1,0:T(8,128)(2,1)S(1)}) custom-call(bf16[256,768]{1,0:T(8,128)(2,1)S(1)} %get-tuple-element.173.d0, bf16[256,768]{1,0:T(8,128)(2,1)S(1)} %collective-permute-done.26.d1, bf16[256,768]{1,0:T(8,128)(2,1)S(1)} %get-tuple-element.163.x0, ...), custom_call_target="tpu_custom_call" | custom-call | flops 1000 | bytes 1000 | tf_op jit(solution)/shard_map/pallas_call | solution.py:105
  127.3 3.2 %collective-permute-done.27.refs_1_ = bf16[2,192,768]{2,1,0:T(8,128)(2,1)S(1)} collective-permute-done((bf16[2,192,768]{2,1,0:T(8,128)(2,1)S(1)}, bf16[2,192,768]{2,1,0:T(8,128)(2,1)S(1)}, u32[]{:S(2)}, u32[]{:S(2)}) %collective-permute-start.27) | collective-permute-done | bytes 589856 | tf_op jit(solution)/shard_map/ppermute | solution.py:36
  131.3 1.7 collective-permute-done.29.got
  133.0 3.5 %shard_map.291 = (bf16[4,192,768]{2,1,0:T(8,128)(2,1)}, bf16[4,192,768]{2,1,0:T(8,128)(2,1)}, f32[256,768]{1,0:T(8,128)S(1)}, bf16[256,768]{1,0:T(8,128)(2,1)S(1)}, f32[3,768]{1,0:T(4,128)S(1)}) custom-call(f32[256,768]{1,0:T(8,128)S(1)} %get-tuple-element.172.sum_two, f32[256,768]{1,0:T(8,128)S(1)} %get-tuple-element.186.part, ...), custom_call_target="tpu_custom_call" | custom-call | flops 1000 | bytes 1000 | tf_op jit(solution)/shard_map/pallas_call | solution.py:105
  139.6 13.1 %shard_map.292 = (bf16[4,96,768]{2,1,0:T(8,128)(2,1)}, bf16[4,96,768]{2,1,0:T(8,128)(2,1)}, bf16[4,96,768]{2,1,0:T(8,128)(2,1)}, bf16[2,96,768]{2,1,0:T(8,128)(2...) custom-call(bf16[256,768]{1,0:T(8,128)(2,1)S(1)} %get-tuple-element.196.a, ...), custom_call_target="tpu_custom_call" | custom-call | flops 1000 | bytes 1000 | tf_op jit(solution)/shard_map/pallas_call | solution.py:105
  154.4 3.3 %all-to-all-start = ((f32[32,8,128]{2,1,0:T(8,128)}), f32[32,8,128]{2,1,0:T(8,128)}, u32[]{:S(2)}, u32[]{:S(2)}) async-start(f32[32,8,128]{2,1,0:T(8,128)} %copy-done.8), calls=%async_computation | async-start | bytes 262144 | tf_op jit(solution)/shard_map/all_to_all | solution.py:1000
  157.7 9.6 %collective-permute-done.32.x = bf16[4,192,768]{2,1,0:T(8,128)(2,1)S(1)} collective-permute-done((bf16[4,192,768]{2,1,0:T(8,128)(2,1)}, bf16[4,192,768]{2,1,0:T(8,128)(2,1)S(1)}, u32[]{:S(2)}, u32[]{:S(2)}) %collective-permute-start.32) | collective-permute-done | bytes 1179680 | tf_op jit(solution)/shard_map/ppermute | solution.py:32
  168.2 1.3 shard_map.293
  170.1 2.1 add_convert_fusion
  174.2 2.0 collective-permute-start.37
  176.2 2.4 %collective-permute-start.38 = (bf16[96,768]{1,0:T(8,128)(2,1)S(1)}, bf16[96,768]{1,0:T(8,128)(2,1)S(1)}, u32[]{:S(2)}, u32[]{:S(2)}) collective-permute-start(bf16[96,768]{1,0:T(8,128)(2,1)S(1)} %copy-done.32), channel_id=1, source_target_pairs={{0,24},{4,28},{8,16},{12,20},{16,8},{20,12},{24,0},{28,4},{1,25},{... | collective-permute-start | bytes 442376 | tf_op jit(solution)/shard_map/ppermute | solution.py:40
  178.6 1.7 collective-permute-done.36.refs_0_
  180.3 7.0 %collective-permute-done.37.refs_1_ = bf16[96,768]{1,0:T(8,128)(2,1)S(1)} collective-permute-done((bf16[96,768]{1,0:T(8,128)(2,1)S(1)}, bf16[96,768]{1,0:T(8,128)(2,1)S(1)}, u32[]{:S(2)}, u32[]{:S(2)}) %collective-permute-start.37) | collective-permute-done | bytes 147488 | tf_op jit(solution)/shard_map/ppermute | solution.py:40
  191.5 2.2 collective-permute-start.41
  193.9 2.2 collective-permute-start.43
  197.9 7.7 %collective-permute-done.42.refs_4_ = bf16[96,768]{1,0:T(8,128)(2,1)S(1)} collective-permute-done((bf16[96,768]{1,0:T(8,128)(2,1)}, bf16[96,768]{1,0:T(8,128)(2,1)S(1)}, u32[]{:S(2)}, u32[]{:S(2)}) %collective-permute-start.42) | collective-permute-done | bytes 147488 | tf_op jit(solution)/shard_map/ppermute | solution.py:40
  206.6 2.2 collective-permute-start.44
  209.6 1.6 collective-permute-start.46
  213.4 8.4 %collective-permute-done.45.two = bf16[96,768]{1,0:T(8,128)(2,1)S(1)} collective-permute-done((bf16[96,768]{1,0:T(8,128)(2,1)}, bf16[96,768]{1,0:T(8,128)(2,1)S(1)}, u32[]{:S(2)}, u32[]{:S(2)}) %collective-permute-start.45) | collective-permute-done | bytes 147488 | tf_op jit(solution)/shard_map/ppermute | solution.py:40
  (153 shorter events, 37.5 us)
Async XLA Ops:
  0.6 23.2 %collective-permute-start.3 = (bf16[256,768]{1,0:T(8,128)(2,1)}, bf16[256,768]{1,0:T(8,128)(2,1)S(1)}, u32[]{:S(2)}, u32[]{:S(2)}) collective-permute-start(bf16[256,768]{1,0:T(8,128)(2,1)} %refs_6_.1), channel_id=1, source_target_pairs={{0,1},{1,0},{2,3},{3,2},{4,5},{5,4},{6,7},{7,6},{8,9},{9,8},{10,11... | collective-permute-start | bytes 1179656 | tf_op jit(solution)/shard_map/ppermute | solution.py:28
  3.8 10.0 %collective-permute-start.2 = (bf16[112,768]{1,0:T(8,128)(2,1)S(1)}, bf16[112,768]{1,0:T(8,128)(2,1)S(1)}, u32[]{:S(2)}, u32[]{:S(2)}) collective-permute-start(bf16[112,768]{1,0:T(8,128)(2,1)S(1)} %get-tuple-element.134), channel_id=1, source_target_pairs={{0,24},{4,28},{8,16},{12,20},{16,8},{20,12},{24,0},{28,4},{1,25},{... | collective-permute-start | bytes 516104 | tf_op jit(solution)/shard_map/ppermute | solution.py:40
  8.5 15.2 %collective-permute-start.1 = (bf16[112,768]{1,0:T(8,128)(2,1)S(1)}, bf16[112,768]{1,0:T(8,128)(2,1)S(1)}, u32[]{:S(2)}, u32[]{:S(2)}) collective-permute-start(bf16[112,768]{1,0:T(8,128)(2,1)S(1)} %get-tuple-element.134), channel_id=1, source_target_pairs={{0,16},{4,20},{8,24},{12,28},{16,0},{20,4},{24,8},{28,12},{1,17},{... | collective-permute-start | bytes 516104 | tf_op jit(solution)/shard_map/ppermute | solution.py:40
  8.5 15.2 %collective-permute-start = (bf16[112,768]{1,0:T(8,128)(2,1)S(1)}, bf16[112,768]{1,0:T(8,128)(2,1)S(1)}, u32[]{:S(2)}, u32[]{:S(2)}) collective-permute-start(bf16[112,768]{1,0:T(8,128)(2,1)S(1)} %get-tuple-element.134), channel_id=1, source_target_pairs={{0,8},{4,12},{8,0},{12,4},{16,24},{20,28},{24,16},{28,20},{1,9},{5... | collective-permute-start | bytes 516104 | tf_op jit(solution)/shard_map/ppermute | solution.py:40
  23.9 18.7 %collective-permute-start.5 = (bf16[4,112,768]{2,1,0:T(8,128)(2,1)S(1)}, bf16[4,112,768]{2,1,0:T(8,128)(2,1)S(1)}, u32[]{:S(2)}, u32[]{:S(2)}) collective-permute-start(bf16[4,112,768]{2,1,0:T(8,128)(2,1)S(1)} %pad_maximum_fusion.1.refs_0_), channel_id=1, source_target_pairs={{0,4},{4,0},{8,12},{12,8},{16,20},{20,16},{24,28},{28,24},{1,5},{5... | collective-permute-start | bytes 2064392 | tf_op jit(solution)/shard_map/ppermute | solution.py:36
  25.5 17.1 %collective-permute-start.4 = (bf16[4,112,768]{2,1,0:T(8,128)(2,1)S(1)}, bf16[4,112,768]{2,1,0:T(8,128)(2,1)S(1)}, u32[]{:S(2)}, u32[]{:S(2)}) collective-permute-start(bf16[4,112,768]{2,1,0:T(8,128)(2,1)S(1)} %pad_maximum_fusion.1.refs_0_), channel_id=1, source_target_pairs={{0,2},{1,3},{2,0},{3,1},{4,6},{5,7},{6,4},{7,5},{8,10},{9,11},{10,... | collective-permute-start | bytes 2064392 | tf_op jit(solution)/shard_map/ppermute | solution.py:32
  26.9 9.2 %collective-permute-start.8 = (bf16[112,768]{1,0:T(8,128)(2,1)S(1)}, bf16[112,768]{1,0:T(8,128)(2,1)S(1)}, u32[]{:S(2)}, u32[]{:S(2)}) collective-permute-start(bf16[112,768]{1,0:T(8,128)(2,1)S(1)} %get-tuple-element.142), channel_id=1, source_target_pairs={{0,24},{4,28},{8,16},{12,20},{16,8},{20,12},{24,0},{28,4},{1,25},{... | collective-permute-start | bytes 516104 | tf_op jit(solution)/shard_map/ppermute | solution.py:40
  29.4 13.1 %collective-permute-start.7 = (bf16[112,768]{1,0:T(8,128)(2,1)S(1)}, bf16[112,768]{1,0:T(8,128)(2,1)S(1)}, u32[]{:S(2)}, u32[]{:S(2)}) collective-permute-start(bf16[112,768]{1,0:T(8,128)(2,1)S(1)} %get-tuple-element.142), channel_id=1, source_target_pairs={{0,16},{4,20},{8,24},{12,28},{16,0},{20,4},{24,8},{28,12},{1,17},{... | collective-permute-start | bytes 516104 | tf_op jit(solution)/shard_map/ppermute | solution.py:40
  29.4 13.1 %collective-permute-start.6 = (bf16[112,768]{1,0:T(8,128)(2,1)S(1)}, bf16[112,768]{1,0:T(8,128)(2,1)S(1)}, u32[]{:S(2)}, u32[]{:S(2)}) collective-permute-start(bf16[112,768]{1,0:T(8,128)(2,1)S(1)} %get-tuple-element.142), channel_id=1, source_target_pairs={{0,8},{4,12},{8,0},{12,4},{16,24},{20,28},{24,16},{28,20},{1,9},{5... | collective-permute-start | bytes 516104 | tf_op jit(solution)/shard_map/ppermute | solution.py:40
  42.6 13.5 %collective-permute-start.9 = (bf16[2,112,768]{2,1,0:T(8,128)(2,1)S(1)}, bf16[2,112,768]{2,1,0:T(8,128)(2,1)S(1)}, u32[]{:S(2)}, u32[]{:S(2)}) collective-permute-start(bf16[2,112,768]{2,1,0:T(8,128)(2,1)S(1)} %slice.81), channel_id=1, source_target_pairs={{0,2},{1,3},{2,0},{3,1},{4,6},{5,7},{6,4},{7,5},{8,10},{9,11},{10,... | collective-permute-start | bytes 1032200 | tf_op jit(solution)/shard_map/ppermute | solution.py:32
  43.9 12.2 %collective-permute-start.10 = (bf16[2,112,768]{2,1,0:T(8,128)(2,1)S(1)}, bf16[2,112,768]{2,1,0:T(8,128)(2,1)S(1)}, u32[]{:S(2)}, u32[]{:S(2)}) collective-permute-start(bf16[2,112,768]{2,1,0:T(8,128)(2,1)S(1)} %slice.82), channel_id=1, source_target_pairs={{0,4},{4,0},{8,12},{12,8},{16,20},{20,16},{24,28},{28,24},{1,5},{5... | collective-permute-start | bytes 1032200 | tf_op jit(solution)/shard_map/ppermute | solution.py:36
  44.4 7.8 %collective-permute-start.13 = (bf16[80,768]{1,0:T(8,128)(2,1)S(1)}, bf16[80,768]{1,0:T(8,128)(2,1)S(1)}, u32[]{:S(2)}, u32[]{:S(2)}) collective-permute-start(bf16[80,768]{1,0:T(8,128)(2,1)S(1)} %get-tuple-element.149), channel_id=1, source_target_pairs={{0,24},{4,28},{8,16},{12,20},{16,8},{20,12},{24,0},{28,4},{1,25},{... | collective-permute-start | bytes 368648 | tf_op jit(solution)/shard_map/ppermute | solution.py:40
  46.8 9.2 %collective-permute-start.12 = (bf16[80,768]{1,0:T(8,128)(2,1)S(1)}, bf16[80,768]{1,0:T(8,128)(2,1)S(1)}, u32[]{:S(2)}, u32[]{:S(2)}) collective-permute-start(bf16[80,768]{1,0:T(8,128)(2,1)S(1)} %get-tuple-element.149), channel_id=1, source_target_pairs={{0,16},{4,20},{8,24},{12,28},{16,0},{20,4},{24,8},{28,12},{1,17},{... | collective-permute-start | bytes 368648 | tf_op jit(solution)/shard_map/ppermute | solution.py:40
  46.8 9.2 %collective-permute-start.11 = (bf16[80,768]{1,0:T(8,128)(2,1)S(1)}, bf16[80,768]{1,0:T(8,128)(2,1)S(1)}, u32[]{:S(2)}, u32[]{:S(2)}) collective-permute-start(bf16[80,768]{1,0:T(8,128)(2,1)S(1)} %get-tuple-element.149), channel_id=1, source_target_pairs={{0,8},{4,12},{8,0},{12,4},{16,24},{20,28},{24,16},{28,20},{1,9},{5... | collective-permute-start | bytes 368648 | tf_op jit(solution)/shard_map/ppermute | solution.py:40
  56.2 3.7 %collective-permute-start.17 = (bf16[2,112,768]{2,1,0:T(8,128)(2,1)S(1)}, bf16[2,112,768]{2,1,0:T(8,128)(2,1)S(1)}, u32[]{:S(2)}, u32[]{:S(2)}) collective-permute-start(bf16[2,112,768]{2,1,0:T(8,128)(2,1)S(1)} %collective-permute-done.9.refs_3_), channel_id=1, source_target_pairs={{0,1},{1,0},{2,3},{3,2},{4,5},{5,4},{6,7},{7,6},{8,9},{9,8},{10,11... | collective-permute-start | bytes 1032200 | tf_op jit(solution)/shard_map/ppermute | solution.py:28
  56.3 4.1 %collective-permute-start.18 = (bf16[2,112,768]{2,1,0:T(8,128)(2,1)S(1)}, bf16[2,112,768]{2,1,0:T(8,128)(2,1)S(1)}, u32[]{:S(2)}, u32[]{:S(2)}) collective-permute-start(bf16[2,112,768]{2,1,0:T(8,128)(2,1)S(1)} %collective-permute-done.10.refs_4_), channel_id=1, source_target_pairs={{0,1},{1,0},{2,3},{3,2},{4,5},{5,4},{6,7},{7,6},{8,9},{9,8},{10,11... | collective-permute-start | bytes 1032200 | tf_op jit(solution)/shard_map/ppermute | solution.py:28
  57.1 27.9 %collective-permute-start.23 = (bf16[4,192,768]{2,1,0:T(8,128)(2,1)S(1)}, bf16[4,192,768]{2,1,0:T(8,128)(2,1)S(1)}, u32[]{:S(2)}, u32[]{:S(2)}) collective-permute-start(bf16[4,192,768]{2,1,0:T(8,128)(2,1)S(1)} %pad_maximum_fusion.refs_0_), channel_id=1, source_target_pairs={{0,2},{1,3},{2,0},{3,1},{4,6},{5,7},{6,4},{7,5},{8,10},{9,11},{10,... | collective-permute-start | bytes 3538952 | tf_op jit(solution)/shard_map/ppermute | solution.py:32
  58.3 28.4 %collective-permute-start.21 = (bf16[4,192,768]{2,1,0:T(8,128)(2,1)S(1)}, bf16[4,192,768]{2,1,0:T(8,128)(2,1)S(1)}, u32[]{:S(2)}, u32[]{:S(2)}) collective-permute-start(bf16[4,192,768]{2,1,0:T(8,128)(2,1)S(1)} %pad_maximum_fusion.refs_0_), channel_id=1, source_target_pairs={{0,4},{4,0},{8,12},{12,8},{16,20},{20,16},{24,28},{28,24},{1,5},{5... | collective-permute-start | bytes 3538952 | tf_op jit(solution)/shard_map/ppermute | solution.py:36
  59.8 2.1 collective-permute-start.14
  59.9 3.1 %collective-permute-start.15 = (bf16[4,112,768]{2,1,0:T(8,128)(2,1)S(1)}, bf16[4,112,768]{2,1,0:T(8,128)(2,1)S(1)}, u32[]{:S(2)}, u32[]{:S(2)}) collective-permute-start(bf16[4,112,768]{2,1,0:T(8,128)(2,1)S(1)} %collective-permute-done.4.refs_1_), channel_id=1, source_target_pairs={{0,1},{1,0},{2,3},{3,2},{4,5},{5,4},{6,7},{7,6},{8,9},{9,8},{10,11... | collective-permute-start | bytes 2064392 | tf_op jit(solution)/shard_map/ppermute | solution.py:28
  60.4 3.5 %collective-permute-start.16 = (bf16[4,112,768]{2,1,0:T(8,128)(2,1)S(1)}, bf16[4,112,768]{2,1,0:T(8,128)(2,1)S(1)}, u32[]{:S(2)}, u32[]{:S(2)}) collective-permute-start(bf16[4,112,768]{2,1,0:T(8,128)(2,1)S(1)} %collective-permute-done.5.refs_2_), channel_id=1, source_target_pairs={{0,1},{1,0},{2,3},{3,2},{4,5},{5,4},{6,7},{7,6},{8,9},{9,8},{10,11... | collective-permute-start | bytes 2064392 | tf_op jit(solution)/shard_map/ppermute | solution.py:28
  76.4 11.5 %collective-permute-start.19 = (bf16[256,384]{1,0:T(8,128)(2,1)S(1)}, bf16[256,384]{1,0:T(8,128)(2,1)S(1)}, u32[]{:S(2)}, u32[]{:S(2)}) collective-permute-start(bf16[256,384]{1,0:T(8,128)(2,1)S(1)} %get-tuple-element.159), channel_id=1, source_target_pairs={{0,1},{1,0},{2,3},{3,2},{4,5},{5,4},{6,7},{7,6},{8,9},{9,8},{10,11... | collective-permute-start | bytes 589832 | tf_op jit(solution)/shard_map/ppermute | solution.py:28
  85.1 15.2 %collective-permute-start.24 = (bf16[2,192,768]{2,1,0:T(8,128)(2,1)S(1)}, bf16[2,192,768]{2,1,0:T(8,128)(2,1)S(1)}, u32[]{:S(2)}, u32[]{:S(2)}) collective-permute-start(bf16[2,192,768]{2,1,0:T(8,128)(2,1)S(1)} %slice.106), channel_id=1, source_target_pairs={{0,4},{4,0},{8,12},{12,8},{16,20},{20,16},{24,28},{28,24},{1,5},{5... | collective-permute-start | bytes 1769480 | tf_op jit(solution)/shard_map/ppermute | solution.py:36
  86.7 14.1 %collective-permute-start.22 = (bf16[2,192,768]{2,1,0:T(8,128)(2,1)S(1)}, bf16[2,192,768]{2,1,0:T(8,128)(2,1)S(1)}, u32[]{:S(2)}, u32[]{:S(2)}) collective-permute-start(bf16[2,192,768]{2,1,0:T(8,128)(2,1)S(1)} %slice.105), channel_id=1, source_target_pairs={{0,2},{1,3},{2,0},{3,1},{4,6},{5,7},{6,4},{7,5},{8,10},{9,11},{10,... | collective-permute-start | bytes 1769480 | tf_op jit(solution)/shard_map/ppermute | solution.py:32
  91.3 1.8 collective-permute-start.20
  104.9 1.8 collective-permute-start.25
  109.9 1.8 collective-permute-start.26
  115.1 15.4 %collective-permute-start.27 = (bf16[2,192,768]{2,1,0:T(8,128)(2,1)S(1)}, bf16[2,192,768]{2,1,0:T(8,128)(2,1)S(1)}, u32[]{:S(2)}, u32[]{:S(2)}) collective-permute-start(bf16[2,192,768]{2,1,0:T(8,128)(2,1)S(1)} %get-tuple-element.189), channel_id=1, source_target_pairs={{0,4},{4,0},{8,12},{12,8},{16,20},{20,16},{24,28},{28,24},{1,5},{5... | collective-permute-start | bytes 1769480 | tf_op jit(solution)/shard_map/ppermute | solution.py:36
  116.2 15.1 %collective-permute-start.28 = (bf16[2,192,768]{2,1,0:T(8,128)(2,1)S(1)}, bf16[2,192,768]{2,1,0:T(8,128)(2,1)S(1)}, u32[]{:S(2)}, u32[]{:S(2)}) collective-permute-start(bf16[2,192,768]{2,1,0:T(8,128)(2,1)S(1)} %get-tuple-element.191), channel_id=1, source_target_pairs={{0,2},{1,3},{2,0},{3,1},{4,6},{5,7},{6,4},{7,5},{8,10},{9,11},{10,... | collective-permute-start | bytes 1769480 | tf_op jit(solution)/shard_map/ppermute | solution.py:32
  131.3 1.7 collective-permute-start.29
  137.4 2.2 collective-permute-start.30
  137.5 29.7 %collective-permute-start.32 = (bf16[4,192,768]{2,1,0:T(8,128)(2,1)}, bf16[4,192,768]{2,1,0:T(8,128)(2,1)S(1)}, u32[]{:S(2)}, u32[]{:S(2)}) collective-permute-start(bf16[4,192,768]{2,1,0:T(8,128)(2,1)} %get-tuple-element.210), channel_id=1, source_target_pairs={{0,2},{1,3},{2,0},{3,1},{4,6},{5,7},{6,4},{7,5},{8,10},{9,11},{10,... | collective-permute-start | bytes 3538952 | tf_op jit(solution)/shard_map/ppermute | solution.py:32
  138.7 29.5 %collective-permute-start.33 = (bf16[4,192,768]{2,1,0:T(8,128)(2,1)}, bf16[4,192,768]{2,1,0:T(8,128)(2,1)S(1)}, u32[]{:S(2)}, u32[]{:S(2)}) collective-permute-start(bf16[4,192,768]{2,1,0:T(8,128)(2,1)} %get-tuple-element.211), channel_id=1, source_target_pairs={{0,4},{4,0},{8,12},{12,8},{16,20},{20,16},{24,28},{28,24},{1,5},{5... | collective-permute-start | bytes 3538952 | tf_op jit(solution)/shard_map/ppermute | solution.py:36
  153.6 15.9 %collective-permute-start.31 = (f32[256,768]{1,0:T(8,128)}, f32[256,768]{1,0:T(8,128)}, u32[]{:S(2)}, u32[]{:S(2)}) collective-permute-start(f32[256,768]{1,0:T(8,128)} %get-tuple-element.204), channel_id=1, source_target_pairs={{0,1},{1,0},{2,3},{3,2},{4,5},{5,4},{6,7},{7,6},{8,9},{9,8},{10,11... | collective-permute-start | bytes 2359304 | tf_op jit(solution)/shard_map/ppermute | solution.py:28
  154.4 17.9 %all-to-all-start = ((f32[32,8,128]{2,1,0:T(8,128)}), f32[32,8,128]{2,1,0:T(8,128)}, u32[]{:S(2)}, u32[]{:S(2)}) async-start(f32[32,8,128]{2,1,0:T(8,128)} %copy-done.8), calls=%async_computation | async-start | bytes 262144 | tf_op jit(solution)/shard_map/all_to_all | solution.py:1000
  172.2 15.0 %collective-permute-start.34 = (bf16[2,96,768]{2,1,0:T(8,128)(2,1)S(1)}, bf16[2,96,768]{2,1,0:T(8,128)(2,1)S(1)}, u32[]{:S(2)}, u32[]{:S(2)}) collective-permute-start(bf16[2,96,768]{2,1,0:T(8,128)(2,1)S(1)} %copy-done.30), channel_id=1, source_target_pairs={{0,2},{1,3},{2,0},{3,1},{4,6},{5,7},{6,4},{7,5},{8,10},{9,11},{10,... | collective-permute-start | bytes 884744 | tf_op jit(solution)/shard_map/ppermute | solution.py:32
  173.2 14.0 %collective-permute-start.35 = (bf16[2,96,768]{2,1,0:T(8,128)(2,1)S(1)}, bf16[2,96,768]{2,1,0:T(8,128)(2,1)S(1)}, u32[]{:S(2)}, u32[]{:S(2)}) collective-permute-start(bf16[2,96,768]{2,1,0:T(8,128)(2,1)S(1)} %copy-done.29), channel_id=1, source_target_pairs={{0,4},{4,0},{8,12},{12,8},{16,20},{20,16},{24,28},{28,24},{1,5},{5... | collective-permute-start | bytes 884744 | tf_op jit(solution)/shard_map/ppermute | solution.py:36
  174.2 6.1 %collective-permute-start.36 = (bf16[96,768]{1,0:T(8,128)(2,1)S(1)}, bf16[96,768]{1,0:T(8,128)(2,1)S(1)}, u32[]{:S(2)}, u32[]{:S(2)}) collective-permute-start(bf16[96,768]{1,0:T(8,128)(2,1)S(1)} %copy-done.34), channel_id=1, source_target_pairs={{0,8},{4,12},{8,0},{12,4},{16,24},{20,28},{24,16},{28,20},{1,9},{5... | collective-permute-start | bytes 442376 | tf_op jit(solution)/shard_map/ppermute | solution.py:40
  174.2 13.1 %collective-permute-start.37 = (bf16[96,768]{1,0:T(8,128)(2,1)S(1)}, bf16[96,768]{1,0:T(8,128)(2,1)S(1)}, u32[]{:S(2)}, u32[]{:S(2)}) collective-permute-start(bf16[96,768]{1,0:T(8,128)(2,1)S(1)} %copy-done.33), channel_id=1, source_target_pairs={{0,16},{4,20},{8,24},{12,28},{16,0},{20,4},{24,8},{28,12},{1,17},{... | collective-permute-start | bytes 442376 | tf_op jit(solution)/shard_map/ppermute | solution.py:40
  176.2 11.1 %collective-permute-start.38 = (bf16[96,768]{1,0:T(8,128)(2,1)S(1)}, bf16[96,768]{1,0:T(8,128)(2,1)S(1)}, u32[]{:S(2)}, u32[]{:S(2)}) collective-permute-start(bf16[96,768]{1,0:T(8,128)(2,1)S(1)} %copy-done.32), channel_id=1, source_target_pairs={{0,24},{4,28},{8,16},{12,20},{16,8},{20,12},{24,0},{28,4},{1,25},{... | collective-permute-start | bytes 442376 | tf_op jit(solution)/shard_map/ppermute | solution.py:40
  188.2 17.4 %collective-permute-start.39 = (bf16[4,96,768]{2,1,0:T(8,128)(2,1)}, bf16[4,96,768]{2,1,0:T(8,128)(2,1)S(1)}, u32[]{:S(2)}, u32[]{:S(2)}) collective-permute-start(bf16[4,96,768]{2,1,0:T(8,128)(2,1)} %get-tuple-element.227), channel_id=1, source_target_pairs={{0,2},{1,3},{2,0},{3,1},{4,6},{5,7},{6,4},{7,5},{8,10},{9,11},{10,... | collective-permute-start | bytes 1769480 | tf_op jit(solution)/shard_map/ppermute | solution.py:32
  189.4 16.2 %collective-permute-start.40 = (bf16[4,96,768]{2,1,0:T(8,128)(2,1)S(1)}, bf16[4,96,768]{2,1,0:T(8,128)(2,1)S(1)}, u32[]{:S(2)}, u32[]{:S(2)}) collective-permute-start(bf16[4,96,768]{2,1,0:T(8,128)(2,1)S(1)} %get-tuple-element.228), channel_id=1, source_target_pairs={{0,4},{4,0},{8,12},{12,8},{16,20},{20,16},{24,28},{28,24},{1,5},{5... | collective-permute-start | bytes 1769480 | tf_op jit(solution)/shard_map/ppermute | solution.py:36
  191.5 6.4 %collective-permute-start.41 = (bf16[96,768]{1,0:T(8,128)(2,1)}, bf16[96,768]{1,0:T(8,128)(2,1)S(1)}, u32[]{:S(2)}, u32[]{:S(2)}) collective-permute-start(bf16[96,768]{1,0:T(8,128)(2,1)} %get-tuple-element.235), channel_id=1, source_target_pairs={{0,8},{4,12},{8,0},{12,4},{16,24},{20,28},{24,16},{28,20},{1,9},{5... | collective-permute-start | bytes 442376 | tf_op jit(solution)/shard_map/ppermute | solution.py:40
  193.7 11.9 %collective-permute-start.42 = (bf16[96,768]{1,0:T(8,128)(2,1)}, bf16[96,768]{1,0:T(8,128)(2,1)S(1)}, u32[]{:S(2)}, u32[]{:S(2)}) collective-permute-start(bf16[96,768]{1,0:T(8,128)(2,1)} %get-tuple-element.236), channel_id=1, source_target_pairs={{0,16},{4,20},{8,24},{12,28},{16,0},{20,4},{24,8},{28,12},{1,17},{... | collective-permute-start | bytes 442376 | tf_op jit(solution)/shard_map/ppermute | solution.py:40
  193.9 11.7 %collective-permute-start.43 = (bf16[96,768]{1,0:T(8,128)(2,1)S(1)}, bf16[96,768]{1,0:T(8,128)(2,1)S(1)}, u32[]{:S(2)}, u32[]{:S(2)}) collective-permute-start(bf16[96,768]{1,0:T(8,128)(2,1)S(1)} %copy-done.31), channel_id=1, source_target_pairs={{0,24},{4,28},{8,16},{12,20},{16,8},{20,12},{24,0},{28,4},{1,25},{... | collective-permute-start | bytes 442376 | tf_op jit(solution)/shard_map/ppermute | solution.py:40
  206.6 6.8 %collective-permute-start.44 = (bf16[96,768]{1,0:T(8,128)(2,1)}, bf16[96,768]{1,0:T(8,128)(2,1)S(1)}, u32[]{:S(2)}, u32[]{:S(2)}) collective-permute-start(bf16[96,768]{1,0:T(8,128)(2,1)} %get-tuple-element.242), channel_id=1, source_target_pairs={{0,8},{4,12},{8,0},{12,4},{16,24},{20,28},{24,16},{28,20},{1,9},{5... | collective-permute-start | bytes 442376 | tf_op jit(solution)/shard_map/ppermute | solution.py:40
  208.8 13.0 %collective-permute-start.45 = (bf16[96,768]{1,0:T(8,128)(2,1)}, bf16[96,768]{1,0:T(8,128)(2,1)S(1)}, u32[]{:S(2)}, u32[]{:S(2)}) collective-permute-start(bf16[96,768]{1,0:T(8,128)(2,1)} %get-tuple-element.243), channel_id=1, source_target_pairs={{0,16},{4,20},{8,24},{12,28},{16,0},{20,4},{24,8},{28,12},{1,17},{... | collective-permute-start | bytes 442376 | tf_op jit(solution)/shard_map/ppermute | solution.py:40
  209.6 12.2 %collective-permute-start.46 = (bf16[96,768]{1,0:T(8,128)(2,1)}, bf16[96,768]{1,0:T(8,128)(2,1)S(1)}, u32[]{:S(2)}, u32[]{:S(2)}) collective-permute-start(bf16[96,768]{1,0:T(8,128)(2,1)} %get-tuple-element.244), channel_id=1, source_target_pairs={{0,24},{4,28},{8,16},{12,20},{16,8},{20,12},{24,0},{28,4},{1,25},{... | collective-permute-start | bytes 442376 | tf_op jit(solution)/shard_map/ppermute | solution.py:40
  (35 other events, 313.8 us)

commit v3 on v2

--- a/solution.py
+++ b/solution.py
@@ -17,6 +17,8 @@
 NORM_EPS = 1e-12
 F32 = jnp.float32
 BF16 = jnp.bfloat16
+
+FIRST = 112
 
 CORE = [(i, i ^ 1) for i in range(4)]
 XPAIR = [(i, i ^ 2) for i in range(4)]
@@ -196,14 +198,14 @@
         for t in range(3):
             at, to = 192 * t + 64 * hh, 192 * hh + 64 * t
             qkv[:, to : to + 64] = total[:, at : at + 64]
-    proj[...] = total[:, 576:]
+    proj[...] = total[:, 576:].T
 
 
 def finish_attend(parts):
     rows = parts[0].shape[0]
     return call(
         finish_attend_kernel,
-        (shape((rows, 576), F32), shape((rows, 192), F32)),
+        (shape((rows, 576), F32), shape((192, rows), F32)),
         tuple(parts),
         cost=est(8 * rows * D, 16 * rows * D),
     )
@@ -268,8 +270,13 @@
     lane = lax.broadcasted_iota(jnp.int32, (8, D), 1)
     mine = jnp.logical_and(lane >= me * width, lane < me * width + width)
     v = jnp.where(mine, v, 0.0)
-    extra = jnp.concatenate([bias[...].astype(F32), jnp.zeros((1, D - half), F32)], 1)
-    v = jnp.concatenate([v, extra, jnp.zeros((7, D), F32)])
+    gap = jnp.zeros((1, D // 2 - half), F32)
+    none = jnp.zeros((1, D // 2), F32)
+    row = bias[...].astype(F32)
+    early = jnp.concatenate([none, row, gap], 1)
+    late = jnp.concatenate([row, gap, none], 1)
+    extra = jnp.where(me < lax.axis_size("batch") * lax.axis_size("head") // 2, early, late)
+    v = v + jnp.concatenate([extra, jnp.zeros((7, D), F32)])
     copies.wait()
     a_out[0:rows_q] = a[0:rows_q]
     q = p[...]
@@ -282,10 +289,10 @@
 
 
 def pack(qkv, proj, up, down, bias, vectors):
-    rows, half = qkv.shape[0] + proj.shape[0] + 16, down.shape[0]
+    rows, half = qkv.shape[0] + proj.shape[0] + 8, down.shape[0]
     return call(
         pack_kernel,
-        (shape((rows, D)), shape((rows, D)), shape((2 * half - rows, D))),
+        (shape((rows, D)), shape((FIRST, D)), shape((2 * half - FIRST, D))),
         (qkv, proj, up, down, bias[None], jnp.stack(vectors)),
         scratch=[
             pltpu.VMEM((rows, D), BF16),
@@ -359,20 +366,21 @@
 def bias_order(slots, row, out):
     for spot in range(4):
         for kz in range(4):
-            b = slots[slot_of(spot, kz), row : row + 1, 0:128].astype(F32)
+            i = slot_of(spot, kz)
+            b = slots[i, row : row + 1].astype(F32)
+            b = jnp.where(i < 16, b[:, D // 2 : D // 2 + 96], b[:, 0:96])
             at = 384 * spot + 96 * kz
-            out[:, at : at + 96] = b[:, 0:96]
+            out[:, at : at + 96] = b
 
 
 def attend_kernel(rows_q, rows_p, bucket, lengths, x0, x1, *refs):
     sources = 10 if rows_q else 2
     weights, refs = refs[:sources], refs[sources:]
-    (ctx0, ctx1, q_out, k_out, v_out, ctx_out, probs_out, wr_out), refs = refs[:8], refs[8:]
+    (ctx0, ctx1, q, k, v, ctx, probs, wr), refs = refs[:8], refs[8:]
     if rows_q:
-        (ub_out, wp_out, small_out), refs = refs[:3], refs[3:]
-        (q, k, v, ctx, probs, wr, mask, xs, slots, wp, small, sems) = refs
-    else:
-        (q, k, v, ctx, probs, wr, mask, xs, w, small, sems) = refs
+        (ub_out, wp, small, mask, xs, slots, sems) = refs
+    else:
+        (mask, xs, w, small, sems) = refs
     copies = Copies(sems)
     c = place_here()[0]
     kind, units = live_units(bucket, lengths)
@@ -399,27 +407,31 @@
                 for hh in range(3):
                     src, dst = (hh * 3 + t) * HEAD_DIM, (t * 6 + g * 3 + hh) * HEAD_DIM
                     wr[dst : dst + HEAD_DIM] = cuts[src : src + HEAD_DIM]
-        small[...] = sum(slots[i, rows_q + rows_p :].astype(F32) for i in range(32))
+        lane = lax.broadcasted_iota(jnp.int32, (8, D), 1)
+        small[...] = sum(
+            jnp.where(
+                jnp.logical_and(lane >= rows_p * i, lane < rows_p * i + rows_p),
+                slots[i, rows_q + rows_p :].astype(F32),
+                0.0,
+            )
+            for i in range(32)
+        )
     else:
         for t in range(3):
             for hd in range(6):
                 src = ((hd // 3) * 9 + (hd % 3) * 3 + t) * HEAD_DIM
                 dst = (t * 6 + hd) * HEAD_DIM
                 wr[dst : dst + HEAD_DIM] = w[src : src + HEAD_DIM]
-    copies.start(wr, wr_out)
     biases = (heads_of(small[0:1], c), None, heads_of(small[1:2], c))
-    for t, (ref, out) in enumerate(((q, q_out), (k, k_out), (v, v_out))):
+    for t, ref in enumerate((q, k, v)):
         val = nt(xs[...], wr[384 * t : 384 * t + 384])
         if biases[t] is not None:
             val = val + biases[t]
         ref[...] = val.astype(BF16)
-        copies.start(ref, out)
     if rows_q:
         for i in range(32):
             wp[rows_p * i : rows_p * i + rows_p] = slots[i, rows_q : rows_q + rows_p]
-        copies.start(wp, wp_out)
-        copies.start(small, small_out)
-        bias_order(slots, rows_q + rows_p + 8, ub_out)
+        bias_order(slots, rows_q + rows_p, ub_out)
     lane = lax.broadcasted_iota(jnp.int32, (half, 128), 1)
     for pair in range(3):
         lanes = slice(128 * pair, 128 * pair + 128)
@@ -438,13 +450,10 @@
             val = jnp.where(lane < HEAD_DIM, outs[0], outs[1]).astype(BF16)
             ctx[rws, lanes] = val
             near[:, lanes] = val
-        for e in range(2):
-            copies.start(probs.at[2 * pair + e], probs_out.at[2 * pair + e])
-    copies.start(ctx, ctx_out)
-    copies.wait()
 
 
 def attend(bucket, lengths, x0, x1, weights, rows_q=0, rows_p=0, rows_s=16):
+    rows_s = 8 if rows_q else rows_s
     half = x0.shape[0]
     n = 2 * half
     direct = rows_q > 0
@@ -458,19 +467,10 @@
         shape((6, n, n)),
         shape((1152, D)),
     ]
-    scratch = [pltpu.VMEM((n, 384), BF16)] * 4 + [
-        pltpu.VMEM((6, n, n), BF16),
-        pltpu.VMEM((1152, D), BF16),
-        pltpu.VMEM((n, n), F32),
-        pltpu.VMEM((n, D), BF16),
-    ]
+    scratch = [pltpu.VMEM((n, n), F32), pltpu.VMEM((n, D), BF16)]
     if direct:
         outs += [shape((1, FF // 2), F32), shape((D, D)), shape((rows_s, D), F32)]
-        scratch += [
-            pltpu.VMEM((32, rows_q + rows_p + rows_s, D), BF16),
-            pltpu.VMEM((D, D), BF16),
-            pltpu.VMEM((rows_s, D), F32),
-        ]
+        scratch += [pltpu.VMEM((32, rows_q + rows_p + rows_s, D), BF16)]
     else:
         scratch += [pltpu.VMEM((1152, D), BF16), pltpu.VMEM((rows_s, D), F32)]
     operands = (bucket, lengths, x0, x1, *weights)
@@ -482,7 +482,6 @@
         cost=est(2 * n * D * 1152 + 8 * n * n * 384, 12e6, 6 * n * n),
         limit=32,
         far_in=range(2, len(operands)),
-        far_out=[i for i in range(2, len(outs)) if i != 8],
         sems=50,
     )
 
@@ -501,26 +500,17 @@
     )
 
 
-def first_kernel(
-    x_in, ctx_own, ctx_in, wp_in, small_in, low, first_out, normal_out, scale, x, wp, small, first, normal, sems
-):
-    copies = Copies(sems)
-    for src, dst in ((wp_in, wp), (x_in, x), (small_in, small)):
-        copies.start(src, dst)
+def first_kernel(x, ctx_own, ctx_in, wp, small, low, first, normal, scale):
     c = place_here()[0]
-    copies.wait()
     mine = pl.multiple_of(c * 384, 128)
     theirs = pl.multiple_of((1 - c) * 384, 128)
     attn = nt(ctx_own[...], wp[:, pl.ds(mine, 384)]) + nt(ctx_in[...], wp[:, pl.ds(theirs, 384)])
     n, r = norm(x[...].astype(F32) + attn + small[2:3])
     normal[...] = n
-    copies.start(normal, normal_out)
     out = n * small[3:4] + small[4:5]
     first[...] = out
-    copies.start(first, first_out)
     low[...] = out.astype(BF16)
     scale[...] = jnp.broadcast_to(r, scale.shape)
-    copies.wait()
 
 
 def first_norm(x, ctx_own, ctx_in, wp, small):
@@ -529,17 +519,8 @@
         first_kernel,
         (shape((n, D)), shape((n, D), F32), shape((n, D), F32), shape((n, 128), F32)),
         (x, ctx_own, ctx_in, wp, small),
-        scratch=[
-            pltpu.VMEM((n, D), BF16),
-            pltpu.VMEM((D, D), BF16),
-            pltpu.VMEM((16, D), F32),
-            pltpu.VMEM((n, D), F32),
-            pltpu.VMEM((n, D), F32),
-        ],
         cost=est(2 * n * D * D, 5e6),
-        far_in=(0, 3, 4),
-        far_out=(1, 2),
-        sems=5,
+        limit=8,
     )
 
 
@@ -559,14 +540,9 @@
         in0 = in1 = None
     else:
         (in0, in1), refs = refs[:2], refs[2:]
-    (hid_out, slope_out, out0, out1), refs = refs[:4], refs[4:]
-    near, (hid, slope, sems) = refs[:count], refs[count:]
-    copies = Copies(sems)
-    for src, dst in zip(far, near):
-        copies.start(src, dst)
-    copies.wait()
+    hid, slope, out0, out1 = refs
     half = x0.shape[0]
-    uw, dw = ffn_weights(near)
+    uw, dw = ffn_weights(far)
     for i, (xr, before, out) in enumerate(((x0, in0, out0), (x1, in1, out1))):
         rws = slice(half * i, half * i + half)
         up = nt(xr[...], uw) + ub[...]
@@ -574,12 +550,9 @@
         hd = (up * phi).astype(BF16)
         hid[rws] = hd
         slope[rws] = (phi + up * jnp.exp(-0.5 * up * up) * 0.3989422804014327).astype(BF16)
-        copies.start(hid.at[rws], hid_out.at[rws])
-        copies.start(slope.at[rws], slope_out.at[rws])
         part = nn(hd, dw)
         part = part if before is None else before[...] + part
         out[...] = part.astype(out.dtype)
-    copies.wait()
 
 
 def ffn(x0, x1, ub, weights, sums, last):
@@ -594,23 +567,15 @@
             shape((half, D), BF16 if last else F32),
         ),
         (x0, x1, ub, *weights, *sums),
-        scratch=[pltpu.VMEM(w.shape, BF16) for w in weights] + [pltpu.VMEM((n, width), BF16)] * 2,
         cost=est(4 * n * D * width, 4 * D * width + 5e6, 2 * n * width),
-        far_in=range(3, 3 + count),
-        far_out=(0, 1),
-        sems=4 + count,
     )
 
 
 def second_kernel(
-    bucket, lengths, first_in, part, got, small_in, cot_in, out, sum_two, low, sums, first, small, cot, sems
+    bucket, lengths, first, part, got, small, cot, out, sum_two, low, sums
 ):
-    copies = Copies(sems)
-    for src, dst in ((first_in, first), (small_in, small), (cot_in, cot)):
-        copies.start(src, dst)
     c = place_here()[0]
     _, units = live_units(bucket, lengths)
-    copies.wait()
     n, r = norm(first[...] + (part[...] + got[...].astype(F32) + small[5:6]))
     out[...] = (n * small[6:7] + small[7:8]).astype(BF16)
     index = lax.broadcasted_iota(jnp.int32, (first.shape[0], 1), 0)
@@ -631,10 +596,8 @@
         second_kernel,
         (shape((n, D)), shape((n, D), F32), shape((n, D)), shape((3, D), F32)),
         (bucket, lengths, first, part, got, small, cot),
-        scratch=[pltpu.VMEM((n, D), F32), pltpu.VMEM((16, D), F32), pltpu.VMEM((n, D), BF16)],
         cost=est(40 * n * D, 5e6),
-        far_in=(2, 5, 6),
-        sems=3,
+        limit=8,
     )
 
 
@@ -644,20 +607,10 @@
         in0 = in1 = None
     else:
         (in0, in1), refs = refs[:2], refs[2:]
-    outs, (ub, out0, out1), near, (hid, slope, sems) = (
-        refs[:count],
-        refs[count : count + 3],
-        refs[count + 3 : 2 * count + 3],
-        refs[2 * count + 3 :],
-    )
-    copies = Copies(sems)
-    half, width = x0.shape[0], hid.shape[1]
-    for src, dst in zip(far, near):
-        copies.start(src, dst)
-    copies.start(slope_in.at[:, pl.ds(lead, width)], slope)
-    copies.start(hid_in.at[:, pl.ds(lead, width)], hid)
-    copies.wait()
-    uw, dw = ffn_weights(near)
+    outs, (ub, out0, out1) = refs[:count], refs[count:]
+    half, width = x0.shape[0], ub.shape[1]
+    slope, hid = slope_in.at[:, pl.ds(lead, width)], hid_in.at[:, pl.ds(lead, width)]
+    uw, dw = ffn_weights(far)
     cots = []
     for i, (d, before, out) in enumerate(((d0, in0, out0), (d1, in1, out1))):
         rws = slice(half * i, half * i + half)
@@ -687,7 +640,6 @@
     half, count = x0.shape[0], len(weights)
     flat = len(weights[0].shape) == 2
     width = weights[0].shape[0] if flat else sum(w.shape[0] * w.shape[1] // 2 for w in weights)
-    near = [pltpu.VMEM(w.shape, BF16) for w in weights]
     *grads, ub, s0, s1 = call(
         functools.partial(ffn_back_kernel, not sums, lead, count),
         (
@@ -697,22 +649,15 @@
             shape((half, D), BF16 if last else F32),
         ),
         (d0, d1, x0, x1, *weights, *kept, *sums),
-        scratch=near + [pltpu.VMEM((2 * half, width), BF16)] * 2,
         cost=est(1000, 1000),
-        far_in=range(4, 6 + count),
-        sems=2 + count,
     )
     return grads, ub, (s0, s1)
 
 
 def first_back_kernel(
-    sum_two, part, got, normal_in, scale, small_in, *refs
+    sum_two, part, got, normal, scale, small, *refs
 ):
-    *refs, sum_one, low, sums, normal, small, sems = refs
-    copies = Copies(sems)
-    copies.start(normal_in, normal)
-    copies.start(small_in, small)
-    copies.wait()
+    *refs, sum_one, low, sums = refs
     fc = sum_two[...] + part[...] + got[...].astype(F32)
     n = normal[...]
     so = norm_back(fc, n, scale[:, 0:1], small[3:4])
@@ -733,28 +678,23 @@
         first_back_kernel,
         (*outs, shape((n, D), F32), shape((n, D)), shape((3, D), F32)),
         (sum_two, part, got, normal, scale, small, *moved),
-        scratch=[pltpu.VMEM((n, D), F32), pltpu.VMEM((16, D), F32)],
         cost=est(1000, 1000),
-        far_in=(3, 5),
-        sems=2,
+        limit=8,
     )
     return added, sum_one, low, sums
 
 
 def attend_back_kernel(sets, a0, a1, *refs):
     far, outs, (in0, in1, sums), refs = refs[:9], refs[9 : 9 + sets], refs[9 + sets : 12 + sets], refs[12 + sets :]
-    wp, v, probs, k, q, wr, x0, x1, ctx, dctx, cots, grads, sems = refs
+    wp, v, probs, k, q, wr, x0, x1, ctx = far
+    dctx, cots, grads, sems = refs
     copies = Copies(sems)
-    near = (wp, v, probs, k, q, wr, x0, x1, ctx)
-    got = [copies.start(src, dst) for src, dst in zip(far, near)]
     c, z, y, x = place_here()
     half = a0.shape[0]
     n = 2 * half
-    copies.wait(got[0])
     wpo = wp[:, pl.ds(pl.multiple_of(c * 384, 128), 384)]
     dctx[0:half] = nn(a0[...], wpo).astype(BF16)
     dctx[half:n] = nn(a1[...], wpo).astype(BF16)
-    copies.wait()
     lane = lax.broadcasted_iota(jnp.int32, (n, 128), 1)
     zero = jnp.zeros((n, 128), BF16)
     scale = HEAD_DIM**-0.5
@@ -828,13 +768,15 @@
         functools.partial(attend_back_kernel, len(sets)),
         (*sets, shape((half, D), F32), shape((half, D), F32), shape((2, D), F32)),
         (a0, a1, *far),
-        scratch=[pltpu.VMEM(f.shape, BF16) for f in far]
-        + [pltpu.VMEM((n, 384), BF16), pltpu.VMEM((n, 1280), BF16), pltpu.VMEM((2, D, D), BF16)],
+        scratch=[
+            pltpu.VMEM((n, 384), BF16),
+            pltpu.VMEM((n, 1280), BF16),
+            pltpu.VMEM((2, D, D), BF16),
+        ],
         cost=est(1000, 1000),
-        limit=32,
-        far_in=range(2, 11),
+        limit=16,
         far_out=range(len(sets)),
-        sems=26,
+        sems=17,
     )
 
 
@@ -992,28 +934,29 @@
         ctx,
         probs,
     )
-    inputs_grad = (sum_one + in_own + core_swap(in_other)).astype(BF16)
+    in_got = core_swap(in_other)
+    inputs_grad = (sum_one + in_own + in_got).astype(BF16)
 
     if direct:
-        f_mine, (f_ups, f_downs) = combine(*scatter_xy(f_parts[0], *added), 2)
+        f_sets = scatter_xy(f_parts[0], *added)
+        f_mine, (f_ups, f_downs) = combine(*f_sets, 2)
         terms = exchange_terms(sums_zero, sums_one, sums_two, ub_parts, devices)
         terms = lax.all_to_all(terms, ("batch", "head"), split_axis=0, concat_axis=0, tiled=True)
         a_zz, a_xx, a_yy, d_lo, d_hi = a_grads
-        d_lo, d_hi = after((d_lo, d_hi), (f_ups, inputs_grad, terms))
+        d_lo, d_hi = after((d_lo, d_hi), (f_sets, in_got, terms))
         d_lo, d_hi = x_swap(d_lo), y_swap(d_hi)
         f_ups = scatter_z(f_ups)
         d_lo, d_hi, f_ups = lax.optimization_barrier((d_lo, d_hi, f_ups))
         a_xx, a_yy = add_moved(a_xx, d_hi, a_yy, d_lo)
         a_sets = scatter_xy(a_zz, a_xx, a_yy)
         f_downs = scatter_z(after(f_downs, f_ups))
-        a_sets, f_downs = lax.optimization_barrier((a_sets, f_downs))
+        a_sets, f_downs, _ = lax.optimization_barrier((a_sets, f_downs, inputs_grad))
         a_mine, (a_others,) = combine(*a_sets, 1)
         up_grad, down_grad = finish_ffn(f_mine, f_ups, f_downs)
         up_grad = up_grad.T
         terms = jnp.sum(terms, 0)
         packed = jnp.concatenate([terms[:, :wp].reshape(-1), terms[0, wp : wp + wf]])
         qkv_grad, proj_grad = finish_attend((a_mine, *scatter_z(a_others)))
-        proj_grad = proj_grad.T
     else:
         vecs = jnp.concatenate([sums_zero, sums_one, sums_two])
         vecs = vecs.reshape(8, devices, wp).transpose(1, 0, 2).reshape(devices, 8 * wp)

time: 224 us -> 212 us (0.946)
  Pallas kernels: 64.5 us -> 41.9 us
  blocking collectives: 0 us -> 18.5 us
  local copies, waits for them, and re-layouts: 8.41 us -> 4.64 us
  starting transfers between devices: 52.3 us -> 49.9 us
    pallas_call x19, Pallas kernels: 64.5 us -> 41.9 us  [call(): pl.pallas_call(kernel, out_shape=out_shape, in_specs=ins, out_specs=outs,...]
    all_to_all x0 -> x1, blocking collectives: none -> 18.5 us  [local(): lax.all_to_all(terms, ('batch', 'head'), split_axis=0, concat_axis=0, til...]
    ppermute x8, waiting for transfers between devices: 4.14 us -> 13.2 us  [y_swap(): return lax.ppermute(v, 'batch', YPAIR)]
    ppermute x8, waiting for transfers between devices: 19.4 us -> 11.6 us  [x_swap(): return lax.ppermute(v, 'head', XPAIR)]
    unnamed x71 -> x48, local copies, waits for them, and re-layouts: 6.36 us -> 2.59 us
    all_to_all x1 -> x0, starting transfers between devices: 3.29 us -> none  [local(): lax.all_to_all(terms, ('batch', 'head'), split_axis=0, concat_axis=0, til...]
  transfers between devices with their start and end apart: 48 -> 47, of which waited for: 25 -> 24; matrix products, arithmetic and copies ran while one was open for 2% -> 2% of each run, Pallas kernels for 22% -> 15%
where the time goes in v3:
time: 212 us
  waiting for transfers between devices  93.2 us (44%)
  starting transfers between devices  49.9 us (24%)
  Pallas kernels  41.9 us (20%)
  blocking collectives  18.5 us (9%)
  local copies, waits for them, and re-layouts  4.64 us (2%)
  other arithmetic  2.4 us (1%)
    ppermute x18, waiting for transfers between devices, z_swap(): return lax.ppermute(v, 'batch', ZPAIR[k])  58.4 us
    pallas_call x19, Pallas kernels, call(): pl.pallas_call(kernel, out_shape=out_shape, in_specs=ins, out_specs=outs,...  41.9 us
    ppermute x18, starting transfers between devices, z_swap(): return lax.ppermute(v, 'batch', ZPAIR[k])  28.5 us
    all_to_all x1, blocking collectives, local(): lax.all_to_all(terms, ('batch', 'head'), split_axis=0, concat_axis=0, til...  18.5 us
    ppermute x8, waiting for transfers between devices, y_swap(): return lax.ppermute(v, 'batch', YPAIR)  13.2 us
    ppermute x8, waiting for transfers between devices, x_swap(): return lax.ppermute(v, 'head', XPAIR)  11.6 us
    ppermute x13, waiting for transfers between devices, core_swap(): return lax.ppermute(v, 'head', CORE)  9.93 us
    ppermute x8, starting transfers between devices, x_swap(): return lax.ppermute(v, 'head', XPAIR)  9.7 us
  transfers between devices with their start and end apart: 47, of which 24 were waited for; matrix products, arithmetic and copies ran while one was open for 2% of the time, Pallas kernels for 15%

profile of v3, /device:TPU:0, one launch (start us, length us, event | category | flops | bytes accessed | tf_op | source)
XLA Modules:
  0.0 211.7 jit_solution(15403534252665558184)
XLA Ops:
  3.8 4.7 %collective-permute-start.2 = (bf16[104,768]{1,0:T(8,128)(2,1)S(1)}, bf16[104,768]{1,0:T(8,128)(2,1)S(1)}, u32[]{:S(2)}, u32[]{:S(2)}) collective-permute-start(bf16[104,768]{1,0:T(8,128)(2,1)S(1)} %get-tuple-element.134), channel_id=1, source_target_pairs={{0,24},{4,28},{8,16},{12,20},{16,8},{20,12},{24,0},{28,4},{1,25},{... | collective-permute-start | bytes 479240 | tf_op jit(solution)/shard_map/ppermute | solution.py:42
  9.1 4.5 %collective-permute-done.2 = bf16[104,768]{1,0:T(8,128)(2,1)S(1)} collective-permute-done((bf16[104,768]{1,0:T(8,128)(2,1)S(1)}, bf16[104,768]{1,0:T(8,128)(2,1)S(1)}, u32[]{:S(2)}, u32[]{:S(2)}) %collective-permute-start.2) | collective-permute-done | bytes 159776 | tf_op jit(solution)/shard_map/ppermute | solution.py:42
  13.6 9.1 %collective-permute-done.1 = bf16[104,768]{1,0:T(8,128)(2,1)S(1)} collective-permute-done((bf16[104,768]{1,0:T(8,128)(2,1)S(1)}, bf16[104,768]{1,0:T(8,128)(2,1)S(1)}, u32[]{:S(2)}, u32[]{:S(2)}) %collective-permute-start.1) | collective-permute-done | bytes 159776 | tf_op jit(solution)/shard_map/ppermute | solution.py:42
  22.8 1.6 collective-permute-start.5
  24.4 1.5 collective-permute-start.4
  25.9 2.5 %collective-permute-start.8 = (bf16[112,768]{1,0:T(8,128)(2,1)S(1)}, bf16[112,768]{1,0:T(8,128)(2,1)S(1)}, u32[]{:S(2)}, u32[]{:S(2)}) collective-permute-start(bf16[112,768]{1,0:T(8,128)(2,1)S(1)} %get-tuple-element.142), channel_id=1, source_target_pairs={{0,24},{4,28},{8,16},{12,20},{16,8},{20,12},{24,0},{28,4},{1,25},{... | collective-permute-start | bytes 516104 | tf_op jit(solution)/shard_map/ppermute | solution.py:42
  28.4 1.9 collective-permute-start.6
  30.3 4.8 %collective-permute-done.8 = bf16[112,768]{1,0:T(8,128)(2,1)S(1)} collective-permute-done((bf16[112,768]{1,0:T(8,128)(2,1)S(1)}, bf16[112,768]{1,0:T(8,128)(2,1)S(1)}, u32[]{:S(2)}, u32[]{:S(2)}) %collective-permute-start.8) | collective-permute-done | bytes 172064 | tf_op jit(solution)/shard_map/ppermute | solution.py:42
  35.1 6.4 %collective-permute-done.7 = bf16[112,768]{1,0:T(8,128)(2,1)S(1)} collective-permute-done((bf16[112,768]{1,0:T(8,128)(2,1)S(1)}, bf16[112,768]{1,0:T(8,128)(2,1)S(1)}, u32[]{:S(2)}, u32[]{:S(2)}) %collective-permute-start.7) | collective-permute-done | bytes 172064 | tf_op jit(solution)/shard_map/ppermute | solution.py:42
  42.7 2.0 collective-permute-start.13
  44.7 2.3 %collective-permute-start.11 = (bf16[80,768]{1,0:T(8,128)(2,1)S(1)}, bf16[80,768]{1,0:T(8,128)(2,1)S(1)}, u32[]{:S(2)}, u32[]{:S(2)}) collective-permute-start(bf16[80,768]{1,0:T(8,128)(2,1)S(1)} %get-tuple-element.149), channel_id=1, source_target_pairs={{0,8},{4,12},{8,0},{12,4},{16,24},{20,28},{24,16},{28,20},{1,9},{5... | collective-permute-start | bytes 368648 | tf_op jit(solution)/shard_map/ppermute | solution.py:42
  47.1 3.7 %collective-permute-done.13 = bf16[80,768]{1,0:T(8,128)(2,1)S(1)} collective-permute-done((bf16[80,768]{1,0:T(8,128)(2,1)S(1)}, bf16[80,768]{1,0:T(8,128)(2,1)S(1)}, u32[]{:S(2)}, u32[]{:S(2)}) %collective-permute-start.13) | collective-permute-done | bytes 122912 | tf_op jit(solution)/shard_map/ppermute | solution.py:42
  50.7 3.9 %collective-permute-done.12 = bf16[80,768]{1,0:T(8,128)(2,1)S(1)} collective-permute-done((bf16[80,768]{1,0:T(8,128)(2,1)S(1)}, bf16[80,768]{1,0:T(8,128)(2,1)S(1)}, u32[]{:S(2)}, u32[]{:S(2)}) %collective-permute-start.12) | collective-permute-done | bytes 122912 | tf_op jit(solution)/shard_map/ppermute | solution.py:42
  55.7 1.6 collective-permute-start.23
  57.2 1.5 collective-permute-start.21
  59.4 1.4 collective-permute-done.14.refs_5_
  63.5 10.3 %shard_map.281 = (bf16[256,384]{1,0:T(8,128)(2,1)S(1)}, bf16[256,384]{1,0:T(8,128)(2,1)S(1)}, bf16[512,384]{1,0:T(8,128)(2,1)S(1)}, bf16[512,384]{1,0:T(8,128)(2...) custom-call(s32[2]{0:T(128)S(1)} %copy-done.10, ...), custom_call_target="tpu_custom_call" | custom-call | flops 1711276032 | bytes 12000000 | tf_op jit(solution)/shard_map/pallas_call | solution.py:107
  74.1 9.5 %collective-permute-done.23.refs_0_ = bf16[4,192,768]{2,1,0:T(8,128)(2,1)S(1)} collective-permute-done((bf16[4,192,768]{2,1,0:T(8,128)(2,1)S(1)}, bf16[4,192,768]{2,1,0:T(8,128)(2,1)S(1)}, u32[]{:S(2)}, u32[]{:S(2)}) %collective-permute-start.23) | collective-permute-done | bytes 1179680 | tf_op jit(solution)/shard_map/ppermute | solution.py:34
  83.6 1.6 collective-permute-start.24
  85.2 1.6 collective-permute-start.22
  87.7 1.7 collective-permute-done.20.x1
  90.7 1.9 shard_map.284
  92.6 5.4 %collective-permute-done.24.refs_1_ = bf16[2,192,768]{2,1,0:T(8,128)(2,1)S(1)} collective-permute-done((bf16[2,192,768]{2,1,0:T(8,128)(2,1)S(1)}, bf16[2,192,768]{2,1,0:T(8,128)(2,1)S(1)}, u32[]{:S(2)}, u32[]{:S(2)}) %collective-permute-start.24) | collective-permute-done | bytes 589856 | tf_op jit(solution)/shard_map/ppermute | solution.py:38
  99.3 1.4 shard_map.285
  100.9 1.7 collective-permute-done.25.got
  102.6 1.9 shard_map.286
  104.6 1.6 collective-permute-done.26.d1
  106.2 1.8 shard_map.287
  110.1 1.8 shard_map.288
  112.0 1.9 shard_map.289
  113.8 1.9 shard_map.290
  115.7 7.8 %collective-permute-done.27.refs_1_ = bf16[2,192,768]{2,1,0:T(8,128)(2,1)S(1)} collective-permute-done((bf16[2,192,768]{2,1,0:T(8,128)(2,1)S(1)}, bf16[2,192,768]{2,1,0:T(8,128)(2,1)S(1)}, u32[]{:S(2)}, u32[]{:S(2)}) %collective-permute-start.27) | collective-permute-done | bytes 589856 | tf_op jit(solution)/shard_map/ppermute | solution.py:38
  124.3 1.7 collective-permute-done.29.got
  128.4 1.5 collective-permute-start.33
  129.9 9.1 %shard_map.292 = (bf16[4,96,768]{2,1,0:T(8,128)(2,1)}, bf16[4,96,768]{2,1,0:T(8,128)(2,1)}, bf16[4,96,768]{2,1,0:T(8,128)(2,1)}, bf16[2,96,768]{2,1,0:T(8,128)(2...) custom-call(bf16[256,768]{1,0:T(8,128)(2,1)S(1)} %get-tuple-element.1, ...), custom_call_target="tpu_custom_call" | custom-call | flops 1000 | bytes 1000 | tf_op jit(solution)/shard_map/pallas_call | solution.py:107
  139.3 18.5 %all_to_all.5 = f32[32,8,128]{2,1,0:T(8,128)S(1)} all-to-all(f32[32,8,128]{2,1,0:T(8,128)S(1)} %shard_map.293), channel_id=1, replica_groups=mesh['batch'=8,'head'=4] {'batch','head'}, dimensions={0} | all-to-all | bytes 262144 | tf_op jit(solution)/shard_map/all_to_all | solution.py:944
  162.1 2.2 %collective-permute-start.37 = (bf16[96,768]{1,0:T(8,128)(2,1)}, bf16[96,768]{1,0:T(8,128)(2,1)S(1)}, u32[]{:S(2)}, u32[]{:S(2)}) collective-permute-start(bf16[96,768]{1,0:T(8,128)(2,1)} %get-tuple-element.222), channel_id=1, source_target_pairs={{0,16},{4,20},{8,24},{12,28},{16,0},{20,4},{24,8},{28,12},{1,17},{... | collective-permute-start | bytes 442376 | tf_op jit(solution)/shard_map/ppermute | solution.py:42
  164.2 2.2 %collective-permute-start.38 = (bf16[96,768]{1,0:T(8,128)(2,1)}, bf16[96,768]{1,0:T(8,128)(2,1)S(1)}, u32[]{:S(2)}, u32[]{:S(2)}) collective-permute-start(bf16[96,768]{1,0:T(8,128)(2,1)} %get-tuple-element.223), channel_id=1, source_target_pairs={{0,24},{4,28},{8,16},{12,20},{16,8},{20,12},{24,0},{28,4},{1,25},{... | collective-permute-start | bytes 442376 | tf_op jit(solution)/shard_map/ppermute | solution.py:42
  166.4 3.1 %collective-permute-done.36.refs_0_ = bf16[96,768]{1,0:T(8,128)(2,1)S(1)} collective-permute-done((bf16[96,768]{1,0:T(8,128)(2,1)}, bf16[96,768]{1,0:T(8,128)(2,1)S(1)}, u32[]{:S(2)}, u32[]{:S(2)}) %collective-permute-start.36) | collective-permute-done | bytes 147488 | tf_op jit(solution)/shard_map/ppermute | solution.py:42
  169.6 6.6 %collective-permute-done.37.refs_1_ = bf16[96,768]{1,0:T(8,128)(2,1)S(1)} collective-permute-done((bf16[96,768]{1,0:T(8,128)(2,1)}, bf16[96,768]{1,0:T(8,128)(2,1)S(1)}, u32[]{:S(2)}, u32[]{:S(2)}) %collective-permute-start.37) | collective-permute-done | bytes 147488 | tf_op jit(solution)/shard_map/ppermute | solution.py:42
  177.3 1.5 collective-permute-start.39
  179.9 2.4 %collective-permute-start.41 = (bf16[96,768]{1,0:T(8,128)(2,1)}, bf16[96,768]{1,0:T(8,128)(2,1)S(1)}, u32[]{:S(2)}, u32[]{:S(2)}) collective-permute-start(bf16[96,768]{1,0:T(8,128)(2,1)} %get-tuple-element.235), channel_id=1, source_target_pairs={{0,8},{4,12},{8,0},{12,4},{16,24},{20,28},{24,16},{28,20},{1,9},{5... | collective-permute-start | bytes 442376 | tf_op jit(solution)/shard_map/ppermute | solution.py:42
  182.5 2.2 %collective-permute-start.43 = (bf16[96,768]{1,0:T(8,128)(2,1)S(1)}, bf16[96,768]{1,0:T(8,128)(2,1)S(1)}, u32[]{:S(2)}, u32[]{:S(2)}) collective-permute-start(bf16[96,768]{1,0:T(8,128)(2,1)S(1)} %copy-done.23), channel_id=1, source_target_pairs={{0,24},{4,28},{8,16},{12,20},{16,8},{20,12},{24,0},{28,4},{1,25},{... | collective-permute-start | bytes 442376 | tf_op jit(solution)/shard_map/ppermute | solution.py:42
  184.7 2.0 add_convert_fusion
  186.9 7.6 %collective-permute-done.42.refs_4_ = bf16[96,768]{1,0:T(8,128)(2,1)S(1)} collective-permute-done((bf16[96,768]{1,0:T(8,128)(2,1)}, bf16[96,768]{1,0:T(8,128)(2,1)S(1)}, u32[]{:S(2)}, u32[]{:S(2)}) %collective-permute-start.42) | collective-permute-done | bytes 147488 | tf_op jit(solution)/shard_map/ppermute | solution.py:42
  195.6 2.7 %collective-permute-start.44 = (bf16[96,768]{1,0:T(8,128)(2,1)}, bf16[96,768]{1,0:T(8,128)(2,1)S(1)}, u32[]{:S(2)}, u32[]{:S(2)}) collective-permute-start(bf16[96,768]{1,0:T(8,128)(2,1)} %get-tuple-element.242), channel_id=1, source_target_pairs={{0,8},{4,12},{8,0},{12,4},{16,24},{20,28},{24,16},{28,20},{1,9},{5... | collective-permute-start | bytes 442376 | tf_op jit(solution)/shard_map/ppermute | solution.py:42
  198.3 2.4 %collective-permute-start.46 = (bf16[96,768]{1,0:T(8,128)(2,1)}, bf16[96,768]{1,0:T(8,128)(2,1)S(1)}, u32[]{:S(2)}, u32[]{:S(2)}) collective-permute-start(bf16[96,768]{1,0:T(8,128)(2,1)} %get-tuple-element.244), channel_id=1, source_target_pairs={{0,24},{4,28},{8,16},{12,20},{16,8},{20,12},{24,0},{28,4},{1,25},{... | collective-permute-start | bytes 442376 | tf_op jit(solution)/shard_map/ppermute | solution.py:42
  202.9 7.9 %collective-permute-done.45.two = bf16[96,768]{1,0:T(8,128)(2,1)S(1)} collective-permute-done((bf16[96,768]{1,0:T(8,128)(2,1)}, bf16[96,768]{1,0:T(8,128)(2,1)S(1)}, u32[]{:S(2)}, u32[]{:S(2)}) %collective-permute-start.45) | collective-permute-done | bytes 147488 | tf_op jit(solution)/shard_map/ppermute | solution.py:42
  (129 shorter events, 29.8 us)
Async XLA Ops:
  0.6 22.1 %collective-permute-start.3 = (bf16[256,768]{1,0:T(8,128)(2,1)}, bf16[256,768]{1,0:T(8,128)(2,1)S(1)}, u32[]{:S(2)}, u32[]{:S(2)}) collective-permute-start(bf16[256,768]{1,0:T(8,128)(2,1)} %refs_6_.1), channel_id=1, source_target_pairs={{0,1},{1,0},{2,3},{3,2},{4,5},{5,4},{6,7},{7,6},{8,9},{9,8},{10,11... | collective-permute-start | bytes 1179656 | tf_op jit(solution)/shard_map/ppermute | solution.py:30
  3.8 9.8 %collective-permute-start.2 = (bf16[104,768]{1,0:T(8,128)(2,1)S(1)}, bf16[104,768]{1,0:T(8,128)(2,1)S(1)}, u32[]{:S(2)}, u32[]{:S(2)}) collective-permute-start(bf16[104,768]{1,0:T(8,128)(2,1)S(1)} %get-tuple-element.134), channel_id=1, source_target_pairs={{0,24},{4,28},{8,16},{12,20},{16,8},{20,12},{24,0},{28,4},{1,25},{... | collective-permute-start | bytes 479240 | tf_op jit(solution)/shard_map/ppermute | solution.py:42
  8.5 14.2 %collective-permute-start.1 = (bf16[104,768]{1,0:T(8,128)(2,1)S(1)}, bf16[104,768]{1,0:T(8,128)(2,1)S(1)}, u32[]{:S(2)}, u32[]{:S(2)}) collective-permute-start(bf16[104,768]{1,0:T(8,128)(2,1)S(1)} %get-tuple-element.134), channel_id=1, source_target_pairs={{0,16},{4,20},{8,24},{12,28},{16,0},{20,4},{24,8},{28,12},{1,17},{... | collective-permute-start | bytes 479240 | tf_op jit(solution)/shard_map/ppermute | solution.py:42
  8.5 14.2 %collective-permute-start = (bf16[104,768]{1,0:T(8,128)(2,1)S(1)}, bf16[104,768]{1,0:T(8,128)(2,1)S(1)}, u32[]{:S(2)}, u32[]{:S(2)}) collective-permute-start(bf16[104,768]{1,0:T(8,128)(2,1)S(1)} %get-tuple-element.134), channel_id=1, source_target_pairs={{0,8},{4,12},{8,0},{12,4},{16,24},{20,28},{24,16},{28,20},{1,9},{5... | collective-permute-start | bytes 479240 | tf_op jit(solution)/shard_map/ppermute | solution.py:42
  22.8 36.0 %copy-start.13 = (bf16[4,104,768]{2,1,0:T(8,128)(2,1)}, bf16[4,104,768]{2,1,0:T(8,128)(2,1)S(1)}, u32[]{:S(2)}) copy-start(bf16[4,104,768]{2,1,0:T(8,128)(2,1)S(1)} %pad_maximum_fusion.1.refs_0_) | copy-start | bytes 1916932
  22.8 18.7 %collective-permute-start.5 = (bf16[4,104,768]{2,1,0:T(8,128)(2,1)S(1)}, bf16[4,104,768]{2,1,0:T(8,128)(2,1)S(1)}, u32[]{:S(2)}, u32[]{:S(2)}) collective-permute-start(bf16[4,104,768]{2,1,0:T(8,128)(2,1)S(1)} %pad_maximum_fusion.1.refs_0_), channel_id=1, source_target_pairs={{0,4},{4,0},{8,12},{12,8},{16,20},{20,16},{24,28},{28,24},{1,5},{5... | collective-permute-start | bytes 1916936 | tf_op jit(solution)/shard_map/ppermute | solution.py:38
  24.4 17.1 %collective-permute-start.4 = (bf16[4,104,768]{2,1,0:T(8,128)(2,1)S(1)}, bf16[4,104,768]{2,1,0:T(8,128)(2,1)S(1)}, u32[]{:S(2)}, u32[]{:S(2)}) collective-permute-start(bf16[4,104,768]{2,1,0:T(8,128)(2,1)S(1)} %pad_maximum_fusion.1.refs_0_), channel_id=1, source_target_pairs={{0,2},{1,3},{2,0},{3,1},{4,6},{5,7},{6,4},{7,5},{8,10},{9,11},{10,... | collective-permute-start | bytes 1916936 | tf_op jit(solution)/shard_map/ppermute | solution.py:34
  25.9 9.2 %collective-permute-start.8 = (bf16[112,768]{1,0:T(8,128)(2,1)S(1)}, bf16[112,768]{1,0:T(8,128)(2,1)S(1)}, u32[]{:S(2)}, u32[]{:S(2)}) collective-permute-start(bf16[112,768]{1,0:T(8,128)(2,1)S(1)} %get-tuple-element.142), channel_id=1, source_target_pairs={{0,24},{4,28},{8,16},{12,20},{16,8},{20,12},{24,0},{28,4},{1,25},{... | collective-permute-start | bytes 516104 | tf_op jit(solution)/shard_map/ppermute | solution.py:42
  28.4 13.1 %collective-permute-start.7 = (bf16[112,768]{1,0:T(8,128)(2,1)S(1)}, bf16[112,768]{1,0:T(8,128)(2,1)S(1)}, u32[]{:S(2)}, u32[]{:S(2)}) collective-permute-start(bf16[112,768]{1,0:T(8,128)(2,1)S(1)} %get-tuple-element.142), channel_id=1, source_target_pairs={{0,16},{4,20},{8,24},{12,28},{16,0},{20,4},{24,8},{28,12},{1,17},{... | collective-permute-start | bytes 516104 | tf_op jit(solution)/shard_map/ppermute | solution.py:42
  28.4 13.1 %collective-permute-start.6 = (bf16[112,768]{1,0:T(8,128)(2,1)S(1)}, bf16[112,768]{1,0:T(8,128)(2,1)S(1)}, u32[]{:S(2)}, u32[]{:S(2)}) collective-permute-start(bf16[112,768]{1,0:T(8,128)(2,1)S(1)} %get-tuple-element.142), channel_id=1, source_target_pairs={{0,8},{4,12},{8,0},{12,4},{16,24},{20,28},{24,16},{28,20},{1,9},{5... | collective-permute-start | bytes 516104 | tf_op jit(solution)/shard_map/ppermute | solution.py:42
  41.6 13.1 %collective-permute-start.9 = (bf16[2,104,768]{2,1,0:T(8,128)(2,1)S(1)}, bf16[2,104,768]{2,1,0:T(8,128)(2,1)S(1)}, u32[]{:S(2)}, u32[]{:S(2)}) collective-permute-start(bf16[2,104,768]{2,1,0:T(8,128)(2,1)S(1)} %slice.81), channel_id=1, source_target_pairs={{0,2},{1,3},{2,0},{3,1},{4,6},{5,7},{6,4},{7,5},{8,10},{9,11},{10,... | collective-permute-start | bytes 958472 | tf_op jit(solution)/shard_map/ppermute | solution.py:34
  42.2 12.5 %collective-permute-start.10 = (bf16[2,104,768]{2,1,0:T(8,128)(2,1)S(1)}, bf16[2,104,768]{2,1,0:T(8,128)(2,1)S(1)}, u32[]{:S(2)}, u32[]{:S(2)}) collective-permute-start(bf16[2,104,768]{2,1,0:T(8,128)(2,1)S(1)} %slice.82), channel_id=1, source_target_pairs={{0,4},{4,0},{8,12},{12,8},{16,20},{20,16},{24,28},{28,24},{1,5},{5... | collective-permute-start | bytes 958472 | tf_op jit(solution)/shard_map/ppermute | solution.py:38
  42.7 8.1 %collective-permute-start.13 = (bf16[80,768]{1,0:T(8,128)(2,1)S(1)}, bf16[80,768]{1,0:T(8,128)(2,1)S(1)}, u32[]{:S(2)}, u32[]{:S(2)}) collective-permute-start(bf16[80,768]{1,0:T(8,128)(2,1)S(1)} %get-tuple-element.149), channel_id=1, source_target_pairs={{0,24},{4,28},{8,16},{12,20},{16,8},{20,12},{24,0},{28,4},{1,25},{... | collective-permute-start | bytes 368648 | tf_op jit(solution)/shard_map/ppermute | solution.py:42
  44.7 9.9 %collective-permute-start.12 = (bf16[80,768]{1,0:T(8,128)(2,1)S(1)}, bf16[80,768]{1,0:T(8,128)(2,1)S(1)}, u32[]{:S(2)}, u32[]{:S(2)}) collective-permute-start(bf16[80,768]{1,0:T(8,128)(2,1)S(1)} %get-tuple-element.149), channel_id=1, source_target_pairs={{0,16},{4,20},{8,24},{12,28},{16,0},{20,4},{24,8},{28,12},{1,17},{... | collective-permute-start | bytes 368648 | tf_op jit(solution)/shard_map/ppermute | solution.py:42
  44.7 9.9 %collective-permute-start.11 = (bf16[80,768]{1,0:T(8,128)(2,1)S(1)}, bf16[80,768]{1,0:T(8,128)(2,1)S(1)}, u32[]{:S(2)}, u32[]{:S(2)}) collective-permute-start(bf16[80,768]{1,0:T(8,128)(2,1)S(1)} %get-tuple-element.149), channel_id=1, source_target_pairs={{0,8},{4,12},{8,0},{12,4},{16,24},{20,28},{24,16},{28,20},{1,9},{5... | collective-permute-start | bytes 368648 | tf_op jit(solution)/shard_map/ppermute | solution.py:42
  54.8 4.0 %collective-permute-start.17 = (bf16[2,104,768]{2,1,0:T(8,128)(2,1)S(1)}, bf16[2,104,768]{2,1,0:T(8,128)(2,1)S(1)}, u32[]{:S(2)}, u32[]{:S(2)}) collective-permute-start(bf16[2,104,768]{2,1,0:T(8,128)(2,1)S(1)} %collective-permute-done.9.refs_3_), channel_id=1, source_target_pairs={{0,1},{1,0},{2,3},{3,2},{4,5},{5,4},{6,7},{7,6},{8,9},{9,8},{10,11... | collective-permute-start | bytes 958472 | tf_op jit(solution)/shard_map/ppermute | solution.py:30
  54.9 4.5 %collective-permute-start.18 = (bf16[2,104,768]{2,1,0:T(8,128)(2,1)S(1)}, bf16[2,104,768]{2,1,0:T(8,128)(2,1)S(1)}, u32[]{:S(2)}, u32[]{:S(2)}) collective-permute-start(bf16[2,104,768]{2,1,0:T(8,128)(2,1)S(1)} %collective-permute-done.10.refs_4_), channel_id=1, source_target_pairs={{0,1},{1,0},{2,3},{3,2},{4,5},{5,4},{6,7},{7,6},{8,9},{9,8},{10,11... | collective-permute-start | bytes 958472 | tf_op jit(solution)/shard_map/ppermute | solution.py:30
  55.7 27.9 %collective-permute-start.23 = (bf16[4,192,768]{2,1,0:T(8,128)(2,1)S(1)}, bf16[4,192,768]{2,1,0:T(8,128)(2,1)S(1)}, u32[]{:S(2)}, u32[]{:S(2)}) collective-permute-start(bf16[4,192,768]{2,1,0:T(8,128)(2,1)S(1)} %pad_maximum_fusion.refs_0_), channel_id=1, source_target_pairs={{0,2},{1,3},{2,0},{3,1},{4,6},{5,7},{6,4},{7,5},{8,10},{9,11},{10,... | collective-permute-start | bytes 3538952 | tf_op jit(solution)/shard_map/ppermute | solution.py:34
  57.2 28.0 %collective-permute-start.21 = (bf16[4,192,768]{2,1,0:T(8,128)(2,1)S(1)}, bf16[4,192,768]{2,1,0:T(8,128)(2,1)S(1)}, u32[]{:S(2)}, u32[]{:S(2)}) collective-permute-start(bf16[4,192,768]{2,1,0:T(8,128)(2,1)S(1)} %pad_maximum_fusion.refs_0_), channel_id=1, source_target_pairs={{0,4},{4,0},{8,12},{12,8},{16,20},{20,16},{24,28},{28,24},{1,5},{5... | collective-permute-start | bytes 3538952 | tf_op jit(solution)/shard_map/ppermute | solution.py:38
  58.7 2.1 collective-permute-start.14
  58.8 3.0 %collective-permute-start.15 = (bf16[4,104,768]{2,1,0:T(8,128)(2,1)S(1)}, bf16[4,104,768]{2,1,0:T(8,128)(2,1)S(1)}, u32[]{:S(2)}, u32[]{:S(2)}) collective-permute-start(bf16[4,104,768]{2,1,0:T(8,128)(2,1)S(1)} %collective-permute-done.4.refs_1_), channel_id=1, source_target_pairs={{0,1},{1,0},{2,3},{3,2},{4,5},{5,4},{6,7},{7,6},{8,9},{9,8},{10,11... | collective-permute-start | bytes 1916936 | tf_op jit(solution)/shard_map/ppermute | solution.py:30
  59.3 3.3 %collective-permute-start.16 = (bf16[4,104,768]{2,1,0:T(8,128)(2,1)S(1)}, bf16[4,104,768]{2,1,0:T(8,128)(2,1)S(1)}, u32[]{:S(2)}, u32[]{:S(2)}) collective-permute-start(bf16[4,104,768]{2,1,0:T(8,128)(2,1)S(1)} %collective-permute-done.5.refs_2_), channel_id=1, source_target_pairs={{0,1},{1,0},{2,3},{3,2},{4,5},{5,4},{6,7},{7,6},{8,9},{9,8},{10,11... | collective-permute-start | bytes 1916936 | tf_op jit(solution)/shard_map/ppermute | solution.py:30
  73.9 12.9 %collective-permute-start.19 = (bf16[256,384]{1,0:T(8,128)(2,1)S(1)}, bf16[256,384]{1,0:T(8,128)(2,1)S(1)}, u32[]{:S(2)}, u32[]{:S(2)}) collective-permute-start(bf16[256,384]{1,0:T(8,128)(2,1)S(1)} %get-tuple-element.159), channel_id=1, source_target_pairs={{0,1},{1,0},{2,3},{3,2},{4,5},{5,4},{6,7},{7,6},{8,9},{9,8},{10,11... | collective-permute-start | bytes 589832 | tf_op jit(solution)/shard_map/ppermute | solution.py:30
  83.6 14.4 %collective-permute-start.24 = (bf16[2,192,768]{2,1,0:T(8,128)(2,1)S(1)}, bf16[2,192,768]{2,1,0:T(8,128)(2,1)S(1)}, u32[]{:S(2)}, u32[]{:S(2)}) collective-permute-start(bf16[2,192,768]{2,1,0:T(8,128)(2,1)S(1)} %slice.106), channel_id=1, source_target_pairs={{0,4},{4,0},{8,12},{12,8},{16,20},{20,16},{24,28},{28,24},{1,5},{5... | collective-permute-start | bytes 1769480 | tf_op jit(solution)/shard_map/ppermute | solution.py:38
  85.2 14.1 %collective-permute-start.22 = (bf16[2,192,768]{2,1,0:T(8,128)(2,1)S(1)}, bf16[2,192,768]{2,1,0:T(8,128)(2,1)S(1)}, u32[]{:S(2)}, u32[]{:S(2)}) collective-permute-start(bf16[2,192,768]{2,1,0:T(8,128)(2,1)S(1)} %slice.105), channel_id=1, source_target_pairs={{0,2},{1,3},{2,0},{3,1},{4,6},{5,7},{6,4},{7,5},{8,10},{9,11},{10,... | collective-permute-start | bytes 1769480 | tf_op jit(solution)/shard_map/ppermute | solution.py:34
  87.6 1.8 collective-permute-start.20
  100.8 1.8 collective-permute-start.25
  104.5 1.7 collective-permute-start.26
  108.1 15.4 %collective-permute-start.27 = (bf16[2,192,768]{2,1,0:T(8,128)(2,1)S(1)}, bf16[2,192,768]{2,1,0:T(8,128)(2,1)S(1)}, u32[]{:S(2)}, u32[]{:S(2)}) collective-permute-start(bf16[2,192,768]{2,1,0:T(8,128)(2,1)S(1)} %get-tuple-element.189), channel_id=1, source_target_pairs={{0,4},{4,0},{8,12},{12,8},{16,20},{20,16},{24,28},{28,24},{1,5},{5... | collective-permute-start | bytes 1769480 | tf_op jit(solution)/shard_map/ppermute | solution.py:38
  109.2 15.1 %collective-permute-start.28 = (bf16[2,192,768]{2,1,0:T(8,128)(2,1)S(1)}, bf16[2,192,768]{2,1,0:T(8,128)(2,1)S(1)}, u32[]{:S(2)}, u32[]{:S(2)}) collective-permute-start(bf16[2,192,768]{2,1,0:T(8,128)(2,1)S(1)} %get-tuple-element.191), channel_id=1, source_target_pairs={{0,2},{1,3},{2,0},{3,1},{4,6},{5,7},{6,4},{7,5},{8,10},{9,11},{10,... | collective-permute-start | bytes 1769480 | tf_op jit(solution)/shard_map/ppermute | solution.py:34
  124.3 1.7 collective-permute-start.29
  127.3 2.7 %collective-permute-start.30 = (bf16[256,768]{1,0:T(8,128)(2,1)S(1)}, bf16[256,768]{1,0:T(8,128)(2,1)S(1)}, u32[]{:S(2)}, u32[]{:S(2)}) collective-permute-start(bf16[256,768]{1,0:T(8,128)(2,1)S(1)} %get-tuple-element.196.a0), channel_id=1, source_target_pairs={{0,1},{1,0},{2,3},{3,2},{4,5},{5,4},{6,7},{7,6},{8,9},{9,8},{10,11... | collective-permute-start | bytes 1179656 | tf_op jit(solution)/shard_map/ppermute | solution.py:30
  127.5 30.3 %collective-permute-start.32 = (bf16[4,192,768]{2,1,0:T(8,128)(2,1)S(1)}, bf16[4,192,768]{2,1,0:T(8,128)(2,1)S(1)}, u32[]{:S(2)}, u32[]{:S(2)}) collective-permute-start(bf16[4,192,768]{2,1,0:T(8,128)(2,1)S(1)} %get-tuple-element.210), channel_id=1, source_target_pairs={{0,2},{1,3},{2,0},{3,1},{4,6},{5,7},{6,4},{7,5},{8,10},{9,11},{10,... | collective-permute-start | bytes 3538952 | tf_op jit(solution)/shard_map/ppermute | solution.py:34
  128.4 29.4 %collective-permute-start.33 = (bf16[4,192,768]{2,1,0:T(8,128)(2,1)S(1)}, bf16[4,192,768]{2,1,0:T(8,128)(2,1)S(1)}, u32[]{:S(2)}, u32[]{:S(2)}) collective-permute-start(bf16[4,192,768]{2,1,0:T(8,128)(2,1)S(1)} %get-tuple-element.211), channel_id=1, source_target_pairs={{0,4},{4,0},{8,12},{12,8},{16,20},{20,16},{24,28},{28,24},{1,5},{5... | collective-permute-start | bytes 3538952 | tf_op jit(solution)/shard_map/ppermute | solution.py:38
  139.1 18.7 %collective-permute-start.31 = (f32[256,768]{1,0:T(8,128)S(1)}, f32[256,768]{1,0:T(8,128)S(1)}, u32[]{:S(2)}, u32[]{:S(2)}) collective-permute-start(f32[256,768]{1,0:T(8,128)S(1)} %get-tuple-element.204), channel_id=1, source_target_pairs={{0,1},{1,0},{2,3},{3,2},{4,5},{5,4},{6,7},{7,6},{8,9},{9,8},{10,11... | collective-permute-start | bytes 2359304 | tf_op jit(solution)/shard_map/ppermute | solution.py:30
  158.7 17.5 %collective-permute-start.34 = (bf16[2,96,768]{2,1,0:T(8,128)(2,1)}, bf16[2,96,768]{2,1,0:T(8,128)(2,1)S(1)}, u32[]{:S(2)}, u32[]{:S(2)}) collective-permute-start(bf16[2,96,768]{2,1,0:T(8,128)(2,1)} %get-tuple-element.219), channel_id=1, source_target_pairs={{0,2},{1,3},{2,0},{3,1},{4,6},{5,7},{6,4},{7,5},{8,10},{9,11},{10,... | collective-permute-start | bytes 884744 | tf_op jit(solution)/shard_map/ppermute | solution.py:34
  159.8 16.4 %collective-permute-start.35 = (bf16[2,96,768]{2,1,0:T(8,128)(2,1)}, bf16[2,96,768]{2,1,0:T(8,128)(2,1)S(1)}, u32[]{:S(2)}, u32[]{:S(2)}) collective-permute-start(bf16[2,96,768]{2,1,0:T(8,128)(2,1)} %get-tuple-element.220), channel_id=1, source_target_pairs={{0,4},{4,0},{8,12},{12,8},{16,20},{20,16},{24,28},{28,24},{1,5},{5... | collective-permute-start | bytes 884744 | tf_op jit(solution)/shard_map/ppermute | solution.py:38
  162.0 7.6 %collective-permute-start.36 = (bf16[96,768]{1,0:T(8,128)(2,1)}, bf16[96,768]{1,0:T(8,128)(2,1)S(1)}, u32[]{:S(2)}, u32[]{:S(2)}) collective-permute-start(bf16[96,768]{1,0:T(8,128)(2,1)} %get-tuple-element.221), channel_id=1, source_target_pairs={{0,8},{4,12},{8,0},{12,4},{16,24},{20,28},{24,16},{28,20},{1,9},{5... | collective-permute-start | bytes 442376 | tf_op jit(solution)/shard_map/ppermute | solution.py:42
  162.1 14.1 %collective-permute-start.37 = (bf16[96,768]{1,0:T(8,128)(2,1)}, bf16[96,768]{1,0:T(8,128)(2,1)S(1)}, u32[]{:S(2)}, u32[]{:S(2)}) collective-permute-start(bf16[96,768]{1,0:T(8,128)(2,1)} %get-tuple-element.222), channel_id=1, source_target_pairs={{0,16},{4,20},{8,24},{12,28},{16,0},{20,4},{24,8},{28,12},{1,17},{... | collective-permute-start | bytes 442376 | tf_op jit(solution)/shard_map/ppermute | solution.py:42
  164.2 11.9 %collective-permute-start.38 = (bf16[96,768]{1,0:T(8,128)(2,1)}, bf16[96,768]{1,0:T(8,128)(2,1)S(1)}, u32[]{:S(2)}, u32[]{:S(2)}) collective-permute-start(bf16[96,768]{1,0:T(8,128)(2,1)} %get-tuple-element.223), channel_id=1, source_target_pairs={{0,24},{4,28},{8,16},{12,20},{16,8},{20,12},{24,0},{28,4},{1,25},{... | collective-permute-start | bytes 442376 | tf_op jit(solution)/shard_map/ppermute | solution.py:42
  177.3 17.2 %collective-permute-start.39 = (bf16[4,96,768]{2,1,0:T(8,128)(2,1)}, bf16[4,96,768]{2,1,0:T(8,128)(2,1)S(1)}, u32[]{:S(2)}, u32[]{:S(2)}) collective-permute-start(bf16[4,96,768]{2,1,0:T(8,128)(2,1)} %get-tuple-element.227), channel_id=1, source_target_pairs={{0,2},{1,3},{2,0},{3,1},{4,6},{5,7},{6,4},{7,5},{8,10},{9,11},{10,... | collective-permute-start | bytes 1769480 | tf_op jit(solution)/shard_map/ppermute | solution.py:34
  178.8 15.7 %collective-permute-start.40 = (bf16[4,96,768]{2,1,0:T(8,128)(2,1)}, bf16[4,96,768]{2,1,0:T(8,128)(2,1)S(1)}, u32[]{:S(2)}, u32[]{:S(2)}) collective-permute-start(bf16[4,96,768]{2,1,0:T(8,128)(2,1)} %get-tuple-element.228), channel_id=1, source_target_pairs={{0,4},{4,0},{8,12},{12,8},{16,20},{20,16},{24,28},{28,24},{1,5},{5... | collective-permute-start | bytes 1769480 | tf_op jit(solution)/shard_map/ppermute | solution.py:38
  179.9 7.0 %collective-permute-start.41 = (bf16[96,768]{1,0:T(8,128)(2,1)}, bf16[96,768]{1,0:T(8,128)(2,1)S(1)}, u32[]{:S(2)}, u32[]{:S(2)}) collective-permute-start(bf16[96,768]{1,0:T(8,128)(2,1)} %get-tuple-element.235), channel_id=1, source_target_pairs={{0,8},{4,12},{8,0},{12,4},{16,24},{20,28},{24,16},{28,20},{1,9},{5... | collective-permute-start | bytes 442376 | tf_op jit(solution)/shard_map/ppermute | solution.py:42
  182.3 12.2 %collective-permute-start.42 = (bf16[96,768]{1,0:T(8,128)(2,1)}, bf16[96,768]{1,0:T(8,128)(2,1)S(1)}, u32[]{:S(2)}, u32[]{:S(2)}) collective-permute-start(bf16[96,768]{1,0:T(8,128)(2,1)} %get-tuple-element.236), channel_id=1, source_target_pairs={{0,16},{4,20},{8,24},{12,28},{16,0},{20,4},{24,8},{28,12},{1,17},{... | collective-permute-start | bytes 442376 | tf_op jit(solution)/shard_map/ppermute | solution.py:42
  182.5 12.0 %collective-permute-start.43 = (bf16[96,768]{1,0:T(8,128)(2,1)S(1)}, bf16[96,768]{1,0:T(8,128)(2,1)S(1)}, u32[]{:S(2)}, u32[]{:S(2)}) collective-permute-start(bf16[96,768]{1,0:T(8,128)(2,1)S(1)} %copy-done.23), channel_id=1, source_target_pairs={{0,24},{4,28},{8,16},{12,20},{16,8},{20,12},{24,0},{28,4},{1,25},{... | collective-permute-start | bytes 442376 | tf_op jit(solution)/shard_map/ppermute | solution.py:42
  195.6 7.3 %collective-permute-start.44 = (bf16[96,768]{1,0:T(8,128)(2,1)}, bf16[96,768]{1,0:T(8,128)(2,1)S(1)}, u32[]{:S(2)}, u32[]{:S(2)}) collective-permute-start(bf16[96,768]{1,0:T(8,128)(2,1)} %get-tuple-element.242), channel_id=1, source_target_pairs={{0,8},{4,12},{8,0},{12,4},{16,24},{20,28},{24,16},{28,20},{1,9},{5... | collective-permute-start | bytes 442376 | tf_op jit(solution)/shard_map/ppermute | solution.py:42
  198.3 12.5 %collective-permute-start.45 = (bf16[96,768]{1,0:T(8,128)(2,1)}, bf16[96,768]{1,0:T(8,128)(2,1)S(1)}, u32[]{:S(2)}, u32[]{:S(2)}) collective-permute-start(bf16[96,768]{1,0:T(8,128)(2,1)} %get-tuple-element.243), channel_id=1, source_target_pairs={{0,16},{4,20},{8,24},{12,28},{16,0},{20,4},{24,8},{28,12},{1,17},{... | collective-permute-start | bytes 442376 | tf_op jit(solution)/shard_map/ppermute | solution.py:42
  198.3 12.5 %collective-permute-start.46 = (bf16[96,768]{1,0:T(8,128)(2,1)}, bf16[96,768]{1,0:T(8,128)(2,1)S(1)}, u32[]{:S(2)}, u32[]{:S(2)}) collective-permute-start(bf16[96,768]{1,0:T(8,128)(2,1)} %get-tuple-element.244), channel_id=1, source_target_pairs={{0,24},{4,28},{8,16},{12,20},{16,8},{20,12},{24,0},{28,4},{1,25},{... | collective-permute-start | bytes 442376 | tf_op jit(solution)/shard_map/ppermute | solution.py:42
  (23 other events, 212.2 us)

commit v4 on v3

--- a/solution.py
+++ b/solution.py
@@ -18,7 +18,8 @@
 F32 = jnp.float32
 BF16 = jnp.bfloat16
 
-FIRST = 112
+ONE, TWO = 80, 16
+FIRST = 104
 
 CORE = [(i, i ^ 1) for i in range(4)]
 XPAIR = [(i, i ^ 2) for i in range(4)]
@@ -238,7 +239,10 @@
         out[i, 0:8, 0:width] = vecs[:, width * i : width * i + width]
     for spot in range(4):
         for kz in range(4):
-            out[slot_of(spot, kz), 0:1, 24:120] = ubs[spot][:, 96 * kz : 96 * kz + 96]
+            to, ub = slot_of(spot, kz), ubs[spot]
+            out[to, 0:1, 24 : 24 + ONE] = ub[:, ONE * kz : ONE * kz + ONE]
+            at = 4 * ONE + TWO * kz
+            out[to, 0:1, 24 + ONE : 24 + ONE + TWO] = ub[:, at : at + TWO]
 
 
 def exchange_terms(zero, one, two, ubs, devices):
@@ -255,7 +259,7 @@
     return a + bit - 2 * a * bit
 
 
-def pack_kernel(qkv_in, proj_in, up_in, down_in, bias, vectors, a_out, fa_out, fb_out, a, p, f, sems):
+def pack_kernel(qkv_in, proj_in, up_in, down_in, bias, vectors, a_out, one_a, one_b, two, a, p, f, sems):
     rows_q, rows_p, half = qkv_in.shape[0], proj_in.shape[0], down_in.shape[0]
     copies = Copies(sems)
     copies.start(qkv_in, a.at[pl.ds(0, rows_q)])
@@ -284,15 +288,21 @@
         [q[:, 192 * i : 192 * i + 192] for i in (0, 2, 1, 3)], 1
     )
     a_out[rows_q + rows_p :] = v.astype(BF16)
-    fa_out[...] = f[0 : fa_out.shape[0]]
-    fb_out[...] = f[fa_out.shape[0] :]
+    one = jnp.concatenate([f[0:ONE], f[half : half + ONE]])
+    one_a[...], one_b[...] = one[0:FIRST], one[FIRST:]
+    two[0:TWO], two[TWO:] = f[ONE:half], f[half + ONE :]
 
 
 def pack(qkv, proj, up, down, bias, vectors):
     rows, half = qkv.shape[0] + proj.shape[0] + 8, down.shape[0]
     return call(
         pack_kernel,
-        (shape((rows, D)), shape((FIRST, D)), shape((2 * half - FIRST, D))),
+        (
+            shape((rows, D)),
+            shape((FIRST, D)),
+            shape((2 * ONE - FIRST, D)),
+            shape((2 * TWO, D)),
+        ),
         (qkv, proj, up, down, bias[None], jnp.stack(vectors)),
         scratch=[
             pltpu.VMEM((rows, D), BF16),
@@ -369,8 +379,10 @@
             i = slot_of(spot, kz)
             b = slots[i, row : row + 1].astype(F32)
             b = jnp.where(i < 16, b[:, D // 2 : D // 2 + 96], b[:, 0:96])
-            at = 384 * spot + 96 * kz
-            out[:, at : at + 96] = b
+            at = 4 * ONE * spot + ONE * kz
+            out[:, at : at + ONE] = b[:, 0:ONE]
+            at = 16 * ONE + 4 * TWO * spot + TWO * kz
+            out[:, at : at + TWO] = b[:, ONE:]
 
 
 def attend_kernel(rows_q, rows_p, bucket, lengths, x0, x1, *refs):
@@ -527,10 +539,21 @@
 def ffn_weights(refs):
     if len(refs[0].shape) == 2:
         return refs[0][...], refs[1][...]
-    half = refs[0].shape[1] // 2
-    blocks = [(r, i) for r in refs for i in range(r.shape[0])]
-    up = jnp.concatenate([r[i, 0:half] for r, i in blocks])
-    down = jnp.concatenate([r[i, half : 2 * half] for r, i in blocks])
+    return stacked(ones_of(refs) if refs[0].shape[1] == 2 * ONE else twos_of(refs, range(4)))
+
+
+def ones_of(refs):
+    return [(r, i) for r in refs for i in range(r.shape[0])]
+
+
+def twos_of(refs, spots):
+    along_z = [(r, i) for r in refs for i in range(0, r.shape[0], 4)]
+    return [(r, i + spot) for spot in spots for r, i in along_z]
+
+
+def stacked(blocks):
+    up = jnp.concatenate([r[i, 0 : r.shape[1] // 2] for r, i in blocks])
+    down = jnp.concatenate([r[i, r.shape[1] // 2 :] for r, i in blocks])
     return up, down
 
 
@@ -601,16 +624,24 @@
     )
 
 
-def ffn_back_kernel(first, lead, count, d0, d1, x0, x1, *refs):
-    far, hid_in, slope_in, refs = refs[:count], refs[count], refs[count + 1], refs[count + 2 :]
+def ffn_back_kernel(first, spot, count, d0, d1, x0, x1, *refs):
+    weights, refs = refs[:count], refs[count:]
+    if spot is None:
+        hid, slope = refs[0], refs[1]
+        refs = refs[2:]
+        uw, dw = ffn_weights(weights)
+    else:
+        (hid1, slope1, hid2, slope2), refs = refs[:4], refs[4:]
+        tail = slice(4 * TWO * spot, 4 * TWO * spot + 4 * TWO)
+        hid = jnp.concatenate([hid1[...], hid2[:, tail]], 1)
+        slope = jnp.concatenate([slope1[...], slope2[:, tail]], 1)
+        uw, dw = stacked(ones_of(weights[:-3]) + twos_of(weights[-3:], [spot]))
     if first:
         in0 = in1 = None
     else:
         (in0, in1), refs = refs[:2], refs[2:]
-    outs, (ub, out0, out1) = refs[:count], refs[count:]
-    half, width = x0.shape[0], ub.shape[1]
-    slope, hid = slope_in.at[:, pl.ds(lead, width)], hid_in.at[:, pl.ds(lead, width)]
-    uw, dw = ffn_weights(far)
+    *outs, ub, out0, out1 = refs
+    half = x0.shape[0]
     cots = []
     for i, (d, before, out) in enumerate(((d0, in0, out0), (d1, in1, out1))):
         rws = slice(half * i, half * i + half)
@@ -624,26 +655,29 @@
     )
     dg = (tn(hid[0:half], d0[...]) + tn(hid[half : 2 * half], d1[...])).astype(BF16)
     ug = (tn(cots[0], x0[...]) + tn(cots[1], x1[...])).astype(BF16)
-    if len(outs[0].shape) == 2:
+    if spot is None:
         outs[0][...], outs[1][...] = ug, dg
-    else:
-        rows = outs[0].shape[1] // 2
-        at = 0
-        for g in outs:
-            for i in range(g.shape[0]):
-                g[i, 0:rows] = ug[at : at + rows]
-                g[i, rows : 2 * rows] = dg[at : at + rows]
-                at += rows
-
-
-def ffn_back(d0, d1, x0, x1, weights, kept, lead, sums, last):
+        return
+    rows = ONE + TWO
+    for k in range(4):
+        out, i = (outs[0], k) if len(outs) == 1 else (outs[k // 2], k % 2)
+        for at, g in ((0, ug), (rows, dg)):
+            out[i, at : at + ONE] = g[ONE * k : ONE * k + ONE]
+            low = 4 * ONE + TWO * k
+            out[i, at + ONE : at + rows] = g[low : low + TWO]
+
+
+def ffn_back(d0, d1, x0, x1, spot, weights, kept, sums, last):
     half, count = x0.shape[0], len(weights)
-    flat = len(weights[0].shape) == 2
-    width = weights[0].shape[0] if flat else sum(w.shape[0] * w.shape[1] // 2 for w in weights)
+    if spot is None:
+        outs, width = [shape(w.shape) for w in weights], weights[0].shape[0]
+    else:
+        width = 4 * (ONE + TWO)
+        outs = [shape((2, width // 2, D))] * 2 if spot == 3 else [shape((4, width // 2, D))]
     *grads, ub, s0, s1 = call(
-        functools.partial(ffn_back_kernel, not sums, lead, count),
+        functools.partial(ffn_back_kernel, not sums, spot, count),
         (
-            *[shape(w.shape) for w in weights],
+            *outs,
             shape((1, width), F32),
             shape((half, D), F32),
             shape((half, D), BF16 if last else F32),
@@ -821,7 +855,7 @@
         second_shift,
     ]
     if direct:
-        a_shard, fa_shard, fb_shard = pack(
+        a_shard, one_a, one_b, two = pack(
             qkv_weight.T, proj_weight.T, up_weight.T, down_weight, up_bias, vectors
         )
     else:
@@ -837,22 +871,33 @@
     other_in = core_swap(inputs)
     k = jnp.arange(batch_count * 2)
     if direct:
-        a_z = jnp.stack(z_line(a_shard))
-        a_z, other_in = lax.optimization_barrier((a_z, other_in))
-        fa_z = z_line(after(fa_shard, a_z))
+        a_z = z_line(a_shard)
+        two = after(two, a_z[1])
+        two_x, two_y = x_swap(two), y_swap(two)
+        two_d = jnp.concatenate([x_swap(two_y[:TWO]), y_swap(two_x[TWO:])])
+        two_lo = jnp.stack([two, two_x, two_y, two_d])
+        a_z, two_lo, other_in = lax.optimization_barrier((jnp.stack(a_z), two_lo, other_in))
+        one_a = z_line(after(one_a, a_z))
         a_x, a_y = x_swap(a_z), y_swap(a_z)
-        a_x, a_y, fa_z = lax.optimization_barrier((a_x, a_y, fa_z))
-        fb_z = z_line(after(fb_shard, fa_z))
+        a_x, a_y, one_a, two_lo = lax.optimization_barrier((a_x, a_y, one_a, two_lo))
+        one_b = after(one_b, one_a)
+        near = z_swap(jnp.concatenate([one_b, two_lo.reshape(8 * TWO, D)]), 1)
+        one_b = [one_b, None, z_swap(one_b, 2), z_swap(one_b, 3)]
         a_d = [x_swap(a_y[:2]), y_swap(a_x[2:])]
-        a_d, fb_z = lax.optimization_barrier((a_d, fb_z))
+        near, one_b[2], one_b[3], a_d = lax.optimization_barrier((near, one_b[2], one_b[3], a_d))
+        one_b[1], two_hi = near[: 2 * ONE - FIRST], near[2 * ONE - FIRST :].reshape(two_lo.shape)
         a_own = [a_z, a_x, a_y, *a_d]
-        a_swapped = [core_swap(v) for v in after(a_own, fb_z)]
-        f_z = jnp.stack([jnp.concatenate(pair) for pair in zip(fa_z, fb_z)])
-        f_x, f_y, *f_d = gather_four(f_z)[1:]
+        a_swapped = [core_swap(v) for v in after(a_own, near)]
+        one_z = jnp.stack([jnp.concatenate(pair) for pair in zip(one_a, one_b)])
+        one_x, one_y = x_swap(one_z), y_swap(one_z)
+        two_far = z_swap(jnp.concatenate([two_lo, two_hi]), 2)
+        one_x, one_y, two_far = lax.optimization_barrier((one_x, one_y, two_far))
+        one_d = [x_swap(one_y[:2]), y_swap(one_x[2:])]
+        twos = [two_lo, two_hi, two_far]
         ctx_own, ctx_other, q, kk, v, ctx, probs, wr, ub_all, proj_w, small_all = attend(
             bucket, lengths, inputs, other_in, (*a_own, *a_swapped), wq, wp
         )
-        f_all = [[f_z], [f_x, f_y], f_d]
+        f_all = [[one_z], [one_x], [one_y], twos, one_d]
     else:
         a_all = lax.all_gather(a_shard, ("batch", "head"), axis=0)
         qkv_all = a_all[:, :wq].reshape(2, 2, 576, D)
@@ -876,9 +921,13 @@
     first_in = core_swap(first_low)
     sums = ()
     kept = []
-    at = 0
-    for weights in f_all:
-        width = (384, 768, 384)[len(kept)] if direct else FF // 4
+    starts = (0, FF // 4)
+    if direct:
+        starts = (0, 4 * ONE, 8 * ONE, 16 * ONE, 12 * ONE)
+    for weights, at in zip(f_all, starts):
+        width = FF // 4
+        if direct:
+            width = 16 * TWO if len(kept) == 3 else 4 * ONE
         hid, slope, *sums = ffn(
             first_low,
             first_in,
@@ -888,7 +937,6 @@
             len(kept) == len(f_all) - 1,
         )
         kept.append((hid, slope))
-        at += width
     layer_out, sum_two, down_low, sums_two = second_norm(
         bucket, lengths, first, sums[0], core_swap(sums[1]), small_all, cotangent
     )
@@ -897,17 +945,25 @@
     sums = ()
     f_parts, ub_parts = [], []
     if direct:
-        sets = (([f_z], 0, 0), ([f_x], 1, 0), ([f_y], 1, 384), (f_d, 2, 0))
-        for weights, which, lead in reversed(sets):
+        for spot, i in ((3, 4), (2, 2), (1, 1), (0, 0)):
+            weights, both = (*f_all[i], *twos), (*kept[i], *kept[3])
             grads, ub, sums = ffn_back(
-                down_low, down_in, first_low, first_in, weights, kept[which], lead, sums, which + lead == 0
+                down_low, down_in, first_low, first_in, spot, weights, both, sums, spot == 0
             )
             f_parts = grads + f_parts
             ub_parts.insert(0, ub)
     else:
         for weights, pair in zip(f_all, kept):
             grads, ub, sums = ffn_back(
-                down_low, down_in, first_low, first_in, weights, pair, 0, sums, len(f_parts) == len(f_all) - 1
+                down_low,
+                down_in,
+                first_low,
+                first_in,
+                None,
+                weights,
+                pair,
+                sums,
+                len(f_parts) == len(f_all) - 1,
             )
             f_parts.append(grads)
             ub_parts.append(ub)

time: 212 us -> 206 us (0.972)
  waiting for transfers between devices: 93.2 us -> 78.4 us
  starting transfers between devices: 49.9 us -> 55.8 us
  Pallas kernels: 41.9 us -> 44.3 us
    ppermute x8 -> x10, waiting for transfers between devices: 11.6 us -> 2.74 us  [x_swap(): return lax.ppermute(v, 'head', XPAIR)]
    ppermute x13, waiting for transfers between devices: 9.93 us -> 6.64 us  [core_swap(): return lax.ppermute(v, 'head', CORE)]
    ppermute x8 -> x10, starting transfers between devices: 9.7 us -> 12.7 us  [x_swap(): return lax.ppermute(v, 'head', XPAIR)]
    ppermute x18 -> x19, waiting for transfers between devices: 58.4 us -> 55.6 us  [z_swap(): return lax.ppermute(v, 'batch', ZPAIR[k])]
    ppermute x8 -> x10, starting transfers between devices: 9.26 us -> 11.8 us  [y_swap(): return lax.ppermute(v, 'batch', YPAIR)]
    pallas_call x19 -> x21, Pallas kernels: 41.9 us -> 44.3 us  [call(): pl.pallas_call(kernel, out_shape=out_shape, in_specs=ins, out_specs=outs,...]
    ppermute x18 -> x19, starting transfers between devices: 28.5 us -> 29.3 us  [z_swap(): return lax.ppermute(v, 'batch', ZPAIR[k])]
    ppermute x8 -> x10, waiting for transfers between devices: 13.2 us -> 13.5 us  [y_swap(): return lax.ppermute(v, 'batch', YPAIR)]
  transfers between devices with their start and end apart: 47 -> 52, of which waited for: 24 -> 24; matrix products, arithmetic and copies ran while one was open for 2% -> 2% of each run, Pallas kernels for 15% -> 16%
where the time goes in v4:
time: 206 us
  waiting for transfers between devices  78.4 us (38%)
  starting transfers between devices  55.8 us (27%)
  Pallas kernels  44.3 us (22%)
  blocking collectives  19.2 us (9%)
  local copies, waits for them, and re-layouts  4.51 us (2%)
  other arithmetic  2.48 us (1%)
    ppermute x19, waiting for transfers between devices, z_swap(): return lax.ppermute(v, 'batch', ZPAIR[k])  55.6 us
    pallas_call x21, Pallas kernels, call(): pl.pallas_call(kernel, out_shape=out_shape, in_specs=ins, out_specs=outs,...  44.3 us
    ppermute x19, starting transfers between devices, z_swap(): return lax.ppermute(v, 'batch', ZPAIR[k])  29.3 us
    all_to_all x1, blocking collectives, local(): lax.all_to_all(terms, ('batch', 'head'), split_axis=0, concat_axis=0, til...  19.2 us
    ppermute x10, waiting for transfers between devices, y_swap(): return lax.ppermute(v, 'batch', YPAIR)  13.5 us
    ppermute x10, starting transfers between devices, x_swap(): return lax.ppermute(v, 'head', XPAIR)  12.7 us
    ppermute x10, starting transfers between devices, y_swap(): return lax.ppermute(v, 'batch', YPAIR)  11.8 us
    ppermute x13, waiting for transfers between devices, core_swap(): return lax.ppermute(v, 'head', CORE)  6.64 us
  transfers between devices with their start and end apart: 52, of which 24 were waited for; matrix products, arithmetic and copies ran while one was open for 2% of the time, Pallas kernels for 16%

profile of v4, /device:TPU:0, one launch (start us, length us, event | category | flops | bytes accessed | tf_op | source)
XLA Modules:
  0.0 205.9 jit_solution(3889877722760618311)
XLA Ops:
  3.3 3.1 %collective-permute-start = (bf16[104,768]{1,0:T(8,128)(2,1)S(1)}, bf16[104,768]{1,0:T(8,128)(2,1)S(1)}, u32[]{:S(2)}, u32[]{:S(2)}) collective-permute-start(bf16[104,768]{1,0:T(8,128)(2,1)S(1)} %get-tuple-element.148), channel_id=1, source_target_pairs={{0,8},{4,12},{8,0},{12,4},{16,24},{20,28},{24,16},{28,20},{1,9},{5... | collective-permute-start | bytes 479240 | tf_op jit(solution)/shard_map/ppermute | solution.py:43
  6.4 2.5 %collective-permute-start.2 = (bf16[104,768]{1,0:T(8,128)(2,1)S(1)}, bf16[104,768]{1,0:T(8,128)(2,1)S(1)}, u32[]{:S(2)}, u32[]{:S(2)}) collective-permute-start(bf16[104,768]{1,0:T(8,128)(2,1)S(1)} %get-tuple-element.148), channel_id=1, source_target_pairs={{0,24},{4,28},{8,16},{12,20},{16,8},{20,12},{24,0},{28,4},{1,25},{... | collective-permute-start | bytes 479240 | tf_op jit(solution)/shard_map/ppermute | solution.py:43
  9.0 1.9 collective-permute-done
  10.9 1.5 collective-permute-start.4
  12.4 1.5 collective-permute-start.3
  15.0 1.5 collective-permute-start.5
  16.5 1.5 collective-permute-start.6
  18.0 5.1 %collective-permute-done.1 = bf16[104,768]{1,0:T(8,128)(2,1)S(1)} collective-permute-done((bf16[104,768]{1,0:T(8,128)(2,1)S(1)}, bf16[104,768]{1,0:T(8,128)(2,1)S(1)}, u32[]{:S(2)}, u32[]{:S(2)}) %collective-permute-start.1) | collective-permute-done | bytes 159776 | tf_op jit(solution)/shard_map/ppermute | solution.py:43
  23.3 1.6 collective-permute-start.9
  24.9 1.5 collective-permute-start.8
  26.3 2.6 %collective-permute-start.12 = (bf16[104,768]{1,0:T(8,128)(2,1)S(1)}, bf16[104,768]{1,0:T(8,128)(2,1)S(1)}, u32[]{:S(2)}, u32[]{:S(2)}) collective-permute-start(bf16[104,768]{1,0:T(8,128)(2,1)S(1)} %get-tuple-element.159), channel_id=1, source_target_pairs={{0,24},{4,28},{8,16},{12,20},{16,8},{20,12},{24,0},{28,4},{1,25},{... | collective-permute-start | bytes 479240 | tf_op jit(solution)/shard_map/ppermute | solution.py:43
  29.0 1.7 collective-permute-start.10
  30.7 4.5 %collective-permute-done.12 = bf16[104,768]{1,0:T(8,128)(2,1)S(1)} collective-permute-done((bf16[104,768]{1,0:T(8,128)(2,1)S(1)}, bf16[104,768]{1,0:T(8,128)(2,1)S(1)}, u32[]{:S(2)}, u32[]{:S(2)}) %collective-permute-start.12) | collective-permute-done | bytes 159776 | tf_op jit(solution)/shard_map/ppermute | solution.py:43
  35.2 5.9 %collective-permute-done.11 = bf16[104,768]{1,0:T(8,128)(2,1)S(1)} collective-permute-done((bf16[104,768]{1,0:T(8,128)(2,1)S(1)}, bf16[104,768]{1,0:T(8,128)(2,1)S(1)}, u32[]{:S(2)}, u32[]{:S(2)}) %collective-permute-start.11) | collective-permute-done | bytes 159776 | tf_op jit(solution)/shard_map/ppermute | solution.py:43
  42.4 2.4 %collective-permute-start.15 = (bf16[56,768]{1,0:T(8,128)(2,1)S(1)}, bf16[56,768]{1,0:T(8,128)(2,1)S(1)}, u32[]{:S(2)}, u32[]{:S(2)}) collective-permute-start(bf16[56,768]{1,0:T(8,128)(2,1)S(1)} %get-tuple-element.163), channel_id=1, source_target_pairs={{0,24},{4,28},{8,16},{12,20},{16,8},{20,12},{24,0},{28,4},{1,25},{... | collective-permute-start | bytes 258056 | tf_op jit(solution)/shard_map/ppermute | solution.py:43
  45.9 6.8 %collective-permute-done.15 = bf16[56,768]{1,0:T(8,128)(2,1)S(1)} collective-permute-done((bf16[56,768]{1,0:T(8,128)(2,1)S(1)}, bf16[56,768]{1,0:T(8,128)(2,1)S(1)}, u32[]{:S(2)}, u32[]{:S(2)}) %collective-permute-start.15) | collective-permute-done | bytes 86048 | tf_op jit(solution)/shard_map/ppermute | solution.py:43
  54.4 1.5 collective-permute-start.26
  56.0 1.5 collective-permute-start.25
  60.5 10.4 %shard_map.281 = (bf16[256,384]{1,0:T(8,128)(2,1)S(1)}, bf16[256,384]{1,0:T(8,128)(2,1)S(1)}, bf16[512,384]{1,0:T(8,128)(2,1)S(1)}, bf16[512,384]{1,0:T(8,128)(2...) custom-call(s32[2]{0:T(128)S(1)} %copy-done.10, ...), custom_call_target="tpu_custom_call" | custom-call | flops 1711276032 | bytes 12000000 | tf_op jit(solution)/shard_map/pallas_call | solution.py:108
  73.4 4.3 %collective-permute-done.27.refs_2_.refs_4_.refs_3_ = bf16[8,32,768]{2,1,0:T(8,128)(2,1)S(1)} collective-permute-done((bf16[8,32,768]{2,1,0:T(8,128)(2,1)S(1)}, bf16[8,32,768]{2,1,0:T(8,128)(2,1)S(1)}, u32[]{:S(2)}, u32[]{:S(2)}) %collective-permute-start.27) | collective-permute-done | bytes 393248 | tf_op jit(solution)/shard_map/ppermute | solution.py:43
  80.3 1.5 collective-permute-start.28
  84.6 1.5 shard_map.285
  87.3 4.9 %collective-permute-done.29.refs_1_ = bf16[2,160,768]{2,1,0:T(8,128)(2,1)S(1)} collective-permute-done((bf16[2,160,768]{2,1,0:T(8,128)(2,1)S(1)}, bf16[2,160,768]{2,1,0:T(8,128)(2,1)S(1)}, u32[]{:S(2)}, u32[]{:S(2)}) %collective-permute-start.29) | collective-permute-done | bytes 491552 | tf_op jit(solution)/shard_map/ppermute | solution.py:39
  93.8 1.7 collective-permute-done.30.got
  95.6 1.9 shard_map.288
  97.6 1.6 collective-permute-done.31.d1
  99.2 1.8 shard_map.289
  101.1 1.5 collective-permute-start.32
  102.5 1.5 collective-permute-start.33
  104.0 1.9 shard_map.290
  105.9 1.9 shard_map.291
  107.8 1.9 shard_map.292
  109.7 6.8 %collective-permute-done.32.refs_1_ = bf16[2,192,768]{2,1,0:T(8,128)(2,1)S(1)} collective-permute-done((bf16[2,192,768]{2,1,0:T(8,128)(2,1)S(1)}, bf16[2,192,768]{2,1,0:T(8,128)(2,1)S(1)}, u32[]{:S(2)}, u32[]{:S(2)}) %collective-permute-start.32) | collective-permute-done | bytes 589856 | tf_op jit(solution)/shard_map/ppermute | solution.py:39
  117.6 1.7 collective-permute-done.34.got
  120.8 1.5 collective-permute-start.37
  122.9 9.3 %shard_map.294 = (bf16[4,96,768]{2,1,0:T(8,128)(2,1)}, bf16[4,96,768]{2,1,0:T(8,128)(2,1)}, bf16[4,96,768]{2,1,0:T(8,128)(2,1)}, bf16[2,96,768]{2,1,0:T(8,128)(2...) custom-call(bf16[256,768]{1,0:T(8,128)(2,1)S(1)} %get-tuple-element.2, ...), custom_call_target="tpu_custom_call" | custom-call | flops 1000 | bytes 1000 | tf_op jit(solution)/shard_map/pallas_call | solution.py:108
  132.5 19.2 %all_to_all.5 = f32[32,8,128]{2,1,0:T(8,128)S(1)} all-to-all(f32[32,8,128]{2,1,0:T(8,128)S(1)} %shard_map.295), channel_id=1, replica_groups=mesh['batch'=8,'head'=4] {'batch','head'}, dimensions={0} | all-to-all | bytes 262144 | tf_op jit(solution)/shard_map/all_to_all | solution.py:1000
  154.7 1.4 collective-permute-start.41
  156.2 1.7 collective-permute-start.42
  159.2 3.0 %collective-permute-done.41.refs_0_ = bf16[96,768]{1,0:T(8,128)(2,1)S(1)} collective-permute-done((bf16[96,768]{1,0:T(8,128)(2,1)}, bf16[96,768]{1,0:T(8,128)(2,1)S(1)}, u32[]{:S(2)}, u32[]{:S(2)}) %collective-permute-start.41) | collective-permute-done | bytes 147488 | tf_op jit(solution)/shard_map/ppermute | solution.py:43
  162.2 7.7 %collective-permute-done.42.refs_1_ = bf16[96,768]{1,0:T(8,128)(2,1)S(1)} collective-permute-done((bf16[96,768]{1,0:T(8,128)(2,1)}, bf16[96,768]{1,0:T(8,128)(2,1)S(1)}, u32[]{:S(2)}, u32[]{:S(2)}) %collective-permute-start.42) | collective-permute-done | bytes 147488 | tf_op jit(solution)/shard_map/ppermute | solution.py:43
  173.9 2.5 %collective-permute-start.46 = (bf16[96,768]{1,0:T(8,128)(2,1)}, bf16[96,768]{1,0:T(8,128)(2,1)S(1)}, u32[]{:S(2)}, u32[]{:S(2)}) collective-permute-start(bf16[96,768]{1,0:T(8,128)(2,1)} %get-tuple-element.263), channel_id=1, source_target_pairs={{0,8},{4,12},{8,0},{12,4},{16,24},{20,28},{24,16},{28,20},{1,9},{5... | collective-permute-start | bytes 442376 | tf_op jit(solution)/shard_map/ppermute | solution.py:43
  176.6 2.3 %collective-permute-start.48 = (bf16[96,768]{1,0:T(8,128)(2,1)S(1)}, bf16[96,768]{1,0:T(8,128)(2,1)S(1)}, u32[]{:S(2)}, u32[]{:S(2)}) collective-permute-start(bf16[96,768]{1,0:T(8,128)(2,1)S(1)} %copy-done.23), channel_id=1, source_target_pairs={{0,24},{4,28},{8,16},{12,20},{16,8},{20,12},{24,0},{28,4},{1,25},{... | collective-permute-start | bytes 442376 | tf_op jit(solution)/shard_map/ppermute | solution.py:43
  178.8 2.0 add_convert_fusion
  181.0 7.7 %collective-permute-done.47.refs_4_ = bf16[96,768]{1,0:T(8,128)(2,1)S(1)} collective-permute-done((bf16[96,768]{1,0:T(8,128)(2,1)}, bf16[96,768]{1,0:T(8,128)(2,1)S(1)}, u32[]{:S(2)}, u32[]{:S(2)}) %collective-permute-start.47) | collective-permute-done | bytes 147488 | tf_op jit(solution)/shard_map/ppermute | solution.py:43
  189.7 2.7 %collective-permute-start.49 = (bf16[96,768]{1,0:T(8,128)(2,1)}, bf16[96,768]{1,0:T(8,128)(2,1)S(1)}, u32[]{:S(2)}, u32[]{:S(2)}) collective-permute-start(bf16[96,768]{1,0:T(8,128)(2,1)} %get-tuple-element.270), channel_id=1, source_target_pairs={{0,8},{4,12},{8,0},{12,4},{16,24},{20,28},{24,16},{28,20},{1,9},{5... | collective-permute-start | bytes 442376 | tf_op jit(solution)/shard_map/ppermute | solution.py:43
  192.4 2.4 %collective-permute-start.51 = (bf16[96,768]{1,0:T(8,128)(2,1)}, bf16[96,768]{1,0:T(8,128)(2,1)S(1)}, u32[]{:S(2)}, u32[]{:S(2)}) collective-permute-start(bf16[96,768]{1,0:T(8,128)(2,1)} %get-tuple-element.272), channel_id=1, source_target_pairs={{0,24},{4,28},{8,16},{12,20},{16,8},{20,12},{24,0},{28,4},{1,25},{... | collective-permute-start | bytes 442376 | tf_op jit(solution)/shard_map/ppermute | solution.py:43
  197.0 8.0 %collective-permute-done.50.two = bf16[96,768]{1,0:T(8,128)(2,1)S(1)} collective-permute-done((bf16[96,768]{1,0:T(8,128)(2,1)}, bf16[96,768]{1,0:T(8,128)(2,1)S(1)}, u32[]{:S(2)}, u32[]{:S(2)}) %collective-permute-start.50) | collective-permute-done | bytes 147488 | tf_op jit(solution)/shard_map/ppermute | solution.py:43
  (150 shorter events, 38.0 us)
Async XLA Ops:
  3.3 7.6 %collective-permute-start = (bf16[104,768]{1,0:T(8,128)(2,1)S(1)}, bf16[104,768]{1,0:T(8,128)(2,1)S(1)}, u32[]{:S(2)}, u32[]{:S(2)}) collective-permute-start(bf16[104,768]{1,0:T(8,128)(2,1)S(1)} %get-tuple-element.148), channel_id=1, source_target_pairs={{0,8},{4,12},{8,0},{12,4},{16,24},{20,28},{24,16},{28,20},{1,9},{5... | collective-permute-start | bytes 479240 | tf_op jit(solution)/shard_map/ppermute | solution.py:43
  6.4 11.6 %collective-permute-start.2 = (bf16[104,768]{1,0:T(8,128)(2,1)S(1)}, bf16[104,768]{1,0:T(8,128)(2,1)S(1)}, u32[]{:S(2)}, u32[]{:S(2)}) collective-permute-start(bf16[104,768]{1,0:T(8,128)(2,1)S(1)} %get-tuple-element.148), channel_id=1, source_target_pairs={{0,24},{4,28},{8,16},{12,20},{16,8},{20,12},{24,0},{28,4},{1,25},{... | collective-permute-start | bytes 479240 | tf_op jit(solution)/shard_map/ppermute | solution.py:43
  8.9 14.2 %collective-permute-start.1 = (bf16[104,768]{1,0:T(8,128)(2,1)S(1)}, bf16[104,768]{1,0:T(8,128)(2,1)S(1)}, u32[]{:S(2)}, u32[]{:S(2)}) collective-permute-start(bf16[104,768]{1,0:T(8,128)(2,1)S(1)} %get-tuple-element.148), channel_id=1, source_target_pairs={{0,16},{4,20},{8,24},{12,28},{16,0},{20,4},{24,8},{28,12},{1,17},{... | collective-permute-start | bytes 479240 | tf_op jit(solution)/shard_map/ppermute | solution.py:43
  10.9 4.1 %collective-permute-start.4 = (bf16[32,768]{1,0:T(8,128)(2,1)S(1)}, bf16[32,768]{1,0:T(8,128)(2,1)S(1)}, u32[]{:S(2)}, u32[]{:S(2)}) collective-permute-start(bf16[32,768]{1,0:T(8,128)(2,1)S(1)} %get-tuple-element.150), channel_id=1, source_target_pairs={{0,4},{4,0},{8,12},{12,8},{16,20},{20,16},{24,28},{28,24},{1,5},{5... | collective-permute-start | bytes 147464 | tf_op jit(solution)/shard_map/ppermute | solution.py:39
  12.4 4.1 %collective-permute-start.3 = (bf16[32,768]{1,0:T(8,128)(2,1)S(1)}, bf16[32,768]{1,0:T(8,128)(2,1)S(1)}, u32[]{:S(2)}, u32[]{:S(2)}) collective-permute-start(bf16[32,768]{1,0:T(8,128)(2,1)S(1)} %get-tuple-element.150), channel_id=1, source_target_pairs={{0,2},{1,3},{2,0},{3,1},{4,6},{5,7},{6,4},{7,5},{8,10},{9,11},{10,... | collective-permute-start | bytes 147464 | tf_op jit(solution)/shard_map/ppermute | solution.py:35
  13.9 9.3 %collective-permute-start.7 = (bf16[256,768]{1,0:T(8,128)(2,1)}, bf16[256,768]{1,0:T(8,128)(2,1)S(1)}, u32[]{:S(2)}, u32[]{:S(2)}) collective-permute-start(bf16[256,768]{1,0:T(8,128)(2,1)} %refs_6_.1), channel_id=1, source_target_pairs={{0,1},{1,0},{2,3},{3,2},{4,5},{5,4},{6,7},{7,6},{8,9},{9,8},{10,11... | collective-permute-start | bytes 1179656 | tf_op jit(solution)/shard_map/ppermute | solution.py:31
  15.0 8.2 %collective-permute-start.5 = (bf16[16,768]{1,0:T(8,128)(2,1)S(1)}, bf16[16,768]{1,0:T(8,128)(2,1)S(1)}, u32[]{:S(2)}, u32[]{:S(2)}) collective-permute-start(bf16[16,768]{1,0:T(8,128)(2,1)S(1)} %slice.129), channel_id=1, source_target_pairs={{0,2},{1,3},{2,0},{3,1},{4,6},{5,7},{6,4},{7,5},{8,10},{9,11},{10,... | collective-permute-start | bytes 73736 | tf_op jit(solution)/shard_map/ppermute | solution.py:35
  16.5 6.7 %collective-permute-start.6 = (bf16[16,768]{1,0:T(8,128)(2,1)S(1)}, bf16[16,768]{1,0:T(8,128)(2,1)S(1)}, u32[]{:S(2)}, u32[]{:S(2)}) collective-permute-start(bf16[16,768]{1,0:T(8,128)(2,1)S(1)} %slice.130), channel_id=1, source_target_pairs={{0,4},{4,0},{8,12},{12,8},{16,20},{20,16},{24,28},{28,24},{1,5},{5... | collective-permute-start | bytes 73736 | tf_op jit(solution)/shard_map/ppermute | solution.py:39
  23.3 17.9 %collective-permute-start.9 = (bf16[4,104,768]{2,1,0:T(8,128)(2,1)S(1)}, bf16[4,104,768]{2,1,0:T(8,128)(2,1)S(1)}, u32[]{:S(2)}, u32[]{:S(2)}) collective-permute-start(bf16[4,104,768]{2,1,0:T(8,128)(2,1)S(1)} %pad_maximum_fusion.1.refs_0_), channel_id=1, source_target_pairs={{0,4},{4,0},{8,12},{12,8},{16,20},{20,16},{24,28},{28,24},{1,5},{5... | collective-permute-start | bytes 1916936 | tf_op jit(solution)/shard_map/ppermute | solution.py:39
  24.9 16.3 %collective-permute-start.8 = (bf16[4,104,768]{2,1,0:T(8,128)(2,1)S(1)}, bf16[4,104,768]{2,1,0:T(8,128)(2,1)S(1)}, u32[]{:S(2)}, u32[]{:S(2)}) collective-permute-start(bf16[4,104,768]{2,1,0:T(8,128)(2,1)S(1)} %pad_maximum_fusion.1.refs_0_), channel_id=1, source_target_pairs={{0,2},{1,3},{2,0},{3,1},{4,6},{5,7},{6,4},{7,5},{8,10},{9,11},{10,... | collective-permute-start | bytes 1916936 | tf_op jit(solution)/shard_map/ppermute | solution.py:35
  26.3 8.8 %collective-permute-start.12 = (bf16[104,768]{1,0:T(8,128)(2,1)S(1)}, bf16[104,768]{1,0:T(8,128)(2,1)S(1)}, u32[]{:S(2)}, u32[]{:S(2)}) collective-permute-start(bf16[104,768]{1,0:T(8,128)(2,1)S(1)} %get-tuple-element.159), channel_id=1, source_target_pairs={{0,24},{4,28},{8,16},{12,20},{16,8},{20,12},{24,0},{28,4},{1,25},{... | collective-permute-start | bytes 479240 | tf_op jit(solution)/shard_map/ppermute | solution.py:43
  29.0 12.1 %collective-permute-start.11 = (bf16[104,768]{1,0:T(8,128)(2,1)S(1)}, bf16[104,768]{1,0:T(8,128)(2,1)S(1)}, u32[]{:S(2)}, u32[]{:S(2)}) collective-permute-start(bf16[104,768]{1,0:T(8,128)(2,1)S(1)} %get-tuple-element.159), channel_id=1, source_target_pairs={{0,16},{4,20},{8,24},{12,28},{16,0},{20,4},{24,8},{28,12},{1,17},{... | collective-permute-start | bytes 479240 | tf_op jit(solution)/shard_map/ppermute | solution.py:43
  29.0 12.1 %collective-permute-start.10 = (bf16[104,768]{1,0:T(8,128)(2,1)S(1)}, bf16[104,768]{1,0:T(8,128)(2,1)S(1)}, u32[]{:S(2)}, u32[]{:S(2)}) collective-permute-start(bf16[104,768]{1,0:T(8,128)(2,1)S(1)} %get-tuple-element.159), channel_id=1, source_target_pairs={{0,8},{4,12},{8,0},{12,4},{16,24},{20,28},{24,16},{28,20},{1,9},{5... | collective-permute-start | bytes 479240 | tf_op jit(solution)/shard_map/ppermute | solution.py:43
  41.2 11.5 %collective-permute-start.16 = (bf16[2,104,768]{2,1,0:T(8,128)(2,1)S(1)}, bf16[2,104,768]{2,1,0:T(8,128)(2,1)S(1)}, u32[]{:S(2)}, u32[]{:S(2)}) collective-permute-start(bf16[2,104,768]{2,1,0:T(8,128)(2,1)S(1)} %slice.101), channel_id=1, source_target_pairs={{0,2},{1,3},{2,0},{3,1},{4,6},{5,7},{6,4},{7,5},{8,10},{9,11},{10,... | collective-permute-start | bytes 958472 | tf_op jit(solution)/shard_map/ppermute | solution.py:35
  41.8 10.9 %collective-permute-start.17 = (bf16[2,104,768]{2,1,0:T(8,128)(2,1)S(1)}, bf16[2,104,768]{2,1,0:T(8,128)(2,1)S(1)}, u32[]{:S(2)}, u32[]{:S(2)}) collective-permute-start(bf16[2,104,768]{2,1,0:T(8,128)(2,1)S(1)} %slice.102), channel_id=1, source_target_pairs={{0,4},{4,0},{8,12},{12,8},{16,20},{20,16},{24,28},{28,24},{1,5},{5... | collective-permute-start | bytes 958472 | tf_op jit(solution)/shard_map/ppermute | solution.py:39
  42.3 10.3 %collective-permute-start.13 = (bf16[184,768]{1,0:T(8,128)(2,1)S(1)}, bf16[184,768]{1,0:T(8,128)(2,1)S(1)}, u32[]{:S(2)}, u32[]{:S(2)}) collective-permute-start(bf16[184,768]{1,0:T(8,128)(2,1)S(1)} %pad_maximum_fusion.3), channel_id=1, source_target_pairs={{0,8},{4,12},{8,0},{12,4},{16,24},{20,28},{24,16},{28,20},{1,9},{5... | collective-permute-start | bytes 847880 | tf_op jit(solution)/shard_map/ppermute | solution.py:43
  42.4 10.2 %collective-permute-start.15 = (bf16[56,768]{1,0:T(8,128)(2,1)S(1)}, bf16[56,768]{1,0:T(8,128)(2,1)S(1)}, u32[]{:S(2)}, u32[]{:S(2)}) collective-permute-start(bf16[56,768]{1,0:T(8,128)(2,1)S(1)} %get-tuple-element.163), channel_id=1, source_target_pairs={{0,24},{4,28},{8,16},{12,20},{16,8},{20,12},{24,0},{28,4},{1,25},{... | collective-permute-start | bytes 258056 | tf_op jit(solution)/shard_map/ppermute | solution.py:43
  44.8 7.9 %collective-permute-start.14 = (bf16[56,768]{1,0:T(8,128)(2,1)S(1)}, bf16[56,768]{1,0:T(8,128)(2,1)S(1)}, u32[]{:S(2)}, u32[]{:S(2)}) collective-permute-start(bf16[56,768]{1,0:T(8,128)(2,1)S(1)} %get-tuple-element.163), channel_id=1, source_target_pairs={{0,16},{4,20},{8,24},{12,28},{16,0},{20,4},{24,8},{28,12},{1,17},{... | collective-permute-start | bytes 258056 | tf_op jit(solution)/shard_map/ppermute | solution.py:43
  52.8 3.1 %collective-permute-start.22 = (bf16[2,104,768]{2,1,0:T(8,128)(2,1)S(1)}, bf16[2,104,768]{2,1,0:T(8,128)(2,1)S(1)}, u32[]{:S(2)}, u32[]{:S(2)}) collective-permute-start(bf16[2,104,768]{2,1,0:T(8,128)(2,1)S(1)} %collective-permute-done.17.refs_4_), channel_id=1, source_target_pairs={{0,1},{1,0},{2,3},{3,2},{4,5},{5,4},{6,7},{7,6},{8,9},{9,8},{10,11... | collective-permute-start | bytes 958472 | tf_op jit(solution)/shard_map/ppermute | solution.py:31
  53.4 4.2 %collective-permute-start.18 = (bf16[4,104,768]{2,1,0:T(8,128)(2,1)S(1)}, bf16[4,104,768]{2,1,0:T(8,128)(2,1)S(1)}, u32[]{:S(2)}, u32[]{:S(2)}) collective-permute-start(bf16[4,104,768]{2,1,0:T(8,128)(2,1)S(1)} %pad_maximum_fusion.1.refs_0_), channel_id=1, source_target_pairs={{0,1},{1,0},{2,3},{3,2},{4,5},{5,4},{6,7},{7,6},{8,9},{9,8},{10,11... | collective-permute-start | bytes 1916936 | tf_op jit(solution)/shard_map/ppermute | solution.py:31
  53.5 5.3 %collective-permute-start.19 = (bf16[4,104,768]{2,1,0:T(8,128)(2,1)S(1)}, bf16[4,104,768]{2,1,0:T(8,128)(2,1)S(1)}, u32[]{:S(2)}, u32[]{:S(2)}) collective-permute-start(bf16[4,104,768]{2,1,0:T(8,128)(2,1)S(1)} %collective-permute-done.8.refs_1_), channel_id=1, source_target_pairs={{0,1},{1,0},{2,3},{3,2},{4,5},{5,4},{6,7},{7,6},{8,9},{9,8},{10,11... | collective-permute-start | bytes 1916936 | tf_op jit(solution)/shard_map/ppermute | solution.py:31
  53.9 4.9 %collective-permute-start.20 = (bf16[4,104,768]{2,1,0:T(8,128)(2,1)S(1)}, bf16[4,104,768]{2,1,0:T(8,128)(2,1)S(1)}, u32[]{:S(2)}, u32[]{:S(2)}) collective-permute-start(bf16[4,104,768]{2,1,0:T(8,128)(2,1)S(1)} %collective-permute-done.9.refs_2_), channel_id=1, source_target_pairs={{0,1},{1,0},{2,3},{3,2},{4,5},{5,4},{6,7},{7,6},{8,9},{9,8},{10,11... | collective-permute-start | bytes 1916936 | tf_op jit(solution)/shard_map/ppermute | solution.py:31
  54.4 24.0 %collective-permute-start.26 = (bf16[4,160,768]{2,1,0:T(8,128)(2,1)S(1)}, bf16[4,160,768]{2,1,0:T(8,128)(2,1)S(1)}, u32[]{:S(2)}, u32[]{:S(2)}) collective-permute-start(bf16[4,160,768]{2,1,0:T(8,128)(2,1)S(1)} %pad_maximum_fusion.refs_0_), channel_id=1, source_target_pairs={{0,4},{4,0},{8,12},{12,8},{16,20},{20,16},{24,28},{28,24},{1,5},{5... | collective-permute-start | bytes 2949128 | tf_op jit(solution)/shard_map/ppermute | solution.py:39
  56.0 23.7 %collective-permute-start.25 = (bf16[4,160,768]{2,1,0:T(8,128)(2,1)S(1)}, bf16[4,160,768]{2,1,0:T(8,128)(2,1)S(1)}, u32[]{:S(2)}, u32[]{:S(2)}) collective-permute-start(bf16[4,160,768]{2,1,0:T(8,128)(2,1)S(1)} %pad_maximum_fusion.refs_0_), channel_id=1, source_target_pairs={{0,2},{1,3},{2,0},{3,1},{4,6},{5,7},{6,4},{7,5},{8,10},{9,11},{10,... | collective-permute-start | bytes 2949128 | tf_op jit(solution)/shard_map/ppermute | solution.py:35
  57.5 20.2 %collective-permute-start.27 = (bf16[8,32,768]{2,1,0:T(8,128)(2,1)S(1)}, bf16[8,32,768]{2,1,0:T(8,128)(2,1)S(1)}, u32[]{:S(2)}, u32[]{:S(2)}) collective-permute-start(bf16[8,32,768]{2,1,0:T(8,128)(2,1)S(1)} %pad_maximum_fusion.2), channel_id=1, source_target_pairs={{0,16},{4,20},{8,24},{12,28},{16,0},{20,4},{24,8},{28,12},{1,17},{... | collective-permute-start | bytes 1179656 | tf_op jit(solution)/shard_map/ppermute | solution.py:43
  73.2 8.7 %collective-permute-start.24 = (bf16[256,768]{1,0:T(8,128)(2,1)S(1)}, bf16[256,768]{1,0:T(8,128)(2,1)S(1)}, u32[]{:S(2)}, u32[]{:S(2)}) collective-permute-start(bf16[256,768]{1,0:T(8,128)(2,1)S(1)} %get-tuple-element.178.x0), channel_id=1, source_target_pairs={{0,1},{1,0},{2,3},{3,2},{4,5},{5,4},{6,7},{7,6},{8,9},{9,8},{10,11... | collective-permute-start | bytes 1179656 | tf_op jit(solution)/shard_map/ppermute | solution.py:31
  79.7 12.4 %collective-permute-start.29 = (bf16[2,160,768]{2,1,0:T(8,128)(2,1)S(1)}, bf16[2,160,768]{2,1,0:T(8,128)(2,1)S(1)}, u32[]{:S(2)}, u32[]{:S(2)}) collective-permute-start(bf16[2,160,768]{2,1,0:T(8,128)(2,1)S(1)} %slice.107), channel_id=1, source_target_pairs={{0,4},{4,0},{8,12},{12,8},{16,20},{20,16},{24,28},{28,24},{1,5},{5... | collective-permute-start | bytes 1474568 | tf_op jit(solution)/shard_map/ppermute | solution.py:39
  80.3 12.1 %collective-permute-start.28 = (bf16[2,160,768]{2,1,0:T(8,128)(2,1)S(1)}, bf16[2,160,768]{2,1,0:T(8,128)(2,1)S(1)}, u32[]{:S(2)}, u32[]{:S(2)}) collective-permute-start(bf16[2,160,768]{2,1,0:T(8,128)(2,1)S(1)} %slice.106), channel_id=1, source_target_pairs={{0,2},{1,3},{2,0},{3,1},{4,6},{5,7},{6,4},{7,5},{8,10},{9,11},{10,... | collective-permute-start | bytes 1474568 | tf_op jit(solution)/shard_map/ppermute | solution.py:35
  93.8 1.8 collective-permute-start.30
  101.1 15.4 %collective-permute-start.32 = (bf16[2,192,768]{2,1,0:T(8,128)(2,1)S(1)}, bf16[2,192,768]{2,1,0:T(8,128)(2,1)S(1)}, u32[]{:S(2)}, u32[]{:S(2)}) collective-permute-start(bf16[2,192,768]{2,1,0:T(8,128)(2,1)S(1)} %get-tuple-element.217), channel_id=1, source_target_pairs={{0,4},{4,0},{8,12},{12,8},{16,20},{20,16},{24,28},{28,24},{1,5},{5... | collective-permute-start | bytes 1769480 | tf_op jit(solution)/shard_map/ppermute | solution.py:39
  102.5 15.1 %collective-permute-start.33 = (bf16[2,192,768]{2,1,0:T(8,128)(2,1)S(1)}, bf16[2,192,768]{2,1,0:T(8,128)(2,1)S(1)}, u32[]{:S(2)}, u32[]{:S(2)}) collective-permute-start(bf16[2,192,768]{2,1,0:T(8,128)(2,1)S(1)} %get-tuple-element.219), channel_id=1, source_target_pairs={{0,2},{1,3},{2,0},{3,1},{4,6},{5,7},{6,4},{7,5},{8,10},{9,11},{10,... | collective-permute-start | bytes 1769480 | tf_op jit(solution)/shard_map/ppermute | solution.py:35
  120.6 2.3 %collective-permute-start.35 = (bf16[256,768]{1,0:T(8,128)(2,1)S(1)}, bf16[256,768]{1,0:T(8,128)(2,1)S(1)}, u32[]{:S(2)}, u32[]{:S(2)}) collective-permute-start(bf16[256,768]{1,0:T(8,128)(2,1)S(1)} %get-tuple-element.224.a0), channel_id=1, source_target_pairs={{0,1},{1,0},{2,3},{3,2},{4,5},{5,4},{6,7},{7,6},{8,9},{9,8},{10,11... | collective-permute-start | bytes 1179656 | tf_op jit(solution)/shard_map/ppermute | solution.py:31
  120.8 30.9 %collective-permute-start.37 = (bf16[4,192,768]{2,1,0:T(8,128)(2,1)S(1)}, bf16[4,192,768]{2,1,0:T(8,128)(2,1)S(1)}, u32[]{:S(2)}, u32[]{:S(2)}) collective-permute-start(bf16[4,192,768]{2,1,0:T(8,128)(2,1)S(1)} %get-tuple-element.238), channel_id=1, source_target_pairs={{0,2},{1,3},{2,0},{3,1},{4,6},{5,7},{6,4},{7,5},{8,10},{9,11},{10,... | collective-permute-start | bytes 3538952 | tf_op jit(solution)/shard_map/ppermute | solution.py:35
  122.3 29.4 %collective-permute-start.38 = (bf16[4,192,768]{2,1,0:T(8,128)(2,1)S(1)}, bf16[4,192,768]{2,1,0:T(8,128)(2,1)S(1)}, u32[]{:S(2)}, u32[]{:S(2)}) collective-permute-start(bf16[4,192,768]{2,1,0:T(8,128)(2,1)S(1)} %get-tuple-element.239), channel_id=1, source_target_pairs={{0,4},{4,0},{8,12},{12,8},{16,20},{20,16},{24,28},{28,24},{1,5},{5... | collective-permute-start | bytes 3538952 | tf_op jit(solution)/shard_map/ppermute | solution.py:39
  132.3 19.4 %collective-permute-start.36 = (f32[256,768]{1,0:T(8,128)S(1)}, f32[256,768]{1,0:T(8,128)S(1)}, u32[]{:S(2)}, u32[]{:S(2)}) collective-permute-start(f32[256,768]{1,0:T(8,128)S(1)} %get-tuple-element.232), channel_id=1, source_target_pairs={{0,1},{1,0},{2,3},{3,2},{4,5},{5,4},{6,7},{7,6},{8,9},{9,8},{10,11... | collective-permute-start | bytes 2359304 | tf_op jit(solution)/shard_map/ppermute | solution.py:31
  151.7 18.1 %collective-permute-start.39 = (bf16[2,96,768]{2,1,0:T(8,128)(2,1)}, bf16[2,96,768]{2,1,0:T(8,128)(2,1)S(1)}, u32[]{:S(2)}, u32[]{:S(2)}) collective-permute-start(bf16[2,96,768]{2,1,0:T(8,128)(2,1)} %get-tuple-element.247), channel_id=1, source_target_pairs={{0,2},{1,3},{2,0},{3,1},{4,6},{5,7},{6,4},{7,5},{8,10},{9,11},{10,... | collective-permute-start | bytes 884744 | tf_op jit(solution)/shard_map/ppermute | solution.py:35
  152.3 17.5 %collective-permute-start.40 = (bf16[2,96,768]{2,1,0:T(8,128)(2,1)}, bf16[2,96,768]{2,1,0:T(8,128)(2,1)S(1)}, u32[]{:S(2)}, u32[]{:S(2)}) collective-permute-start(bf16[2,96,768]{2,1,0:T(8,128)(2,1)} %get-tuple-element.248), channel_id=1, source_target_pairs={{0,4},{4,0},{8,12},{12,8},{16,20},{20,16},{24,28},{28,24},{1,5},{5... | collective-permute-start | bytes 884744 | tf_op jit(solution)/shard_map/ppermute | solution.py:39
  154.7 7.4 %collective-permute-start.41 = (bf16[96,768]{1,0:T(8,128)(2,1)}, bf16[96,768]{1,0:T(8,128)(2,1)S(1)}, u32[]{:S(2)}, u32[]{:S(2)}) collective-permute-start(bf16[96,768]{1,0:T(8,128)(2,1)} %get-tuple-element.249), channel_id=1, source_target_pairs={{0,8},{4,12},{8,0},{12,4},{16,24},{20,28},{24,16},{28,20},{1,9},{5... | collective-permute-start | bytes 442376 | tf_op jit(solution)/shard_map/ppermute | solution.py:43
  156.2 13.7 %collective-permute-start.42 = (bf16[96,768]{1,0:T(8,128)(2,1)}, bf16[96,768]{1,0:T(8,128)(2,1)S(1)}, u32[]{:S(2)}, u32[]{:S(2)}) collective-permute-start(bf16[96,768]{1,0:T(8,128)(2,1)} %get-tuple-element.250), channel_id=1, source_target_pairs={{0,16},{4,20},{8,24},{12,28},{16,0},{20,4},{24,8},{28,12},{1,17},{... | collective-permute-start | bytes 442376 | tf_op jit(solution)/shard_map/ppermute | solution.py:43
  157.9 12.0 %collective-permute-start.43 = (bf16[96,768]{1,0:T(8,128)(2,1)}, bf16[96,768]{1,0:T(8,128)(2,1)S(1)}, u32[]{:S(2)}, u32[]{:S(2)}) collective-permute-start(bf16[96,768]{1,0:T(8,128)(2,1)} %get-tuple-element.251), channel_id=1, source_target_pairs={{0,24},{4,28},{8,16},{12,20},{16,8},{20,12},{24,0},{28,4},{1,25},{... | collective-permute-start | bytes 442376 | tf_op jit(solution)/shard_map/ppermute | solution.py:43
  171.0 17.7 %collective-permute-start.44 = (bf16[4,96,768]{2,1,0:T(8,128)(2,1)}, bf16[4,96,768]{2,1,0:T(8,128)(2,1)S(1)}, u32[]{:S(2)}, u32[]{:S(2)}) collective-permute-start(bf16[4,96,768]{2,1,0:T(8,128)(2,1)} %get-tuple-element.255), channel_id=1, source_target_pairs={{0,2},{1,3},{2,0},{3,1},{4,6},{5,7},{6,4},{7,5},{8,10},{9,11},{10,... | collective-permute-start | bytes 1769480 | tf_op jit(solution)/shard_map/ppermute | solution.py:35
  172.0 16.7 %collective-permute-start.45 = (bf16[4,96,768]{2,1,0:T(8,128)(2,1)}, bf16[4,96,768]{2,1,0:T(8,128)(2,1)S(1)}, u32[]{:S(2)}, u32[]{:S(2)}) collective-permute-start(bf16[4,96,768]{2,1,0:T(8,128)(2,1)} %get-tuple-element.256), channel_id=1, source_target_pairs={{0,4},{4,0},{8,12},{12,8},{16,20},{20,16},{24,28},{28,24},{1,5},{5... | collective-permute-start | bytes 1769480 | tf_op jit(solution)/shard_map/ppermute | solution.py:39
  173.9 7.1 %collective-permute-start.46 = (bf16[96,768]{1,0:T(8,128)(2,1)}, bf16[96,768]{1,0:T(8,128)(2,1)S(1)}, u32[]{:S(2)}, u32[]{:S(2)}) collective-permute-start(bf16[96,768]{1,0:T(8,128)(2,1)} %get-tuple-element.263), channel_id=1, source_target_pairs={{0,8},{4,12},{8,0},{12,4},{16,24},{20,28},{24,16},{28,20},{1,9},{5... | collective-permute-start | bytes 442376 | tf_op jit(solution)/shard_map/ppermute | solution.py:43
  176.4 12.3 %collective-permute-start.47 = (bf16[96,768]{1,0:T(8,128)(2,1)}, bf16[96,768]{1,0:T(8,128)(2,1)S(1)}, u32[]{:S(2)}, u32[]{:S(2)}) collective-permute-start(bf16[96,768]{1,0:T(8,128)(2,1)} %get-tuple-element.264), channel_id=1, source_target_pairs={{0,16},{4,20},{8,24},{12,28},{16,0},{20,4},{24,8},{28,12},{1,17},{... | collective-permute-start | bytes 442376 | tf_op jit(solution)/shard_map/ppermute | solution.py:43
  176.6 12.1 %collective-permute-start.48 = (bf16[96,768]{1,0:T(8,128)(2,1)S(1)}, bf16[96,768]{1,0:T(8,128)(2,1)S(1)}, u32[]{:S(2)}, u32[]{:S(2)}) collective-permute-start(bf16[96,768]{1,0:T(8,128)(2,1)S(1)} %copy-done.23), channel_id=1, source_target_pairs={{0,24},{4,28},{8,16},{12,20},{16,8},{20,12},{24,0},{28,4},{1,25},{... | collective-permute-start | bytes 442376 | tf_op jit(solution)/shard_map/ppermute | solution.py:43
  189.7 7.3 %collective-permute-start.49 = (bf16[96,768]{1,0:T(8,128)(2,1)}, bf16[96,768]{1,0:T(8,128)(2,1)S(1)}, u32[]{:S(2)}, u32[]{:S(2)}) collective-permute-start(bf16[96,768]{1,0:T(8,128)(2,1)} %get-tuple-element.270), channel_id=1, source_target_pairs={{0,8},{4,12},{8,0},{12,4},{16,24},{20,28},{24,16},{28,20},{1,9},{5... | collective-permute-start | bytes 442376 | tf_op jit(solution)/shard_map/ppermute | solution.py:43
  192.4 12.6 %collective-permute-start.50 = (bf16[96,768]{1,0:T(8,128)(2,1)}, bf16[96,768]{1,0:T(8,128)(2,1)S(1)}, u32[]{:S(2)}, u32[]{:S(2)}) collective-permute-start(bf16[96,768]{1,0:T(8,128)(2,1)} %get-tuple-element.271), channel_id=1, source_target_pairs={{0,16},{4,20},{8,24},{12,28},{16,0},{20,4},{24,8},{28,12},{1,17},{... | collective-permute-start | bytes 442376 | tf_op jit(solution)/shard_map/ppermute | solution.py:43
  192.4 12.6 %collective-permute-start.51 = (bf16[96,768]{1,0:T(8,128)(2,1)}, bf16[96,768]{1,0:T(8,128)(2,1)S(1)}, u32[]{:S(2)}, u32[]{:S(2)}) collective-permute-start(bf16[96,768]{1,0:T(8,128)(2,1)} %get-tuple-element.272), channel_id=1, source_target_pairs={{0,24},{4,28},{8,16},{12,20},{16,8},{20,12},{24,0},{28,4},{1,25},{... | collective-permute-start | bytes 442376 | tf_op jit(solution)/shard_map/ppermute | solution.py:43
  (28 other events, 257.8 us)

commit v5 on v4

--- a/solution.py
+++ b/solution.py
@@ -141,52 +141,116 @@
     return jax.ShapeDtypeStruct(dims, dtype)
 
 
-def add_moved_kernel(x, for_x, y, for_y, x_out, y_out):
-    y_out[0:2] = add_low(y[0:2], for_y[...])
-    y_out[2:4] = y[2:4]
-    x_out[0:2] = x[0:2]
-    x_out[2:4] = add_low(x[2:4], for_x[...])
-
-
-def add_moved(x, for_x, y, for_y):
-    return call(
-        add_moved_kernel,
-        (shape(x.shape), shape(y.shape)),
-        (x, for_x, y, for_y),
-        cost=est(1000, 1000),
-        limit=8,
-    )
-
-
-def combine_kernel(parts, z, x, y, *refs):
-    outs, (mine, low, sems) = refs[: 1 + 3 * parts], refs[1 + 3 * parts :]
-    copies = Copies(sems)
-    rows = z.shape[1] // parts
-    for k in (1, 2, 3, 0):
+def add_first_kernel(x_up, x_down, for_x, y_up, y_down, for_y, *outs):
+    half = x_up.shape[1]
+    for i, (x, y) in enumerate(((x_up, y_up), (x_down, y_down))):
+        rows = slice(half * i, half * i + half)
+        x_out, y_out = outs[2 * i : 2 * i + 2]
+        x_out[0:2] = x[0:2]
+        y_out[2:4] = y[2:4]
+        for k in range(2):
+            x_out[2 + k] = add_low(x[2 + k], for_x[k, rows])
+            y_out[k] = add_low(y[k], for_y[k, rows])
+
+
+def combine_kernel(z, x, y, *refs):
+    outs, (mine, low, sems) = refs[:4], refs[4:]
+    sum_places(z, x, y, outs, mine, low, Copies(sems)).wait()
+
+
+def sum_places(z, x, y, outs, mine, low, copies, arrived=None):
+    for i, k in enumerate((1, 2, 3, 0)):
+        if arrived:
+            copies.wait(*arrived[i])
         total = z[k].astype(F32) + x[k].astype(F32) + y[k].astype(F32)
         if k == 0:
             mine[...] = total
             copies.start(mine, outs[0])
         else:
             low[k - 1] = total.astype(BF16)
-            for i in range(parts):
-                copies.start(low.at[k - 1, pl.ds(rows * i, rows)], outs[1 + 3 * i + k - 1])
-    copies.wait()
-
-
-def combine(z, x, y, parts):
+            copies.start(low.at[k - 1], outs[k])
+    return copies
+
+
+def combine(z, x, y):
     rows = z.shape[1]
     mine, *others = call(
-        functools.partial(combine_kernel, parts),
-        (shape((rows, D), F32),) + (shape((rows // parts, D)),) * (3 * parts),
+        combine_kernel,
+        (shape((rows, D), F32),) + (shape((rows, D)),) * 3,
         (z, x, y),
         scratch=[pltpu.VMEM((rows, D), F32), pltpu.VMEM((3, rows, D), BF16)],
         cost=est(1000, 1000),
         limit=8,
-        far_out=range(1 + 3 * parts),
-        sems=1 + 3 * parts,
-    )
-    return mine, [others[3 * i : 3 * i + 3] for i in range(parts)]
+        far_out=range(4),
+        sems=4,
+    )
+    return mine, others
+
+
+def combine_last_kernel(z, x, y, mine, *refs):
+    outs, (low, sems) = refs[:3], refs[3:]
+    copies = Copies(sems)
+    for k in (1, 2, 3, 0):
+        total = z[k].astype(F32) + x[k].astype(F32) + y[k].astype(F32)
+        if k == 0:
+            mine[...] = total
+        else:
+            low[k - 1] = total.astype(BF16)
+            copies.start(low.at[k - 1], outs[k - 1])
+    copies.wait()
+
+
+def combine_last(z, x, y):
+    rows = z.shape[1]
+    mine, *others = call(
+        combine_last_kernel,
+        (shape((rows, D), F32),) + (shape((rows, D)),) * 3,
+        (z, x, y),
+        scratch=[pltpu.VMEM((3, rows, D), BF16)],
+        cost=est(1000, 1000),
+        limit=8,
+        far_out=range(1, 4),
+        sems=3,
+    )
+    return mine, others
+
+
+def turn_kernel(x, y, z, by_x_far, by_y_far, x_out, y_out, *refs):
+    outs, (by_x, by_y, mine, low, sems) = refs[:4], refs[4:]
+    copies = Copies(sems)
+    arrived = []
+    for k in (1, 2, 3, 0, 4):
+        rows = pl.ds(k, 1 if k < 4 else 2)
+        arrived.append(
+            (
+                copies.start(by_x_far.at[rows], by_x.at[rows]),
+                copies.start(by_y_far.at[rows], by_y.at[rows]),
+            )
+        )
+    sum_places(z, by_x, by_y, outs, mine, low, copies, arrived)
+    copies.wait(*arrived[4])
+    y_out[0:2] = add_low(y[0:2], by_x[4:6])
+    y_out[2:4] = y[2:4]
+    x_out[0:2] = x[0:2]
+    x_out[2:4] = add_low(x[2:4], by_y[4:6])
+    copies.wait()
+
+
+def turn(x, y, z, by_x, by_y):
+    rows = z.shape[1]
+    x, y, mine, *others = call(
+        turn_kernel,
+        (shape(x.shape), shape(y.shape), shape((rows, D), F32)) + (shape((rows, D)),) * 3,
+        (x, y, z, by_x, by_y),
+        scratch=[pltpu.VMEM(by_x.shape, BF16)] * 2
+        + [pltpu.VMEM((rows, D), F32), pltpu.VMEM((3, rows, D), BF16)],
+        cost=est(1000, 1000),
+        limit=8,
+        far_in=(3, 4),
+        far_out=range(2, 6),
+        sems=14,
+    )
+    return (x, y), mine, others
 
 
 def total_of(refs):
@@ -209,22 +273,21 @@
         (shape((rows, 576), F32), shape((192, rows), F32)),
         tuple(parts),
         cost=est(8 * rows * D, 16 * rows * D),
-    )
-
-
-def finish_ffn_kernel(mine, *refs):
-    ups, downs, (up, down) = refs[:3], refs[3:6], refs[6:]
-    half = mine.shape[0] // 2
-    up[...] = mine[0:half] + sum(r[...].astype(F32) for r in ups)
-    down[...] = mine[half:] + sum(r[...].astype(F32) for r in downs)
-
-
-def finish_ffn(mine, ups, downs):
-    half = mine.shape[0] // 2
+        limit=8,
+    )
+
+
+def finish_ffn_kernel(*refs):
+    up, down = refs[8:]
+    up[...], down[...] = total_of(refs[0:4]), total_of(refs[4:8])
+
+
+def finish_ffn(ups, downs):
+    dims = ups[0].shape
     return call(
         finish_ffn_kernel,
-        (shape((half, D), F32), shape((half, D), F32)),
-        (mine, *ups, *downs),
+        (shape(dims, F32), shape(dims, F32)),
+        (*ups, *downs),
         cost=est(1000, 1000),
         limit=8,
     )
@@ -259,17 +322,22 @@
     return a + bit - 2 * a * bit
 
 
-def pack_kernel(qkv_in, proj_in, up_in, down_in, bias, vectors, a_out, one_a, one_b, two, a, p, f, sems):
+def pack_kernel(qkv_in, proj_in, up_in, down_in, bias_in, *refs):
+    vectors_in, (a_out, one_a, one_b, two, a, p, f, bias, vectors, sems) = refs[:8], refs[8:]
     rows_q, rows_p, half = qkv_in.shape[0], proj_in.shape[0], down_in.shape[0]
     copies = Copies(sems)
     copies.start(qkv_in, a.at[pl.ds(0, rows_q)])
     copies.start(proj_in, p)
     copies.start(up_in, f.at[pl.ds(0, half)])
     copies.start(down_in, f.at[pl.ds(half, half)])
-    width = vectors.shape[1]
+    copies.start(bias_in, bias)
+    for i, r in enumerate(vectors_in):
+        copies.start(r, vectors.at[i])
+    width = vectors.shape[2]
     b, h = lax.axis_index("batch"), lax.axis_index("head")
     me = b * lax.axis_size("head") + h
-    v = vectors[...].astype(F32)
+    copies.wait()
+    v = jnp.concatenate([vectors[i] for i in range(8)]).astype(F32)
     v = jnp.concatenate([v] * (D // width), 1)
     lane = lax.broadcasted_iota(jnp.int32, (8, D), 1)
     mine = jnp.logical_and(lane >= me * width, lane < me * width + width)
@@ -281,7 +349,6 @@
     late = jnp.concatenate([row, gap, none], 1)
     extra = jnp.where(me < lax.axis_size("batch") * lax.axis_size("head") // 2, early, late)
     v = v + jnp.concatenate([extra, jnp.zeros((7, D), F32)])
-    copies.wait()
     a_out[0:rows_q] = a[0:rows_q]
     q = p[...]
     a_out[rows_q : rows_q + rows_p] = jnp.concatenate(
@@ -303,16 +370,18 @@
             shape((2 * ONE - FIRST, D)),
             shape((2 * TWO, D)),
         ),
-        (qkv, proj, up, down, bias[None], jnp.stack(vectors)),
+        (qkv, proj, up, down, bias[None], *[v[None] for v in vectors]),
         scratch=[
             pltpu.VMEM((rows, D), BF16),
             pltpu.VMEM(proj.shape, BF16),
             pltpu.VMEM((2 * half, D), BF16),
+            pltpu.VMEM((1,) + bias.shape, BF16),
+            pltpu.VMEM((8, 1) + vectors[0].shape, BF16),
         ],
         cost=est(1000, 1000),
         limit=8,
-        far_in=(0, 1, 2, 3),
-        sems=4,
+        far_in=range(13),
+        sems=13,
     )
 
 
@@ -660,8 +729,8 @@
         return
     rows = ONE + TWO
     for k in range(4):
-        out, i = (outs[0], k) if len(outs) == 1 else (outs[k // 2], k % 2)
-        for at, g in ((0, ug), (rows, dg)):
+        for e, g in enumerate((ug, dg)):
+            out, i, at = (outs[k // 2], k % 2, rows * e) if spot == 3 else (outs[e], k, 0)
             out[i, at : at + ONE] = g[ONE * k : ONE * k + ONE]
             low = 4 * ONE + TWO * k
             out[i, at + ONE : at + rows] = g[low : low + TWO]
@@ -673,7 +742,8 @@
         outs, width = [shape(w.shape) for w in weights], weights[0].shape[0]
     else:
         width = 4 * (ONE + TWO)
-        outs = [shape((2, width // 2, D))] * 2 if spot == 3 else [shape((4, width // 2, D))]
+        rows = ONE + TWO
+        outs = [shape((2, 2 * rows, D)) if spot == 3 else shape((4, rows, D))] * 2
     *grads, ub, s0, s1 = call(
         functools.partial(ffn_back_kernel, not sums, spot, count),
         (
@@ -702,12 +772,12 @@
     sums[1:2] = jnp.sum(fc * n, 0, keepdims=True)
     sums[2:3] = jnp.sum(fc, 0, keepdims=True)
     if refs:
-        add_moved_kernel(*refs)
+        add_first_kernel(*refs)
 
 
 def first_back(sum_two, part, got, normal, scale, small, moved=()):
     n = sum_two.shape[0]
-    outs = [shape(moved[0].shape), shape(moved[2].shape)] if moved else []
+    outs = [shape(moved[i].shape) for i in (0, 3, 1, 4)] if moved else []
     *added, sum_one, low, sums = call(
         first_back_kernel,
         (*outs, shape((n, D), F32), shape((n, D)), shape((3, D), F32)),
@@ -719,10 +789,13 @@
 
 
 def attend_back_kernel(sets, a0, a1, *refs):
+    downs, refs = ((), refs) if sets == 1 else (refs[:2], refs[2:])
     far, outs, (in0, in1, sums), refs = refs[:9], refs[9 : 9 + sets], refs[9 + sets : 12 + sets], refs[12 + sets :]
     wp, v, probs, k, q, wr, x0, x1, ctx = far
     dctx, cots, grads, sems = refs
     copies = Copies(sems)
+    for down, out in zip(downs, outs[3:]):
+        copies.start(down, out.at[pl.ds(0, 4)])
     c, z, y, x = place_here()
     half = a0.shape[0]
     n = 2 * half
@@ -786,31 +859,31 @@
             for kz in range(4):
                 zi = flip(lax.rem(z, 2), kz % 2) + 2 * flip(lax.div(z, 2), kz // 2)
                 at = pl.multiple_of((2 * zi + yi) * rows, rows)
-                dst = outs[spot].at[kz] if spot < 3 else outs[3 + kz // 2].at[kz % 2]
+                dst = outs[spot].at[kz] if spot < 3 else outs[3 + kz // 2].at[4 + kz % 2]
                 copies.start(grads.at[g, pl.ds(at, rows)], dst)
     copies.wait()
 
 
-def attend_back(direct, a0, a1, x0, x1, wp, wr, q, k, v, ctx, probs):
+def attend_back(downs, a0, a1, x0, x1, wp, wr, q, k, v, ctx, probs):
     half = a0.shape[0]
     n = 2 * half
     sets = (shape((2, D, D)),)
-    if direct:
-        sets = (shape((4, 96, D)),) * 3 + (shape((2, 96, D)),) * 2
+    if downs:
+        sets = (shape((4, 96, D)),) * 3 + (shape((6, 96, D)),) * 2
     far = (wp, v, probs, k, q, wr, x0, x1, ctx)
     return call(
         functools.partial(attend_back_kernel, len(sets)),
         (*sets, shape((half, D), F32), shape((half, D), F32), shape((2, D), F32)),
-        (a0, a1, *far),
+        (a0, a1, *downs, *far),
         scratch=[
             pltpu.VMEM((n, 384), BF16),
             pltpu.VMEM((n, 1280), BF16),
             pltpu.VMEM((2, D, D), BF16),
         ],
-        cost=est(1000, 1000),
+        cost=est(8e9, 14e6),
         limit=16,
         far_out=range(len(sets)),
-        sems=17,
+        sems=20,
     )
 
 
@@ -887,9 +960,10 @@
         near, one_b[2], one_b[3], a_d = lax.optimization_barrier((near, one_b[2], one_b[3], a_d))
         one_b[1], two_hi = near[: 2 * ONE - FIRST], near[2 * ONE - FIRST :].reshape(two_lo.shape)
         a_own = [a_z, a_x, a_y, *a_d]
-        a_swapped = [core_swap(v) for v in after(a_own, near)]
         one_z = jnp.stack([jnp.concatenate(pair) for pair in zip(one_a, one_b)])
+        one_z, a_own = lax.optimization_barrier((one_z, a_own))
         one_x, one_y = x_swap(one_z), y_swap(one_z)
+        a_swapped = [core_swap(v) for v in a_own]
         two_far = z_swap(jnp.concatenate([two_lo, two_hi]), 2)
         one_x, one_y, two_far = lax.optimization_barrier((one_x, one_y, two_far))
         one_d = [x_swap(one_y[:2]), y_swap(one_x[2:])]
@@ -950,7 +1024,7 @@
             grads, ub, sums = ffn_back(
                 down_low, down_in, first_low, first_in, spot, weights, both, sums, spot == 0
             )
-            f_parts = grads + f_parts
+            f_parts.append(grads)
             ub_parts.insert(0, ub)
     else:
         for weights, pair in zip(f_all, kept):
@@ -970,14 +1044,15 @@
     part_own, part_other = sums
     moved = ()
     if direct:
-        moved = (f_parts[1], y_swap(f_parts[4]), f_parts[2], x_swap(f_parts[3]))
+        (d_lo, d_hi), y_sets, x_sets, z_sets = f_parts
+        moved = (*x_sets, y_swap(d_hi), *y_sets, x_swap(d_lo))
         part_other = after(part_other, moved)
     added, sum_one, attn_low, sums_one = first_back(
         sum_two, part_own, core_swap(part_other), first_n, first_r, small_all, moved
     )
     attn_in = core_swap(attn_low)
     *a_grads, in_own, in_other, sums_zero = attend_back(
-        direct,
+        added[2:],
         attn_low,
         attn_in,
         inputs,
@@ -994,25 +1069,29 @@
     inputs_grad = (sum_one + in_own + in_got).astype(BF16)
 
     if direct:
-        f_sets = scatter_xy(f_parts[0], *added)
-        f_mine, (f_ups, f_downs) = combine(*f_sets, 2)
+        up_sets = scatter_xy(z_sets[0], *added[:2])
         terms = exchange_terms(sums_zero, sums_one, sums_two, ub_parts, devices)
+        a_zz, a_xx, a_yy, by_x, by_y = a_grads
+        by_x, by_y, up_sets = lax.optimization_barrier((by_x, by_y, up_sets))
+        by_x, by_y = x_swap(by_x), y_swap(by_y)
+        up_mine, up_others = combine(*up_sets)
+        terms = after(terms, up_others)
         terms = lax.all_to_all(terms, ("batch", "head"), split_axis=0, concat_axis=0, tiled=True)
-        a_zz, a_xx, a_yy, d_lo, d_hi = a_grads
-        d_lo, d_hi = after((d_lo, d_hi), (f_sets, in_got, terms))
-        d_lo, d_hi = x_swap(d_lo), y_swap(d_hi)
-        f_ups = scatter_z(f_ups)
-        d_lo, d_hi, f_ups = lax.optimization_barrier((d_lo, d_hi, f_ups))
-        a_xx, a_yy = add_moved(a_xx, d_hi, a_yy, d_lo)
-        a_sets = scatter_xy(a_zz, a_xx, a_yy)
-        f_downs = scatter_z(after(f_downs, f_ups))
-        a_sets, f_downs, _ = lax.optimization_barrier((a_sets, f_downs, inputs_grad))
-        a_mine, (a_others,) = combine(*a_sets, 1)
-        up_grad, down_grad = finish_ffn(f_mine, f_ups, f_downs)
+        up_others = scatter_z(up_others)
+        by_x, by_y, up_others, terms, _ = lax.optimization_barrier(
+            (by_x, by_y, up_others, terms, inputs_grad)
+        )
+        a_xy, down_mine, down_others = turn(a_xx, a_yy, z_sets[1], by_x, by_y)
+        a_sets = scatter_xy(a_zz, *a_xy)
+        down_others = scatter_z(down_others)
+        a_sets, down_others = lax.optimization_barrier((a_sets, down_others))
+        a_mine, a_others = combine_last(*a_sets)
+        a_others = scatter_z(a_others)
+        up_grad, down_grad = finish_ffn((up_mine, *up_others), (down_mine, *down_others))
         up_grad = up_grad.T
         terms = jnp.sum(terms, 0)
         packed = jnp.concatenate([terms[:, :wp].reshape(-1), terms[0, wp : wp + wf]])
-        qkv_grad, proj_grad = finish_attend((a_mine, *scatter_z(a_others)))
+        qkv_grad, proj_grad = finish_attend((a_mine, *a_others))
     else:
         vecs = jnp.concatenate([sums_zero, sums_one, sums_two])
         vecs = vecs.reshape(8, devices, wp).transpose(1, 0, 2).reshape(devices, 8 * wp)

time: 206 us -> 197 us (0.956)
  blocking collectives: 19.2 us -> 0 us
  starting transfers between devices: 55.8 us -> 60.5 us
  Pallas kernels: 44.3 us -> 48.1 us
    all_to_all x1 -> x0, blocking collectives: 19.2 us -> none  [local(): lax.all_to_all(terms, ('batch', 'head'), split_axis=0, concat_axis=0, til...]
    ppermute x19, waiting for transfers between devices: 55.6 us -> 49.5 us  [z_swap(): return lax.ppermute(v, 'batch', ZPAIR[k])]
    pallas_call x21, Pallas kernels: 44.3 us -> 48.1 us  [call(): pl.pallas_call(kernel, out_shape=out_shape, in_specs=ins, out_specs=outs,...]
    all_to_all x0 -> x1, starting transfers between devices: none -> 3.39 us  [local(): lax.all_to_all(terms, ('batch', 'head'), split_axis=0, concat_axis=0, til...]
    ppermute x10, waiting for transfers between devices: 2.74 us -> 5.7 us  [x_swap(): return lax.ppermute(v, 'head', XPAIR)]
    all_to_all x0 -> x1, waiting for transfers between devices: none -> 2.74 us  [local(): lax.all_to_all(terms, ('batch', 'head'), split_axis=0, concat_axis=0, til...]
  transfers between devices with their start and end apart: 52 -> 53, of which waited for: 24 -> 25; matrix products, arithmetic and copies ran while one was open for 2% -> 2% of each run, Pallas kernels for 16% -> 18%
where the time goes in v5:
time: 197 us
  waiting for transfers between devices  79.6 us (40%)
  starting transfers between devices  60.5 us (31%)
  Pallas kernels  48.1 us (24%)
  local copies, waits for them, and re-layouts  4.3 us (2%)
  other arithmetic  3.3 us (2%)
    ppermute x19, waiting for transfers between devices, z_swap(): return lax.ppermute(v, 'batch', ZPAIR[k])  49.5 us
    pallas_call x21, Pallas kernels, call(): pl.pallas_call(kernel, out_shape=out_shape, in_specs=ins, out_specs=outs,...  48.1 us
    ppermute x19, starting transfers between devices, z_swap(): return lax.ppermute(v, 'batch', ZPAIR[k])  30.9 us
    ppermute x10, waiting for transfers between devices, y_swap(): return lax.ppermute(v, 'batch', YPAIR)  14.7 us
    ppermute x10, starting transfers between devices, x_swap(): return lax.ppermute(v, 'head', XPAIR)  12.9 us
    ppermute x10, starting transfers between devices, y_swap(): return lax.ppermute(v, 'batch', YPAIR)  11.5 us
    ppermute x13, waiting for transfers between devices, core_swap(): return lax.ppermute(v, 'head', CORE)  6.98 us
    ppermute x10, waiting for transfers between devices, x_swap(): return lax.ppermute(v, 'head', XPAIR)  5.7 us
  transfers between devices with their start and end apart: 53, of which 25 were waited for; matrix products, arithmetic and copies ran while one was open for 2% of the time, Pallas kernels for 18%

profile of v5, /device:TPU:0, one launch (start us, length us, event | category | flops | bytes accessed | tf_op | source)
XLA Modules:
  0.0 197.1 jit_solution(5802402545823007982)
XLA Ops:
  2.0 3.1 %collective-permute-start = (bf16[104,768]{1,0:T(8,128)(2,1)S(1)}, bf16[104,768]{1,0:T(8,128)(2,1)S(1)}, u32[]{:S(2)}, u32[]{:S(2)}) collective-permute-start(bf16[104,768]{1,0:T(8,128)(2,1)S(1)} %get-tuple-element.157), channel_id=1, source_target_pairs={{0,8},{4,12},{8,0},{12,4},{16,24},{20,28},{24,16},{28,20},{1,9},{5... | collective-permute-start | bytes 479240 | tf_op jit(solution)/shard_map/ppermute | solution.py:43
  5.1 2.5 %collective-permute-start.2 = (bf16[104,768]{1,0:T(8,128)(2,1)S(1)}, bf16[104,768]{1,0:T(8,128)(2,1)S(1)}, u32[]{:S(2)}, u32[]{:S(2)}) collective-permute-start(bf16[104,768]{1,0:T(8,128)(2,1)S(1)} %get-tuple-element.157), channel_id=1, source_target_pairs={{0,24},{4,28},{8,16},{12,20},{16,8},{20,12},{24,0},{28,4},{1,25},{... | collective-permute-start | bytes 479240 | tf_op jit(solution)/shard_map/ppermute | solution.py:43
  7.7 1.9 collective-permute-done
  9.6 1.5 collective-permute-start.4
  11.1 1.5 collective-permute-start.3
  13.7 1.5 collective-permute-start.5
  15.2 1.5 collective-permute-start.6
  16.7 5.1 %collective-permute-done.1 = bf16[104,768]{1,0:T(8,128)(2,1)S(1)} collective-permute-done((bf16[104,768]{1,0:T(8,128)(2,1)S(1)}, bf16[104,768]{1,0:T(8,128)(2,1)S(1)}, u32[]{:S(2)}, u32[]{:S(2)}) %collective-permute-start.1) | collective-permute-done | bytes 159776 | tf_op jit(solution)/shard_map/ppermute | solution.py:43
  21.9 1.6 collective-permute-start.9
  23.5 1.5 collective-permute-start.8
  25.0 2.6 %collective-permute-start.12 = (bf16[104,768]{1,0:T(8,128)(2,1)S(1)}, bf16[104,768]{1,0:T(8,128)(2,1)S(1)}, u32[]{:S(2)}, u32[]{:S(2)}) collective-permute-start(bf16[104,768]{1,0:T(8,128)(2,1)S(1)} %get-tuple-element.165), channel_id=1, source_target_pairs={{0,24},{4,28},{8,16},{12,20},{16,8},{20,12},{24,0},{28,4},{1,25},{... | collective-permute-start | bytes 479240 | tf_op jit(solution)/shard_map/ppermute | solution.py:43
  27.7 1.7 collective-permute-start.10
  29.4 4.5 %collective-permute-done.12 = bf16[104,768]{1,0:T(8,128)(2,1)S(1)} collective-permute-done((bf16[104,768]{1,0:T(8,128)(2,1)S(1)}, bf16[104,768]{1,0:T(8,128)(2,1)S(1)}, u32[]{:S(2)}, u32[]{:S(2)}) %collective-permute-start.12) | collective-permute-done | bytes 159776 | tf_op jit(solution)/shard_map/ppermute | solution.py:43
  33.9 5.9 %collective-permute-done.11 = bf16[104,768]{1,0:T(8,128)(2,1)S(1)} collective-permute-done((bf16[104,768]{1,0:T(8,128)(2,1)S(1)}, bf16[104,768]{1,0:T(8,128)(2,1)S(1)}, u32[]{:S(2)}, u32[]{:S(2)}) %collective-permute-start.11) | collective-permute-done | bytes 159776 | tf_op jit(solution)/shard_map/ppermute | solution.py:43
  41.1 2.4 %collective-permute-start.15 = (bf16[56,768]{1,0:T(8,128)(2,1)S(1)}, bf16[56,768]{1,0:T(8,128)(2,1)S(1)}, u32[]{:S(2)}, u32[]{:S(2)}) collective-permute-start(bf16[56,768]{1,0:T(8,128)(2,1)S(1)} %get-tuple-element.170), channel_id=1, source_target_pairs={{0,24},{4,28},{8,16},{12,20},{16,8},{20,12},{24,0},{28,4},{1,25},{... | collective-permute-start | bytes 258056 | tf_op jit(solution)/shard_map/ppermute | solution.py:43
  44.6 6.8 %collective-permute-done.15 = bf16[56,768]{1,0:T(8,128)(2,1)S(1)} collective-permute-done((bf16[56,768]{1,0:T(8,128)(2,1)S(1)}, bf16[56,768]{1,0:T(8,128)(2,1)S(1)}, u32[]{:S(2)}, u32[]{:S(2)}) %collective-permute-start.15) | collective-permute-done | bytes 86048 | tf_op jit(solution)/shard_map/ppermute | solution.py:43
  53.8 1.5 collective-permute-start.26
  55.3 1.5 collective-permute-start.25
  59.9 10.3 %shard_map.281 = (bf16[256,384]{1,0:T(8,128)(2,1)S(1)}, bf16[256,384]{1,0:T(8,128)(2,1)S(1)}, bf16[512,384]{1,0:T(8,128)(2,1)S(1)}, bf16[512,384]{1,0:T(8,128)(2...) custom-call(s32[2]{0:T(128)S(1)} %copy-done.10, ...), custom_call_target="tpu_custom_call" | custom-call | flops 1711276032 | bytes 12000000 | tf_op jit(solution)/shard_map/pallas_call | solution.py:108
  72.8 4.1 %collective-permute-done.27.refs_2_.refs_4_.refs_3_ = bf16[8,32,768]{2,1,0:T(8,128)(2,1)S(1)} collective-permute-done((bf16[8,32,768]{2,1,0:T(8,128)(2,1)S(1)}, bf16[8,32,768]{2,1,0:T(8,128)(2,1)S(1)}, u32[]{:S(2)}, u32[]{:S(2)}) %collective-permute-start.27) | collective-permute-done | bytes 393248 | tf_op jit(solution)/shard_map/ppermute | solution.py:43
  79.7 1.5 collective-permute-start.28
  83.9 1.5 shard_map.285
  86.7 4.5 %collective-permute-done.29.refs_1_ = bf16[2,160,768]{2,1,0:T(8,128)(2,1)S(1)} collective-permute-done((bf16[2,160,768]{2,1,0:T(8,128)(2,1)S(1)}, bf16[2,160,768]{2,1,0:T(8,128)(2,1)S(1)}, u32[]{:S(2)}, u32[]{:S(2)}) %collective-permute-start.29) | collective-permute-done | bytes 491552 | tf_op jit(solution)/shard_map/ppermute | solution.py:39
  93.2 1.7 collective-permute-done.30.got
  94.9 1.9 shard_map.288
  97.0 1.6 collective-permute-done.31.d1
  98.6 1.8 shard_map.289
  103.0 1.8 shard_map.290
  104.9 1.8 shard_map.291
  106.7 1.9 shard_map.292
  108.6 7.3 %collective-permute-done.32.refs_2_ = bf16[2,192,768]{2,1,0:T(8,128)(2,1)S(1)} collective-permute-done((bf16[2,192,768]{2,1,0:T(8,128)(2,1)S(1)}, bf16[2,192,768]{2,1,0:T(8,128)(2,1)S(1)}, u32[]{:S(2)}, u32[]{:S(2)}) %collective-permute-start.32) | collective-permute-done | bytes 589856 | tf_op jit(solution)/shard_map/ppermute | solution.py:39
  116.6 1.7 collective-permute-done.34.got
  119.6 1.5 collective-permute-start.37
  122.1 10.1 %shard_map.294 = (bf16[4,96,768]{2,1,0:T(8,128)(2,1)}, bf16[4,96,768]{2,1,0:T(8,128)(2,1)}, bf16[4,96,768]{2,1,0:T(8,128)(2,1)}, bf16[6,96,768]{2,1,0:T(8,128)(2...) custom-call(bf16[256,768]{1,0:T(8,128)(2,1)S(1)} %get-tuple-element.236.a, ...), custom_call_target="tpu_custom_call" | custom-call | flops 8000000000 | bytes 14000000 | tf_op jit(solution)/shard_map/pallas_call | solution.py:108
  132.2 3.0 %collective-permute-done.37.x = bf16[4,96,768]{2,1,0:T(8,128)(2,1)S(1)} collective-permute-done((bf16[4,96,768]{2,1,0:T(8,128)(2,1)S(1)}, bf16[4,96,768]{2,1,0:T(8,128)(2,1)S(1)}, u32[]{:S(2)}, u32[]{:S(2)}) %collective-permute-start.37) | collective-permute-done | bytes 589856 | tf_op jit(solution)/shard_map/ppermute | solution.py:35
  140.9 1.7 collective-permute-start.42
  142.7 3.4 %all-to-all-start = ((f32[32,8,128]{2,1,0:T(8,128)}), f32[32,8,128]{2,1,0:T(8,128)}, u32[]{:S(2)}, u32[]{:S(2)}) async-start(f32[32,8,128]{2,1,0:T(8,128)} %shard_map.296), calls=%async_computation | async-start | bytes 262144 | tf_op jit(solution)/shard_map/all_to_all | solution.py:1079
  146.1 3.6 %collective-permute-start.43 = (bf16[96,768]{1,0:T(8,128)(2,1)}, bf16[96,768]{1,0:T(8,128)(2,1)S(1)}, u32[]{:S(2)}, u32[]{:S(2)}) collective-permute-start(bf16[96,768]{1,0:T(8,128)(2,1)} %get-tuple-element.263), channel_id=1, source_target_pairs={{0,24},{4,28},{8,16},{12,20},{16,8},{20,12},{24,0},{28,4},{1,25},{... | collective-permute-start | bytes 442376 | tf_op jit(solution)/shard_map/ppermute | solution.py:43
  149.7 2.0 %add_convert_fusion = bf16[256,768]{1,0:T(8,128)(2,1)} fusion(f32[256,768]{1,0:T(8,128)} %collective-permute-done.36, f32[256,768]{1,0:T(8,128)S(1)} %get-tuple-element.235, f32[256,768]{1,0:T(8,128)S(1)} %get-tuple-element.245), kind=kLoop, calls=%fused_computation.1 | loop fusion | flops 589824 | bytes 2752512 | tf_op jit(solution)/shard_map/convert_element_type | solution.py:1069
  151.7 4.2 %collective-permute-done.43.refs_3_ = bf16[96,768]{1,0:T(8,128)(2,1)S(1)} collective-permute-done((bf16[96,768]{1,0:T(8,128)(2,1)}, bf16[96,768]{1,0:T(8,128)(2,1)S(1)}, u32[]{:S(2)}, u32[]{:S(2)}) %collective-permute-start.43) | collective-permute-done | bytes 147488 | tf_op jit(solution)/shard_map/ppermute | solution.py:43
  156.6 2.7 %all-to-all-done = f32[32,8,128]{2,1,0:T(8,128)} async-done(((f32[32,8,128]{2,1,0:T(8,128)}), f32[32,8,128]{2,1,0:T(8,128)}, u32[]{:S(2)}, u32[]{:S(2)}) %all-to-all-start) | async-done | bytes 131104 | tf_op jit(solution)/shard_map/all_to_all | solution.py:1079
  159.4 3.3 %shard_map.297 = (bf16[4,96,768]{2,1,0:T(8,128)(2,1)}, bf16[4,96,768]{2,1,0:T(8,128)(2,1)}, f32[96,768]{1,0:T(8,128)}, bf16[96,768]{1,0:T(8,128)(2,1)}, bf16[96,...) custom-call(bf16[4,96,768]{2,1,0:T(8,128)(2,1)S(1)} %copy-done.1, bf16[4,96,768]{2,1,0:T(8,128)(2,1)S(1)} %copy-done.2, ...), custom_call_target="tpu_custom_call" | custom-call | flops 1000 | bytes 1000 | tf_op jit(solution)/shard_map/pallas_call | solution.py:108
  166.5 1.7 collective-permute-start.47
  172.2 7.9 %collective-permute-done.47.refs_6_ = bf16[96,768]{1,0:T(8,128)(2,1)S(1)} collective-permute-done((bf16[96,768]{1,0:T(8,128)(2,1)}, bf16[96,768]{1,0:T(8,128)(2,1)S(1)}, u32[]{:S(2)}, u32[]{:S(2)}) %collective-permute-start.47) | collective-permute-done | bytes 147488 | tf_op jit(solution)/shard_map/ppermute | solution.py:43
  180.9 2.6 %collective-permute-start.49 = (bf16[96,768]{1,0:T(8,128)(2,1)}, bf16[96,768]{1,0:T(8,128)(2,1)S(1)}, u32[]{:S(2)}, u32[]{:S(2)}) collective-permute-start(bf16[96,768]{1,0:T(8,128)(2,1)} %get-tuple-element.283), channel_id=1, source_target_pairs={{0,8},{4,12},{8,0},{12,4},{16,24},{20,28},{24,16},{28,20},{1,9},{5... | collective-permute-start | bytes 442376 | tf_op jit(solution)/shard_map/ppermute | solution.py:43
  183.7 2.3 %collective-permute-start.51 = (bf16[96,768]{1,0:T(8,128)(2,1)}, bf16[96,768]{1,0:T(8,128)(2,1)S(1)}, u32[]{:S(2)}, u32[]{:S(2)}) collective-permute-start(bf16[96,768]{1,0:T(8,128)(2,1)} %get-tuple-element.285), channel_id=1, source_target_pairs={{0,24},{4,28},{8,16},{12,20},{16,8},{20,12},{24,0},{28,4},{1,25},{... | collective-permute-start | bytes 442376 | tf_op jit(solution)/shard_map/ppermute | solution.py:43
  186.6 1.8 shard_map.300
  188.3 7.8 %collective-permute-done.50.two = bf16[96,768]{1,0:T(8,128)(2,1)S(1)} collective-permute-done((bf16[96,768]{1,0:T(8,128)(2,1)}, bf16[96,768]{1,0:T(8,128)(2,1)S(1)}, u32[]{:S(2)}, u32[]{:S(2)}) %collective-permute-start.50) | collective-permute-done | bytes 147488 | tf_op jit(solution)/shard_map/ppermute | solution.py:43
  (148 shorter events, 44.2 us)
Async XLA Ops:
  2.0 7.6 %collective-permute-start = (bf16[104,768]{1,0:T(8,128)(2,1)S(1)}, bf16[104,768]{1,0:T(8,128)(2,1)S(1)}, u32[]{:S(2)}, u32[]{:S(2)}) collective-permute-start(bf16[104,768]{1,0:T(8,128)(2,1)S(1)} %get-tuple-element.157), channel_id=1, source_target_pairs={{0,8},{4,12},{8,0},{12,4},{16,24},{20,28},{24,16},{28,20},{1,9},{5... | collective-permute-start | bytes 479240 | tf_op jit(solution)/shard_map/ppermute | solution.py:43
  5.1 11.6 %collective-permute-start.2 = (bf16[104,768]{1,0:T(8,128)(2,1)S(1)}, bf16[104,768]{1,0:T(8,128)(2,1)S(1)}, u32[]{:S(2)}, u32[]{:S(2)}) collective-permute-start(bf16[104,768]{1,0:T(8,128)(2,1)S(1)} %get-tuple-element.157), channel_id=1, source_target_pairs={{0,24},{4,28},{8,16},{12,20},{16,8},{20,12},{24,0},{28,4},{1,25},{... | collective-permute-start | bytes 479240 | tf_op jit(solution)/shard_map/ppermute | solution.py:43
  7.5 14.2 %collective-permute-start.1 = (bf16[104,768]{1,0:T(8,128)(2,1)S(1)}, bf16[104,768]{1,0:T(8,128)(2,1)S(1)}, u32[]{:S(2)}, u32[]{:S(2)}) collective-permute-start(bf16[104,768]{1,0:T(8,128)(2,1)S(1)} %get-tuple-element.157), channel_id=1, source_target_pairs={{0,16},{4,20},{8,24},{12,28},{16,0},{20,4},{24,8},{28,12},{1,17},{... | collective-permute-start | bytes 479240 | tf_op jit(solution)/shard_map/ppermute | solution.py:43
  9.6 4.1 %collective-permute-start.4 = (bf16[32,768]{1,0:T(8,128)(2,1)S(1)}, bf16[32,768]{1,0:T(8,128)(2,1)S(1)}, u32[]{:S(2)}, u32[]{:S(2)}) collective-permute-start(bf16[32,768]{1,0:T(8,128)(2,1)S(1)} %get-tuple-element.159), channel_id=1, source_target_pairs={{0,4},{4,0},{8,12},{12,8},{16,20},{20,16},{24,28},{28,24},{1,5},{5... | collective-permute-start | bytes 147464 | tf_op jit(solution)/shard_map/ppermute | solution.py:39
  11.1 4.1 %collective-permute-start.3 = (bf16[32,768]{1,0:T(8,128)(2,1)S(1)}, bf16[32,768]{1,0:T(8,128)(2,1)S(1)}, u32[]{:S(2)}, u32[]{:S(2)}) collective-permute-start(bf16[32,768]{1,0:T(8,128)(2,1)S(1)} %get-tuple-element.159), channel_id=1, source_target_pairs={{0,2},{1,3},{2,0},{3,1},{4,6},{5,7},{6,4},{7,5},{8,10},{9,11},{10,... | collective-permute-start | bytes 147464 | tf_op jit(solution)/shard_map/ppermute | solution.py:35
  12.6 9.3 %collective-permute-start.7 = (bf16[256,768]{1,0:T(8,128)(2,1)}, bf16[256,768]{1,0:T(8,128)(2,1)S(1)}, u32[]{:S(2)}, u32[]{:S(2)}) collective-permute-start(bf16[256,768]{1,0:T(8,128)(2,1)} %refs_8_.1), channel_id=1, source_target_pairs={{0,1},{1,0},{2,3},{3,2},{4,5},{5,4},{6,7},{7,6},{8,9},{9,8},{10,11... | collective-permute-start | bytes 1179656 | tf_op jit(solution)/shard_map/ppermute | solution.py:31
  13.7 8.2 %collective-permute-start.5 = (bf16[16,768]{1,0:T(8,128)(2,1)S(1)}, bf16[16,768]{1,0:T(8,128)(2,1)S(1)}, u32[]{:S(2)}, u32[]{:S(2)}) collective-permute-start(bf16[16,768]{1,0:T(8,128)(2,1)S(1)} %slice.129), channel_id=1, source_target_pairs={{0,2},{1,3},{2,0},{3,1},{4,6},{5,7},{6,4},{7,5},{8,10},{9,11},{10,... | collective-permute-start | bytes 73736 | tf_op jit(solution)/shard_map/ppermute | solution.py:35
  15.2 6.7 %collective-permute-start.6 = (bf16[16,768]{1,0:T(8,128)(2,1)S(1)}, bf16[16,768]{1,0:T(8,128)(2,1)S(1)}, u32[]{:S(2)}, u32[]{:S(2)}) collective-permute-start(bf16[16,768]{1,0:T(8,128)(2,1)S(1)} %slice.130), channel_id=1, source_target_pairs={{0,4},{4,0},{8,12},{12,8},{16,20},{20,16},{24,28},{28,24},{1,5},{5... | collective-permute-start | bytes 73736 | tf_op jit(solution)/shard_map/ppermute | solution.py:39
  21.9 17.9 %collective-permute-start.9 = (bf16[4,104,768]{2,1,0:T(8,128)(2,1)S(1)}, bf16[4,104,768]{2,1,0:T(8,128)(2,1)S(1)}, u32[]{:S(2)}, u32[]{:S(2)}) collective-permute-start(bf16[4,104,768]{2,1,0:T(8,128)(2,1)S(1)} %pad_maximum_fusion.1.refs_0_), channel_id=1, source_target_pairs={{0,4},{4,0},{8,12},{12,8},{16,20},{20,16},{24,28},{28,24},{1,5},{5... | collective-permute-start | bytes 1916936 | tf_op jit(solution)/shard_map/ppermute | solution.py:39
  23.5 16.3 %collective-permute-start.8 = (bf16[4,104,768]{2,1,0:T(8,128)(2,1)S(1)}, bf16[4,104,768]{2,1,0:T(8,128)(2,1)S(1)}, u32[]{:S(2)}, u32[]{:S(2)}) collective-permute-start(bf16[4,104,768]{2,1,0:T(8,128)(2,1)S(1)} %pad_maximum_fusion.1.refs_0_), channel_id=1, source_target_pairs={{0,2},{1,3},{2,0},{3,1},{4,6},{5,7},{6,4},{7,5},{8,10},{9,11},{10,... | collective-permute-start | bytes 1916936 | tf_op jit(solution)/shard_map/ppermute | solution.py:35
  25.0 8.8 %collective-permute-start.12 = (bf16[104,768]{1,0:T(8,128)(2,1)S(1)}, bf16[104,768]{1,0:T(8,128)(2,1)S(1)}, u32[]{:S(2)}, u32[]{:S(2)}) collective-permute-start(bf16[104,768]{1,0:T(8,128)(2,1)S(1)} %get-tuple-element.165), channel_id=1, source_target_pairs={{0,24},{4,28},{8,16},{12,20},{16,8},{20,12},{24,0},{28,4},{1,25},{... | collective-permute-start | bytes 479240 | tf_op jit(solution)/shard_map/ppermute | solution.py:43
  27.7 12.1 %collective-permute-start.11 = (bf16[104,768]{1,0:T(8,128)(2,1)S(1)}, bf16[104,768]{1,0:T(8,128)(2,1)S(1)}, u32[]{:S(2)}, u32[]{:S(2)}) collective-permute-start(bf16[104,768]{1,0:T(8,128)(2,1)S(1)} %get-tuple-element.165), channel_id=1, source_target_pairs={{0,16},{4,20},{8,24},{12,28},{16,0},{20,4},{24,8},{28,12},{1,17},{... | collective-permute-start | bytes 479240 | tf_op jit(solution)/shard_map/ppermute | solution.py:43
  27.7 12.1 %collective-permute-start.10 = (bf16[104,768]{1,0:T(8,128)(2,1)S(1)}, bf16[104,768]{1,0:T(8,128)(2,1)S(1)}, u32[]{:S(2)}, u32[]{:S(2)}) collective-permute-start(bf16[104,768]{1,0:T(8,128)(2,1)S(1)} %get-tuple-element.165), channel_id=1, source_target_pairs={{0,8},{4,12},{8,0},{12,4},{16,24},{20,28},{24,16},{28,20},{1,9},{5... | collective-permute-start | bytes 479240 | tf_op jit(solution)/shard_map/ppermute | solution.py:43
  39.9 11.5 %collective-permute-start.17 = (bf16[2,104,768]{2,1,0:T(8,128)(2,1)S(1)}, bf16[2,104,768]{2,1,0:T(8,128)(2,1)S(1)}, u32[]{:S(2)}, u32[]{:S(2)}) collective-permute-start(bf16[2,104,768]{2,1,0:T(8,128)(2,1)S(1)} %slice.102), channel_id=1, source_target_pairs={{0,4},{4,0},{8,12},{12,8},{16,20},{20,16},{24,28},{28,24},{1,5},{5... | collective-permute-start | bytes 958472 | tf_op jit(solution)/shard_map/ppermute | solution.py:39
  40.5 10.9 %collective-permute-start.16 = (bf16[2,104,768]{2,1,0:T(8,128)(2,1)S(1)}, bf16[2,104,768]{2,1,0:T(8,128)(2,1)S(1)}, u32[]{:S(2)}, u32[]{:S(2)}) collective-permute-start(bf16[2,104,768]{2,1,0:T(8,128)(2,1)S(1)} %slice.101), channel_id=1, source_target_pairs={{0,2},{1,3},{2,0},{3,1},{4,6},{5,7},{6,4},{7,5},{8,10},{9,11},{10,... | collective-permute-start | bytes 958472 | tf_op jit(solution)/shard_map/ppermute | solution.py:35
  41.0 10.3 %collective-permute-start.13 = (bf16[184,768]{1,0:T(8,128)(2,1)S(1)}, bf16[184,768]{1,0:T(8,128)(2,1)S(1)}, u32[]{:S(2)}, u32[]{:S(2)}) collective-permute-start(bf16[184,768]{1,0:T(8,128)(2,1)S(1)} %pad_maximum_fusion.3), channel_id=1, source_target_pairs={{0,8},{4,12},{8,0},{12,4},{16,24},{20,28},{24,16},{28,20},{1,9},{5... | collective-permute-start | bytes 847880 | tf_op jit(solution)/shard_map/ppermute | solution.py:43
  41.1 10.2 %collective-permute-start.15 = (bf16[56,768]{1,0:T(8,128)(2,1)S(1)}, bf16[56,768]{1,0:T(8,128)(2,1)S(1)}, u32[]{:S(2)}, u32[]{:S(2)}) collective-permute-start(bf16[56,768]{1,0:T(8,128)(2,1)S(1)} %get-tuple-element.170), channel_id=1, source_target_pairs={{0,24},{4,28},{8,16},{12,20},{16,8},{20,12},{24,0},{28,4},{1,25},{... | collective-permute-start | bytes 258056 | tf_op jit(solution)/shard_map/ppermute | solution.py:43
  43.5 7.9 %collective-permute-start.14 = (bf16[56,768]{1,0:T(8,128)(2,1)S(1)}, bf16[56,768]{1,0:T(8,128)(2,1)S(1)}, u32[]{:S(2)}, u32[]{:S(2)}) collective-permute-start(bf16[56,768]{1,0:T(8,128)(2,1)S(1)} %get-tuple-element.170), channel_id=1, source_target_pairs={{0,16},{4,20},{8,24},{12,28},{16,0},{20,4},{24,8},{28,12},{1,17},{... | collective-permute-start | bytes 258056 | tf_op jit(solution)/shard_map/ppermute | solution.py:43
  52.2 3.1 %collective-permute-start.22 = (bf16[2,104,768]{2,1,0:T(8,128)(2,1)S(1)}, bf16[2,104,768]{2,1,0:T(8,128)(2,1)S(1)}, u32[]{:S(2)}, u32[]{:S(2)}) collective-permute-start(bf16[2,104,768]{2,1,0:T(8,128)(2,1)S(1)} %collective-permute-done.17.refs_4_), channel_id=1, source_target_pairs={{0,1},{1,0},{2,3},{3,2},{4,5},{5,4},{6,7},{7,6},{8,9},{9,8},{10,11... | collective-permute-start | bytes 958472 | tf_op jit(solution)/shard_map/ppermute | solution.py:31
  52.7 4.2 %collective-permute-start.18 = (bf16[4,104,768]{2,1,0:T(8,128)(2,1)S(1)}, bf16[4,104,768]{2,1,0:T(8,128)(2,1)S(1)}, u32[]{:S(2)}, u32[]{:S(2)}) collective-permute-start(bf16[4,104,768]{2,1,0:T(8,128)(2,1)S(1)} %pad_maximum_fusion.1.refs_0_), channel_id=1, source_target_pairs={{0,1},{1,0},{2,3},{3,2},{4,5},{5,4},{6,7},{7,6},{8,9},{9,8},{10,11... | collective-permute-start | bytes 1916936 | tf_op jit(solution)/shard_map/ppermute | solution.py:31
  52.8 5.4 %collective-permute-start.19 = (bf16[4,104,768]{2,1,0:T(8,128)(2,1)S(1)}, bf16[4,104,768]{2,1,0:T(8,128)(2,1)S(1)}, u32[]{:S(2)}, u32[]{:S(2)}) collective-permute-start(bf16[4,104,768]{2,1,0:T(8,128)(2,1)S(1)} %collective-permute-done.8.refs_1_), channel_id=1, source_target_pairs={{0,1},{1,0},{2,3},{3,2},{4,5},{5,4},{6,7},{7,6},{8,9},{9,8},{10,11... | collective-permute-start | bytes 1916936 | tf_op jit(solution)/shard_map/ppermute | solution.py:31
  53.2 5.0 %collective-permute-start.20 = (bf16[4,104,768]{2,1,0:T(8,128)(2,1)S(1)}, bf16[4,104,768]{2,1,0:T(8,128)(2,1)S(1)}, u32[]{:S(2)}, u32[]{:S(2)}) collective-permute-start(bf16[4,104,768]{2,1,0:T(8,128)(2,1)S(1)} %collective-permute-done.9.refs_2_), channel_id=1, source_target_pairs={{0,1},{1,0},{2,3},{3,2},{4,5},{5,4},{6,7},{7,6},{8,9},{9,8},{10,11... | collective-permute-start | bytes 1916936 | tf_op jit(solution)/shard_map/ppermute | solution.py:31
  53.8 23.8 %collective-permute-start.26 = (bf16[4,160,768]{2,1,0:T(8,128)(2,1)S(1)}, bf16[4,160,768]{2,1,0:T(8,128)(2,1)S(1)}, u32[]{:S(2)}, u32[]{:S(2)}) collective-permute-start(bf16[4,160,768]{2,1,0:T(8,128)(2,1)S(1)} %pad_maximum_fusion.refs_0_), channel_id=1, source_target_pairs={{0,4},{4,0},{8,12},{12,8},{16,20},{20,16},{24,28},{28,24},{1,5},{5... | collective-permute-start | bytes 2949128 | tf_op jit(solution)/shard_map/ppermute | solution.py:39
  55.3 23.5 %collective-permute-start.25 = (bf16[4,160,768]{2,1,0:T(8,128)(2,1)S(1)}, bf16[4,160,768]{2,1,0:T(8,128)(2,1)S(1)}, u32[]{:S(2)}, u32[]{:S(2)}) collective-permute-start(bf16[4,160,768]{2,1,0:T(8,128)(2,1)S(1)} %pad_maximum_fusion.refs_0_), channel_id=1, source_target_pairs={{0,2},{1,3},{2,0},{3,1},{4,6},{5,7},{6,4},{7,5},{8,10},{9,11},{10,... | collective-permute-start | bytes 2949128 | tf_op jit(solution)/shard_map/ppermute | solution.py:35
  56.9 20.0 %collective-permute-start.27 = (bf16[8,32,768]{2,1,0:T(8,128)(2,1)S(1)}, bf16[8,32,768]{2,1,0:T(8,128)(2,1)S(1)}, u32[]{:S(2)}, u32[]{:S(2)}) collective-permute-start(bf16[8,32,768]{2,1,0:T(8,128)(2,1)S(1)} %pad_maximum_fusion.2), channel_id=1, source_target_pairs={{0,16},{4,20},{8,24},{12,28},{16,0},{20,4},{24,8},{28,12},{1,17},{... | collective-permute-start | bytes 1179656 | tf_op jit(solution)/shard_map/ppermute | solution.py:43
  72.6 8.7 %collective-permute-start.24 = (bf16[256,768]{1,0:T(8,128)(2,1)S(1)}, bf16[256,768]{1,0:T(8,128)(2,1)S(1)}, u32[]{:S(2)}, u32[]{:S(2)}) collective-permute-start(bf16[256,768]{1,0:T(8,128)(2,1)S(1)} %get-tuple-element.189.x0), channel_id=1, source_target_pairs={{0,1},{1,0},{2,3},{3,2},{4,5},{5,4},{6,7},{7,6},{8,9},{9,8},{10,11... | collective-permute-start | bytes 1179656 | tf_op jit(solution)/shard_map/ppermute | solution.py:31
  78.9 12.2 %collective-permute-start.29 = (bf16[2,160,768]{2,1,0:T(8,128)(2,1)S(1)}, bf16[2,160,768]{2,1,0:T(8,128)(2,1)S(1)}, u32[]{:S(2)}, u32[]{:S(2)}) collective-permute-start(bf16[2,160,768]{2,1,0:T(8,128)(2,1)S(1)} %slice.107), channel_id=1, source_target_pairs={{0,4},{4,0},{8,12},{12,8},{16,20},{20,16},{24,28},{28,24},{1,5},{5... | collective-permute-start | bytes 1474568 | tf_op jit(solution)/shard_map/ppermute | solution.py:39
  79.7 12.1 %collective-permute-start.28 = (bf16[2,160,768]{2,1,0:T(8,128)(2,1)S(1)}, bf16[2,160,768]{2,1,0:T(8,128)(2,1)S(1)}, u32[]{:S(2)}, u32[]{:S(2)}) collective-permute-start(bf16[2,160,768]{2,1,0:T(8,128)(2,1)S(1)} %slice.106), channel_id=1, source_target_pairs={{0,2},{1,3},{2,0},{3,1},{4,6},{5,7},{6,4},{7,5},{8,10},{9,11},{10,... | collective-permute-start | bytes 1474568 | tf_op jit(solution)/shard_map/ppermute | solution.py:35
  100.4 15.4 %collective-permute-start.32 = (bf16[2,192,768]{2,1,0:T(8,128)(2,1)S(1)}, bf16[2,192,768]{2,1,0:T(8,128)(2,1)S(1)}, u32[]{:S(2)}, u32[]{:S(2)}) collective-permute-start(bf16[2,192,768]{2,1,0:T(8,128)(2,1)S(1)} %get-tuple-element.228), channel_id=1, source_target_pairs={{0,4},{4,0},{8,12},{12,8},{16,20},{20,16},{24,28},{28,24},{1,5},{5... | collective-permute-start | bytes 1769480 | tf_op jit(solution)/shard_map/ppermute | solution.py:39
  101.5 15.1 %collective-permute-start.33 = (bf16[2,192,768]{2,1,0:T(8,128)(2,1)S(1)}, bf16[2,192,768]{2,1,0:T(8,128)(2,1)S(1)}, u32[]{:S(2)}, u32[]{:S(2)}) collective-permute-start(bf16[2,192,768]{2,1,0:T(8,128)(2,1)S(1)} %get-tuple-element.231), channel_id=1, source_target_pairs={{0,2},{1,3},{2,0},{3,1},{4,6},{5,7},{6,4},{7,5},{8,10},{9,11},{10,... | collective-permute-start | bytes 1769480 | tf_op jit(solution)/shard_map/ppermute | solution.py:35
  119.4 2.7 %collective-permute-start.35 = (bf16[256,768]{1,0:T(8,128)(2,1)S(1)}, bf16[256,768]{1,0:T(8,128)(2,1)S(1)}, u32[]{:S(2)}, u32[]{:S(2)}) collective-permute-start(bf16[256,768]{1,0:T(8,128)(2,1)S(1)} %get-tuple-element.236.a0), channel_id=1, source_target_pairs={{0,1},{1,0},{2,3},{3,2},{4,5},{5,4},{6,7},{7,6},{8,9},{9,8},{10,11... | collective-permute-start | bytes 1179656 | tf_op jit(solution)/shard_map/ppermute | solution.py:31
  119.6 15.6 %collective-permute-start.37 = (bf16[4,96,768]{2,1,0:T(8,128)(2,1)S(1)}, bf16[4,96,768]{2,1,0:T(8,128)(2,1)S(1)}, u32[]{:S(2)}, u32[]{:S(2)}) collective-permute-start(bf16[4,96,768]{2,1,0:T(8,128)(2,1)S(1)} %get-tuple-element.254), channel_id=1, source_target_pairs={{0,2},{1,3},{2,0},{3,1},{4,6},{5,7},{6,4},{7,5},{8,10},{9,11},{10,... | collective-permute-start | bytes 1769480 | tf_op jit(solution)/shard_map/ppermute | solution.py:35
  121.1 15.3 %collective-permute-start.38 = (bf16[4,96,768]{2,1,0:T(8,128)(2,1)S(1)}, bf16[4,96,768]{2,1,0:T(8,128)(2,1)S(1)}, u32[]{:S(2)}, u32[]{:S(2)}) collective-permute-start(bf16[4,96,768]{2,1,0:T(8,128)(2,1)S(1)} %get-tuple-element.255), channel_id=1, source_target_pairs={{0,4},{4,0},{8,12},{12,8},{16,20},{20,16},{24,28},{28,24},{1,5},{5... | collective-permute-start | bytes 1769480 | tf_op jit(solution)/shard_map/ppermute | solution.py:39
  132.2 13.9 %collective-permute-start.36 = (f32[256,768]{1,0:T(8,128)}, f32[256,768]{1,0:T(8,128)}, u32[]{:S(2)}, u32[]{:S(2)}) collective-permute-start(f32[256,768]{1,0:T(8,128)} %get-tuple-element.246), channel_id=1, source_target_pairs={{0,1},{1,0},{2,3},{3,2},{4,5},{5,4},{6,7},{7,6},{8,9},{9,8},{10,11... | collective-permute-start | bytes 2359304 | tf_op jit(solution)/shard_map/ppermute | solution.py:31
  136.4 22.9 %collective-permute-start.39 = (bf16[6,96,768]{2,1,0:T(8,128)(2,1)}, bf16[6,96,768]{2,1,0:T(8,128)(2,1)}, u32[]{:S(2)}, u32[]{:S(2)}) collective-permute-start(bf16[6,96,768]{2,1,0:T(8,128)(2,1)} %get-tuple-element.256), channel_id=1, source_target_pairs={{0,2},{1,3},{2,0},{3,1},{4,6},{5,7},{6,4},{7,5},{8,10},{9,11},{10,... | collective-permute-start | bytes 2654216 | tf_op jit(solution)/shard_map/ppermute | solution.py:35
  136.9 22.4 %collective-permute-start.40 = (bf16[6,96,768]{2,1,0:T(8,128)(2,1)}, bf16[6,96,768]{2,1,0:T(8,128)(2,1)}, u32[]{:S(2)}, u32[]{:S(2)}) collective-permute-start(bf16[6,96,768]{2,1,0:T(8,128)(2,1)} %get-tuple-element.257), channel_id=1, source_target_pairs={{0,4},{4,0},{8,12},{12,8},{16,20},{20,16},{24,28},{28,24},{1,5},{5... | collective-permute-start | bytes 2654216 | tf_op jit(solution)/shard_map/ppermute | solution.py:39
  139.7 12.0 %collective-permute-start.41 = (bf16[96,768]{1,0:T(8,128)(2,1)}, bf16[96,768]{1,0:T(8,128)(2,1)S(1)}, u32[]{:S(2)}, u32[]{:S(2)}) collective-permute-start(bf16[96,768]{1,0:T(8,128)(2,1)} %get-tuple-element.261), channel_id=1, source_target_pairs={{0,8},{4,12},{8,0},{12,4},{16,24},{20,28},{24,16},{28,20},{1,9},{5... | collective-permute-start | bytes 442376 | tf_op jit(solution)/shard_map/ppermute | solution.py:43
  140.9 10.8 %collective-permute-start.42 = (bf16[96,768]{1,0:T(8,128)(2,1)}, bf16[96,768]{1,0:T(8,128)(2,1)}, u32[]{:S(2)}, u32[]{:S(2)}) collective-permute-start(bf16[96,768]{1,0:T(8,128)(2,1)} %get-tuple-element.262), channel_id=1, source_target_pairs={{0,16},{4,20},{8,24},{12,28},{16,0},{20,4},{24,8},{28,12},{1,17},{... | collective-permute-start | bytes 442376 | tf_op jit(solution)/shard_map/ppermute | solution.py:43
  142.7 16.7 %all-to-all-start = ((f32[32,8,128]{2,1,0:T(8,128)}), f32[32,8,128]{2,1,0:T(8,128)}, u32[]{:S(2)}, u32[]{:S(2)}) async-start(f32[32,8,128]{2,1,0:T(8,128)} %shard_map.296), calls=%async_computation | async-start | bytes 262144 | tf_op jit(solution)/shard_map/all_to_all | solution.py:1079
  146.1 9.8 %collective-permute-start.43 = (bf16[96,768]{1,0:T(8,128)(2,1)}, bf16[96,768]{1,0:T(8,128)(2,1)S(1)}, u32[]{:S(2)}, u32[]{:S(2)}) collective-permute-start(bf16[96,768]{1,0:T(8,128)(2,1)} %get-tuple-element.263), channel_id=1, source_target_pairs={{0,24},{4,28},{8,16},{12,20},{16,8},{20,12},{24,0},{28,4},{1,25},{... | collective-permute-start | bytes 442376 | tf_op jit(solution)/shard_map/ppermute | solution.py:43
  162.7 17.4 %collective-permute-start.44 = (bf16[4,96,768]{2,1,0:T(8,128)(2,1)}, bf16[4,96,768]{2,1,0:T(8,128)(2,1)S(1)}, u32[]{:S(2)}, u32[]{:S(2)}) collective-permute-start(bf16[4,96,768]{2,1,0:T(8,128)(2,1)} %get-tuple-element.274), channel_id=1, source_target_pairs={{0,2},{1,3},{2,0},{3,1},{4,6},{5,7},{6,4},{7,5},{8,10},{9,11},{10,... | collective-permute-start | bytes 1769480 | tf_op jit(solution)/shard_map/ppermute | solution.py:35
  164.1 16.0 %collective-permute-start.45 = (bf16[4,96,768]{2,1,0:T(8,128)(2,1)}, bf16[4,96,768]{2,1,0:T(8,128)(2,1)S(1)}, u32[]{:S(2)}, u32[]{:S(2)}) collective-permute-start(bf16[4,96,768]{2,1,0:T(8,128)(2,1)} %get-tuple-element.275), channel_id=1, source_target_pairs={{0,4},{4,0},{8,12},{12,8},{16,20},{20,16},{24,28},{28,24},{1,5},{5... | collective-permute-start | bytes 1769480 | tf_op jit(solution)/shard_map/ppermute | solution.py:39
  165.0 7.2 %collective-permute-start.46 = (bf16[96,768]{1,0:T(8,128)(2,1)}, bf16[96,768]{1,0:T(8,128)(2,1)S(1)}, u32[]{:S(2)}, u32[]{:S(2)}) collective-permute-start(bf16[96,768]{1,0:T(8,128)(2,1)} %get-tuple-element.276), channel_id=1, source_target_pairs={{0,8},{4,12},{8,0},{12,4},{16,24},{20,28},{24,16},{28,20},{1,9},{5... | collective-permute-start | bytes 442376 | tf_op jit(solution)/shard_map/ppermute | solution.py:43
  166.5 13.6 %collective-permute-start.47 = (bf16[96,768]{1,0:T(8,128)(2,1)}, bf16[96,768]{1,0:T(8,128)(2,1)S(1)}, u32[]{:S(2)}, u32[]{:S(2)}) collective-permute-start(bf16[96,768]{1,0:T(8,128)(2,1)} %get-tuple-element.277), channel_id=1, source_target_pairs={{0,16},{4,20},{8,24},{12,28},{16,0},{20,4},{24,8},{28,12},{1,17},{... | collective-permute-start | bytes 442376 | tf_op jit(solution)/shard_map/ppermute | solution.py:43
  168.2 11.9 %collective-permute-start.48 = (bf16[96,768]{1,0:T(8,128)(2,1)}, bf16[96,768]{1,0:T(8,128)(2,1)S(1)}, u32[]{:S(2)}, u32[]{:S(2)}) collective-permute-start(bf16[96,768]{1,0:T(8,128)(2,1)} %get-tuple-element.278), channel_id=1, source_target_pairs={{0,24},{4,28},{8,16},{12,20},{16,8},{20,12},{24,0},{28,4},{1,25},{... | collective-permute-start | bytes 442376 | tf_op jit(solution)/shard_map/ppermute | solution.py:43
  180.9 7.4 %collective-permute-start.49 = (bf16[96,768]{1,0:T(8,128)(2,1)}, bf16[96,768]{1,0:T(8,128)(2,1)S(1)}, u32[]{:S(2)}, u32[]{:S(2)}) collective-permute-start(bf16[96,768]{1,0:T(8,128)(2,1)} %get-tuple-element.283), channel_id=1, source_target_pairs={{0,8},{4,12},{8,0},{12,4},{16,24},{20,28},{24,16},{28,20},{1,9},{5... | collective-permute-start | bytes 442376 | tf_op jit(solution)/shard_map/ppermute | solution.py:43
  183.5 12.6 %collective-permute-start.50 = (bf16[96,768]{1,0:T(8,128)(2,1)}, bf16[96,768]{1,0:T(8,128)(2,1)S(1)}, u32[]{:S(2)}, u32[]{:S(2)}) collective-permute-start(bf16[96,768]{1,0:T(8,128)(2,1)} %get-tuple-element.284), channel_id=1, source_target_pairs={{0,16},{4,20},{8,24},{12,28},{16,0},{20,4},{24,8},{28,12},{1,17},{... | collective-permute-start | bytes 442376 | tf_op jit(solution)/shard_map/ppermute | solution.py:43
  183.7 12.5 %collective-permute-start.51 = (bf16[96,768]{1,0:T(8,128)(2,1)}, bf16[96,768]{1,0:T(8,128)(2,1)S(1)}, u32[]{:S(2)}, u32[]{:S(2)}) collective-permute-start(bf16[96,768]{1,0:T(8,128)(2,1)} %get-tuple-element.285), channel_id=1, source_target_pairs={{0,24},{4,28},{8,16},{12,20},{16,8},{20,12},{24,0},{28,4},{1,25},{... | collective-permute-start | bytes 442376 | tf_op jit(solution)/shard_map/ppermute | solution.py:43
  (28 other events, 283.0 us)

commit v6 on v5

--- a/solution.py
+++ b/solution.py
@@ -297,12 +297,13 @@
     ubs, out = refs[:4], refs[4]
     vecs = jnp.concatenate([zero[...], one[...], two[...]])
     width = D // out.shape[0]
-    out[...] = jnp.zeros(out.shape, F32)
+    vecs = vecs.astype(BF16)
+    out[...] = jnp.zeros(out.shape, BF16)
     for i in range(out.shape[0]):
         out[i, 0:8, 0:width] = vecs[:, width * i : width * i + width]
     for spot in range(4):
         for kz in range(4):
-            to, ub = slot_of(spot, kz), ubs[spot]
+            to, ub = slot_of(spot, kz), ubs[spot][...].astype(BF16)
             out[to, 0:1, 24 : 24 + ONE] = ub[:, ONE * kz : ONE * kz + ONE]
             at = 4 * ONE + TWO * kz
             out[to, 0:1, 24 + ONE : 24 + ONE + TWO] = ub[:, at : at + TWO]
@@ -311,7 +312,7 @@
 def exchange_terms(zero, one, two, ubs, devices):
     return call(
         exchange_kernel,
-        (shape((devices, 8, 128), F32),),
+        (shape((devices, 8, 128)),),
         (zero, one, two, *ubs),
         cost=est(1000, 1000),
         limit=8,
@@ -560,7 +561,7 @@
         outs,
         operands,
         scratch=scratch,
-        cost=est(2 * n * D * 1152 + 8 * n * n * 384, 12e6, 6 * n * n),
+        cost=est(1000, 1000),
         limit=32,
         far_in=range(2, len(operands)),
         sems=50,
@@ -600,7 +601,7 @@
         first_kernel,
         (shape((n, D)), shape((n, D), F32), shape((n, D), F32), shape((n, 128), F32)),
         (x, ctx_own, ctx_in, wp, small),
-        cost=est(2 * n * D * D, 5e6),
+        cost=est(1000, 1000),
         limit=8,
     )
 
@@ -663,32 +664,50 @@
     )
 
 
-def second_kernel(
-    bucket, lengths, first, part, got, small, cot, out, sum_two, low, sums
-):
+def second_kernel(bucket, lengths, first, part, got, small, cot, low, sum_two, normal):
     c = place_here()[0]
     _, units = live_units(bucket, lengths)
     n, r = norm(first[...] + (part[...] + got[...].astype(F32) + small[5:6]))
-    out[...] = (n * small[6:7] + small[7:8]).astype(BF16)
     index = lax.broadcasted_iota(jnp.int32, (first.shape[0], 1), 0)
     live = live_of(place_of(index, c), units)
     oc = jnp.where(live, cot[...].astype(F32), 0.0)
     st = norm_back(oc, n, r, small[6:7])
+    low[...] = st.astype(BF16)
     sum_two[...] = st
-    lo = st.astype(BF16)
-    low[...] = lo
-    sums[0:1] = jnp.sum(lo.astype(F32), 0, keepdims=True)
-    sums[1:2] = jnp.sum(oc * n, 0, keepdims=True)
-    sums[2:3] = jnp.sum(oc, 0, keepdims=True)
+    normal[...] = n
 
 
 def second_norm(bucket, lengths, first, part, got, small, cot):
     n = first.shape[0]
     return call(
         second_kernel,
-        (shape((n, D)), shape((n, D), F32), shape((n, D)), shape((3, D), F32)),
+        (shape((n, D)), shape((n, D), F32), shape((n, D), F32)),
         (bucket, lengths, first, part, got, small, cot),
-        cost=est(40 * n * D, 5e6),
+        cost=est(1000, 1000),
+        limit=8,
+    )
+
+
+def second_rest_kernel(bucket, lengths, normal, small, cot, low, out, sums):
+    c = place_here()[0]
+    _, units = live_units(bucket, lengths)
+    n = normal[...]
+    out[...] = (n * small[6:7] + small[7:8]).astype(BF16)
+    index = lax.broadcasted_iota(jnp.int32, (normal.shape[0], 1), 0)
+    live = live_of(place_of(index, c), units)
+    oc = jnp.where(live, cot[...].astype(F32), 0.0)
+    sums[0:1] = jnp.sum(low[...].astype(F32), 0, keepdims=True)
+    sums[1:2] = jnp.sum(oc * n, 0, keepdims=True)
+    sums[2:3] = jnp.sum(oc, 0, keepdims=True)
+
+
+def second_rest(bucket, lengths, normal, small, cot, low):
+    n = normal.shape[0]
+    return call(
+        second_rest_kernel,
+        (shape((n, D)), shape((3, D), F32)),
+        (bucket, lengths, normal, small, cot, low),
+        cost=est(1000, 1000),
         limit=8,
     )
 
@@ -1011,7 +1030,7 @@
             len(kept) == len(f_all) - 1,
         )
         kept.append((hid, slope))
-    layer_out, sum_two, down_low, sums_two = second_norm(
+    down_low, sum_two, second_n = second_norm(
         bucket, lengths, first, sums[0], core_swap(sums[1]), small_all, cotangent
     )
     down_in = core_swap(down_low)
@@ -1042,11 +1061,14 @@
             f_parts.append(grads)
             ub_parts.append(ub)
     part_own, part_other = sums
+    layer_out, sums_two = second_rest(
+        bucket, lengths, after(second_n, part_other), small_all, cotangent, down_low
+    )
+    sum_two = after(sum_two, sums_two)
     moved = ()
     if direct:
         (d_lo, d_hi), y_sets, x_sets, z_sets = f_parts
         moved = (*x_sets, y_swap(d_hi), *y_sets, x_swap(d_lo))
-        part_other = after(part_other, moved)
     added, sum_one, attn_low, sums_one = first_back(
         sum_two, part_own, core_swap(part_other), first_n, first_r, small_all, moved
     )
@@ -1070,12 +1092,12 @@
 
     if direct:
         up_sets = scatter_xy(z_sets[0], *added[:2])
-        terms = exchange_terms(sums_zero, sums_one, sums_two, ub_parts, devices)
         a_zz, a_xx, a_yy, by_x, by_y = a_grads
         by_x, by_y, up_sets = lax.optimization_barrier((by_x, by_y, up_sets))
         by_x, by_y = x_swap(by_x), y_swap(by_y)
         up_mine, up_others = combine(*up_sets)
-        terms = after(terms, up_others)
+        sums_zero = after(sums_zero, up_others)
+        terms = exchange_terms(sums_zero, sums_one, sums_two, ub_parts, devices)
         terms = lax.all_to_all(terms, ("batch", "head"), split_axis=0, concat_axis=0, tiled=True)
         up_others = scatter_z(up_others)
         by_x, by_y, up_others, terms, _ = lax.optimization_barrier(
@@ -1089,7 +1111,7 @@
         a_others = scatter_z(a_others)
         up_grad, down_grad = finish_ffn((up_mine, *up_others), (down_mine, *down_others))
         up_grad = up_grad.T
-        terms = jnp.sum(terms, 0)
+        terms = jnp.sum(terms.astype(F32), 0)
         packed = jnp.concatenate([terms[:, :wp].reshape(-1), terms[0, wp : wp + wf]])
         qkv_grad, proj_grad = finish_attend((a_mine, *a_others))
     else:

time: 197 us -> 193 us (0.980)
  waiting for transfers between devices: 79.6 us -> 77.4 us
    all_to_all x1, waiting for transfers between devices: 2.74 us -> 6.9 us  [local(): lax.all_to_all(terms, ('batch', 'head'), split_axis=0, concat_axis=0, til...]
    ppermute x19, waiting for transfers between devices: 49.5 us -> 46.4 us  [z_swap(): return lax.ppermute(v, 'batch', ZPAIR[k])]
    ppermute x10, waiting for transfers between devices: 14.7 us -> 12.3 us  [y_swap(): return lax.ppermute(v, 'batch', YPAIR)]
    pallas_call x21 -> x22, Pallas kernels: 48.1 us -> 48.4 us  [call(): pl.pallas_call(kernel, out_shape=out_shape, in_specs=ins, out_specs=outs,...]
  transfers between devices with their start and end apart: 53 -> 53, of which waited for: 25 -> 24; matrix products, arithmetic and copies ran while one was open for 2% -> 2% of each run, Pallas kernels for 18% -> 20%
where the time goes in v6:
time: 193 us; the launch traced here: 192 us
  waiting for transfers between devices  77.4 us (40%)
  starting transfers between devices  60.2 us (31%)
  Pallas kernels  48.4 us (25%)
  local copies, waits for them, and re-layouts  2.81 us (1%)
  other arithmetic  2.4 us (1%)
    pallas_call x22, Pallas kernels, call(): pl.pallas_call(kernel, out_shape=out_shape, in_specs=ins, out_specs=outs,...  48.4 us
    ppermute x19, waiting for transfers between devices, z_swap(): return lax.ppermute(v, 'batch', ZPAIR[k])  46.4 us
    ppermute x19, starting transfers between devices, z_swap(): return lax.ppermute(v, 'batch', ZPAIR[k])  31 us
    ppermute x10, starting transfers between devices, x_swap(): return lax.ppermute(v, 'head', XPAIR)  13.1 us
    ppermute x10, waiting for transfers between devices, y_swap(): return lax.ppermute(v, 'batch', YPAIR)  12.3 us
    ppermute x10, starting transfers between devices, y_swap(): return lax.ppermute(v, 'batch', YPAIR)  10.5 us
    all_to_all x1, waiting for transfers between devices, local(): lax.all_to_all(terms, ('batch', 'head'), split_axis=0, concat_axis=0, til...  6.9 us
    ppermute x10, waiting for transfers between devices, x_swap(): return lax.ppermute(v, 'head', XPAIR)  5.88 us
  transfers between devices with their start and end apart: 53, of which 24 were waited for; matrix products, arithmetic and copies ran while one was open for 2% of the time, Pallas kernels for 20%

profile of v6, /device:TPU:0, one launch (start us, length us, event | category | flops | bytes accessed | tf_op | source)
XLA Modules:
  0.0 192.4 jit_solution(15330557959647614451)
XLA Ops:
  2.0 3.1 %collective-permute-start = (bf16[104,768]{1,0:T(8,128)(2,1)S(1)}, bf16[104,768]{1,0:T(8,128)(2,1)S(1)}, u32[]{:S(2)}, u32[]{:S(2)}) collective-permute-start(bf16[104,768]{1,0:T(8,128)(2,1)S(1)} %get-tuple-element.159), channel_id=1, source_target_pairs={{0,8},{4,12},{8,0},{12,4},{16,24},{20,28},{24,16},{28,20},{1,9},{5... | collective-permute-start | bytes 479240 | tf_op jit(solution)/shard_map/ppermute | solution.py:43
  5.1 2.5 %collective-permute-start.2 = (bf16[104,768]{1,0:T(8,128)(2,1)S(1)}, bf16[104,768]{1,0:T(8,128)(2,1)S(1)}, u32[]{:S(2)}, u32[]{:S(2)}) collective-permute-start(bf16[104,768]{1,0:T(8,128)(2,1)S(1)} %get-tuple-element.159), channel_id=1, source_target_pairs={{0,24},{4,28},{8,16},{12,20},{16,8},{20,12},{24,0},{28,4},{1,25},{... | collective-permute-start | bytes 479240 | tf_op jit(solution)/shard_map/ppermute | solution.py:43
  7.7 1.9 collective-permute-done
  9.6 1.5 collective-permute-start.4
  11.1 1.5 collective-permute-start.3
  13.7 1.5 collective-permute-start.5
  15.2 1.5 collective-permute-start.6
  16.7 5.1 %collective-permute-done.1 = bf16[104,768]{1,0:T(8,128)(2,1)S(1)} collective-permute-done((bf16[104,768]{1,0:T(8,128)(2,1)S(1)}, bf16[104,768]{1,0:T(8,128)(2,1)S(1)}, u32[]{:S(2)}, u32[]{:S(2)}) %collective-permute-start.1) | collective-permute-done | bytes 159776 | tf_op jit(solution)/shard_map/ppermute | solution.py:43
  21.9 1.6 collective-permute-start.9
  23.5 1.5 collective-permute-start.8
  25.0 2.6 %collective-permute-start.12 = (bf16[104,768]{1,0:T(8,128)(2,1)S(1)}, bf16[104,768]{1,0:T(8,128)(2,1)S(1)}, u32[]{:S(2)}, u32[]{:S(2)}) collective-permute-start(bf16[104,768]{1,0:T(8,128)(2,1)S(1)} %get-tuple-element.167), channel_id=1, source_target_pairs={{0,24},{4,28},{8,16},{12,20},{16,8},{20,12},{24,0},{28,4},{1,25},{... | collective-permute-start | bytes 479240 | tf_op jit(solution)/shard_map/ppermute | solution.py:43
  27.7 1.7 collective-permute-start.10
  29.4 4.5 %collective-permute-done.12 = bf16[104,768]{1,0:T(8,128)(2,1)S(1)} collective-permute-done((bf16[104,768]{1,0:T(8,128)(2,1)S(1)}, bf16[104,768]{1,0:T(8,128)(2,1)S(1)}, u32[]{:S(2)}, u32[]{:S(2)}) %collective-permute-start.12) | collective-permute-done | bytes 159776 | tf_op jit(solution)/shard_map/ppermute | solution.py:43
  33.9 5.9 %collective-permute-done.11 = bf16[104,768]{1,0:T(8,128)(2,1)S(1)} collective-permute-done((bf16[104,768]{1,0:T(8,128)(2,1)S(1)}, bf16[104,768]{1,0:T(8,128)(2,1)S(1)}, u32[]{:S(2)}, u32[]{:S(2)}) %collective-permute-start.11) | collective-permute-done | bytes 159776 | tf_op jit(solution)/shard_map/ppermute | solution.py:43
  41.1 2.4 %collective-permute-start.15 = (bf16[56,768]{1,0:T(8,128)(2,1)S(1)}, bf16[56,768]{1,0:T(8,128)(2,1)S(1)}, u32[]{:S(2)}, u32[]{:S(2)}) collective-permute-start(bf16[56,768]{1,0:T(8,128)(2,1)S(1)} %get-tuple-element.172), channel_id=1, source_target_pairs={{0,24},{4,28},{8,16},{12,20},{16,8},{20,12},{24,0},{28,4},{1,25},{... | collective-permute-start | bytes 258056 | tf_op jit(solution)/shard_map/ppermute | solution.py:43
  44.6 6.8 %collective-permute-done.15 = bf16[56,768]{1,0:T(8,128)(2,1)S(1)} collective-permute-done((bf16[56,768]{1,0:T(8,128)(2,1)S(1)}, bf16[56,768]{1,0:T(8,128)(2,1)S(1)}, u32[]{:S(2)}, u32[]{:S(2)}) %collective-permute-start.15) | collective-permute-done | bytes 86048 | tf_op jit(solution)/shard_map/ppermute | solution.py:43
  52.8 1.5 collective-permute-start.26
  54.3 1.5 collective-permute-start.25
  59.7 10.4 %shard_map.281 = (bf16[256,384]{1,0:T(8,128)(2,1)S(1)}, bf16[256,384]{1,0:T(8,128)(2,1)S(1)}, bf16[512,384]{1,0:T(8,128)(2,1)S(1)}, bf16[512,384]{1,0:T(8,128)(2...) custom-call(s32[2]{0:T(128)S(1)} %copy-done.10, ...), custom_call_target="tpu_custom_call" | custom-call | flops 1000 | bytes 1000 | tf_op jit(solution)/shard_map/pallas_call | solution.py:108
  72.7 4.3 %collective-permute-done.27.refs_2_.refs_4_.refs_3_ = bf16[8,32,768]{2,1,0:T(8,128)(2,1)S(1)} collective-permute-done((bf16[8,32,768]{2,1,0:T(8,128)(2,1)S(1)}, bf16[8,32,768]{2,1,0:T(8,128)(2,1)S(1)}, u32[]{:S(2)}, u32[]{:S(2)}) %collective-permute-start.27) | collective-permute-done | bytes 393248 | tf_op jit(solution)/shard_map/ppermute | solution.py:43
  78.8 1.5 collective-permute-start.28
  83.0 1.5 shard_map.285
  85.7 5.0 %collective-permute-done.29.refs_1_ = bf16[2,160,768]{2,1,0:T(8,128)(2,1)S(1)} collective-permute-done((bf16[2,160,768]{2,1,0:T(8,128)(2,1)S(1)}, bf16[2,160,768]{2,1,0:T(8,128)(2,1)S(1)}, u32[]{:S(2)}, u32[]{:S(2)}) %collective-permute-start.29) | collective-permute-done | bytes 491552 | tf_op jit(solution)/shard_map/ppermute | solution.py:39
  92.4 1.7 collective-permute-done.30.got
  95.6 1.6 collective-permute-done.31.d1
  97.1 1.8 shard_map.289
  100.5 1.5 collective-permute-start.34
  102.0 1.9 shard_map.290
  103.8 1.9 shard_map.291
  105.7 1.9 shard_map.292
  107.7 1.6 shard_map.293
  109.4 5.0 %collective-permute-done.33.refs_2_ = bf16[2,192,768]{2,1,0:T(8,128)(2,1)S(1)} collective-permute-done((bf16[2,192,768]{2,1,0:T(8,128)(2,1)S(1)}, bf16[2,192,768]{2,1,0:T(8,128)(2,1)S(1)}, u32[]{:S(2)}, u32[]{:S(2)}) %collective-permute-start.33) | collective-permute-done | bytes 589856 | tf_op jit(solution)/shard_map/ppermute | solution.py:39
  116.7 1.5 collective-permute-start.37
  118.9 10.3 %shard_map.295 = (bf16[4,96,768]{2,1,0:T(8,128)(2,1)}, bf16[4,96,768]{2,1,0:T(8,128)(2,1)}, bf16[4,96,768]{2,1,0:T(8,128)(2,1)}, bf16[6,96,768]{2,1,0:T(8,128)(2...) custom-call(bf16[256,768]{1,0:T(8,128)(2,1)S(1)} %get-tuple-element.241.a, ...), custom_call_target="tpu_custom_call" | custom-call | flops 8000000000 | bytes 14000000 | tf_op jit(solution)/shard_map/pallas_call | solution.py:108
  129.2 3.2 %collective-permute-done.37.x = bf16[4,96,768]{2,1,0:T(8,128)(2,1)S(1)} collective-permute-done((bf16[4,96,768]{2,1,0:T(8,128)(2,1)S(1)}, bf16[4,96,768]{2,1,0:T(8,128)(2,1)S(1)}, u32[]{:S(2)}, u32[]{:S(2)}) %collective-permute-start.37) | collective-permute-done | bytes 589856 | tf_op jit(solution)/shard_map/ppermute | solution.py:35
  137.2 1.7 collective-permute-start.42
  139.8 3.5 %all-to-all-start = ((bf16[32,8,128]{2,1,0:T(8,128)(2,1)}), bf16[32,8,128]{2,1,0:T(8,128)(2,1)S(1)}, u32[]{:S(2)}, u32[]{:S(2)}) async-start(bf16[32,8,128]{2,1,0:T(8,128)(2,1)} %shard_map.297), calls=%async_computation | async-start | bytes 131072 | tf_op jit(solution)/shard_map/all_to_all | solution.py:1101
  143.3 3.7 %collective-permute-start.43 = (bf16[96,768]{1,0:T(8,128)(2,1)}, bf16[96,768]{1,0:T(8,128)(2,1)}, u32[]{:S(2)}, u32[]{:S(2)}) collective-permute-start(bf16[96,768]{1,0:T(8,128)(2,1)} %get-tuple-element.268), channel_id=1, source_target_pairs={{0,24},{4,28},{8,16},{12,20},{16,8},{20,12},{24,0},{28,4},{1,25},{... | collective-permute-start | bytes 442376 | tf_op jit(solution)/shard_map/ppermute | solution.py:43
  147.0 2.0 %add_convert_fusion = bf16[256,768]{1,0:T(8,128)(2,1)} fusion(f32[256,768]{1,0:T(8,128)} %collective-permute-done.36, f32[256,768]{1,0:T(8,128)S(1)} %get-tuple-element.240, f32[256,768]{1,0:T(8,128)S(1)} %get-tuple-element.250), kind=kLoop, calls=%fused_computation.1 | loop fusion | flops 589824 | bytes 2752512 | tf_op jit(solution)/shard_map/convert_element_type | solution.py:1091
  149.0 6.9 %all-to-all-done = bf16[32,8,128]{2,1,0:T(8,128)(2,1)S(1)} async-done(((bf16[32,8,128]{2,1,0:T(8,128)(2,1)}), bf16[32,8,128]{2,1,0:T(8,128)(2,1)S(1)}, u32[]{:S(2)}, u32[]{:S(2)}) %all-to-all-start) | async-done | bytes 65568 | tf_op jit(solution)/shard_map/all_to_all | solution.py:1101
  155.9 2.3 %shard_map.298 = (bf16[4,96,768]{2,1,0:T(8,128)(2,1)S(1)}, bf16[4,96,768]{2,1,0:T(8,128)(2,1)S(1)}, f32[96,768]{1,0:T(8,128)}, bf16[96,768]{1,0:T(8,128)(2,1)}, ...) custom-call(bf16[4,96,768]{2,1,0:T(8,128)(2,1)S(1)} %copy-done.3, bf16[4,96,768]{2,1,0:T(8,128)(2,1)S(1)} %copy-done.4, ...), custom_call_target="tpu_custom_call" | custom-call | flops 1000 | bytes 1000 | tf_op jit(solution)/shard_map/pallas_call | solution.py:108
  161.7 1.7 collective-permute-start.47
  165.3 2.4 %collective-permute-done.46.refs_5_ = bf16[96,768]{1,0:T(8,128)(2,1)S(1)} collective-permute-done((bf16[96,768]{1,0:T(8,128)(2,1)}, bf16[96,768]{1,0:T(8,128)(2,1)S(1)}, u32[]{:S(2)}, u32[]{:S(2)}) %collective-permute-start.46) | collective-permute-done | bytes 147488 | tf_op jit(solution)/shard_map/ppermute | solution.py:43
  167.7 7.7 %collective-permute-done.47.refs_6_ = bf16[96,768]{1,0:T(8,128)(2,1)S(1)} collective-permute-done((bf16[96,768]{1,0:T(8,128)(2,1)}, bf16[96,768]{1,0:T(8,128)(2,1)S(1)}, u32[]{:S(2)}, u32[]{:S(2)}) %collective-permute-start.47) | collective-permute-done | bytes 147488 | tf_op jit(solution)/shard_map/ppermute | solution.py:43
  176.3 2.5 %collective-permute-start.49 = (bf16[96,768]{1,0:T(8,128)(2,1)}, bf16[96,768]{1,0:T(8,128)(2,1)S(1)}, u32[]{:S(2)}, u32[]{:S(2)}) collective-permute-start(bf16[96,768]{1,0:T(8,128)(2,1)} %get-tuple-element.287), channel_id=1, source_target_pairs={{0,8},{4,12},{8,0},{12,4},{16,24},{20,28},{24,16},{28,20},{1,9},{5... | collective-permute-start | bytes 442376 | tf_op jit(solution)/shard_map/ppermute | solution.py:43
  178.9 2.3 %collective-permute-start.51 = (bf16[96,768]{1,0:T(8,128)(2,1)}, bf16[96,768]{1,0:T(8,128)(2,1)S(1)}, u32[]{:S(2)}, u32[]{:S(2)}) collective-permute-start(bf16[96,768]{1,0:T(8,128)(2,1)} %get-tuple-element.289), channel_id=1, source_target_pairs={{0,24},{4,28},{8,16},{12,20},{16,8},{20,12},{24,0},{28,4},{1,25},{... | collective-permute-start | bytes 442376 | tf_op jit(solution)/shard_map/ppermute | solution.py:43
  181.8 1.9 shard_map.301
  183.7 7.8 %collective-permute-done.50.two = bf16[96,768]{1,0:T(8,128)(2,1)S(1)} collective-permute-done((bf16[96,768]{1,0:T(8,128)(2,1)}, bf16[96,768]{1,0:T(8,128)(2,1)S(1)}, u32[]{:S(2)}, u32[]{:S(2)}) %collective-permute-start.50) | collective-permute-done | bytes 147488 | tf_op jit(solution)/shard_map/ppermute | solution.py:43
  (145 shorter events, 39.6 us)
Async XLA Ops:
  2.0 7.6 %collective-permute-start = (bf16[104,768]{1,0:T(8,128)(2,1)S(1)}, bf16[104,768]{1,0:T(8,128)(2,1)S(1)}, u32[]{:S(2)}, u32[]{:S(2)}) collective-permute-start(bf16[104,768]{1,0:T(8,128)(2,1)S(1)} %get-tuple-element.159), channel_id=1, source_target_pairs={{0,8},{4,12},{8,0},{12,4},{16,24},{20,28},{24,16},{28,20},{1,9},{5... | collective-permute-start | bytes 479240 | tf_op jit(solution)/shard_map/ppermute | solution.py:43
  5.1 11.6 %collective-permute-start.2 = (bf16[104,768]{1,0:T(8,128)(2,1)S(1)}, bf16[104,768]{1,0:T(8,128)(2,1)S(1)}, u32[]{:S(2)}, u32[]{:S(2)}) collective-permute-start(bf16[104,768]{1,0:T(8,128)(2,1)S(1)} %get-tuple-element.159), channel_id=1, source_target_pairs={{0,24},{4,28},{8,16},{12,20},{16,8},{20,12},{24,0},{28,4},{1,25},{... | collective-permute-start | bytes 479240 | tf_op jit(solution)/shard_map/ppermute | solution.py:43
  7.5 14.2 %collective-permute-start.1 = (bf16[104,768]{1,0:T(8,128)(2,1)S(1)}, bf16[104,768]{1,0:T(8,128)(2,1)S(1)}, u32[]{:S(2)}, u32[]{:S(2)}) collective-permute-start(bf16[104,768]{1,0:T(8,128)(2,1)S(1)} %get-tuple-element.159), channel_id=1, source_target_pairs={{0,16},{4,20},{8,24},{12,28},{16,0},{20,4},{24,8},{28,12},{1,17},{... | collective-permute-start | bytes 479240 | tf_op jit(solution)/shard_map/ppermute | solution.py:43
  9.6 4.1 %collective-permute-start.4 = (bf16[32,768]{1,0:T(8,128)(2,1)S(1)}, bf16[32,768]{1,0:T(8,128)(2,1)S(1)}, u32[]{:S(2)}, u32[]{:S(2)}) collective-permute-start(bf16[32,768]{1,0:T(8,128)(2,1)S(1)} %get-tuple-element.161), channel_id=1, source_target_pairs={{0,4},{4,0},{8,12},{12,8},{16,20},{20,16},{24,28},{28,24},{1,5},{5... | collective-permute-start | bytes 147464 | tf_op jit(solution)/shard_map/ppermute | solution.py:39
  11.1 4.1 %collective-permute-start.3 = (bf16[32,768]{1,0:T(8,128)(2,1)S(1)}, bf16[32,768]{1,0:T(8,128)(2,1)S(1)}, u32[]{:S(2)}, u32[]{:S(2)}) collective-permute-start(bf16[32,768]{1,0:T(8,128)(2,1)S(1)} %get-tuple-element.161), channel_id=1, source_target_pairs={{0,2},{1,3},{2,0},{3,1},{4,6},{5,7},{6,4},{7,5},{8,10},{9,11},{10,... | collective-permute-start | bytes 147464 | tf_op jit(solution)/shard_map/ppermute | solution.py:35
  12.6 9.3 %collective-permute-start.7 = (bf16[256,768]{1,0:T(8,128)(2,1)}, bf16[256,768]{1,0:T(8,128)(2,1)S(1)}, u32[]{:S(2)}, u32[]{:S(2)}) collective-permute-start(bf16[256,768]{1,0:T(8,128)(2,1)} %refs_8_.1), channel_id=1, source_target_pairs={{0,1},{1,0},{2,3},{3,2},{4,5},{5,4},{6,7},{7,6},{8,9},{9,8},{10,11... | collective-permute-start | bytes 1179656 | tf_op jit(solution)/shard_map/ppermute | solution.py:31
  13.7 8.2 %collective-permute-start.5 = (bf16[16,768]{1,0:T(8,128)(2,1)S(1)}, bf16[16,768]{1,0:T(8,128)(2,1)S(1)}, u32[]{:S(2)}, u32[]{:S(2)}) collective-permute-start(bf16[16,768]{1,0:T(8,128)(2,1)S(1)} %slice.129), channel_id=1, source_target_pairs={{0,2},{1,3},{2,0},{3,1},{4,6},{5,7},{6,4},{7,5},{8,10},{9,11},{10,... | collective-permute-start | bytes 73736 | tf_op jit(solution)/shard_map/ppermute | solution.py:35
  15.2 6.7 %collective-permute-start.6 = (bf16[16,768]{1,0:T(8,128)(2,1)S(1)}, bf16[16,768]{1,0:T(8,128)(2,1)S(1)}, u32[]{:S(2)}, u32[]{:S(2)}) collective-permute-start(bf16[16,768]{1,0:T(8,128)(2,1)S(1)} %slice.130), channel_id=1, source_target_pairs={{0,4},{4,0},{8,12},{12,8},{16,20},{20,16},{24,28},{28,24},{1,5},{5... | collective-permute-start | bytes 73736 | tf_op jit(solution)/shard_map/ppermute | solution.py:39
  21.9 17.9 %collective-permute-start.9 = (bf16[4,104,768]{2,1,0:T(8,128)(2,1)S(1)}, bf16[4,104,768]{2,1,0:T(8,128)(2,1)S(1)}, u32[]{:S(2)}, u32[]{:S(2)}) collective-permute-start(bf16[4,104,768]{2,1,0:T(8,128)(2,1)S(1)} %pad_maximum_fusion.1.refs_0_), channel_id=1, source_target_pairs={{0,4},{4,0},{8,12},{12,8},{16,20},{20,16},{24,28},{28,24},{1,5},{5... | collective-permute-start | bytes 1916936 | tf_op jit(solution)/shard_map/ppermute | solution.py:39
  23.5 16.3 %collective-permute-start.8 = (bf16[4,104,768]{2,1,0:T(8,128)(2,1)S(1)}, bf16[4,104,768]{2,1,0:T(8,128)(2,1)S(1)}, u32[]{:S(2)}, u32[]{:S(2)}) collective-permute-start(bf16[4,104,768]{2,1,0:T(8,128)(2,1)S(1)} %pad_maximum_fusion.1.refs_0_), channel_id=1, source_target_pairs={{0,2},{1,3},{2,0},{3,1},{4,6},{5,7},{6,4},{7,5},{8,10},{9,11},{10,... | collective-permute-start | bytes 1916936 | tf_op jit(solution)/shard_map/ppermute | solution.py:35
  25.0 8.8 %collective-permute-start.12 = (bf16[104,768]{1,0:T(8,128)(2,1)S(1)}, bf16[104,768]{1,0:T(8,128)(2,1)S(1)}, u32[]{:S(2)}, u32[]{:S(2)}) collective-permute-start(bf16[104,768]{1,0:T(8,128)(2,1)S(1)} %get-tuple-element.167), channel_id=1, source_target_pairs={{0,24},{4,28},{8,16},{12,20},{16,8},{20,12},{24,0},{28,4},{1,25},{... | collective-permute-start | bytes 479240 | tf_op jit(solution)/shard_map/ppermute | solution.py:43
  27.7 12.1 %collective-permute-start.11 = (bf16[104,768]{1,0:T(8,128)(2,1)S(1)}, bf16[104,768]{1,0:T(8,128)(2,1)S(1)}, u32[]{:S(2)}, u32[]{:S(2)}) collective-permute-start(bf16[104,768]{1,0:T(8,128)(2,1)S(1)} %get-tuple-element.167), channel_id=1, source_target_pairs={{0,16},{4,20},{8,24},{12,28},{16,0},{20,4},{24,8},{28,12},{1,17},{... | collective-permute-start | bytes 479240 | tf_op jit(solution)/shard_map/ppermute | solution.py:43
  27.7 12.1 %collective-permute-start.10 = (bf16[104,768]{1,0:T(8,128)(2,1)S(1)}, bf16[104,768]{1,0:T(8,128)(2,1)S(1)}, u32[]{:S(2)}, u32[]{:S(2)}) collective-permute-start(bf16[104,768]{1,0:T(8,128)(2,1)S(1)} %get-tuple-element.167), channel_id=1, source_target_pairs={{0,8},{4,12},{8,0},{12,4},{16,24},{20,28},{24,16},{28,20},{1,9},{5... | collective-permute-start | bytes 479240 | tf_op jit(solution)/shard_map/ppermute | solution.py:43
  39.9 11.5 %collective-permute-start.17 = (bf16[2,104,768]{2,1,0:T(8,128)(2,1)S(1)}, bf16[2,104,768]{2,1,0:T(8,128)(2,1)S(1)}, u32[]{:S(2)}, u32[]{:S(2)}) collective-permute-start(bf16[2,104,768]{2,1,0:T(8,128)(2,1)S(1)} %slice.102), channel_id=1, source_target_pairs={{0,4},{4,0},{8,12},{12,8},{16,20},{20,16},{24,28},{28,24},{1,5},{5... | collective-permute-start | bytes 958472 | tf_op jit(solution)/shard_map/ppermute | solution.py:39
  40.5 10.9 %collective-permute-start.16 = (bf16[2,104,768]{2,1,0:T(8,128)(2,1)S(1)}, bf16[2,104,768]{2,1,0:T(8,128)(2,1)S(1)}, u32[]{:S(2)}, u32[]{:S(2)}) collective-permute-start(bf16[2,104,768]{2,1,0:T(8,128)(2,1)S(1)} %slice.101), channel_id=1, source_target_pairs={{0,2},{1,3},{2,0},{3,1},{4,6},{5,7},{6,4},{7,5},{8,10},{9,11},{10,... | collective-permute-start | bytes 958472 | tf_op jit(solution)/shard_map/ppermute | solution.py:35
  41.0 10.3 %collective-permute-start.13 = (bf16[184,768]{1,0:T(8,128)(2,1)S(1)}, bf16[184,768]{1,0:T(8,128)(2,1)S(1)}, u32[]{:S(2)}, u32[]{:S(2)}) collective-permute-start(bf16[184,768]{1,0:T(8,128)(2,1)S(1)} %pad_maximum_fusion.3), channel_id=1, source_target_pairs={{0,8},{4,12},{8,0},{12,4},{16,24},{20,28},{24,16},{28,20},{1,9},{5... | collective-permute-start | bytes 847880 | tf_op jit(solution)/shard_map/ppermute | solution.py:43
  41.1 10.2 %collective-permute-start.15 = (bf16[56,768]{1,0:T(8,128)(2,1)S(1)}, bf16[56,768]{1,0:T(8,128)(2,1)S(1)}, u32[]{:S(2)}, u32[]{:S(2)}) collective-permute-start(bf16[56,768]{1,0:T(8,128)(2,1)S(1)} %get-tuple-element.172), channel_id=1, source_target_pairs={{0,24},{4,28},{8,16},{12,20},{16,8},{20,12},{24,0},{28,4},{1,25},{... | collective-permute-start | bytes 258056 | tf_op jit(solution)/shard_map/ppermute | solution.py:43
  43.5 7.9 %collective-permute-start.14 = (bf16[56,768]{1,0:T(8,128)(2,1)S(1)}, bf16[56,768]{1,0:T(8,128)(2,1)S(1)}, u32[]{:S(2)}, u32[]{:S(2)}) collective-permute-start(bf16[56,768]{1,0:T(8,128)(2,1)S(1)} %get-tuple-element.172), channel_id=1, source_target_pairs={{0,16},{4,20},{8,24},{12,28},{16,0},{20,4},{24,8},{28,12},{1,17},{... | collective-permute-start | bytes 258056 | tf_op jit(solution)/shard_map/ppermute | solution.py:43
  52.2 3.6 %collective-permute-start.21 = (bf16[2,104,768]{2,1,0:T(8,128)(2,1)S(1)}, bf16[2,104,768]{2,1,0:T(8,128)(2,1)S(1)}, u32[]{:S(2)}, u32[]{:S(2)}) collective-permute-start(bf16[2,104,768]{2,1,0:T(8,128)(2,1)S(1)} %collective-permute-done.16.refs_3_), channel_id=1, source_target_pairs={{0,1},{1,0},{2,3},{3,2},{4,5},{5,4},{6,7},{7,6},{8,9},{9,8},{10,11... | collective-permute-start | bytes 958472 | tf_op jit(solution)/shard_map/ppermute | solution.py:31
  52.2 3.7 %collective-permute-start.22 = (bf16[2,104,768]{2,1,0:T(8,128)(2,1)S(1)}, bf16[2,104,768]{2,1,0:T(8,128)(2,1)S(1)}, u32[]{:S(2)}, u32[]{:S(2)}) collective-permute-start(bf16[2,104,768]{2,1,0:T(8,128)(2,1)S(1)} %collective-permute-done.17.refs_4_), channel_id=1, source_target_pairs={{0,1},{1,0},{2,3},{3,2},{4,5},{5,4},{6,7},{7,6},{8,9},{9,8},{10,11... | collective-permute-start | bytes 958472 | tf_op jit(solution)/shard_map/ppermute | solution.py:31
  52.7 3.8 %collective-permute-start.18 = (bf16[4,104,768]{2,1,0:T(8,128)(2,1)S(1)}, bf16[4,104,768]{2,1,0:T(8,128)(2,1)S(1)}, u32[]{:S(2)}, u32[]{:S(2)}) collective-permute-start(bf16[4,104,768]{2,1,0:T(8,128)(2,1)S(1)} %pad_maximum_fusion.1.refs_0_), channel_id=1, source_target_pairs={{0,1},{1,0},{2,3},{3,2},{4,5},{5,4},{6,7},{7,6},{8,9},{9,8},{10,11... | collective-permute-start | bytes 1916936 | tf_op jit(solution)/shard_map/ppermute | solution.py:31
  52.8 24.2 %collective-permute-start.26 = (bf16[4,160,768]{2,1,0:T(8,128)(2,1)S(1)}, bf16[4,160,768]{2,1,0:T(8,128)(2,1)S(1)}, u32[]{:S(2)}, u32[]{:S(2)}) collective-permute-start(bf16[4,160,768]{2,1,0:T(8,128)(2,1)S(1)} %pad_maximum_fusion.refs_0_), channel_id=1, source_target_pairs={{0,4},{4,0},{8,12},{12,8},{16,20},{20,16},{24,28},{28,24},{1,5},{5... | collective-permute-start | bytes 2949128 | tf_op jit(solution)/shard_map/ppermute | solution.py:39
  54.3 23.8 %collective-permute-start.25 = (bf16[4,160,768]{2,1,0:T(8,128)(2,1)S(1)}, bf16[4,160,768]{2,1,0:T(8,128)(2,1)S(1)}, u32[]{:S(2)}, u32[]{:S(2)}) collective-permute-start(bf16[4,160,768]{2,1,0:T(8,128)(2,1)S(1)} %pad_maximum_fusion.refs_0_), channel_id=1, source_target_pairs={{0,2},{1,3},{2,0},{3,1},{4,6},{5,7},{6,4},{7,5},{8,10},{9,11},{10,... | collective-permute-start | bytes 2949128 | tf_op jit(solution)/shard_map/ppermute | solution.py:35
  55.9 2.9 %collective-permute-start.20 = (bf16[4,104,768]{2,1,0:T(8,128)(2,1)S(1)}, bf16[4,104,768]{2,1,0:T(8,128)(2,1)S(1)}, u32[]{:S(2)}, u32[]{:S(2)}) collective-permute-start(bf16[4,104,768]{2,1,0:T(8,128)(2,1)S(1)} %collective-permute-done.9.refs_2_), channel_id=1, source_target_pairs={{0,1},{1,0},{2,3},{3,2},{4,5},{5,4},{6,7},{7,6},{8,9},{9,8},{10,11... | collective-permute-start | bytes 1916936 | tf_op jit(solution)/shard_map/ppermute | solution.py:31
  56.5 20.5 %collective-permute-start.27 = (bf16[8,32,768]{2,1,0:T(8,128)(2,1)S(1)}, bf16[8,32,768]{2,1,0:T(8,128)(2,1)S(1)}, u32[]{:S(2)}, u32[]{:S(2)}) collective-permute-start(bf16[8,32,768]{2,1,0:T(8,128)(2,1)S(1)} %pad_maximum_fusion.2), channel_id=1, source_target_pairs={{0,16},{4,20},{8,24},{12,28},{16,0},{20,4},{24,8},{28,12},{1,17},{... | collective-permute-start | bytes 1179656 | tf_op jit(solution)/shard_map/ppermute | solution.py:43
  72.5 7.9 %collective-permute-start.24 = (bf16[256,768]{1,0:T(8,128)(2,1)S(1)}, bf16[256,768]{1,0:T(8,128)(2,1)S(1)}, u32[]{:S(2)}, u32[]{:S(2)}) collective-permute-start(bf16[256,768]{1,0:T(8,128)(2,1)S(1)} %get-tuple-element.191.x0), channel_id=1, source_target_pairs={{0,1},{1,0},{2,3},{3,2},{4,5},{5,4},{6,7},{7,6},{8,9},{9,8},{10,11... | collective-permute-start | bytes 1179656 | tf_op jit(solution)/shard_map/ppermute | solution.py:31
  78.2 12.5 %collective-permute-start.29 = (bf16[2,160,768]{2,1,0:T(8,128)(2,1)S(1)}, bf16[2,160,768]{2,1,0:T(8,128)(2,1)S(1)}, u32[]{:S(2)}, u32[]{:S(2)}) collective-permute-start(bf16[2,160,768]{2,1,0:T(8,128)(2,1)S(1)} %slice.107), channel_id=1, source_target_pairs={{0,4},{4,0},{8,12},{12,8},{16,20},{20,16},{24,28},{28,24},{1,5},{5... | collective-permute-start | bytes 1474568 | tf_op jit(solution)/shard_map/ppermute | solution.py:39
  78.8 12.3 %collective-permute-start.28 = (bf16[2,160,768]{2,1,0:T(8,128)(2,1)S(1)}, bf16[2,160,768]{2,1,0:T(8,128)(2,1)S(1)}, u32[]{:S(2)}, u32[]{:S(2)}) collective-permute-start(bf16[2,160,768]{2,1,0:T(8,128)(2,1)S(1)} %slice.106), channel_id=1, source_target_pairs={{0,2},{1,3},{2,0},{3,1},{4,6},{5,7},{6,4},{7,5},{8,10},{9,11},{10,... | collective-permute-start | bytes 1474568 | tf_op jit(solution)/shard_map/ppermute | solution.py:35
  99.0 15.4 %collective-permute-start.33 = (bf16[2,192,768]{2,1,0:T(8,128)(2,1)S(1)}, bf16[2,192,768]{2,1,0:T(8,128)(2,1)S(1)}, u32[]{:S(2)}, u32[]{:S(2)}) collective-permute-start(bf16[2,192,768]{2,1,0:T(8,128)(2,1)S(1)} %get-tuple-element.236), channel_id=1, source_target_pairs={{0,4},{4,0},{8,12},{12,8},{16,20},{20,16},{24,28},{28,24},{1,5},{5... | collective-permute-start | bytes 1769480 | tf_op jit(solution)/shard_map/ppermute | solution.py:39
  100.5 15.1 %collective-permute-start.34 = (bf16[2,192,768]{2,1,0:T(8,128)(2,1)S(1)}, bf16[2,192,768]{2,1,0:T(8,128)(2,1)S(1)}, u32[]{:S(2)}, u32[]{:S(2)}) collective-permute-start(bf16[2,192,768]{2,1,0:T(8,128)(2,1)S(1)} %get-tuple-element.239), channel_id=1, source_target_pairs={{0,2},{1,3},{2,0},{3,1},{4,6},{5,7},{6,4},{7,5},{8,10},{9,11},{10,... | collective-permute-start | bytes 1769480 | tf_op jit(solution)/shard_map/ppermute | solution.py:35
  116.7 2.2 %collective-permute-start.35 = (bf16[256,768]{1,0:T(8,128)(2,1)S(1)}, bf16[256,768]{1,0:T(8,128)(2,1)S(1)}, u32[]{:S(2)}, u32[]{:S(2)}) collective-permute-start(bf16[256,768]{1,0:T(8,128)(2,1)S(1)} %get-tuple-element.241.a0), channel_id=1, source_target_pairs={{0,1},{1,0},{2,3},{3,2},{4,5},{5,4},{6,7},{7,6},{8,9},{9,8},{10,11... | collective-permute-start | bytes 1179656 | tf_op jit(solution)/shard_map/ppermute | solution.py:31
  116.7 15.7 %collective-permute-start.37 = (bf16[4,96,768]{2,1,0:T(8,128)(2,1)S(1)}, bf16[4,96,768]{2,1,0:T(8,128)(2,1)S(1)}, u32[]{:S(2)}, u32[]{:S(2)}) collective-permute-start(bf16[4,96,768]{2,1,0:T(8,128)(2,1)S(1)} %get-tuple-element.259), channel_id=1, source_target_pairs={{0,2},{1,3},{2,0},{3,1},{4,6},{5,7},{6,4},{7,5},{8,10},{9,11},{10,... | collective-permute-start | bytes 1769480 | tf_op jit(solution)/shard_map/ppermute | solution.py:35
  118.3 15.4 %collective-permute-start.38 = (bf16[4,96,768]{2,1,0:T(8,128)(2,1)S(1)}, bf16[4,96,768]{2,1,0:T(8,128)(2,1)S(1)}, u32[]{:S(2)}, u32[]{:S(2)}) collective-permute-start(bf16[4,96,768]{2,1,0:T(8,128)(2,1)S(1)} %get-tuple-element.260), channel_id=1, source_target_pairs={{0,4},{4,0},{8,12},{12,8},{16,20},{20,16},{24,28},{28,24},{1,5},{5... | collective-permute-start | bytes 1769480 | tf_op jit(solution)/shard_map/ppermute | solution.py:39
  129.2 14.1 %collective-permute-start.36 = (f32[256,768]{1,0:T(8,128)}, f32[256,768]{1,0:T(8,128)}, u32[]{:S(2)}, u32[]{:S(2)}) collective-permute-start(f32[256,768]{1,0:T(8,128)} %get-tuple-element.251), channel_id=1, source_target_pairs={{0,1},{1,0},{2,3},{3,2},{4,5},{5,4},{6,7},{7,6},{8,9},{9,8},{10,11... | collective-permute-start | bytes 2359304 | tf_op jit(solution)/shard_map/ppermute | solution.py:31
  133.7 22.2 %collective-permute-start.39 = (bf16[6,96,768]{2,1,0:T(8,128)(2,1)}, bf16[6,96,768]{2,1,0:T(8,128)(2,1)}, u32[]{:S(2)}, u32[]{:S(2)}) collective-permute-start(bf16[6,96,768]{2,1,0:T(8,128)(2,1)} %get-tuple-element.261), channel_id=1, source_target_pairs={{0,2},{1,3},{2,0},{3,1},{4,6},{5,7},{6,4},{7,5},{8,10},{9,11},{10,... | collective-permute-start | bytes 2654216 | tf_op jit(solution)/shard_map/ppermute | solution.py:35
  134.2 21.7 %collective-permute-start.40 = (bf16[6,96,768]{2,1,0:T(8,128)(2,1)}, bf16[6,96,768]{2,1,0:T(8,128)(2,1)}, u32[]{:S(2)}, u32[]{:S(2)}) collective-permute-start(bf16[6,96,768]{2,1,0:T(8,128)(2,1)} %get-tuple-element.262), channel_id=1, source_target_pairs={{0,4},{4,0},{8,12},{12,8},{16,20},{20,16},{24,28},{28,24},{1,5},{5... | collective-permute-start | bytes 2654216 | tf_op jit(solution)/shard_map/ppermute | solution.py:39
  135.8 20.1 %collective-permute-start.41 = (bf16[96,768]{1,0:T(8,128)(2,1)}, bf16[96,768]{1,0:T(8,128)(2,1)S(1)}, u32[]{:S(2)}, u32[]{:S(2)}) collective-permute-start(bf16[96,768]{1,0:T(8,128)(2,1)} %get-tuple-element.266), channel_id=1, source_target_pairs={{0,8},{4,12},{8,0},{12,4},{16,24},{20,28},{24,16},{28,20},{1,9},{5... | collective-permute-start | bytes 442376 | tf_op jit(solution)/shard_map/ppermute | solution.py:43
  137.2 18.7 %collective-permute-start.42 = (bf16[96,768]{1,0:T(8,128)(2,1)}, bf16[96,768]{1,0:T(8,128)(2,1)}, u32[]{:S(2)}, u32[]{:S(2)}) collective-permute-start(bf16[96,768]{1,0:T(8,128)(2,1)} %get-tuple-element.267), channel_id=1, source_target_pairs={{0,16},{4,20},{8,24},{12,28},{16,0},{20,4},{24,8},{28,12},{1,17},{... | collective-permute-start | bytes 442376 | tf_op jit(solution)/shard_map/ppermute | solution.py:43
  139.8 16.1 %all-to-all-start = ((bf16[32,8,128]{2,1,0:T(8,128)(2,1)}), bf16[32,8,128]{2,1,0:T(8,128)(2,1)S(1)}, u32[]{:S(2)}, u32[]{:S(2)}) async-start(bf16[32,8,128]{2,1,0:T(8,128)(2,1)} %shard_map.297), calls=%async_computation | async-start | bytes 131072 | tf_op jit(solution)/shard_map/all_to_all | solution.py:1101
  143.3 12.6 %collective-permute-start.43 = (bf16[96,768]{1,0:T(8,128)(2,1)}, bf16[96,768]{1,0:T(8,128)(2,1)}, u32[]{:S(2)}, u32[]{:S(2)}) collective-permute-start(bf16[96,768]{1,0:T(8,128)(2,1)} %get-tuple-element.268), channel_id=1, source_target_pairs={{0,24},{4,28},{8,16},{12,20},{16,8},{20,12},{24,0},{28,4},{1,25},{... | collective-permute-start | bytes 442376 | tf_op jit(solution)/shard_map/ppermute | solution.py:43
  158.2 17.2 %collective-permute-start.44 = (bf16[4,96,768]{2,1,0:T(8,128)(2,1)S(1)}, bf16[4,96,768]{2,1,0:T(8,128)(2,1)S(1)}, u32[]{:S(2)}, u32[]{:S(2)}) collective-permute-start(bf16[4,96,768]{2,1,0:T(8,128)(2,1)S(1)} %get-tuple-element.278), channel_id=1, source_target_pairs={{0,2},{1,3},{2,0},{3,1},{4,6},{5,7},{6,4},{7,5},{8,10},{9,11},{10,... | collective-permute-start | bytes 1769480 | tf_op jit(solution)/shard_map/ppermute | solution.py:35
  159.7 15.7 %collective-permute-start.45 = (bf16[4,96,768]{2,1,0:T(8,128)(2,1)S(1)}, bf16[4,96,768]{2,1,0:T(8,128)(2,1)S(1)}, u32[]{:S(2)}, u32[]{:S(2)}) collective-permute-start(bf16[4,96,768]{2,1,0:T(8,128)(2,1)S(1)} %get-tuple-element.279), channel_id=1, source_target_pairs={{0,4},{4,0},{8,12},{12,8},{16,20},{20,16},{24,28},{28,24},{1,5},{5... | collective-permute-start | bytes 1769480 | tf_op jit(solution)/shard_map/ppermute | solution.py:39
  160.3 7.4 %collective-permute-start.46 = (bf16[96,768]{1,0:T(8,128)(2,1)}, bf16[96,768]{1,0:T(8,128)(2,1)S(1)}, u32[]{:S(2)}, u32[]{:S(2)}) collective-permute-start(bf16[96,768]{1,0:T(8,128)(2,1)} %get-tuple-element.280), channel_id=1, source_target_pairs={{0,8},{4,12},{8,0},{12,4},{16,24},{20,28},{24,16},{28,20},{1,9},{5... | collective-permute-start | bytes 442376 | tf_op jit(solution)/shard_map/ppermute | solution.py:43
  161.7 13.7 %collective-permute-start.47 = (bf16[96,768]{1,0:T(8,128)(2,1)}, bf16[96,768]{1,0:T(8,128)(2,1)S(1)}, u32[]{:S(2)}, u32[]{:S(2)}) collective-permute-start(bf16[96,768]{1,0:T(8,128)(2,1)} %get-tuple-element.281), channel_id=1, source_target_pairs={{0,16},{4,20},{8,24},{12,28},{16,0},{20,4},{24,8},{28,12},{1,17},{... | collective-permute-start | bytes 442376 | tf_op jit(solution)/shard_map/ppermute | solution.py:43
  163.4 12.0 %collective-permute-start.48 = (bf16[96,768]{1,0:T(8,128)(2,1)}, bf16[96,768]{1,0:T(8,128)(2,1)S(1)}, u32[]{:S(2)}, u32[]{:S(2)}) collective-permute-start(bf16[96,768]{1,0:T(8,128)(2,1)} %get-tuple-element.282), channel_id=1, source_target_pairs={{0,24},{4,28},{8,16},{12,20},{16,8},{20,12},{24,0},{28,4},{1,25},{... | collective-permute-start | bytes 442376 | tf_op jit(solution)/shard_map/ppermute | solution.py:43
  176.3 7.4 %collective-permute-start.49 = (bf16[96,768]{1,0:T(8,128)(2,1)}, bf16[96,768]{1,0:T(8,128)(2,1)S(1)}, u32[]{:S(2)}, u32[]{:S(2)}) collective-permute-start(bf16[96,768]{1,0:T(8,128)(2,1)} %get-tuple-element.287), channel_id=1, source_target_pairs={{0,8},{4,12},{8,0},{12,4},{16,24},{20,28},{24,16},{28,20},{1,9},{5... | collective-permute-start | bytes 442376 | tf_op jit(solution)/shard_map/ppermute | solution.py:43
  178.8 12.7 %collective-permute-start.50 = (bf16[96,768]{1,0:T(8,128)(2,1)}, bf16[96,768]{1,0:T(8,128)(2,1)S(1)}, u32[]{:S(2)}, u32[]{:S(2)}) collective-permute-start(bf16[96,768]{1,0:T(8,128)(2,1)} %get-tuple-element.288), channel_id=1, source_target_pairs={{0,16},{4,20},{8,24},{12,28},{16,0},{20,4},{24,8},{28,12},{1,17},{... | collective-permute-start | bytes 442376 | tf_op jit(solution)/shard_map/ppermute | solution.py:43
  178.9 12.6 %collective-permute-start.51 = (bf16[96,768]{1,0:T(8,128)(2,1)}, bf16[96,768]{1,0:T(8,128)(2,1)S(1)}, u32[]{:S(2)}, u32[]{:S(2)}) collective-permute-start(bf16[96,768]{1,0:T(8,128)(2,1)} %get-tuple-element.289), channel_id=1, source_target_pairs={{0,24},{4,28},{8,16},{12,20},{16,8},{20,12},{24,0},{28,4},{1,25},{... | collective-permute-start | bytes 442376 | tf_op jit(solution)/shard_map/ppermute | solution.py:43
  (26 other events, 263.5 us)

commit v7 on v6

--- a/solution.py
+++ b/solution.py
@@ -855,7 +855,7 @@
         total = 0.0
         for t in range(3):
             total = total + nn(parts[t][rws], wr[384 * t : 384 * t + 384])
-        out[...] = total
+        out[...] = total.astype(out.dtype)
     for row, t in ((0, 0), (1, 2)):
         s = jnp.sum(parts[t].astype(F32), 0, keepdims=True)
         for g in range(2):
@@ -892,7 +892,7 @@
     far = (wp, v, probs, k, q, wr, x0, x1, ctx)
     return call(
         functools.partial(attend_back_kernel, len(sets)),
-        (*sets, shape((half, D), F32), shape((half, D), F32), shape((2, D), F32)),
+        (*sets, shape((half, D), F32), shape((half, D)), shape((2, D), F32)),
         (a0, a1, *downs, *far),
         scratch=[
             pltpu.VMEM((n, 384), BF16),
@@ -969,15 +969,17 @@
         two_d = jnp.concatenate([x_swap(two_y[:TWO]), y_swap(two_x[TWO:])])
         two_lo = jnp.stack([two, two_x, two_y, two_d])
         a_z, two_lo, other_in = lax.optimization_barrier((jnp.stack(a_z), two_lo, other_in))
-        one_a = z_line(after(one_a, a_z))
+        one_a = after(one_a, a_z)
+        near = z_swap(jnp.concatenate([one_a, two_lo.reshape(8 * TWO, D)]), 1)
+        one_a = [one_a, None, z_swap(one_a, 2), z_swap(one_a, 3)]
         a_x, a_y = x_swap(a_z), y_swap(a_z)
-        a_x, a_y, one_a, two_lo = lax.optimization_barrier((a_x, a_y, one_a, two_lo))
-        one_b = after(one_b, one_a)
-        near = z_swap(jnp.concatenate([one_b, two_lo.reshape(8 * TWO, D)]), 1)
-        one_b = [one_b, None, z_swap(one_b, 2), z_swap(one_b, 3)]
+        a_x, a_y, near, one_a[2], one_a[3] = lax.optimization_barrier(
+            (a_x, a_y, near, one_a[2], one_a[3])
+        )
+        one_a[1], two_hi = near[:FIRST], near[FIRST:].reshape(two_lo.shape)
+        one_b = z_line(after(one_b, near))
         a_d = [x_swap(a_y[:2]), y_swap(a_x[2:])]
-        near, one_b[2], one_b[3], a_d = lax.optimization_barrier((near, one_b[2], one_b[3], a_d))
-        one_b[1], two_hi = near[: 2 * ONE - FIRST], near[2 * ONE - FIRST :].reshape(two_lo.shape)
+        one_b, a_d = lax.optimization_barrier((one_b, a_d))
         a_own = [a_z, a_x, a_y, *a_d]
         one_z = jnp.stack([jnp.concatenate(pair) for pair in zip(one_a, one_b)])
         one_z, a_own = lax.optimization_barrier((one_z, a_own))
@@ -1093,7 +1095,7 @@
     if direct:
         up_sets = scatter_xy(z_sets[0], *added[:2])
         a_zz, a_xx, a_yy, by_x, by_y = a_grads
-        by_x, by_y, up_sets = lax.optimization_barrier((by_x, by_y, up_sets))
+        by_x, by_y, up_sets, in_got = lax.optimization_barrier((by_x, by_y, up_sets, in_got))
         by_x, by_y = x_swap(by_x), y_swap(by_y)
         up_mine, up_others = combine(*up_sets)
         sums_zero = after(sums_zero, up_others)

time: 193 us -> 192 us (level)
  transfers between devices with their start and end apart: 53 -> 53, of which waited for: 24 -> 25; matrix products, arithmetic and copies ran while one was open for 2% -> 2% of each run, Pallas kernels for 20% -> 19%
where the time goes in v7:
time: 192 us; the launch traced here: 191 us
  waiting for transfers between devices  77.6 us (40%)
  starting transfers between devices  59.7 us (31%)
  Pallas kernels  47.2 us (25%)
  local copies, waits for them, and re-layouts  3.42 us (2%)
  other arithmetic  2.28 us (1%)
    pallas_call x22, Pallas kernels, call(): pl.pallas_call(kernel, out_shape=out_shape, in_specs=ins, out_specs=outs,...  47.2 us
    ppermute x19, waiting for transfers between devices, z_swap(): return lax.ppermute(v, 'batch', ZPAIR[k])  45.1 us
    ppermute x19, starting transfers between devices, z_swap(): return lax.ppermute(v, 'batch', ZPAIR[k])  29.2 us
    ppermute x10, starting transfers between devices, x_swap(): return lax.ppermute(v, 'head', XPAIR)  13.3 us
    ppermute x10, waiting for transfers between devices, y_swap(): return lax.ppermute(v, 'batch', YPAIR)  12.4 us
    ppermute x10, starting transfers between devices, y_swap(): return lax.ppermute(v, 'batch', YPAIR)  10.5 us
    all_to_all x1, waiting for transfers between devices, local(): lax.all_to_all(terms, ('batch', 'head'), split_axis=0, concat_axis=0, til...  8.23 us
    ppermute x10, waiting for transfers between devices, x_swap(): return lax.ppermute(v, 'head', XPAIR)  6.8 us
  transfers between devices with their start and end apart: 53, of which 25 were waited for; matrix products, arithmetic and copies ran while one was open for 2% of the time, Pallas kernels for 19%

profile of v7, /device:TPU:0, one launch (start us, length us, event | category | flops | bytes accessed | tf_op | source)
XLA Modules:
  0.0 191.4 jit_solution(976068409372710199)
XLA Ops:
  2.0 3.1 %collective-permute-start = (bf16[104,768]{1,0:T(8,128)(2,1)S(1)}, bf16[104,768]{1,0:T(8,128)(2,1)S(1)}, u32[]{:S(2)}, u32[]{:S(2)}) collective-permute-start(bf16[104,768]{1,0:T(8,128)(2,1)S(1)} %get-tuple-element.158), channel_id=1, source_target_pairs={{0,8},{4,12},{8,0},{12,4},{16,24},{20,28},{24,16},{28,20},{1,9},{5... | collective-permute-start | bytes 479240 | tf_op jit(solution)/shard_map/ppermute | solution.py:43
  5.1 2.5 %collective-permute-start.2 = (bf16[104,768]{1,0:T(8,128)(2,1)S(1)}, bf16[104,768]{1,0:T(8,128)(2,1)S(1)}, u32[]{:S(2)}, u32[]{:S(2)}) collective-permute-start(bf16[104,768]{1,0:T(8,128)(2,1)S(1)} %get-tuple-element.158), channel_id=1, source_target_pairs={{0,24},{4,28},{8,16},{12,20},{16,8},{20,12},{24,0},{28,4},{1,25},{... | collective-permute-start | bytes 479240 | tf_op jit(solution)/shard_map/ppermute | solution.py:43
  7.7 1.9 %collective-permute-done = bf16[104,768]{1,0:T(8,128)(2,1)S(1)} collective-permute-done((bf16[104,768]{1,0:T(8,128)(2,1)S(1)}, bf16[104,768]{1,0:T(8,128)(2,1)S(1)}, u32[]{:S(2)}, u32[]{:S(2)}) %collective-permute-start) | collective-permute-done | bytes 159776 | tf_op jit(solution)/shard_map/ppermute | solution.py:43
  9.6 1.5 collective-permute-start.4
  11.1 1.5 collective-permute-start.3
  13.7 1.5 collective-permute-start.5
  15.2 1.5 collective-permute-start.6
  16.7 5.1 %collective-permute-done.1 = bf16[104,768]{1,0:T(8,128)(2,1)S(1)} collective-permute-done((bf16[104,768]{1,0:T(8,128)(2,1)S(1)}, bf16[104,768]{1,0:T(8,128)(2,1)S(1)}, u32[]{:S(2)}, u32[]{:S(2)}) %collective-permute-start.1) | collective-permute-done | bytes 159776 | tf_op jit(solution)/shard_map/ppermute | solution.py:43
  21.9 1.6 collective-permute-start.9
  23.5 1.5 collective-permute-start.8
  25.1 2.7 %collective-permute-start.12 = (bf16[104,768]{1,0:T(8,128)(2,1)S(1)}, bf16[104,768]{1,0:T(8,128)(2,1)S(1)}, u32[]{:S(2)}, u32[]{:S(2)}) collective-permute-start(bf16[104,768]{1,0:T(8,128)(2,1)S(1)} %get-tuple-element.164), channel_id=1, source_target_pairs={{0,24},{4,28},{8,16},{12,20},{16,8},{20,12},{24,0},{28,4},{1,25},{... | collective-permute-start | bytes 479240 | tf_op jit(solution)/shard_map/ppermute | solution.py:43
  28.6 11.2 %collective-permute-done.12 = bf16[104,768]{1,0:T(8,128)(2,1)S(1)} collective-permute-done((bf16[104,768]{1,0:T(8,128)(2,1)S(1)}, bf16[104,768]{1,0:T(8,128)(2,1)S(1)}, u32[]{:S(2)}, u32[]{:S(2)}) %collective-permute-start.12) | collective-permute-done | bytes 159776 | tf_op jit(solution)/shard_map/ppermute | solution.py:43
  41.8 3.0 %collective-permute-start.15 = (bf16[56,768]{1,0:T(8,128)(2,1)S(1)}, bf16[56,768]{1,0:T(8,128)(2,1)S(1)}, u32[]{:S(2)}, u32[]{:S(2)}) collective-permute-start(bf16[56,768]{1,0:T(8,128)(2,1)S(1)} %get-tuple-element.171), channel_id=1, source_target_pairs={{0,24},{4,28},{8,16},{12,20},{16,8},{20,12},{24,0},{28,4},{1,25},{... | collective-permute-start | bytes 258056 | tf_op jit(solution)/shard_map/ppermute | solution.py:43
  46.2 1.9 collective-permute-done.15
  48.1 2.2 %collective-permute-done.14 = bf16[56,768]{1,0:T(8,128)(2,1)S(1)} collective-permute-done((bf16[56,768]{1,0:T(8,128)(2,1)S(1)}, bf16[56,768]{1,0:T(8,128)(2,1)S(1)}, u32[]{:S(2)}, u32[]{:S(2)}) %collective-permute-start.14) | collective-permute-done | bytes 86048 | tf_op jit(solution)/shard_map/ppermute | solution.py:43
  51.7 1.5 collective-permute-start.26
  53.2 1.6 collective-permute-start.25
  55.5 2.1 %collective-permute-start.27 = (bf16[8,32,768]{2,1,0:T(8,128)(2,1)S(1)}, bf16[8,32,768]{2,1,0:T(8,128)(2,1)S(1)}, u32[]{:S(2)}, u32[]{:S(2)}) collective-permute-start(bf16[8,32,768]{2,1,0:T(8,128)(2,1)S(1)} %pad_maximum_fusion.2), channel_id=1, source_target_pairs={{0,16},{4,20},{8,24},{12,28},{16,0},{20,4},{24,8},{28,12},{1,17},{... | collective-permute-start | bytes 1179656 | tf_op jit(solution)/shard_map/ppermute | solution.py:43
  59.3 10.3 %shard_map.281 = (bf16[256,384]{1,0:T(8,128)(2,1)S(1)}, bf16[256,384]{1,0:T(8,128)(2,1)S(1)}, bf16[512,384]{1,0:T(8,128)(2,1)S(1)}, bf16[512,384]{1,0:T(8,128)(2...) custom-call(s32[2]{0:T(128)S(1)} %copy-done.10, ...), custom_call_target="tpu_custom_call" | custom-call | flops 1000 | bytes 1000 | tf_op jit(solution)/shard_map/pallas_call | solution.py:108
  72.2 3.8 %collective-permute-done.27.refs_2_.refs_4_.refs_3_ = bf16[8,32,768]{2,1,0:T(8,128)(2,1)S(1)} collective-permute-done((bf16[8,32,768]{2,1,0:T(8,128)(2,1)S(1)}, bf16[8,32,768]{2,1,0:T(8,128)(2,1)S(1)}, u32[]{:S(2)}, u32[]{:S(2)}) %collective-permute-start.27) | collective-permute-done | bytes 393248 | tf_op jit(solution)/shard_map/ppermute | solution.py:43
  77.7 1.5 collective-permute-start.28
  81.8 1.5 shard_map.285
  84.6 5.0 %collective-permute-done.29.refs_1_ = bf16[2,160,768]{2,1,0:T(8,128)(2,1)S(1)} collective-permute-done((bf16[2,160,768]{2,1,0:T(8,128)(2,1)S(1)}, bf16[2,160,768]{2,1,0:T(8,128)(2,1)S(1)}, u32[]{:S(2)}, u32[]{:S(2)}) %collective-permute-start.29) | collective-permute-done | bytes 491552 | tf_op jit(solution)/shard_map/ppermute | solution.py:39
  91.3 1.7 collective-permute-done.30.got
  94.4 1.6 collective-permute-done.31.d1
  96.0 1.8 shard_map.289
  97.8 1.5 collective-permute-start.33
  99.3 1.6 collective-permute-start.34
  100.9 1.9 shard_map.290
  102.8 1.9 shard_map.291
  104.7 1.8 shard_map.292
  106.6 1.5 shard_map.293
  108.3 5.0 %collective-permute-done.33.refs_2_ = bf16[2,192,768]{2,1,0:T(8,128)(2,1)S(1)} collective-permute-done((bf16[2,192,768]{2,1,0:T(8,128)(2,1)S(1)}, bf16[2,192,768]{2,1,0:T(8,128)(2,1)S(1)}, u32[]{:S(2)}, u32[]{:S(2)}) %collective-permute-start.33) | collective-permute-done | bytes 589856 | tf_op jit(solution)/shard_map/ppermute | solution.py:39
  115.5 1.6 collective-permute-start.37
  117.8 9.2 %shard_map.295 = (bf16[4,96,768]{2,1,0:T(8,128)(2,1)}, bf16[4,96,768]{2,1,0:T(8,128)(2,1)}, bf16[4,96,768]{2,1,0:T(8,128)(2,1)}, bf16[6,96,768]{2,1,0:T(8,128)(2...) custom-call(bf16[256,768]{1,0:T(8,128)(2,1)S(1)} %get-tuple-element., ...), custom_call_target="tpu_custom_call" | custom-call | flops 8000000000 | bytes 14000000 | tf_op jit(solution)/shard_map/pallas_call | solution.py:108
  127.0 4.2 %collective-permute-done.37.x = bf16[4,96,768]{2,1,0:T(8,128)(2,1)S(1)} collective-permute-done((bf16[4,96,768]{2,1,0:T(8,128)(2,1)S(1)}, bf16[4,96,768]{2,1,0:T(8,128)(2,1)S(1)}, u32[]{:S(2)}, u32[]{:S(2)}) %collective-permute-start.37) | collective-permute-done | bytes 589856 | tf_op jit(solution)/shard_map/ppermute | solution.py:35
  135.7 2.2 %collective-permute-start.42 = (bf16[96,768]{1,0:T(8,128)(2,1)}, bf16[96,768]{1,0:T(8,128)(2,1)}, u32[]{:S(2)}, u32[]{:S(2)}) collective-permute-start(bf16[96,768]{1,0:T(8,128)(2,1)} %get-tuple-element.265), channel_id=1, source_target_pairs={{0,16},{4,20},{8,24},{12,28},{16,0},{20,4},{24,8},{28,12},{1,17},{... | collective-permute-start | bytes 442376 | tf_op jit(solution)/shard_map/ppermute | solution.py:43
  140.0 4.7 %all-to-all-start = ((bf16[32,8,128]{2,1,0:T(8,128)(2,1)}), bf16[32,8,128]{2,1,0:T(8,128)(2,1)S(1)}, u32[]{:S(2)}, u32[]{:S(2)}) async-start(bf16[32,8,128]{2,1,0:T(8,128)(2,1)} %shard_map.297), calls=%async_computation | async-start | bytes 131072 | tf_op jit(solution)/shard_map/all_to_all | solution.py:1103
  144.8 1.9 add_convert_fusion
  146.6 8.2 %all-to-all-done = bf16[32,8,128]{2,1,0:T(8,128)(2,1)S(1)} async-done(((bf16[32,8,128]{2,1,0:T(8,128)(2,1)}), bf16[32,8,128]{2,1,0:T(8,128)(2,1)S(1)}, u32[]{:S(2)}, u32[]{:S(2)}) %all-to-all-start) | async-done | bytes 65568 | tf_op jit(solution)/shard_map/all_to_all | solution.py:1103
  154.9 2.3 %shard_map.298 = (bf16[4,96,768]{2,1,0:T(8,128)(2,1)S(1)}, bf16[4,96,768]{2,1,0:T(8,128)(2,1)S(1)}, f32[96,768]{1,0:T(8,128)}, bf16[96,768]{1,0:T(8,128)(2,1)}, ...) custom-call(bf16[4,96,768]{2,1,0:T(8,128)(2,1)S(1)} %copy-done.3, bf16[4,96,768]{2,1,0:T(8,128)(2,1)S(1)} %copy-done.4, ...), custom_call_target="tpu_custom_call" | custom-call | flops 1000 | bytes 1000 | tf_op jit(solution)/shard_map/pallas_call | solution.py:108
  157.2 1.5 collective-permute-start.44
  160.3 2.1 %collective-permute-start.47 = (bf16[96,768]{1,0:T(8,128)(2,1)}, bf16[96,768]{1,0:T(8,128)(2,1)S(1)}, u32[]{:S(2)}, u32[]{:S(2)}) collective-permute-start(bf16[96,768]{1,0:T(8,128)(2,1)} %get-tuple-element.279), channel_id=1, source_target_pairs={{0,16},{4,20},{8,24},{12,28},{16,0},{20,4},{24,8},{28,12},{1,17},{... | collective-permute-start | bytes 442376 | tf_op jit(solution)/shard_map/ppermute | solution.py:43
  164.3 2.6 %collective-permute-done.46.refs_5_ = bf16[96,768]{1,0:T(8,128)(2,1)S(1)} collective-permute-done((bf16[96,768]{1,0:T(8,128)(2,1)}, bf16[96,768]{1,0:T(8,128)(2,1)S(1)}, u32[]{:S(2)}, u32[]{:S(2)}) %collective-permute-start.46) | collective-permute-done | bytes 147488 | tf_op jit(solution)/shard_map/ppermute | solution.py:43
  166.8 7.5 %collective-permute-done.47.refs_6_ = bf16[96,768]{1,0:T(8,128)(2,1)S(1)} collective-permute-done((bf16[96,768]{1,0:T(8,128)(2,1)}, bf16[96,768]{1,0:T(8,128)(2,1)S(1)}, u32[]{:S(2)}, u32[]{:S(2)}) %collective-permute-start.47) | collective-permute-done | bytes 147488 | tf_op jit(solution)/shard_map/ppermute | solution.py:43
  175.2 2.2 %collective-permute-start.49 = (bf16[96,768]{1,0:T(8,128)(2,1)}, bf16[96,768]{1,0:T(8,128)(2,1)S(1)}, u32[]{:S(2)}, u32[]{:S(2)}) collective-permute-start(bf16[96,768]{1,0:T(8,128)(2,1)} %get-tuple-element.285), channel_id=1, source_target_pairs={{0,8},{4,12},{8,0},{12,4},{16,24},{20,28},{24,16},{28,20},{1,9},{5... | collective-permute-start | bytes 442376 | tf_op jit(solution)/shard_map/ppermute | solution.py:43
  180.5 1.9 shard_map.301
  182.4 8.1 %collective-permute-done.50.two = bf16[96,768]{1,0:T(8,128)(2,1)S(1)} collective-permute-done((bf16[96,768]{1,0:T(8,128)(2,1)}, bf16[96,768]{1,0:T(8,128)(2,1)S(1)}, u32[]{:S(2)}, u32[]{:S(2)}) %collective-permute-start.50) | collective-permute-done | bytes 147488 | tf_op jit(solution)/shard_map/ppermute | solution.py:43
  (147 shorter events, 39.8 us)
Async XLA Ops:
  2.0 7.6 %collective-permute-start = (bf16[104,768]{1,0:T(8,128)(2,1)S(1)}, bf16[104,768]{1,0:T(8,128)(2,1)S(1)}, u32[]{:S(2)}, u32[]{:S(2)}) collective-permute-start(bf16[104,768]{1,0:T(8,128)(2,1)S(1)} %get-tuple-element.158), channel_id=1, source_target_pairs={{0,8},{4,12},{8,0},{12,4},{16,24},{20,28},{24,16},{28,20},{1,9},{5... | collective-permute-start | bytes 479240 | tf_op jit(solution)/shard_map/ppermute | solution.py:43
  5.1 11.6 %collective-permute-start.2 = (bf16[104,768]{1,0:T(8,128)(2,1)S(1)}, bf16[104,768]{1,0:T(8,128)(2,1)S(1)}, u32[]{:S(2)}, u32[]{:S(2)}) collective-permute-start(bf16[104,768]{1,0:T(8,128)(2,1)S(1)} %get-tuple-element.158), channel_id=1, source_target_pairs={{0,24},{4,28},{8,16},{12,20},{16,8},{20,12},{24,0},{28,4},{1,25},{... | collective-permute-start | bytes 479240 | tf_op jit(solution)/shard_map/ppermute | solution.py:43
  7.5 14.2 %collective-permute-start.1 = (bf16[104,768]{1,0:T(8,128)(2,1)S(1)}, bf16[104,768]{1,0:T(8,128)(2,1)S(1)}, u32[]{:S(2)}, u32[]{:S(2)}) collective-permute-start(bf16[104,768]{1,0:T(8,128)(2,1)S(1)} %get-tuple-element.158), channel_id=1, source_target_pairs={{0,16},{4,20},{8,24},{12,28},{16,0},{20,4},{24,8},{28,12},{1,17},{... | collective-permute-start | bytes 479240 | tf_op jit(solution)/shard_map/ppermute | solution.py:43
  9.6 4.1 %collective-permute-start.4 = (bf16[32,768]{1,0:T(8,128)(2,1)S(1)}, bf16[32,768]{1,0:T(8,128)(2,1)S(1)}, u32[]{:S(2)}, u32[]{:S(2)}) collective-permute-start(bf16[32,768]{1,0:T(8,128)(2,1)S(1)} %get-tuple-element.160), channel_id=1, source_target_pairs={{0,4},{4,0},{8,12},{12,8},{16,20},{20,16},{24,28},{28,24},{1,5},{5... | collective-permute-start | bytes 147464 | tf_op jit(solution)/shard_map/ppermute | solution.py:39
  11.1 4.1 %collective-permute-start.3 = (bf16[32,768]{1,0:T(8,128)(2,1)S(1)}, bf16[32,768]{1,0:T(8,128)(2,1)S(1)}, u32[]{:S(2)}, u32[]{:S(2)}) collective-permute-start(bf16[32,768]{1,0:T(8,128)(2,1)S(1)} %get-tuple-element.160), channel_id=1, source_target_pairs={{0,2},{1,3},{2,0},{3,1},{4,6},{5,7},{6,4},{7,5},{8,10},{9,11},{10,... | collective-permute-start | bytes 147464 | tf_op jit(solution)/shard_map/ppermute | solution.py:35
  12.6 9.3 %collective-permute-start.7 = (bf16[256,768]{1,0:T(8,128)(2,1)}, bf16[256,768]{1,0:T(8,128)(2,1)S(1)}, u32[]{:S(2)}, u32[]{:S(2)}) collective-permute-start(bf16[256,768]{1,0:T(8,128)(2,1)} %refs_8_.1), channel_id=1, source_target_pairs={{0,1},{1,0},{2,3},{3,2},{4,5},{5,4},{6,7},{7,6},{8,9},{9,8},{10,11... | collective-permute-start | bytes 1179656 | tf_op jit(solution)/shard_map/ppermute | solution.py:31
  13.7 8.2 %collective-permute-start.5 = (bf16[16,768]{1,0:T(8,128)(2,1)S(1)}, bf16[16,768]{1,0:T(8,128)(2,1)S(1)}, u32[]{:S(2)}, u32[]{:S(2)}) collective-permute-start(bf16[16,768]{1,0:T(8,128)(2,1)S(1)} %slice.129), channel_id=1, source_target_pairs={{0,2},{1,3},{2,0},{3,1},{4,6},{5,7},{6,4},{7,5},{8,10},{9,11},{10,... | collective-permute-start | bytes 73736 | tf_op jit(solution)/shard_map/ppermute | solution.py:35
  15.2 6.7 %collective-permute-start.6 = (bf16[16,768]{1,0:T(8,128)(2,1)S(1)}, bf16[16,768]{1,0:T(8,128)(2,1)S(1)}, u32[]{:S(2)}, u32[]{:S(2)}) collective-permute-start(bf16[16,768]{1,0:T(8,128)(2,1)S(1)} %slice.130), channel_id=1, source_target_pairs={{0,4},{4,0},{8,12},{12,8},{16,20},{20,16},{24,28},{28,24},{1,5},{5... | collective-permute-start | bytes 73736 | tf_op jit(solution)/shard_map/ppermute | solution.py:39
  21.9 18.7 %collective-permute-start.9 = (bf16[4,104,768]{2,1,0:T(8,128)(2,1)S(1)}, bf16[4,104,768]{2,1,0:T(8,128)(2,1)S(1)}, u32[]{:S(2)}, u32[]{:S(2)}) collective-permute-start(bf16[4,104,768]{2,1,0:T(8,128)(2,1)S(1)} %pad_maximum_fusion.1.refs_0_), channel_id=1, source_target_pairs={{0,4},{4,0},{8,12},{12,8},{16,20},{20,16},{24,28},{28,24},{1,5},{5... | collective-permute-start | bytes 1916936 | tf_op jit(solution)/shard_map/ppermute | solution.py:39
  23.5 17.1 %collective-permute-start.8 = (bf16[4,104,768]{2,1,0:T(8,128)(2,1)S(1)}, bf16[4,104,768]{2,1,0:T(8,128)(2,1)S(1)}, u32[]{:S(2)}, u32[]{:S(2)}) collective-permute-start(bf16[4,104,768]{2,1,0:T(8,128)(2,1)S(1)} %pad_maximum_fusion.1.refs_0_), channel_id=1, source_target_pairs={{0,2},{1,3},{2,0},{3,1},{4,6},{5,7},{6,4},{7,5},{8,10},{9,11},{10,... | collective-permute-start | bytes 1916936 | tf_op jit(solution)/shard_map/ppermute | solution.py:35
  25.0 15.5 %collective-permute-start.10 = (bf16[232,768]{1,0:T(8,128)(2,1)S(1)}, bf16[232,768]{1,0:T(8,128)(2,1)S(1)}, u32[]{:S(2)}, u32[]{:S(2)}) collective-permute-start(bf16[232,768]{1,0:T(8,128)(2,1)S(1)} %pad_maximum_fusion.3), channel_id=1, source_target_pairs={{0,8},{4,12},{8,0},{12,4},{16,24},{20,28},{24,16},{28,20},{1,9},{5... | collective-permute-start | bytes 1069064 | tf_op jit(solution)/shard_map/ppermute | solution.py:43
  25.1 14.7 %collective-permute-start.12 = (bf16[104,768]{1,0:T(8,128)(2,1)S(1)}, bf16[104,768]{1,0:T(8,128)(2,1)S(1)}, u32[]{:S(2)}, u32[]{:S(2)}) collective-permute-start(bf16[104,768]{1,0:T(8,128)(2,1)S(1)} %get-tuple-element.164), channel_id=1, source_target_pairs={{0,24},{4,28},{8,16},{12,20},{16,8},{20,12},{24,0},{28,4},{1,25},{... | collective-permute-start | bytes 479240 | tf_op jit(solution)/shard_map/ppermute | solution.py:43
  27.8 12.0 %collective-permute-start.11 = (bf16[104,768]{1,0:T(8,128)(2,1)S(1)}, bf16[104,768]{1,0:T(8,128)(2,1)S(1)}, u32[]{:S(2)}, u32[]{:S(2)}) collective-permute-start(bf16[104,768]{1,0:T(8,128)(2,1)S(1)} %get-tuple-element.164), channel_id=1, source_target_pairs={{0,16},{4,20},{8,24},{12,28},{16,0},{20,4},{24,8},{28,12},{1,17},{... | collective-permute-start | bytes 479240 | tf_op jit(solution)/shard_map/ppermute | solution.py:43
  40.7 9.6 %collective-permute-start.17 = (bf16[2,104,768]{2,1,0:T(8,128)(2,1)S(1)}, bf16[2,104,768]{2,1,0:T(8,128)(2,1)S(1)}, u32[]{:S(2)}, u32[]{:S(2)}) collective-permute-start(bf16[2,104,768]{2,1,0:T(8,128)(2,1)S(1)} %slice.102), channel_id=1, source_target_pairs={{0,4},{4,0},{8,12},{12,8},{16,20},{20,16},{24,28},{28,24},{1,5},{5... | collective-permute-start | bytes 958472 | tf_op jit(solution)/shard_map/ppermute | solution.py:39
  41.2 9.0 %collective-permute-start.16 = (bf16[2,104,768]{2,1,0:T(8,128)(2,1)S(1)}, bf16[2,104,768]{2,1,0:T(8,128)(2,1)S(1)}, u32[]{:S(2)}, u32[]{:S(2)}) collective-permute-start(bf16[2,104,768]{2,1,0:T(8,128)(2,1)S(1)} %slice.101), channel_id=1, source_target_pairs={{0,2},{1,3},{2,0},{3,1},{4,6},{5,7},{6,4},{7,5},{8,10},{9,11},{10,... | collective-permute-start | bytes 958472 | tf_op jit(solution)/shard_map/ppermute | solution.py:35
  41.8 6.3 %collective-permute-start.15 = (bf16[56,768]{1,0:T(8,128)(2,1)S(1)}, bf16[56,768]{1,0:T(8,128)(2,1)S(1)}, u32[]{:S(2)}, u32[]{:S(2)}) collective-permute-start(bf16[56,768]{1,0:T(8,128)(2,1)S(1)} %get-tuple-element.171), channel_id=1, source_target_pairs={{0,24},{4,28},{8,16},{12,20},{16,8},{20,12},{24,0},{28,4},{1,25},{... | collective-permute-start | bytes 258056 | tf_op jit(solution)/shard_map/ppermute | solution.py:43
  44.8 5.4 %collective-permute-start.14 = (bf16[56,768]{1,0:T(8,128)(2,1)S(1)}, bf16[56,768]{1,0:T(8,128)(2,1)S(1)}, u32[]{:S(2)}, u32[]{:S(2)}) collective-permute-start(bf16[56,768]{1,0:T(8,128)(2,1)S(1)} %get-tuple-element.171), channel_id=1, source_target_pairs={{0,16},{4,20},{8,24},{12,28},{16,0},{20,4},{24,8},{28,12},{1,17},{... | collective-permute-start | bytes 258056 | tf_op jit(solution)/shard_map/ppermute | solution.py:43
  44.8 5.4 %collective-permute-start.13 = (bf16[56,768]{1,0:T(8,128)(2,1)S(1)}, bf16[56,768]{1,0:T(8,128)(2,1)S(1)}, u32[]{:S(2)}, u32[]{:S(2)}) collective-permute-start(bf16[56,768]{1,0:T(8,128)(2,1)S(1)} %get-tuple-element.171), channel_id=1, source_target_pairs={{0,8},{4,12},{8,0},{12,4},{16,24},{20,28},{24,16},{28,20},{1,9},{5... | collective-permute-start | bytes 258056 | tf_op jit(solution)/shard_map/ppermute | solution.py:43
  51.1 3.7 %collective-permute-start.21 = (bf16[2,104,768]{2,1,0:T(8,128)(2,1)S(1)}, bf16[2,104,768]{2,1,0:T(8,128)(2,1)S(1)}, u32[]{:S(2)}, u32[]{:S(2)}) collective-permute-start(bf16[2,104,768]{2,1,0:T(8,128)(2,1)S(1)} %collective-permute-done.16.refs_3_), channel_id=1, source_target_pairs={{0,1},{1,0},{2,3},{3,2},{4,5},{5,4},{6,7},{7,6},{8,9},{9,8},{10,11... | collective-permute-start | bytes 958472 | tf_op jit(solution)/shard_map/ppermute | solution.py:31
  51.1 3.8 %collective-permute-start.22 = (bf16[2,104,768]{2,1,0:T(8,128)(2,1)S(1)}, bf16[2,104,768]{2,1,0:T(8,128)(2,1)S(1)}, u32[]{:S(2)}, u32[]{:S(2)}) collective-permute-start(bf16[2,104,768]{2,1,0:T(8,128)(2,1)S(1)} %collective-permute-done.17.refs_4_), channel_id=1, source_target_pairs={{0,1},{1,0},{2,3},{3,2},{4,5},{5,4},{6,7},{7,6},{8,9},{9,8},{10,11... | collective-permute-start | bytes 958472 | tf_op jit(solution)/shard_map/ppermute | solution.py:31
  51.6 3.9 %collective-permute-start.18 = (bf16[4,104,768]{2,1,0:T(8,128)(2,1)S(1)}, bf16[4,104,768]{2,1,0:T(8,128)(2,1)S(1)}, u32[]{:S(2)}, u32[]{:S(2)}) collective-permute-start(bf16[4,104,768]{2,1,0:T(8,128)(2,1)S(1)} %pad_maximum_fusion.1.refs_0_), channel_id=1, source_target_pairs={{0,1},{1,0},{2,3},{3,2},{4,5},{5,4},{6,7},{7,6},{8,9},{9,8},{10,11... | collective-permute-start | bytes 1916936 | tf_op jit(solution)/shard_map/ppermute | solution.py:31
  51.7 24.3 %collective-permute-start.26 = (bf16[4,160,768]{2,1,0:T(8,128)(2,1)S(1)}, bf16[4,160,768]{2,1,0:T(8,128)(2,1)S(1)}, u32[]{:S(2)}, u32[]{:S(2)}) collective-permute-start(bf16[4,160,768]{2,1,0:T(8,128)(2,1)S(1)} %pad_maximum_fusion.refs_0_), channel_id=1, source_target_pairs={{0,4},{4,0},{8,12},{12,8},{16,20},{20,16},{24,28},{28,24},{1,5},{5... | collective-permute-start | bytes 2949128 | tf_op jit(solution)/shard_map/ppermute | solution.py:39
  53.2 23.8 %collective-permute-start.25 = (bf16[4,160,768]{2,1,0:T(8,128)(2,1)S(1)}, bf16[4,160,768]{2,1,0:T(8,128)(2,1)S(1)}, u32[]{:S(2)}, u32[]{:S(2)}) collective-permute-start(bf16[4,160,768]{2,1,0:T(8,128)(2,1)S(1)} %pad_maximum_fusion.refs_0_), channel_id=1, source_target_pairs={{0,2},{1,3},{2,0},{3,1},{4,6},{5,7},{6,4},{7,5},{8,10},{9,11},{10,... | collective-permute-start | bytes 2949128 | tf_op jit(solution)/shard_map/ppermute | solution.py:35
  54.8 2.8 %collective-permute-start.19 = (bf16[4,104,768]{2,1,0:T(8,128)(2,1)S(1)}, bf16[4,104,768]{2,1,0:T(8,128)(2,1)S(1)}, u32[]{:S(2)}, u32[]{:S(2)}) collective-permute-start(bf16[4,104,768]{2,1,0:T(8,128)(2,1)S(1)} %collective-permute-done.8.refs_1_), channel_id=1, source_target_pairs={{0,1},{1,0},{2,3},{3,2},{4,5},{5,4},{6,7},{7,6},{8,9},{9,8},{10,11... | collective-permute-start | bytes 1916936 | tf_op jit(solution)/shard_map/ppermute | solution.py:31
  54.9 2.9 %collective-permute-start.20 = (bf16[4,104,768]{2,1,0:T(8,128)(2,1)S(1)}, bf16[4,104,768]{2,1,0:T(8,128)(2,1)S(1)}, u32[]{:S(2)}, u32[]{:S(2)}) collective-permute-start(bf16[4,104,768]{2,1,0:T(8,128)(2,1)S(1)} %collective-permute-done.9.refs_2_), channel_id=1, source_target_pairs={{0,1},{1,0},{2,3},{3,2},{4,5},{5,4},{6,7},{7,6},{8,9},{9,8},{10,11... | collective-permute-start | bytes 1916936 | tf_op jit(solution)/shard_map/ppermute | solution.py:31
  55.5 20.5 %collective-permute-start.27 = (bf16[8,32,768]{2,1,0:T(8,128)(2,1)S(1)}, bf16[8,32,768]{2,1,0:T(8,128)(2,1)S(1)}, u32[]{:S(2)}, u32[]{:S(2)}) collective-permute-start(bf16[8,32,768]{2,1,0:T(8,128)(2,1)S(1)} %pad_maximum_fusion.2), channel_id=1, source_target_pairs={{0,16},{4,20},{8,24},{12,28},{16,0},{20,4},{24,8},{28,12},{1,17},{... | collective-permute-start | bytes 1179656 | tf_op jit(solution)/shard_map/ppermute | solution.py:43
  72.0 7.2 %collective-permute-start.24 = (bf16[256,768]{1,0:T(8,128)(2,1)S(1)}, bf16[256,768]{1,0:T(8,128)(2,1)S(1)}, u32[]{:S(2)}, u32[]{:S(2)}) collective-permute-start(bf16[256,768]{1,0:T(8,128)(2,1)S(1)} %get-tuple-element.189.x0), channel_id=1, source_target_pairs={{0,1},{1,0},{2,3},{3,2},{4,5},{5,4},{6,7},{7,6},{8,9},{9,8},{10,11... | collective-permute-start | bytes 1179656 | tf_op jit(solution)/shard_map/ppermute | solution.py:31
  77.1 12.5 %collective-permute-start.29 = (bf16[2,160,768]{2,1,0:T(8,128)(2,1)S(1)}, bf16[2,160,768]{2,1,0:T(8,128)(2,1)S(1)}, u32[]{:S(2)}, u32[]{:S(2)}) collective-permute-start(bf16[2,160,768]{2,1,0:T(8,128)(2,1)S(1)} %slice.107), channel_id=1, source_target_pairs={{0,4},{4,0},{8,12},{12,8},{16,20},{20,16},{24,28},{28,24},{1,5},{5... | collective-permute-start | bytes 1474568 | tf_op jit(solution)/shard_map/ppermute | solution.py:39
  77.7 12.3 %collective-permute-start.28 = (bf16[2,160,768]{2,1,0:T(8,128)(2,1)S(1)}, bf16[2,160,768]{2,1,0:T(8,128)(2,1)S(1)}, u32[]{:S(2)}, u32[]{:S(2)}) collective-permute-start(bf16[2,160,768]{2,1,0:T(8,128)(2,1)S(1)} %slice.106), channel_id=1, source_target_pairs={{0,2},{1,3},{2,0},{3,1},{4,6},{5,7},{6,4},{7,5},{8,10},{9,11},{10,... | collective-permute-start | bytes 1474568 | tf_op jit(solution)/shard_map/ppermute | solution.py:35
  97.8 15.4 %collective-permute-start.33 = (bf16[2,192,768]{2,1,0:T(8,128)(2,1)S(1)}, bf16[2,192,768]{2,1,0:T(8,128)(2,1)S(1)}, u32[]{:S(2)}, u32[]{:S(2)}) collective-permute-start(bf16[2,192,768]{2,1,0:T(8,128)(2,1)S(1)} %get-tuple-element.234), channel_id=1, source_target_pairs={{0,4},{4,0},{8,12},{12,8},{16,20},{20,16},{24,28},{28,24},{1,5},{5... | collective-permute-start | bytes 1769480 | tf_op jit(solution)/shard_map/ppermute | solution.py:39
  99.3 15.1 %collective-permute-start.34 = (bf16[2,192,768]{2,1,0:T(8,128)(2,1)S(1)}, bf16[2,192,768]{2,1,0:T(8,128)(2,1)S(1)}, u32[]{:S(2)}, u32[]{:S(2)}) collective-permute-start(bf16[2,192,768]{2,1,0:T(8,128)(2,1)S(1)} %get-tuple-element.237), channel_id=1, source_target_pairs={{0,2},{1,3},{2,0},{3,1},{4,6},{5,7},{6,4},{7,5},{8,10},{9,11},{10,... | collective-permute-start | bytes 1769480 | tf_op jit(solution)/shard_map/ppermute | solution.py:35
  115.5 15.7 %collective-permute-start.37 = (bf16[4,96,768]{2,1,0:T(8,128)(2,1)S(1)}, bf16[4,96,768]{2,1,0:T(8,128)(2,1)S(1)}, u32[]{:S(2)}, u32[]{:S(2)}) collective-permute-start(bf16[4,96,768]{2,1,0:T(8,128)(2,1)S(1)} %get-tuple-element.257), channel_id=1, source_target_pairs={{0,2},{1,3},{2,0},{3,1},{4,6},{5,7},{6,4},{7,5},{8,10},{9,11},{10,... | collective-permute-start | bytes 1769480 | tf_op jit(solution)/shard_map/ppermute | solution.py:35
  117.2 15.4 %collective-permute-start.38 = (bf16[4,96,768]{2,1,0:T(8,128)(2,1)S(1)}, bf16[4,96,768]{2,1,0:T(8,128)(2,1)S(1)}, u32[]{:S(2)}, u32[]{:S(2)}) collective-permute-start(bf16[4,96,768]{2,1,0:T(8,128)(2,1)S(1)} %get-tuple-element.258), channel_id=1, source_target_pairs={{0,4},{4,0},{8,12},{12,8},{16,20},{20,16},{24,28},{28,24},{1,5},{5... | collective-permute-start | bytes 1769480 | tf_op jit(solution)/shard_map/ppermute | solution.py:39
  127.0 5.6 %collective-permute-start.36 = (bf16[256,768]{1,0:T(8,128)(2,1)S(1)}, bf16[256,768]{1,0:T(8,128)(2,1)S(1)}, u32[]{:S(2)}, u32[]{:S(2)}) collective-permute-start(bf16[256,768]{1,0:T(8,128)(2,1)S(1)} %get-tuple-element.249), channel_id=1, source_target_pairs={{0,1},{1,0},{2,3},{3,2},{4,5},{5,4},{6,7},{7,6},{8,9},{9,8},{10,11... | collective-permute-start | bytes 1179656 | tf_op jit(solution)/shard_map/ppermute | solution.py:31
  132.6 22.3 %collective-permute-start.39 = (bf16[6,96,768]{2,1,0:T(8,128)(2,1)}, bf16[6,96,768]{2,1,0:T(8,128)(2,1)}, u32[]{:S(2)}, u32[]{:S(2)}) collective-permute-start(bf16[6,96,768]{2,1,0:T(8,128)(2,1)} %get-tuple-element.259), channel_id=1, source_target_pairs={{0,2},{1,3},{2,0},{3,1},{4,6},{5,7},{6,4},{7,5},{8,10},{9,11},{10,... | collective-permute-start | bytes 2654216 | tf_op jit(solution)/shard_map/ppermute | solution.py:35
  133.1 21.8 %collective-permute-start.40 = (bf16[6,96,768]{2,1,0:T(8,128)(2,1)}, bf16[6,96,768]{2,1,0:T(8,128)(2,1)}, u32[]{:S(2)}, u32[]{:S(2)}) collective-permute-start(bf16[6,96,768]{2,1,0:T(8,128)(2,1)} %get-tuple-element.260), channel_id=1, source_target_pairs={{0,4},{4,0},{8,12},{12,8},{16,20},{20,16},{24,28},{28,24},{1,5},{5... | collective-permute-start | bytes 2654216 | tf_op jit(solution)/shard_map/ppermute | solution.py:39
  134.7 20.2 %collective-permute-start.41 = (bf16[96,768]{1,0:T(8,128)(2,1)}, bf16[96,768]{1,0:T(8,128)(2,1)S(1)}, u32[]{:S(2)}, u32[]{:S(2)}) collective-permute-start(bf16[96,768]{1,0:T(8,128)(2,1)} %get-tuple-element.264), channel_id=1, source_target_pairs={{0,8},{4,12},{8,0},{12,4},{16,24},{20,28},{24,16},{28,20},{1,9},{5... | collective-permute-start | bytes 442376 | tf_op jit(solution)/shard_map/ppermute | solution.py:43
  135.7 19.2 %collective-permute-start.42 = (bf16[96,768]{1,0:T(8,128)(2,1)}, bf16[96,768]{1,0:T(8,128)(2,1)}, u32[]{:S(2)}, u32[]{:S(2)}) collective-permute-start(bf16[96,768]{1,0:T(8,128)(2,1)} %get-tuple-element.265), channel_id=1, source_target_pairs={{0,16},{4,20},{8,24},{12,28},{16,0},{20,4},{24,8},{28,12},{1,17},{... | collective-permute-start | bytes 442376 | tf_op jit(solution)/shard_map/ppermute | solution.py:43
  137.9 17.0 %collective-permute-start.43 = (bf16[96,768]{1,0:T(8,128)(2,1)}, bf16[96,768]{1,0:T(8,128)(2,1)}, u32[]{:S(2)}, u32[]{:S(2)}) collective-permute-start(bf16[96,768]{1,0:T(8,128)(2,1)} %get-tuple-element.266), channel_id=1, source_target_pairs={{0,24},{4,28},{8,16},{12,20},{16,8},{20,12},{24,0},{28,4},{1,25},{... | collective-permute-start | bytes 442376 | tf_op jit(solution)/shard_map/ppermute | solution.py:43
  140.0 14.8 %all-to-all-start = ((bf16[32,8,128]{2,1,0:T(8,128)(2,1)}), bf16[32,8,128]{2,1,0:T(8,128)(2,1)S(1)}, u32[]{:S(2)}, u32[]{:S(2)}) async-start(bf16[32,8,128]{2,1,0:T(8,128)(2,1)} %shard_map.297), calls=%async_computation | async-start | bytes 131072 | tf_op jit(solution)/shard_map/all_to_all | solution.py:1103
  157.2 17.1 %collective-permute-start.44 = (bf16[4,96,768]{2,1,0:T(8,128)(2,1)S(1)}, bf16[4,96,768]{2,1,0:T(8,128)(2,1)S(1)}, u32[]{:S(2)}, u32[]{:S(2)}) collective-permute-start(bf16[4,96,768]{2,1,0:T(8,128)(2,1)S(1)} %get-tuple-element.276), channel_id=1, source_target_pairs={{0,2},{1,3},{2,0},{3,1},{4,6},{5,7},{6,4},{7,5},{8,10},{9,11},{10,... | collective-permute-start | bytes 1769480 | tf_op jit(solution)/shard_map/ppermute | solution.py:35
  158.7 15.7 %collective-permute-start.45 = (bf16[4,96,768]{2,1,0:T(8,128)(2,1)S(1)}, bf16[4,96,768]{2,1,0:T(8,128)(2,1)S(1)}, u32[]{:S(2)}, u32[]{:S(2)}) collective-permute-start(bf16[4,96,768]{2,1,0:T(8,128)(2,1)S(1)} %get-tuple-element.277), channel_id=1, source_target_pairs={{0,4},{4,0},{8,12},{12,8},{16,20},{20,16},{24,28},{28,24},{1,5},{5... | collective-permute-start | bytes 1769480 | tf_op jit(solution)/shard_map/ppermute | solution.py:39
  159.3 7.5 %collective-permute-start.46 = (bf16[96,768]{1,0:T(8,128)(2,1)}, bf16[96,768]{1,0:T(8,128)(2,1)S(1)}, u32[]{:S(2)}, u32[]{:S(2)}) collective-permute-start(bf16[96,768]{1,0:T(8,128)(2,1)} %get-tuple-element.278), channel_id=1, source_target_pairs={{0,8},{4,12},{8,0},{12,4},{16,24},{20,28},{24,16},{28,20},{1,9},{5... | collective-permute-start | bytes 442376 | tf_op jit(solution)/shard_map/ppermute | solution.py:43
  160.3 14.1 %collective-permute-start.47 = (bf16[96,768]{1,0:T(8,128)(2,1)}, bf16[96,768]{1,0:T(8,128)(2,1)S(1)}, u32[]{:S(2)}, u32[]{:S(2)}) collective-permute-start(bf16[96,768]{1,0:T(8,128)(2,1)} %get-tuple-element.279), channel_id=1, source_target_pairs={{0,16},{4,20},{8,24},{12,28},{16,0},{20,4},{24,8},{28,12},{1,17},{... | collective-permute-start | bytes 442376 | tf_op jit(solution)/shard_map/ppermute | solution.py:43
  162.4 12.0 %collective-permute-start.48 = (bf16[96,768]{1,0:T(8,128)(2,1)}, bf16[96,768]{1,0:T(8,128)(2,1)S(1)}, u32[]{:S(2)}, u32[]{:S(2)}) collective-permute-start(bf16[96,768]{1,0:T(8,128)(2,1)} %get-tuple-element.280), channel_id=1, source_target_pairs={{0,24},{4,28},{8,16},{12,20},{16,8},{20,12},{24,0},{28,4},{1,25},{... | collective-permute-start | bytes 442376 | tf_op jit(solution)/shard_map/ppermute | solution.py:43
  175.2 7.2 %collective-permute-start.49 = (bf16[96,768]{1,0:T(8,128)(2,1)}, bf16[96,768]{1,0:T(8,128)(2,1)S(1)}, u32[]{:S(2)}, u32[]{:S(2)}) collective-permute-start(bf16[96,768]{1,0:T(8,128)(2,1)} %get-tuple-element.285), channel_id=1, source_target_pairs={{0,8},{4,12},{8,0},{12,4},{16,24},{20,28},{24,16},{28,20},{1,9},{5... | collective-permute-start | bytes 442376 | tf_op jit(solution)/shard_map/ppermute | solution.py:43
  177.4 13.1 %collective-permute-start.50 = (bf16[96,768]{1,0:T(8,128)(2,1)}, bf16[96,768]{1,0:T(8,128)(2,1)S(1)}, u32[]{:S(2)}, u32[]{:S(2)}) collective-permute-start(bf16[96,768]{1,0:T(8,128)(2,1)} %get-tuple-element.286), channel_id=1, source_target_pairs={{0,16},{4,20},{8,24},{12,28},{16,0},{20,4},{24,8},{28,12},{1,17},{... | collective-permute-start | bytes 442376 | tf_op jit(solution)/shard_map/ppermute | solution.py:43
  178.5 12.1 %collective-permute-start.51 = (bf16[96,768]{1,0:T(8,128)(2,1)}, bf16[96,768]{1,0:T(8,128)(2,1)S(1)}, u32[]{:S(2)}, u32[]{:S(2)}) collective-permute-start(bf16[96,768]{1,0:T(8,128)(2,1)} %get-tuple-element.287), channel_id=1, source_target_pairs={{0,24},{4,28},{8,16},{12,20},{16,8},{20,12},{24,0},{28,4},{1,25},{... | collective-permute-start | bytes 442376 | tf_op jit(solution)/shard_map/ppermute | solution.py:43
  (27 other events, 265.4 us)

commit v8 on v7

--- a/solution.py
+++ b/solution.py
@@ -664,6 +664,26 @@
     )
 
 
+def ffn_half_kernel(x, ub, w0, w1, before, hid, slope, out):
+    uw, dw = ffn_weights((w0, w1))
+    up = nt(x[...], uw) + ub[...]
+    phi = 0.5 + 0.5 * lax.erf(up * (2.0**-0.5))
+    hd = (up * phi).astype(BF16)
+    hid[...] = hd
+    slope[...] = (phi + up * jnp.exp(-0.5 * up * up) * 0.3989422804014327).astype(BF16)
+    out[...] = (before[...] + nn(hd, dw)).astype(out.dtype)
+
+
+def ffn_half(x, ub, weights, before, dtype):
+    n, width = x.shape[0], ub.shape[1]
+    return call(
+        ffn_half_kernel,
+        (shape((n, width)), shape((n, width)), shape((n, D), dtype)),
+        (x, ub, *weights, before),
+        cost=est(1000, 1000),
+    )
+
+
 def second_kernel(bucket, lengths, first, part, got, small, cot, low, sum_two, normal):
     c = place_here()[0]
     _, units = live_units(bucket, lengths)
@@ -753,6 +773,57 @@
             out[i, at : at + ONE] = g[ONE * k : ONE * k + ONE]
             low = 4 * ONE + TWO * k
             out[i, at + ONE : at + rows] = g[low : low + TWO]
+
+
+def diagonal_of(refs, rows):
+    *weights, hid1, slope1, hid2, slope2 = refs
+    tail = slice(12 * TWO, 16 * TWO)
+    hid = jnp.concatenate([hid1[...], hid2[rows, tail]], 1)
+    slope = jnp.concatenate([slope1[...], slope2[rows, tail]], 1)
+    return hid, slope, *stacked(ones_of(weights[:-3]) + twos_of(weights[-3:], [3]))
+
+
+def diagonal_own_kernel(d, x, *refs):
+    *refs, down, up, ub, part = refs
+    hid, slope, uw, dw = diagonal_of(refs, slice(0, d.shape[0]))
+    cot = (nt(d[...], dw) * slope.astype(F32)).astype(BF16)
+    part[...] = nn(cot, uw)
+    ub[...] = jnp.sum(cot.astype(F32), 0, keepdims=True)
+    down[...], up[...] = tn(hid, d[...]), tn(cot, x[...])
+
+
+def diagonal_other_kernel(d, x, down, up, ub_own, *refs):
+    *refs, lo, hi, ub, part = refs
+    half, rows = d.shape[0], ONE + TWO
+    hid, slope, uw, dw = diagonal_of(refs, slice(half, 2 * half))
+    cot = (nt(d[...], dw) * slope.astype(F32)).astype(BF16)
+    part[...] = nn(cot, uw)
+    ub[...] = ub_own[...] + jnp.sum(cot.astype(F32), 0, keepdims=True)
+    dg = (down[...] + tn(hid, d[...])).astype(BF16)
+    ug = (up[...] + tn(cot, x[...])).astype(BF16)
+    for k in range(4):
+        out, i = (lo, hi)[k // 2], k % 2
+        for at, g in ((0, ug), (rows, dg)):
+            out[i, at : at + ONE] = g[ONE * k : ONE * k + ONE]
+            low = 4 * ONE + TWO * k
+            out[i, at + ONE : at + rows] = g[low : low + TWO]
+
+
+def ffn_back_diagonal(d0, d1, x0, x1, weights, own_kept, other_kept):
+    half, width = x0.shape[0], 4 * (ONE + TWO)
+    down, up, ub, own = call(
+        diagonal_own_kernel,
+        (shape((width, D), F32),) * 2 + (shape((1, width), F32), shape((half, D), F32)),
+        (d0, x0, *weights, *own_kept),
+        cost=est(1000, 1000),
+    )
+    lo, hi, ub, other = call(
+        diagonal_other_kernel,
+        (shape((2, width // 2, D)),) * 2 + (shape((1, width), F32), shape((half, D), F32)),
+        (d1, x1, down, up, ub, *weights, *other_kept),
+        cost=est(1000, 1000),
+    )
+    return [lo, hi], ub, (own, other)
 
 
 def ffn_back(d0, d1, x0, x1, spot, weights, kept, sums, last):
@@ -1023,6 +1094,13 @@
         width = FF // 4
         if direct:
             width = 16 * TWO if len(kept) == 3 else 4 * ONE
+        if direct and len(kept) == 4:
+            ub = ub_all[:, at : at + width]
+            hid1, slope1, part1 = ffn_half(first_in, ub, weights, sums[1], BF16)
+            hid0, slope0, part0 = ffn_half(first_low, ub, weights, sums[0], F32)
+            kept.append(((hid0, slope0), (hid1, slope1)))
+            sums = (part0, part1)
+            continue
         hid, slope, *sums = ffn(
             first_low,
             first_in,
@@ -1041,10 +1119,15 @@
     f_parts, ub_parts = [], []
     if direct:
         for spot, i in ((3, 4), (2, 2), (1, 1), (0, 0)):
-            weights, both = (*f_all[i], *twos), (*kept[i], *kept[3])
-            grads, ub, sums = ffn_back(
-                down_low, down_in, first_low, first_in, spot, weights, both, sums, spot == 0
-            )
+            weights = (*f_all[i], *twos)
+            rows = (down_low, down_in, first_low, first_in)
+            if spot == 3:
+                own, other = [(*half, *kept[3]) for half in kept[i]]
+                grads, ub, sums = ffn_back_diagonal(*rows, weights, own, other)
+            else:
+                grads, ub, sums = ffn_back(
+                    *rows, spot, weights, (*kept[i], *kept[3]), sums, spot == 0
+                )
             f_parts.append(grads)
             ub_parts.insert(0, ub)
     else:

time: 192 us -> 190 us (0.990)
    pallas_call x22 -> x24, Pallas kernels: 47.2 us -> 47.7 us  [call(): pl.pallas_call(kernel, out_shape=out_shape, in_specs=ins, out_specs=outs,...]
  transfers between devices with their start and end apart: 53 -> 53, of which waited for: 25 -> 25; matrix products, arithmetic and copies ran while one was open for 2% -> 2% of each run, Pallas kernels for 19% -> 20%
where the time goes in v8:
time: 190 us
  waiting for transfers between devices  75.7 us (40%)
  starting transfers between devices  59.6 us (31%)
  Pallas kernels  47.7 us (25%)
  local copies, waits for them, and re-layouts  3.4 us (2%)
  other arithmetic  2.37 us (1%)
    pallas_call x24, Pallas kernels, call(): pl.pallas_call(kernel, out_shape=out_shape, in_specs=ins, out_specs=outs,...  47.7 us
    ppermute x19, waiting for transfers between devices, z_swap(): return lax.ppermute(v, 'batch', ZPAIR[k])  45.1 us
    ppermute x19, starting transfers between devices, z_swap(): return lax.ppermute(v, 'batch', ZPAIR[k])  29.2 us
    ppermute x10, starting transfers between devices, x_swap(): return lax.ppermute(v, 'head', XPAIR)  13.2 us
    ppermute x10, waiting for transfers between devices, y_swap(): return lax.ppermute(v, 'batch', YPAIR)  12.4 us
    ppermute x10, starting transfers between devices, y_swap(): return lax.ppermute(v, 'batch', YPAIR)  10.6 us
    all_to_all x1, waiting for transfers between devices, local(): lax.all_to_all(terms, ('batch', 'head'), split_axis=0, concat_axis=0, til...  8.16 us
    ppermute x10, waiting for transfers between devices, x_swap(): return lax.ppermute(v, 'head', XPAIR)  6.75 us
  transfers between devices with their start and end apart: 53, of which 25 were waited for; matrix products, arithmetic and copies ran while one was open for 2% of the time, Pallas kernels for 20%

profile of v8, /device:TPU:0, one launch (start us, length us, event | category | flops | bytes accessed | tf_op | source)
XLA Modules:
  0.0 190.1 jit_solution(15998083328878567744)
XLA Ops:
  2.0 3.1 %collective-permute-start = (bf16[104,768]{1,0:T(8,128)(2,1)S(1)}, bf16[104,768]{1,0:T(8,128)(2,1)S(1)}, u32[]{:S(2)}, u32[]{:S(2)}) collective-permute-start(bf16[104,768]{1,0:T(8,128)(2,1)S(1)} %get-tuple-element.163), channel_id=1, source_target_pairs={{0,8},{4,12},{8,0},{12,4},{16,24},{20,28},{24,16},{28,20},{1,9},{5... | collective-permute-start | bytes 479240 | tf_op jit(solution)/shard_map/ppermute | solution.py:43
  5.1 2.5 %collective-permute-start.2 = (bf16[104,768]{1,0:T(8,128)(2,1)S(1)}, bf16[104,768]{1,0:T(8,128)(2,1)S(1)}, u32[]{:S(2)}, u32[]{:S(2)}) collective-permute-start(bf16[104,768]{1,0:T(8,128)(2,1)S(1)} %get-tuple-element.163), channel_id=1, source_target_pairs={{0,24},{4,28},{8,16},{12,20},{16,8},{20,12},{24,0},{28,4},{1,25},{... | collective-permute-start | bytes 479240 | tf_op jit(solution)/shard_map/ppermute | solution.py:43
  7.7 1.9 %collective-permute-done = bf16[104,768]{1,0:T(8,128)(2,1)S(1)} collective-permute-done((bf16[104,768]{1,0:T(8,128)(2,1)S(1)}, bf16[104,768]{1,0:T(8,128)(2,1)S(1)}, u32[]{:S(2)}, u32[]{:S(2)}) %collective-permute-start) | collective-permute-done | bytes 159776 | tf_op jit(solution)/shard_map/ppermute | solution.py:43
  9.6 1.5 collective-permute-start.4
  11.1 1.5 collective-permute-start.3
  13.7 1.5 collective-permute-start.5
  15.2 1.5 collective-permute-start.6
  16.7 5.1 %collective-permute-done.1 = bf16[104,768]{1,0:T(8,128)(2,1)S(1)} collective-permute-done((bf16[104,768]{1,0:T(8,128)(2,1)S(1)}, bf16[104,768]{1,0:T(8,128)(2,1)S(1)}, u32[]{:S(2)}, u32[]{:S(2)}) %collective-permute-start.1) | collective-permute-done | bytes 159776 | tf_op jit(solution)/shard_map/ppermute | solution.py:43
  21.9 1.6 collective-permute-start.9
  23.5 1.5 collective-permute-start.8
  25.1 2.7 %collective-permute-start.12 = (bf16[104,768]{1,0:T(8,128)(2,1)S(1)}, bf16[104,768]{1,0:T(8,128)(2,1)S(1)}, u32[]{:S(2)}, u32[]{:S(2)}) collective-permute-start(bf16[104,768]{1,0:T(8,128)(2,1)S(1)} %get-tuple-element.169), channel_id=1, source_target_pairs={{0,24},{4,28},{8,16},{12,20},{16,8},{20,12},{24,0},{28,4},{1,25},{... | collective-permute-start | bytes 479240 | tf_op jit(solution)/shard_map/ppermute | solution.py:43
  28.6 11.2 %collective-permute-done.12 = bf16[104,768]{1,0:T(8,128)(2,1)S(1)} collective-permute-done((bf16[104,768]{1,0:T(8,128)(2,1)S(1)}, bf16[104,768]{1,0:T(8,128)(2,1)S(1)}, u32[]{:S(2)}, u32[]{:S(2)}) %collective-permute-start.12) | collective-permute-done | bytes 159776 | tf_op jit(solution)/shard_map/ppermute | solution.py:43
  41.8 3.0 %collective-permute-start.15 = (bf16[56,768]{1,0:T(8,128)(2,1)S(1)}, bf16[56,768]{1,0:T(8,128)(2,1)S(1)}, u32[]{:S(2)}, u32[]{:S(2)}) collective-permute-start(bf16[56,768]{1,0:T(8,128)(2,1)S(1)} %get-tuple-element.176), channel_id=1, source_target_pairs={{0,24},{4,28},{8,16},{12,20},{16,8},{20,12},{24,0},{28,4},{1,25},{... | collective-permute-start | bytes 258056 | tf_op jit(solution)/shard_map/ppermute | solution.py:43
  44.8 1.3 collective-permute-start.13
  46.2 1.9 collective-permute-done.15
  48.1 2.2 %collective-permute-done.14 = bf16[56,768]{1,0:T(8,128)(2,1)S(1)} collective-permute-done((bf16[56,768]{1,0:T(8,128)(2,1)S(1)}, bf16[56,768]{1,0:T(8,128)(2,1)S(1)}, u32[]{:S(2)}, u32[]{:S(2)}) %collective-permute-start.14) | collective-permute-done | bytes 86048 | tf_op jit(solution)/shard_map/ppermute | solution.py:43
  51.7 1.5 collective-permute-start.25
  53.2 1.6 collective-permute-start.24
  55.5 2.1 %collective-permute-start.26 = (bf16[8,32,768]{2,1,0:T(8,128)(2,1)S(1)}, bf16[8,32,768]{2,1,0:T(8,128)(2,1)S(1)}, u32[]{:S(2)}, u32[]{:S(2)}) collective-permute-start(bf16[8,32,768]{2,1,0:T(8,128)(2,1)S(1)} %pad_maximum_fusion.2), channel_id=1, source_target_pairs={{0,16},{4,20},{8,24},{12,28},{16,0},{20,4},{24,8},{28,12},{1,17},{... | collective-permute-start | bytes 1179656 | tf_op jit(solution)/shard_map/ppermute | solution.py:43
  59.3 10.3 %shard_map.281 = (bf16[256,384]{1,0:T(8,128)(2,1)S(1)}, bf16[256,384]{1,0:T(8,128)(2,1)S(1)}, bf16[512,384]{1,0:T(8,128)(2,1)S(1)}, bf16[512,384]{1,0:T(8,128)(2...) custom-call(s32[2]{0:T(128)S(1)} %copy-done.10, ...), custom_call_target="tpu_custom_call" | custom-call | flops 1000 | bytes 1000 | tf_op jit(solution)/shard_map/pallas_call | solution.py:108
  69.7 1.4 collective-permute-done.23.ctx_in
  72.2 3.8 %collective-permute-done.26.refs_2_.refs_4_.refs_3_ = bf16[8,32,768]{2,1,0:T(8,128)(2,1)S(1)} collective-permute-done((bf16[8,32,768]{2,1,0:T(8,128)(2,1)S(1)}, bf16[8,32,768]{2,1,0:T(8,128)(2,1)S(1)}, u32[]{:S(2)}, u32[]{:S(2)}) %collective-permute-start.26) | collective-permute-done | bytes 393248 | tf_op jit(solution)/shard_map/ppermute | solution.py:43
  77.7 1.5 collective-permute-start.27
  81.8 1.5 shard_map.285
  84.6 5.0 %collective-permute-done.28.w1.refs_1_ = bf16[2,160,768]{2,1,0:T(8,128)(2,1)S(1)} collective-permute-done((bf16[2,160,768]{2,1,0:T(8,128)(2,1)S(1)}, bf16[2,160,768]{2,1,0:T(8,128)(2,1)S(1)}, u32[]{:S(2)}, u32[]{:S(2)}) %collective-permute-start.28) | collective-permute-done | bytes 491552 | tf_op jit(solution)/shard_map/ppermute | solution.py:39
  96.5 1.5 collective-permute-start.33
  98.0 1.6 collective-permute-start.34
  99.6 1.9 shard_map.292
  101.5 1.9 shard_map.293
  103.4 1.9 shard_map.294
  105.3 1.5 shard_map.295
  107.0 5.0 %collective-permute-done.33.refs_2_ = bf16[2,192,768]{2,1,0:T(8,128)(2,1)S(1)} collective-permute-done((bf16[2,192,768]{2,1,0:T(8,128)(2,1)S(1)}, bf16[2,192,768]{2,1,0:T(8,128)(2,1)S(1)}, u32[]{:S(2)}, u32[]{:S(2)}) %collective-permute-start.33) | collective-permute-done | bytes 589856 | tf_op jit(solution)/shard_map/ppermute | solution.py:39
  114.3 1.6 collective-permute-start.37
  116.5 9.2 %shard_map.297 = (bf16[4,96,768]{2,1,0:T(8,128)(2,1)}, bf16[4,96,768]{2,1,0:T(8,128)(2,1)}, bf16[4,96,768]{2,1,0:T(8,128)(2,1)}, bf16[6,96,768]{2,1,0:T(8,128)(2...) custom-call(bf16[256,768]{1,0:T(8,128)(2,1)S(1)} %get-tuple-element., ...), custom_call_target="tpu_custom_call" | custom-call | flops 8000000000 | bytes 14000000 | tf_op jit(solution)/shard_map/pallas_call | solution.py:108
  125.8 4.2 %collective-permute-done.37.x = bf16[4,96,768]{2,1,0:T(8,128)(2,1)S(1)} collective-permute-done((bf16[4,96,768]{2,1,0:T(8,128)(2,1)S(1)}, bf16[4,96,768]{2,1,0:T(8,128)(2,1)S(1)}, u32[]{:S(2)}, u32[]{:S(2)}) %collective-permute-start.37) | collective-permute-done | bytes 589856 | tf_op jit(solution)/shard_map/ppermute | solution.py:35
  134.4 2.2 %collective-permute-start.42 = (bf16[96,768]{1,0:T(8,128)(2,1)}, bf16[96,768]{1,0:T(8,128)(2,1)}, u32[]{:S(2)}, u32[]{:S(2)}) collective-permute-start(bf16[96,768]{1,0:T(8,128)(2,1)} %get-tuple-element.275), channel_id=1, source_target_pairs={{0,16},{4,20},{8,24},{12,28},{16,0},{20,4},{24,8},{28,12},{1,17},{... | collective-permute-start | bytes 442376 | tf_op jit(solution)/shard_map/ppermute | solution.py:43
  138.7 4.7 %all-to-all-start = ((bf16[32,8,128]{2,1,0:T(8,128)(2,1)}), bf16[32,8,128]{2,1,0:T(8,128)(2,1)S(1)}, u32[]{:S(2)}, u32[]{:S(2)}) async-start(bf16[32,8,128]{2,1,0:T(8,128)(2,1)} %shard_map.299), calls=%async_computation | async-start | bytes 131072 | tf_op jit(solution)/shard_map/all_to_all | solution.py:1186
  143.5 2.0 %add_convert_fusion = bf16[256,768]{1,0:T(8,128)(2,1)} fusion(bf16[256,768]{1,0:T(8,128)(2,1)} %copy-done.17, f32[256,768]{1,0:T(8,128)S(1)} %get-tuple-element.248, f32[256,768]{1,0:T(8,128)S(1)} %get-tuple-element.258), kind=kLoop, calls=%fused_computation.1 | loop fusion | flops 786432 | bytes 2359296 | tf_op jit(solution)/shard_map/convert_element_type | solution.py:1176
  145.4 8.2 %all-to-all-done = bf16[32,8,128]{2,1,0:T(8,128)(2,1)S(1)} async-done(((bf16[32,8,128]{2,1,0:T(8,128)(2,1)}), bf16[32,8,128]{2,1,0:T(8,128)(2,1)S(1)}, u32[]{:S(2)}, u32[]{:S(2)}) %all-to-all-start) | async-done | bytes 65568 | tf_op jit(solution)/shard_map/all_to_all | solution.py:1186
  153.6 2.3 %shard_map.300 = (bf16[4,96,768]{2,1,0:T(8,128)(2,1)S(1)}, bf16[4,96,768]{2,1,0:T(8,128)(2,1)S(1)}, f32[96,768]{1,0:T(8,128)}, bf16[96,768]{1,0:T(8,128)(2,1)}, ...) custom-call(bf16[4,96,768]{2,1,0:T(8,128)(2,1)S(1)} %copy-done.3, bf16[4,96,768]{2,1,0:T(8,128)(2,1)S(1)} %copy-done.4, ...), custom_call_target="tpu_custom_call" | custom-call | flops 1000 | bytes 1000 | tf_op jit(solution)/shard_map/pallas_call | solution.py:108
  155.9 1.4 collective-permute-start.44
  158.9 2.1 %collective-permute-start.47 = (bf16[96,768]{1,0:T(8,128)(2,1)}, bf16[96,768]{1,0:T(8,128)(2,1)S(1)}, u32[]{:S(2)}, u32[]{:S(2)}) collective-permute-start(bf16[96,768]{1,0:T(8,128)(2,1)} %get-tuple-element.289), channel_id=1, source_target_pairs={{0,16},{4,20},{8,24},{12,28},{16,0},{20,4},{24,8},{28,12},{1,17},{... | collective-permute-start | bytes 442376 | tf_op jit(solution)/shard_map/ppermute | solution.py:43
  162.9 2.6 %collective-permute-done.46.refs_5_ = bf16[96,768]{1,0:T(8,128)(2,1)S(1)} collective-permute-done((bf16[96,768]{1,0:T(8,128)(2,1)}, bf16[96,768]{1,0:T(8,128)(2,1)S(1)}, u32[]{:S(2)}, u32[]{:S(2)}) %collective-permute-start.46) | collective-permute-done | bytes 147488 | tf_op jit(solution)/shard_map/ppermute | solution.py:43
  165.5 7.5 %collective-permute-done.47.refs_6_ = bf16[96,768]{1,0:T(8,128)(2,1)S(1)} collective-permute-done((bf16[96,768]{1,0:T(8,128)(2,1)}, bf16[96,768]{1,0:T(8,128)(2,1)S(1)}, u32[]{:S(2)}, u32[]{:S(2)}) %collective-permute-start.47) | collective-permute-done | bytes 147488 | tf_op jit(solution)/shard_map/ppermute | solution.py:43
  173.9 2.2 %collective-permute-start.49 = (bf16[96,768]{1,0:T(8,128)(2,1)}, bf16[96,768]{1,0:T(8,128)(2,1)S(1)}, u32[]{:S(2)}, u32[]{:S(2)}) collective-permute-start(bf16[96,768]{1,0:T(8,128)(2,1)} %get-tuple-element.295), channel_id=1, source_target_pairs={{0,8},{4,12},{8,0},{12,4},{16,24},{20,28},{24,16},{28,20},{1,9},{5... | collective-permute-start | bytes 442376 | tf_op jit(solution)/shard_map/ppermute | solution.py:43
  177.1 1.4 collective-permute-start.51
  179.1 1.9 shard_map.303
  181.1 8.1 %collective-permute-done.50.two = bf16[96,768]{1,0:T(8,128)(2,1)S(1)} collective-permute-done((bf16[96,768]{1,0:T(8,128)(2,1)}, bf16[96,768]{1,0:T(8,128)(2,1)S(1)}, u32[]{:S(2)}, u32[]{:S(2)}) %collective-permute-start.50) | collective-permute-done | bytes 147488 | tf_op jit(solution)/shard_map/ppermute | solution.py:43
  (149 shorter events, 39.5 us)
Async XLA Ops:
  2.0 7.6 %collective-permute-start = (bf16[104,768]{1,0:T(8,128)(2,1)S(1)}, bf16[104,768]{1,0:T(8,128)(2,1)S(1)}, u32[]{:S(2)}, u32[]{:S(2)}) collective-permute-start(bf16[104,768]{1,0:T(8,128)(2,1)S(1)} %get-tuple-element.163), channel_id=1, source_target_pairs={{0,8},{4,12},{8,0},{12,4},{16,24},{20,28},{24,16},{28,20},{1,9},{5... | collective-permute-start | bytes 479240 | tf_op jit(solution)/shard_map/ppermute | solution.py:43
  5.1 11.6 %collective-permute-start.2 = (bf16[104,768]{1,0:T(8,128)(2,1)S(1)}, bf16[104,768]{1,0:T(8,128)(2,1)S(1)}, u32[]{:S(2)}, u32[]{:S(2)}) collective-permute-start(bf16[104,768]{1,0:T(8,128)(2,1)S(1)} %get-tuple-element.163), channel_id=1, source_target_pairs={{0,24},{4,28},{8,16},{12,20},{16,8},{20,12},{24,0},{28,4},{1,25},{... | collective-permute-start | bytes 479240 | tf_op jit(solution)/shard_map/ppermute | solution.py:43
  7.5 14.2 %collective-permute-start.1 = (bf16[104,768]{1,0:T(8,128)(2,1)S(1)}, bf16[104,768]{1,0:T(8,128)(2,1)S(1)}, u32[]{:S(2)}, u32[]{:S(2)}) collective-permute-start(bf16[104,768]{1,0:T(8,128)(2,1)S(1)} %get-tuple-element.163), channel_id=1, source_target_pairs={{0,16},{4,20},{8,24},{12,28},{16,0},{20,4},{24,8},{28,12},{1,17},{... | collective-permute-start | bytes 479240 | tf_op jit(solution)/shard_map/ppermute | solution.py:43
  9.6 4.1 %collective-permute-start.4 = (bf16[32,768]{1,0:T(8,128)(2,1)S(1)}, bf16[32,768]{1,0:T(8,128)(2,1)S(1)}, u32[]{:S(2)}, u32[]{:S(2)}) collective-permute-start(bf16[32,768]{1,0:T(8,128)(2,1)S(1)} %get-tuple-element.165), channel_id=1, source_target_pairs={{0,4},{4,0},{8,12},{12,8},{16,20},{20,16},{24,28},{28,24},{1,5},{5... | collective-permute-start | bytes 147464 | tf_op jit(solution)/shard_map/ppermute | solution.py:39
  11.1 4.1 %collective-permute-start.3 = (bf16[32,768]{1,0:T(8,128)(2,1)S(1)}, bf16[32,768]{1,0:T(8,128)(2,1)S(1)}, u32[]{:S(2)}, u32[]{:S(2)}) collective-permute-start(bf16[32,768]{1,0:T(8,128)(2,1)S(1)} %get-tuple-element.165), channel_id=1, source_target_pairs={{0,2},{1,3},{2,0},{3,1},{4,6},{5,7},{6,4},{7,5},{8,10},{9,11},{10,... | collective-permute-start | bytes 147464 | tf_op jit(solution)/shard_map/ppermute | solution.py:35
  12.6 9.3 %collective-permute-start.7 = (bf16[256,768]{1,0:T(8,128)(2,1)}, bf16[256,768]{1,0:T(8,128)(2,1)S(1)}, u32[]{:S(2)}, u32[]{:S(2)}) collective-permute-start(bf16[256,768]{1,0:T(8,128)(2,1)} %refs_8_.1), channel_id=1, source_target_pairs={{0,1},{1,0},{2,3},{3,2},{4,5},{5,4},{6,7},{7,6},{8,9},{9,8},{10,11... | collective-permute-start | bytes 1179656 | tf_op jit(solution)/shard_map/ppermute | solution.py:31
  13.7 8.2 %collective-permute-start.5 = (bf16[16,768]{1,0:T(8,128)(2,1)S(1)}, bf16[16,768]{1,0:T(8,128)(2,1)S(1)}, u32[]{:S(2)}, u32[]{:S(2)}) collective-permute-start(bf16[16,768]{1,0:T(8,128)(2,1)S(1)} %slice.129), channel_id=1, source_target_pairs={{0,2},{1,3},{2,0},{3,1},{4,6},{5,7},{6,4},{7,5},{8,10},{9,11},{10,... | collective-permute-start | bytes 73736 | tf_op jit(solution)/shard_map/ppermute | solution.py:35
  15.2 6.7 %collective-permute-start.6 = (bf16[16,768]{1,0:T(8,128)(2,1)S(1)}, bf16[16,768]{1,0:T(8,128)(2,1)S(1)}, u32[]{:S(2)}, u32[]{:S(2)}) collective-permute-start(bf16[16,768]{1,0:T(8,128)(2,1)S(1)} %slice.130), channel_id=1, source_target_pairs={{0,4},{4,0},{8,12},{12,8},{16,20},{20,16},{24,28},{28,24},{1,5},{5... | collective-permute-start | bytes 73736 | tf_op jit(solution)/shard_map/ppermute | solution.py:39
  21.9 18.7 %collective-permute-start.9 = (bf16[4,104,768]{2,1,0:T(8,128)(2,1)S(1)}, bf16[4,104,768]{2,1,0:T(8,128)(2,1)S(1)}, u32[]{:S(2)}, u32[]{:S(2)}) collective-permute-start(bf16[4,104,768]{2,1,0:T(8,128)(2,1)S(1)} %pad_maximum_fusion.1.refs_0_), channel_id=1, source_target_pairs={{0,4},{4,0},{8,12},{12,8},{16,20},{20,16},{24,28},{28,24},{1,5},{5... | collective-permute-start | bytes 1916936 | tf_op jit(solution)/shard_map/ppermute | solution.py:39
  23.5 17.1 %collective-permute-start.8 = (bf16[4,104,768]{2,1,0:T(8,128)(2,1)S(1)}, bf16[4,104,768]{2,1,0:T(8,128)(2,1)S(1)}, u32[]{:S(2)}, u32[]{:S(2)}) collective-permute-start(bf16[4,104,768]{2,1,0:T(8,128)(2,1)S(1)} %pad_maximum_fusion.1.refs_0_), channel_id=1, source_target_pairs={{0,2},{1,3},{2,0},{3,1},{4,6},{5,7},{6,4},{7,5},{8,10},{9,11},{10,... | collective-permute-start | bytes 1916936 | tf_op jit(solution)/shard_map/ppermute | solution.py:35
  25.0 15.5 %collective-permute-start.10 = (bf16[232,768]{1,0:T(8,128)(2,1)S(1)}, bf16[232,768]{1,0:T(8,128)(2,1)S(1)}, u32[]{:S(2)}, u32[]{:S(2)}) collective-permute-start(bf16[232,768]{1,0:T(8,128)(2,1)S(1)} %pad_maximum_fusion.3), channel_id=1, source_target_pairs={{0,8},{4,12},{8,0},{12,4},{16,24},{20,28},{24,16},{28,20},{1,9},{5... | collective-permute-start | bytes 1069064 | tf_op jit(solution)/shard_map/ppermute | solution.py:43
  25.1 14.7 %collective-permute-start.12 = (bf16[104,768]{1,0:T(8,128)(2,1)S(1)}, bf16[104,768]{1,0:T(8,128)(2,1)S(1)}, u32[]{:S(2)}, u32[]{:S(2)}) collective-permute-start(bf16[104,768]{1,0:T(8,128)(2,1)S(1)} %get-tuple-element.169), channel_id=1, source_target_pairs={{0,24},{4,28},{8,16},{12,20},{16,8},{20,12},{24,0},{28,4},{1,25},{... | collective-permute-start | bytes 479240 | tf_op jit(solution)/shard_map/ppermute | solution.py:43
  27.8 12.0 %collective-permute-start.11 = (bf16[104,768]{1,0:T(8,128)(2,1)S(1)}, bf16[104,768]{1,0:T(8,128)(2,1)S(1)}, u32[]{:S(2)}, u32[]{:S(2)}) collective-permute-start(bf16[104,768]{1,0:T(8,128)(2,1)S(1)} %get-tuple-element.169), channel_id=1, source_target_pairs={{0,16},{4,20},{8,24},{12,28},{16,0},{20,4},{24,8},{28,12},{1,17},{... | collective-permute-start | bytes 479240 | tf_op jit(solution)/shard_map/ppermute | solution.py:43
  40.7 9.6 %collective-permute-start.17 = (bf16[2,104,768]{2,1,0:T(8,128)(2,1)S(1)}, bf16[2,104,768]{2,1,0:T(8,128)(2,1)S(1)}, u32[]{:S(2)}, u32[]{:S(2)}) collective-permute-start(bf16[2,104,768]{2,1,0:T(8,128)(2,1)S(1)} %slice.102), channel_id=1, source_target_pairs={{0,4},{4,0},{8,12},{12,8},{16,20},{20,16},{24,28},{28,24},{1,5},{5... | collective-permute-start | bytes 958472 | tf_op jit(solution)/shard_map/ppermute | solution.py:39
  41.2 9.0 %collective-permute-start.16 = (bf16[2,104,768]{2,1,0:T(8,128)(2,1)S(1)}, bf16[2,104,768]{2,1,0:T(8,128)(2,1)S(1)}, u32[]{:S(2)}, u32[]{:S(2)}) collective-permute-start(bf16[2,104,768]{2,1,0:T(8,128)(2,1)S(1)} %slice.101), channel_id=1, source_target_pairs={{0,2},{1,3},{2,0},{3,1},{4,6},{5,7},{6,4},{7,5},{8,10},{9,11},{10,... | collective-permute-start | bytes 958472 | tf_op jit(solution)/shard_map/ppermute | solution.py:35
  41.8 6.3 %collective-permute-start.15 = (bf16[56,768]{1,0:T(8,128)(2,1)S(1)}, bf16[56,768]{1,0:T(8,128)(2,1)S(1)}, u32[]{:S(2)}, u32[]{:S(2)}) collective-permute-start(bf16[56,768]{1,0:T(8,128)(2,1)S(1)} %get-tuple-element.176), channel_id=1, source_target_pairs={{0,24},{4,28},{8,16},{12,20},{16,8},{20,12},{24,0},{28,4},{1,25},{... | collective-permute-start | bytes 258056 | tf_op jit(solution)/shard_map/ppermute | solution.py:43
  44.8 5.4 %collective-permute-start.14 = (bf16[56,768]{1,0:T(8,128)(2,1)S(1)}, bf16[56,768]{1,0:T(8,128)(2,1)S(1)}, u32[]{:S(2)}, u32[]{:S(2)}) collective-permute-start(bf16[56,768]{1,0:T(8,128)(2,1)S(1)} %get-tuple-element.176), channel_id=1, source_target_pairs={{0,16},{4,20},{8,24},{12,28},{16,0},{20,4},{24,8},{28,12},{1,17},{... | collective-permute-start | bytes 258056 | tf_op jit(solution)/shard_map/ppermute | solution.py:43
  44.8 5.4 %collective-permute-start.13 = (bf16[56,768]{1,0:T(8,128)(2,1)S(1)}, bf16[56,768]{1,0:T(8,128)(2,1)S(1)}, u32[]{:S(2)}, u32[]{:S(2)}) collective-permute-start(bf16[56,768]{1,0:T(8,128)(2,1)S(1)} %get-tuple-element.176), channel_id=1, source_target_pairs={{0,8},{4,12},{8,0},{12,4},{16,24},{20,28},{24,16},{28,20},{1,9},{5... | collective-permute-start | bytes 258056 | tf_op jit(solution)/shard_map/ppermute | solution.py:43
  51.1 3.7 %collective-permute-start.21 = (bf16[2,104,768]{2,1,0:T(8,128)(2,1)S(1)}, bf16[2,104,768]{2,1,0:T(8,128)(2,1)S(1)}, u32[]{:S(2)}, u32[]{:S(2)}) collective-permute-start(bf16[2,104,768]{2,1,0:T(8,128)(2,1)S(1)} %collective-permute-done.16.refs_3_), channel_id=1, source_target_pairs={{0,1},{1,0},{2,3},{3,2},{4,5},{5,4},{6,7},{7,6},{8,9},{9,8},{10,11... | collective-permute-start | bytes 958472 | tf_op jit(solution)/shard_map/ppermute | solution.py:31
  51.1 3.8 %collective-permute-start.22 = (bf16[2,104,768]{2,1,0:T(8,128)(2,1)S(1)}, bf16[2,104,768]{2,1,0:T(8,128)(2,1)S(1)}, u32[]{:S(2)}, u32[]{:S(2)}) collective-permute-start(bf16[2,104,768]{2,1,0:T(8,128)(2,1)S(1)} %collective-permute-done.17.refs_4_), channel_id=1, source_target_pairs={{0,1},{1,0},{2,3},{3,2},{4,5},{5,4},{6,7},{7,6},{8,9},{9,8},{10,11... | collective-permute-start | bytes 958472 | tf_op jit(solution)/shard_map/ppermute | solution.py:31
  51.6 3.9 %collective-permute-start.18 = (bf16[4,104,768]{2,1,0:T(8,128)(2,1)S(1)}, bf16[4,104,768]{2,1,0:T(8,128)(2,1)S(1)}, u32[]{:S(2)}, u32[]{:S(2)}) collective-permute-start(bf16[4,104,768]{2,1,0:T(8,128)(2,1)S(1)} %pad_maximum_fusion.1.refs_0_), channel_id=1, source_target_pairs={{0,1},{1,0},{2,3},{3,2},{4,5},{5,4},{6,7},{7,6},{8,9},{9,8},{10,11... | collective-permute-start | bytes 1916936 | tf_op jit(solution)/shard_map/ppermute | solution.py:31
  51.7 24.3 %collective-permute-start.25 = (bf16[4,160,768]{2,1,0:T(8,128)(2,1)S(1)}, bf16[4,160,768]{2,1,0:T(8,128)(2,1)S(1)}, u32[]{:S(2)}, u32[]{:S(2)}) collective-permute-start(bf16[4,160,768]{2,1,0:T(8,128)(2,1)S(1)} %pad_maximum_fusion.refs_0_), channel_id=1, source_target_pairs={{0,4},{4,0},{8,12},{12,8},{16,20},{20,16},{24,28},{28,24},{1,5},{5... | collective-permute-start | bytes 2949128 | tf_op jit(solution)/shard_map/ppermute | solution.py:39
  53.2 23.8 %collective-permute-start.24 = (bf16[4,160,768]{2,1,0:T(8,128)(2,1)S(1)}, bf16[4,160,768]{2,1,0:T(8,128)(2,1)S(1)}, u32[]{:S(2)}, u32[]{:S(2)}) collective-permute-start(bf16[4,160,768]{2,1,0:T(8,128)(2,1)S(1)} %pad_maximum_fusion.refs_0_), channel_id=1, source_target_pairs={{0,2},{1,3},{2,0},{3,1},{4,6},{5,7},{6,4},{7,5},{8,10},{9,11},{10,... | collective-permute-start | bytes 2949128 | tf_op jit(solution)/shard_map/ppermute | solution.py:35
  54.8 2.8 %collective-permute-start.19 = (bf16[4,104,768]{2,1,0:T(8,128)(2,1)S(1)}, bf16[4,104,768]{2,1,0:T(8,128)(2,1)S(1)}, u32[]{:S(2)}, u32[]{:S(2)}) collective-permute-start(bf16[4,104,768]{2,1,0:T(8,128)(2,1)S(1)} %collective-permute-done.8.refs_1_), channel_id=1, source_target_pairs={{0,1},{1,0},{2,3},{3,2},{4,5},{5,4},{6,7},{7,6},{8,9},{9,8},{10,11... | collective-permute-start | bytes 1916936 | tf_op jit(solution)/shard_map/ppermute | solution.py:31
  54.9 2.9 %collective-permute-start.20 = (bf16[4,104,768]{2,1,0:T(8,128)(2,1)S(1)}, bf16[4,104,768]{2,1,0:T(8,128)(2,1)S(1)}, u32[]{:S(2)}, u32[]{:S(2)}) collective-permute-start(bf16[4,104,768]{2,1,0:T(8,128)(2,1)S(1)} %collective-permute-done.9.refs_2_), channel_id=1, source_target_pairs={{0,1},{1,0},{2,3},{3,2},{4,5},{5,4},{6,7},{7,6},{8,9},{9,8},{10,11... | collective-permute-start | bytes 1916936 | tf_op jit(solution)/shard_map/ppermute | solution.py:31
  55.5 20.5 %collective-permute-start.26 = (bf16[8,32,768]{2,1,0:T(8,128)(2,1)S(1)}, bf16[8,32,768]{2,1,0:T(8,128)(2,1)S(1)}, u32[]{:S(2)}, u32[]{:S(2)}) collective-permute-start(bf16[8,32,768]{2,1,0:T(8,128)(2,1)S(1)} %pad_maximum_fusion.2), channel_id=1, source_target_pairs={{0,16},{4,20},{8,24},{12,28},{16,0},{20,4},{24,8},{28,12},{1,17},{... | collective-permute-start | bytes 1179656 | tf_op jit(solution)/shard_map/ppermute | solution.py:43
  72.0 7.2 %collective-permute-start.29 = (bf16[256,768]{1,0:T(8,128)(2,1)S(1)}, bf16[256,768]{1,0:T(8,128)(2,1)S(1)}, u32[]{:S(2)}, u32[]{:S(2)}) collective-permute-start(bf16[256,768]{1,0:T(8,128)(2,1)S(1)} %get-tuple-element.194.x0.x), channel_id=1, source_target_pairs={{0,1},{1,0},{2,3},{3,2},{4,5},{5,4},{6,7},{7,6},{8,9},{9,8},{10,11... | collective-permute-start | bytes 1179656 | tf_op jit(solution)/shard_map/ppermute | solution.py:31
  77.1 12.5 %collective-permute-start.28 = (bf16[2,160,768]{2,1,0:T(8,128)(2,1)S(1)}, bf16[2,160,768]{2,1,0:T(8,128)(2,1)S(1)}, u32[]{:S(2)}, u32[]{:S(2)}) collective-permute-start(bf16[2,160,768]{2,1,0:T(8,128)(2,1)S(1)} %slice.107), channel_id=1, source_target_pairs={{0,4},{4,0},{8,12},{12,8},{16,20},{20,16},{24,28},{28,24},{1,5},{5... | collective-permute-start | bytes 1474568 | tf_op jit(solution)/shard_map/ppermute | solution.py:39
  77.7 12.3 %collective-permute-start.27 = (bf16[2,160,768]{2,1,0:T(8,128)(2,1)S(1)}, bf16[2,160,768]{2,1,0:T(8,128)(2,1)S(1)}, u32[]{:S(2)}, u32[]{:S(2)}) collective-permute-start(bf16[2,160,768]{2,1,0:T(8,128)(2,1)S(1)} %slice.106), channel_id=1, source_target_pairs={{0,2},{1,3},{2,0},{3,1},{4,6},{5,7},{6,4},{7,5},{8,10},{9,11},{10,... | collective-permute-start | bytes 1474568 | tf_op jit(solution)/shard_map/ppermute | solution.py:35
  96.5 15.4 %collective-permute-start.33 = (bf16[2,192,768]{2,1,0:T(8,128)(2,1)S(1)}, bf16[2,192,768]{2,1,0:T(8,128)(2,1)S(1)}, u32[]{:S(2)}, u32[]{:S(2)}) collective-permute-start(bf16[2,192,768]{2,1,0:T(8,128)(2,1)S(1)} %get-tuple-element.244), channel_id=1, source_target_pairs={{0,4},{4,0},{8,12},{12,8},{16,20},{20,16},{24,28},{28,24},{1,5},{5... | collective-permute-start | bytes 1769480 | tf_op jit(solution)/shard_map/ppermute | solution.py:39
  98.0 15.1 %collective-permute-start.34 = (bf16[2,192,768]{2,1,0:T(8,128)(2,1)S(1)}, bf16[2,192,768]{2,1,0:T(8,128)(2,1)S(1)}, u32[]{:S(2)}, u32[]{:S(2)}) collective-permute-start(bf16[2,192,768]{2,1,0:T(8,128)(2,1)S(1)} %get-tuple-element.247), channel_id=1, source_target_pairs={{0,2},{1,3},{2,0},{3,1},{4,6},{5,7},{6,4},{7,5},{8,10},{9,11},{10,... | collective-permute-start | bytes 1769480 | tf_op jit(solution)/shard_map/ppermute | solution.py:35
  114.3 15.7 %collective-permute-start.37 = (bf16[4,96,768]{2,1,0:T(8,128)(2,1)S(1)}, bf16[4,96,768]{2,1,0:T(8,128)(2,1)S(1)}, u32[]{:S(2)}, u32[]{:S(2)}) collective-permute-start(bf16[4,96,768]{2,1,0:T(8,128)(2,1)S(1)} %get-tuple-element.267), channel_id=1, source_target_pairs={{0,2},{1,3},{2,0},{3,1},{4,6},{5,7},{6,4},{7,5},{8,10},{9,11},{10,... | collective-permute-start | bytes 1769480 | tf_op jit(solution)/shard_map/ppermute | solution.py:35
  115.9 15.4 %collective-permute-start.38 = (bf16[4,96,768]{2,1,0:T(8,128)(2,1)S(1)}, bf16[4,96,768]{2,1,0:T(8,128)(2,1)S(1)}, u32[]{:S(2)}, u32[]{:S(2)}) collective-permute-start(bf16[4,96,768]{2,1,0:T(8,128)(2,1)S(1)} %get-tuple-element.268), channel_id=1, source_target_pairs={{0,4},{4,0},{8,12},{12,8},{16,20},{20,16},{24,28},{28,24},{1,5},{5... | collective-permute-start | bytes 1769480 | tf_op jit(solution)/shard_map/ppermute | solution.py:39
  125.7 5.6 %collective-permute-start.36 = (bf16[256,768]{1,0:T(8,128)(2,1)S(1)}, bf16[256,768]{1,0:T(8,128)(2,1)S(1)}, u32[]{:S(2)}, u32[]{:S(2)}) collective-permute-start(bf16[256,768]{1,0:T(8,128)(2,1)S(1)} %get-tuple-element.259), channel_id=1, source_target_pairs={{0,1},{1,0},{2,3},{3,2},{4,5},{5,4},{6,7},{7,6},{8,9},{9,8},{10,11... | collective-permute-start | bytes 1179656 | tf_op jit(solution)/shard_map/ppermute | solution.py:31
  131.3 22.3 %collective-permute-start.39 = (bf16[6,96,768]{2,1,0:T(8,128)(2,1)}, bf16[6,96,768]{2,1,0:T(8,128)(2,1)}, u32[]{:S(2)}, u32[]{:S(2)}) collective-permute-start(bf16[6,96,768]{2,1,0:T(8,128)(2,1)} %get-tuple-element.269), channel_id=1, source_target_pairs={{0,2},{1,3},{2,0},{3,1},{4,6},{5,7},{6,4},{7,5},{8,10},{9,11},{10,... | collective-permute-start | bytes 2654216 | tf_op jit(solution)/shard_map/ppermute | solution.py:35
  131.8 21.8 %collective-permute-start.40 = (bf16[6,96,768]{2,1,0:T(8,128)(2,1)}, bf16[6,96,768]{2,1,0:T(8,128)(2,1)}, u32[]{:S(2)}, u32[]{:S(2)}) collective-permute-start(bf16[6,96,768]{2,1,0:T(8,128)(2,1)} %get-tuple-element.270), channel_id=1, source_target_pairs={{0,4},{4,0},{8,12},{12,8},{16,20},{20,16},{24,28},{28,24},{1,5},{5... | collective-permute-start | bytes 2654216 | tf_op jit(solution)/shard_map/ppermute | solution.py:39
  133.3 20.2 %collective-permute-start.41 = (bf16[96,768]{1,0:T(8,128)(2,1)}, bf16[96,768]{1,0:T(8,128)(2,1)S(1)}, u32[]{:S(2)}, u32[]{:S(2)}) collective-permute-start(bf16[96,768]{1,0:T(8,128)(2,1)} %get-tuple-element.274), channel_id=1, source_target_pairs={{0,8},{4,12},{8,0},{12,4},{16,24},{20,28},{24,16},{28,20},{1,9},{5... | collective-permute-start | bytes 442376 | tf_op jit(solution)/shard_map/ppermute | solution.py:43
  134.4 19.2 %collective-permute-start.42 = (bf16[96,768]{1,0:T(8,128)(2,1)}, bf16[96,768]{1,0:T(8,128)(2,1)}, u32[]{:S(2)}, u32[]{:S(2)}) collective-permute-start(bf16[96,768]{1,0:T(8,128)(2,1)} %get-tuple-element.275), channel_id=1, source_target_pairs={{0,16},{4,20},{8,24},{12,28},{16,0},{20,4},{24,8},{28,12},{1,17},{... | collective-permute-start | bytes 442376 | tf_op jit(solution)/shard_map/ppermute | solution.py:43
  136.6 17.0 %collective-permute-start.43 = (bf16[96,768]{1,0:T(8,128)(2,1)}, bf16[96,768]{1,0:T(8,128)(2,1)}, u32[]{:S(2)}, u32[]{:S(2)}) collective-permute-start(bf16[96,768]{1,0:T(8,128)(2,1)} %get-tuple-element.276), channel_id=1, source_target_pairs={{0,24},{4,28},{8,16},{12,20},{16,8},{20,12},{24,0},{28,4},{1,25},{... | collective-permute-start | bytes 442376 | tf_op jit(solution)/shard_map/ppermute | solution.py:43
  138.7 14.9 %all-to-all-start = ((bf16[32,8,128]{2,1,0:T(8,128)(2,1)}), bf16[32,8,128]{2,1,0:T(8,128)(2,1)S(1)}, u32[]{:S(2)}, u32[]{:S(2)}) async-start(bf16[32,8,128]{2,1,0:T(8,128)(2,1)} %shard_map.299), calls=%async_computation | async-start | bytes 131072 | tf_op jit(solution)/shard_map/all_to_all | solution.py:1186
  155.9 17.1 %collective-permute-start.44 = (bf16[4,96,768]{2,1,0:T(8,128)(2,1)S(1)}, bf16[4,96,768]{2,1,0:T(8,128)(2,1)S(1)}, u32[]{:S(2)}, u32[]{:S(2)}) collective-permute-start(bf16[4,96,768]{2,1,0:T(8,128)(2,1)S(1)} %get-tuple-element.286), channel_id=1, source_target_pairs={{0,2},{1,3},{2,0},{3,1},{4,6},{5,7},{6,4},{7,5},{8,10},{9,11},{10,... | collective-permute-start | bytes 1769480 | tf_op jit(solution)/shard_map/ppermute | solution.py:35
  157.4 15.7 %collective-permute-start.45 = (bf16[4,96,768]{2,1,0:T(8,128)(2,1)S(1)}, bf16[4,96,768]{2,1,0:T(8,128)(2,1)S(1)}, u32[]{:S(2)}, u32[]{:S(2)}) collective-permute-start(bf16[4,96,768]{2,1,0:T(8,128)(2,1)S(1)} %get-tuple-element.287), channel_id=1, source_target_pairs={{0,4},{4,0},{8,12},{12,8},{16,20},{20,16},{24,28},{28,24},{1,5},{5... | collective-permute-start | bytes 1769480 | tf_op jit(solution)/shard_map/ppermute | solution.py:39
  158.0 7.5 %collective-permute-start.46 = (bf16[96,768]{1,0:T(8,128)(2,1)}, bf16[96,768]{1,0:T(8,128)(2,1)S(1)}, u32[]{:S(2)}, u32[]{:S(2)}) collective-permute-start(bf16[96,768]{1,0:T(8,128)(2,1)} %get-tuple-element.288), channel_id=1, source_target_pairs={{0,8},{4,12},{8,0},{12,4},{16,24},{20,28},{24,16},{28,20},{1,9},{5... | collective-permute-start | bytes 442376 | tf_op jit(solution)/shard_map/ppermute | solution.py:43
  158.9 14.1 %collective-permute-start.47 = (bf16[96,768]{1,0:T(8,128)(2,1)}, bf16[96,768]{1,0:T(8,128)(2,1)S(1)}, u32[]{:S(2)}, u32[]{:S(2)}) collective-permute-start(bf16[96,768]{1,0:T(8,128)(2,1)} %get-tuple-element.289), channel_id=1, source_target_pairs={{0,16},{4,20},{8,24},{12,28},{16,0},{20,4},{24,8},{28,12},{1,17},{... | collective-permute-start | bytes 442376 | tf_op jit(solution)/shard_map/ppermute | solution.py:43
  161.0 12.0 %collective-permute-start.48 = (bf16[96,768]{1,0:T(8,128)(2,1)}, bf16[96,768]{1,0:T(8,128)(2,1)S(1)}, u32[]{:S(2)}, u32[]{:S(2)}) collective-permute-start(bf16[96,768]{1,0:T(8,128)(2,1)} %get-tuple-element.290), channel_id=1, source_target_pairs={{0,24},{4,28},{8,16},{12,20},{16,8},{20,12},{24,0},{28,4},{1,25},{... | collective-permute-start | bytes 442376 | tf_op jit(solution)/shard_map/ppermute | solution.py:43
  173.9 7.2 %collective-permute-start.49 = (bf16[96,768]{1,0:T(8,128)(2,1)}, bf16[96,768]{1,0:T(8,128)(2,1)S(1)}, u32[]{:S(2)}, u32[]{:S(2)}) collective-permute-start(bf16[96,768]{1,0:T(8,128)(2,1)} %get-tuple-element.295), channel_id=1, source_target_pairs={{0,8},{4,12},{8,0},{12,4},{16,24},{20,28},{24,16},{28,20},{1,9},{5... | collective-permute-start | bytes 442376 | tf_op jit(solution)/shard_map/ppermute | solution.py:43
  176.1 13.1 %collective-permute-start.50 = (bf16[96,768]{1,0:T(8,128)(2,1)}, bf16[96,768]{1,0:T(8,128)(2,1)S(1)}, u32[]{:S(2)}, u32[]{:S(2)}) collective-permute-start(bf16[96,768]{1,0:T(8,128)(2,1)} %get-tuple-element.296), channel_id=1, source_target_pairs={{0,16},{4,20},{8,24},{12,28},{16,0},{20,4},{24,8},{28,12},{1,17},{... | collective-permute-start | bytes 442376 | tf_op jit(solution)/shard_map/ppermute | solution.py:43
  177.1 12.1 %collective-permute-start.51 = (bf16[96,768]{1,0:T(8,128)(2,1)}, bf16[96,768]{1,0:T(8,128)(2,1)S(1)}, u32[]{:S(2)}, u32[]{:S(2)}) collective-permute-start(bf16[96,768]{1,0:T(8,128)(2,1)} %get-tuple-element.297), channel_id=1, source_target_pairs={{0,24},{4,28},{8,16},{12,20},{16,8},{20,12},{24,0},{28,4},{1,25},{... | collective-permute-start | bytes 442376 | tf_op jit(solution)/shard_map/ppermute | solution.py:43
  (27 other events, 234.2 us)

commit v9 on v8

--- a/solution.py
+++ b/solution.py
@@ -187,17 +187,10 @@
     return mine, others
 
 
-def combine_last_kernel(z, x, y, mine, *refs):
-    outs, (low, sems) = refs[:3], refs[3:]
-    copies = Copies(sems)
-    for k in (1, 2, 3, 0):
+def combine_last_kernel(z, x, y, *outs):
+    for k, out in enumerate(outs):
         total = z[k].astype(F32) + x[k].astype(F32) + y[k].astype(F32)
-        if k == 0:
-            mine[...] = total
-        else:
-            low[k - 1] = total.astype(BF16)
-            copies.start(low.at[k - 1], outs[k - 1])
-    copies.wait()
+        out[...] = total.astype(out.dtype)
 
 
 def combine_last(z, x, y):
@@ -206,11 +199,8 @@
         combine_last_kernel,
         (shape((rows, D), F32),) + (shape((rows, D)),) * 3,
         (z, x, y),
-        scratch=[pltpu.VMEM((3, rows, D), BF16)],
         cost=est(1000, 1000),
         limit=8,
-        far_out=range(1, 4),
-        sems=3,
     )
     return mine, others
 

time: 190 us -> 189 us (level)
  transfers between devices with their start and end apart: 53 -> 53, of which waited for: 25 -> 24; matrix products, arithmetic and copies ran while one was open for 2% -> 2% of each run, Pallas kernels for 20% -> 20%
where the time goes in v9:
time: 189 us
  waiting for transfers between devices  75.5 us (40%)
  starting transfers between devices  59.6 us (32%)
  Pallas kernels  47.1 us (25%)
  local copies, waits for them, and re-layouts  3.4 us (2%)
  other arithmetic  2.37 us (1%)
    pallas_call x24, Pallas kernels, call(): pl.pallas_call(kernel, out_shape=out_shape, in_specs=ins, out_specs=outs,...  47.1 us
    ppermute x19, waiting for transfers between devices, z_swap(): return lax.ppermute(v, 'batch', ZPAIR[k])  44.9 us
    ppermute x19, starting transfers between devices, z_swap(): return lax.ppermute(v, 'batch', ZPAIR[k])  29.2 us
    ppermute x10, starting transfers between devices, x_swap(): return lax.ppermute(v, 'head', XPAIR)  13.2 us
    ppermute x10, waiting for transfers between devices, y_swap(): return lax.ppermute(v, 'batch', YPAIR)  12.4 us
    ppermute x10, starting transfers between devices, y_swap(): return lax.ppermute(v, 'batch', YPAIR)  10.6 us
    all_to_all x1, waiting for transfers between devices, local(): lax.all_to_all(terms, ('batch', 'head'), split_axis=0, concat_axis=0, til...  8.16 us
    ppermute x10, waiting for transfers between devices, x_swap(): return lax.ppermute(v, 'head', XPAIR)  6.75 us
  transfers between devices with their start and end apart: 53, of which 24 were waited for; matrix products, arithmetic and copies ran while one was open for 2% of the time, Pallas kernels for 20%

profile of v9, /device:TPU:0, one launch (start us, length us, event | category | flops | bytes accessed | tf_op | source)
XLA Modules:
  0.0 189.2 jit_solution(2797733134888283136)
XLA Ops:
  2.0 3.1 %collective-permute-start = (bf16[104,768]{1,0:T(8,128)(2,1)S(1)}, bf16[104,768]{1,0:T(8,128)(2,1)S(1)}, u32[]{:S(2)}, u32[]{:S(2)}) collective-permute-start(bf16[104,768]{1,0:T(8,128)(2,1)S(1)} %get-tuple-element.163), channel_id=1, source_target_pairs={{0,8},{4,12},{8,0},{12,4},{16,24},{20,28},{24,16},{28,20},{1,9},{5... | collective-permute-start | bytes 479240 | tf_op jit(solution)/shard_map/ppermute | solution.py:43
  5.1 2.5 %collective-permute-start.2 = (bf16[104,768]{1,0:T(8,128)(2,1)S(1)}, bf16[104,768]{1,0:T(8,128)(2,1)S(1)}, u32[]{:S(2)}, u32[]{:S(2)}) collective-permute-start(bf16[104,768]{1,0:T(8,128)(2,1)S(1)} %get-tuple-element.163), channel_id=1, source_target_pairs={{0,24},{4,28},{8,16},{12,20},{16,8},{20,12},{24,0},{28,4},{1,25},{... | collective-permute-start | bytes 479240 | tf_op jit(solution)/shard_map/ppermute | solution.py:43
  7.7 1.9 %collective-permute-done = bf16[104,768]{1,0:T(8,128)(2,1)S(1)} collective-permute-done((bf16[104,768]{1,0:T(8,128)(2,1)S(1)}, bf16[104,768]{1,0:T(8,128)(2,1)S(1)}, u32[]{:S(2)}, u32[]{:S(2)}) %collective-permute-start) | collective-permute-done | bytes 159776 | tf_op jit(solution)/shard_map/ppermute | solution.py:43
  9.6 1.5 collective-permute-start.4
  11.1 1.5 collective-permute-start.3
  13.7 1.5 collective-permute-start.5
  15.2 1.5 collective-permute-start.6
  16.7 5.1 %collective-permute-done.1 = bf16[104,768]{1,0:T(8,128)(2,1)S(1)} collective-permute-done((bf16[104,768]{1,0:T(8,128)(2,1)S(1)}, bf16[104,768]{1,0:T(8,128)(2,1)S(1)}, u32[]{:S(2)}, u32[]{:S(2)}) %collective-permute-start.1) | collective-permute-done | bytes 159776 | tf_op jit(solution)/shard_map/ppermute | solution.py:43
  21.9 1.6 collective-permute-start.9
  23.5 1.5 collective-permute-start.8
  25.1 2.7 %collective-permute-start.12 = (bf16[104,768]{1,0:T(8,128)(2,1)S(1)}, bf16[104,768]{1,0:T(8,128)(2,1)S(1)}, u32[]{:S(2)}, u32[]{:S(2)}) collective-permute-start(bf16[104,768]{1,0:T(8,128)(2,1)S(1)} %get-tuple-element.169), channel_id=1, source_target_pairs={{0,24},{4,28},{8,16},{12,20},{16,8},{20,12},{24,0},{28,4},{1,25},{... | collective-permute-start | bytes 479240 | tf_op jit(solution)/shard_map/ppermute | solution.py:43
  28.6 11.2 %collective-permute-done.12 = bf16[104,768]{1,0:T(8,128)(2,1)S(1)} collective-permute-done((bf16[104,768]{1,0:T(8,128)(2,1)S(1)}, bf16[104,768]{1,0:T(8,128)(2,1)S(1)}, u32[]{:S(2)}, u32[]{:S(2)}) %collective-permute-start.12) | collective-permute-done | bytes 159776 | tf_op jit(solution)/shard_map/ppermute | solution.py:43
  41.8 3.0 %collective-permute-start.15 = (bf16[56,768]{1,0:T(8,128)(2,1)S(1)}, bf16[56,768]{1,0:T(8,128)(2,1)S(1)}, u32[]{:S(2)}, u32[]{:S(2)}) collective-permute-start(bf16[56,768]{1,0:T(8,128)(2,1)S(1)} %get-tuple-element.176), channel_id=1, source_target_pairs={{0,24},{4,28},{8,16},{12,20},{16,8},{20,12},{24,0},{28,4},{1,25},{... | collective-permute-start | bytes 258056 | tf_op jit(solution)/shard_map/ppermute | solution.py:43
  44.8 1.3 collective-permute-start.13
  46.2 1.9 collective-permute-done.15
  48.1 2.2 %collective-permute-done.14 = bf16[56,768]{1,0:T(8,128)(2,1)S(1)} collective-permute-done((bf16[56,768]{1,0:T(8,128)(2,1)S(1)}, bf16[56,768]{1,0:T(8,128)(2,1)S(1)}, u32[]{:S(2)}, u32[]{:S(2)}) %collective-permute-start.14) | collective-permute-done | bytes 86048 | tf_op jit(solution)/shard_map/ppermute | solution.py:43
  51.7 1.5 collective-permute-start.25
  53.2 1.6 collective-permute-start.24
  55.5 2.1 %collective-permute-start.26 = (bf16[8,32,768]{2,1,0:T(8,128)(2,1)S(1)}, bf16[8,32,768]{2,1,0:T(8,128)(2,1)S(1)}, u32[]{:S(2)}, u32[]{:S(2)}) collective-permute-start(bf16[8,32,768]{2,1,0:T(8,128)(2,1)S(1)} %pad_maximum_fusion.2), channel_id=1, source_target_pairs={{0,16},{4,20},{8,24},{12,28},{16,0},{20,4},{24,8},{28,12},{1,17},{... | collective-permute-start | bytes 1179656 | tf_op jit(solution)/shard_map/ppermute | solution.py:43
  59.3 10.3 %shard_map.281 = (bf16[256,384]{1,0:T(8,128)(2,1)S(1)}, bf16[256,384]{1,0:T(8,128)(2,1)S(1)}, bf16[512,384]{1,0:T(8,128)(2,1)S(1)}, bf16[512,384]{1,0:T(8,128)(2...) custom-call(s32[2]{0:T(128)S(1)} %copy-done.10, ...), custom_call_target="tpu_custom_call" | custom-call | flops 1000 | bytes 1000 | tf_op jit(solution)/shard_map/pallas_call | solution.py:108
  69.7 1.4 collective-permute-done.23.ctx_in
  72.2 3.8 %collective-permute-done.26.refs_2_.refs_4_.refs_3_ = bf16[8,32,768]{2,1,0:T(8,128)(2,1)S(1)} collective-permute-done((bf16[8,32,768]{2,1,0:T(8,128)(2,1)S(1)}, bf16[8,32,768]{2,1,0:T(8,128)(2,1)S(1)}, u32[]{:S(2)}, u32[]{:S(2)}) %collective-permute-start.26) | collective-permute-done | bytes 393248 | tf_op jit(solution)/shard_map/ppermute | solution.py:43
  77.7 1.5 collective-permute-start.27
  81.8 1.5 shard_map.285
  84.6 5.0 %collective-permute-done.28.w1.refs_1_ = bf16[2,160,768]{2,1,0:T(8,128)(2,1)S(1)} collective-permute-done((bf16[2,160,768]{2,1,0:T(8,128)(2,1)S(1)}, bf16[2,160,768]{2,1,0:T(8,128)(2,1)S(1)}, u32[]{:S(2)}, u32[]{:S(2)}) %collective-permute-start.28) | collective-permute-done | bytes 491552 | tf_op jit(solution)/shard_map/ppermute | solution.py:39
  96.5 1.5 collective-permute-start.33
  98.0 1.6 collective-permute-start.34
  99.6 1.9 shard_map.292
  101.5 1.9 shard_map.293
  103.4 1.9 shard_map.294
  105.3 1.5 shard_map.295
  107.0 5.0 %collective-permute-done.33.refs_2_ = bf16[2,192,768]{2,1,0:T(8,128)(2,1)S(1)} collective-permute-done((bf16[2,192,768]{2,1,0:T(8,128)(2,1)S(1)}, bf16[2,192,768]{2,1,0:T(8,128)(2,1)S(1)}, u32[]{:S(2)}, u32[]{:S(2)}) %collective-permute-start.33) | collective-permute-done | bytes 589856 | tf_op jit(solution)/shard_map/ppermute | solution.py:39
  114.3 1.6 collective-permute-start.37
  116.5 9.2 %shard_map.297 = (bf16[4,96,768]{2,1,0:T(8,128)(2,1)}, bf16[4,96,768]{2,1,0:T(8,128)(2,1)}, bf16[4,96,768]{2,1,0:T(8,128)(2,1)}, bf16[6,96,768]{2,1,0:T(8,128)(2...) custom-call(bf16[256,768]{1,0:T(8,128)(2,1)S(1)} %get-tuple-element., ...), custom_call_target="tpu_custom_call" | custom-call | flops 8000000000 | bytes 14000000 | tf_op jit(solution)/shard_map/pallas_call | solution.py:108
  125.8 4.2 %collective-permute-done.37.x = bf16[4,96,768]{2,1,0:T(8,128)(2,1)S(1)} collective-permute-done((bf16[4,96,768]{2,1,0:T(8,128)(2,1)S(1)}, bf16[4,96,768]{2,1,0:T(8,128)(2,1)S(1)}, u32[]{:S(2)}, u32[]{:S(2)}) %collective-permute-start.37) | collective-permute-done | bytes 589856 | tf_op jit(solution)/shard_map/ppermute | solution.py:35
  134.4 2.2 %collective-permute-start.42 = (bf16[96,768]{1,0:T(8,128)(2,1)}, bf16[96,768]{1,0:T(8,128)(2,1)}, u32[]{:S(2)}, u32[]{:S(2)}) collective-permute-start(bf16[96,768]{1,0:T(8,128)(2,1)} %get-tuple-element.275), channel_id=1, source_target_pairs={{0,16},{4,20},{8,24},{12,28},{16,0},{20,4},{24,8},{28,12},{1,17},{... | collective-permute-start | bytes 442376 | tf_op jit(solution)/shard_map/ppermute | solution.py:43
  138.7 4.7 %all-to-all-start = ((bf16[32,8,128]{2,1,0:T(8,128)(2,1)}), bf16[32,8,128]{2,1,0:T(8,128)(2,1)S(1)}, u32[]{:S(2)}, u32[]{:S(2)}) async-start(bf16[32,8,128]{2,1,0:T(8,128)(2,1)} %shard_map.299), calls=%async_computation | async-start | bytes 131072 | tf_op jit(solution)/shard_map/all_to_all | solution.py:1176
  143.5 2.0 %add_convert_fusion = bf16[256,768]{1,0:T(8,128)(2,1)} fusion(bf16[256,768]{1,0:T(8,128)(2,1)} %copy-done.17, f32[256,768]{1,0:T(8,128)S(1)} %get-tuple-element.248, f32[256,768]{1,0:T(8,128)S(1)} %get-tuple-element.258), kind=kLoop, calls=%fused_computation.1 | loop fusion | flops 786432 | bytes 2359296 | tf_op jit(solution)/shard_map/convert_element_type | solution.py:1166
  145.4 8.2 %all-to-all-done = bf16[32,8,128]{2,1,0:T(8,128)(2,1)S(1)} async-done(((bf16[32,8,128]{2,1,0:T(8,128)(2,1)}), bf16[32,8,128]{2,1,0:T(8,128)(2,1)S(1)}, u32[]{:S(2)}, u32[]{:S(2)}) %all-to-all-start) | async-done | bytes 65568 | tf_op jit(solution)/shard_map/all_to_all | solution.py:1176
  153.6 2.3 %shard_map.300 = (bf16[4,96,768]{2,1,0:T(8,128)(2,1)S(1)}, bf16[4,96,768]{2,1,0:T(8,128)(2,1)S(1)}, f32[96,768]{1,0:T(8,128)}, bf16[96,768]{1,0:T(8,128)(2,1)}, ...) custom-call(bf16[4,96,768]{2,1,0:T(8,128)(2,1)S(1)} %copy-done.3, bf16[4,96,768]{2,1,0:T(8,128)(2,1)S(1)} %copy-done.4, ...), custom_call_target="tpu_custom_call" | custom-call | flops 1000 | bytes 1000 | tf_op jit(solution)/shard_map/pallas_call | solution.py:108
  155.9 1.4 collective-permute-start.44
  158.9 2.1 %collective-permute-start.47 = (bf16[96,768]{1,0:T(8,128)(2,1)}, bf16[96,768]{1,0:T(8,128)(2,1)S(1)}, u32[]{:S(2)}, u32[]{:S(2)}) collective-permute-start(bf16[96,768]{1,0:T(8,128)(2,1)} %get-tuple-element.289), channel_id=1, source_target_pairs={{0,16},{4,20},{8,24},{12,28},{16,0},{20,4},{24,8},{28,12},{1,17},{... | collective-permute-start | bytes 442376 | tf_op jit(solution)/shard_map/ppermute | solution.py:43
  162.9 2.6 %collective-permute-done.46.refs_5_ = bf16[96,768]{1,0:T(8,128)(2,1)S(1)} collective-permute-done((bf16[96,768]{1,0:T(8,128)(2,1)}, bf16[96,768]{1,0:T(8,128)(2,1)S(1)}, u32[]{:S(2)}, u32[]{:S(2)}) %collective-permute-start.46) | collective-permute-done | bytes 147488 | tf_op jit(solution)/shard_map/ppermute | solution.py:43
  165.5 7.5 %collective-permute-done.47.refs_6_ = bf16[96,768]{1,0:T(8,128)(2,1)S(1)} collective-permute-done((bf16[96,768]{1,0:T(8,128)(2,1)}, bf16[96,768]{1,0:T(8,128)(2,1)S(1)}, u32[]{:S(2)}, u32[]{:S(2)}) %collective-permute-start.47) | collective-permute-done | bytes 147488 | tf_op jit(solution)/shard_map/ppermute | solution.py:43
  173.3 2.2 %collective-permute-start.49 = (bf16[96,768]{1,0:T(8,128)(2,1)S(1)}, bf16[96,768]{1,0:T(8,128)(2,1)S(1)}, u32[]{:S(2)}, u32[]{:S(2)}) collective-permute-start(bf16[96,768]{1,0:T(8,128)(2,1)S(1)} %get-tuple-element.295), channel_id=1, source_target_pairs={{0,8},{4,12},{8,0},{12,4},{16,24},{20,28},{24,16},{28,20},{1,9},{5... | collective-permute-start | bytes 442376 | tf_op jit(solution)/shard_map/ppermute | solution.py:43
  176.5 1.4 collective-permute-start.51
  178.5 1.9 shard_map.303
  180.4 8.0 %collective-permute-done.50.two = bf16[96,768]{1,0:T(8,128)(2,1)S(1)} collective-permute-done((bf16[96,768]{1,0:T(8,128)(2,1)S(1)}, bf16[96,768]{1,0:T(8,128)(2,1)S(1)}, u32[]{:S(2)}, u32[]{:S(2)}) %collective-permute-start.50) | collective-permute-done | bytes 147488 | tf_op jit(solution)/shard_map/ppermute | solution.py:43
  (149 shorter events, 38.7 us)
Async XLA Ops:
  2.0 7.6 %collective-permute-start = (bf16[104,768]{1,0:T(8,128)(2,1)S(1)}, bf16[104,768]{1,0:T(8,128)(2,1)S(1)}, u32[]{:S(2)}, u32[]{:S(2)}) collective-permute-start(bf16[104,768]{1,0:T(8,128)(2,1)S(1)} %get-tuple-element.163), channel_id=1, source_target_pairs={{0,8},{4,12},{8,0},{12,4},{16,24},{20,28},{24,16},{28,20},{1,9},{5... | collective-permute-start | bytes 479240 | tf_op jit(solution)/shard_map/ppermute | solution.py:43
  5.1 11.6 %collective-permute-start.2 = (bf16[104,768]{1,0:T(8,128)(2,1)S(1)}, bf16[104,768]{1,0:T(8,128)(2,1)S(1)}, u32[]{:S(2)}, u32[]{:S(2)}) collective-permute-start(bf16[104,768]{1,0:T(8,128)(2,1)S(1)} %get-tuple-element.163), channel_id=1, source_target_pairs={{0,24},{4,28},{8,16},{12,20},{16,8},{20,12},{24,0},{28,4},{1,25},{... | collective-permute-start | bytes 479240 | tf_op jit(solution)/shard_map/ppermute | solution.py:43
  7.5 14.2 %collective-permute-start.1 = (bf16[104,768]{1,0:T(8,128)(2,1)S(1)}, bf16[104,768]{1,0:T(8,128)(2,1)S(1)}, u32[]{:S(2)}, u32[]{:S(2)}) collective-permute-start(bf16[104,768]{1,0:T(8,128)(2,1)S(1)} %get-tuple-element.163), channel_id=1, source_target_pairs={{0,16},{4,20},{8,24},{12,28},{16,0},{20,4},{24,8},{28,12},{1,17},{... | collective-permute-start | bytes 479240 | tf_op jit(solution)/shard_map/ppermute | solution.py:43
  9.6 4.1 %collective-permute-start.4 = (bf16[32,768]{1,0:T(8,128)(2,1)S(1)}, bf16[32,768]{1,0:T(8,128)(2,1)S(1)}, u32[]{:S(2)}, u32[]{:S(2)}) collective-permute-start(bf16[32,768]{1,0:T(8,128)(2,1)S(1)} %get-tuple-element.165), channel_id=1, source_target_pairs={{0,4},{4,0},{8,12},{12,8},{16,20},{20,16},{24,28},{28,24},{1,5},{5... | collective-permute-start | bytes 147464 | tf_op jit(solution)/shard_map/ppermute | solution.py:39
  11.1 4.1 %collective-permute-start.3 = (bf16[32,768]{1,0:T(8,128)(2,1)S(1)}, bf16[32,768]{1,0:T(8,128)(2,1)S(1)}, u32[]{:S(2)}, u32[]{:S(2)}) collective-permute-start(bf16[32,768]{1,0:T(8,128)(2,1)S(1)} %get-tuple-element.165), channel_id=1, source_target_pairs={{0,2},{1,3},{2,0},{3,1},{4,6},{5,7},{6,4},{7,5},{8,10},{9,11},{10,... | collective-permute-start | bytes 147464 | tf_op jit(solution)/shard_map/ppermute | solution.py:35
  12.6 9.3 %collective-permute-start.7 = (bf16[256,768]{1,0:T(8,128)(2,1)}, bf16[256,768]{1,0:T(8,128)(2,1)S(1)}, u32[]{:S(2)}, u32[]{:S(2)}) collective-permute-start(bf16[256,768]{1,0:T(8,128)(2,1)} %refs_8_.1), channel_id=1, source_target_pairs={{0,1},{1,0},{2,3},{3,2},{4,5},{5,4},{6,7},{7,6},{8,9},{9,8},{10,11... | collective-permute-start | bytes 1179656 | tf_op jit(solution)/shard_map/ppermute | solution.py:31
  13.7 8.2 %collective-permute-start.5 = (bf16[16,768]{1,0:T(8,128)(2,1)S(1)}, bf16[16,768]{1,0:T(8,128)(2,1)S(1)}, u32[]{:S(2)}, u32[]{:S(2)}) collective-permute-start(bf16[16,768]{1,0:T(8,128)(2,1)S(1)} %slice.129), channel_id=1, source_target_pairs={{0,2},{1,3},{2,0},{3,1},{4,6},{5,7},{6,4},{7,5},{8,10},{9,11},{10,... | collective-permute-start | bytes 73736 | tf_op jit(solution)/shard_map/ppermute | solution.py:35
  15.2 6.7 %collective-permute-start.6 = (bf16[16,768]{1,0:T(8,128)(2,1)S(1)}, bf16[16,768]{1,0:T(8,128)(2,1)S(1)}, u32[]{:S(2)}, u32[]{:S(2)}) collective-permute-start(bf16[16,768]{1,0:T(8,128)(2,1)S(1)} %slice.130), channel_id=1, source_target_pairs={{0,4},{4,0},{8,12},{12,8},{16,20},{20,16},{24,28},{28,24},{1,5},{5... | collective-permute-start | bytes 73736 | tf_op jit(solution)/shard_map/ppermute | solution.py:39
  21.9 18.7 %collective-permute-start.9 = (bf16[4,104,768]{2,1,0:T(8,128)(2,1)S(1)}, bf16[4,104,768]{2,1,0:T(8,128)(2,1)S(1)}, u32[]{:S(2)}, u32[]{:S(2)}) collective-permute-start(bf16[4,104,768]{2,1,0:T(8,128)(2,1)S(1)} %pad_maximum_fusion.1.refs_0_), channel_id=1, source_target_pairs={{0,4},{4,0},{8,12},{12,8},{16,20},{20,16},{24,28},{28,24},{1,5},{5... | collective-permute-start | bytes 1916936 | tf_op jit(solution)/shard_map/ppermute | solution.py:39
  23.5 17.1 %collective-permute-start.8 = (bf16[4,104,768]{2,1,0:T(8,128)(2,1)S(1)}, bf16[4,104,768]{2,1,0:T(8,128)(2,1)S(1)}, u32[]{:S(2)}, u32[]{:S(2)}) collective-permute-start(bf16[4,104,768]{2,1,0:T(8,128)(2,1)S(1)} %pad_maximum_fusion.1.refs_0_), channel_id=1, source_target_pairs={{0,2},{1,3},{2,0},{3,1},{4,6},{5,7},{6,4},{7,5},{8,10},{9,11},{10,... | collective-permute-start | bytes 1916936 | tf_op jit(solution)/shard_map/ppermute | solution.py:35
  25.0 15.5 %collective-permute-start.10 = (bf16[232,768]{1,0:T(8,128)(2,1)S(1)}, bf16[232,768]{1,0:T(8,128)(2,1)S(1)}, u32[]{:S(2)}, u32[]{:S(2)}) collective-permute-start(bf16[232,768]{1,0:T(8,128)(2,1)S(1)} %pad_maximum_fusion.3), channel_id=1, source_target_pairs={{0,8},{4,12},{8,0},{12,4},{16,24},{20,28},{24,16},{28,20},{1,9},{5... | collective-permute-start | bytes 1069064 | tf_op jit(solution)/shard_map/ppermute | solution.py:43
  25.1 14.7 %collective-permute-start.12 = (bf16[104,768]{1,0:T(8,128)(2,1)S(1)}, bf16[104,768]{1,0:T(8,128)(2,1)S(1)}, u32[]{:S(2)}, u32[]{:S(2)}) collective-permute-start(bf16[104,768]{1,0:T(8,128)(2,1)S(1)} %get-tuple-element.169), channel_id=1, source_target_pairs={{0,24},{4,28},{8,16},{12,20},{16,8},{20,12},{24,0},{28,4},{1,25},{... | collective-permute-start | bytes 479240 | tf_op jit(solution)/shard_map/ppermute | solution.py:43
  27.8 12.0 %collective-permute-start.11 = (bf16[104,768]{1,0:T(8,128)(2,1)S(1)}, bf16[104,768]{1,0:T(8,128)(2,1)S(1)}, u32[]{:S(2)}, u32[]{:S(2)}) collective-permute-start(bf16[104,768]{1,0:T(8,128)(2,1)S(1)} %get-tuple-element.169), channel_id=1, source_target_pairs={{0,16},{4,20},{8,24},{12,28},{16,0},{20,4},{24,8},{28,12},{1,17},{... | collective-permute-start | bytes 479240 | tf_op jit(solution)/shard_map/ppermute | solution.py:43
  40.7 9.6 %collective-permute-start.17 = (bf16[2,104,768]{2,1,0:T(8,128)(2,1)S(1)}, bf16[2,104,768]{2,1,0:T(8,128)(2,1)S(1)}, u32[]{:S(2)}, u32[]{:S(2)}) collective-permute-start(bf16[2,104,768]{2,1,0:T(8,128)(2,1)S(1)} %slice.102), channel_id=1, source_target_pairs={{0,4},{4,0},{8,12},{12,8},{16,20},{20,16},{24,28},{28,24},{1,5},{5... | collective-permute-start | bytes 958472 | tf_op jit(solution)/shard_map/ppermute | solution.py:39
  41.2 9.0 %collective-permute-start.16 = (bf16[2,104,768]{2,1,0:T(8,128)(2,1)S(1)}, bf16[2,104,768]{2,1,0:T(8,128)(2,1)S(1)}, u32[]{:S(2)}, u32[]{:S(2)}) collective-permute-start(bf16[2,104,768]{2,1,0:T(8,128)(2,1)S(1)} %slice.101), channel_id=1, source_target_pairs={{0,2},{1,3},{2,0},{3,1},{4,6},{5,7},{6,4},{7,5},{8,10},{9,11},{10,... | collective-permute-start | bytes 958472 | tf_op jit(solution)/shard_map/ppermute | solution.py:35
  41.8 6.3 %collective-permute-start.15 = (bf16[56,768]{1,0:T(8,128)(2,1)S(1)}, bf16[56,768]{1,0:T(8,128)(2,1)S(1)}, u32[]{:S(2)}, u32[]{:S(2)}) collective-permute-start(bf16[56,768]{1,0:T(8,128)(2,1)S(1)} %get-tuple-element.176), channel_id=1, source_target_pairs={{0,24},{4,28},{8,16},{12,20},{16,8},{20,12},{24,0},{28,4},{1,25},{... | collective-permute-start | bytes 258056 | tf_op jit(solution)/shard_map/ppermute | solution.py:43
  44.8 5.4 %collective-permute-start.14 = (bf16[56,768]{1,0:T(8,128)(2,1)S(1)}, bf16[56,768]{1,0:T(8,128)(2,1)S(1)}, u32[]{:S(2)}, u32[]{:S(2)}) collective-permute-start(bf16[56,768]{1,0:T(8,128)(2,1)S(1)} %get-tuple-element.176), channel_id=1, source_target_pairs={{0,16},{4,20},{8,24},{12,28},{16,0},{20,4},{24,8},{28,12},{1,17},{... | collective-permute-start | bytes 258056 | tf_op jit(solution)/shard_map/ppermute | solution.py:43
  44.8 5.4 %collective-permute-start.13 = (bf16[56,768]{1,0:T(8,128)(2,1)S(1)}, bf16[56,768]{1,0:T(8,128)(2,1)S(1)}, u32[]{:S(2)}, u32[]{:S(2)}) collective-permute-start(bf16[56,768]{1,0:T(8,128)(2,1)S(1)} %get-tuple-element.176), channel_id=1, source_target_pairs={{0,8},{4,12},{8,0},{12,4},{16,24},{20,28},{24,16},{28,20},{1,9},{5... | collective-permute-start | bytes 258056 | tf_op jit(solution)/shard_map/ppermute | solution.py:43
  51.1 3.7 %collective-permute-start.21 = (bf16[2,104,768]{2,1,0:T(8,128)(2,1)S(1)}, bf16[2,104,768]{2,1,0:T(8,128)(2,1)S(1)}, u32[]{:S(2)}, u32[]{:S(2)}) collective-permute-start(bf16[2,104,768]{2,1,0:T(8,128)(2,1)S(1)} %collective-permute-done.16.refs_3_), channel_id=1, source_target_pairs={{0,1},{1,0},{2,3},{3,2},{4,5},{5,4},{6,7},{7,6},{8,9},{9,8},{10,11... | collective-permute-start | bytes 958472 | tf_op jit(solution)/shard_map/ppermute | solution.py:31
  51.1 3.8 %collective-permute-start.22 = (bf16[2,104,768]{2,1,0:T(8,128)(2,1)S(1)}, bf16[2,104,768]{2,1,0:T(8,128)(2,1)S(1)}, u32[]{:S(2)}, u32[]{:S(2)}) collective-permute-start(bf16[2,104,768]{2,1,0:T(8,128)(2,1)S(1)} %collective-permute-done.17.refs_4_), channel_id=1, source_target_pairs={{0,1},{1,0},{2,3},{3,2},{4,5},{5,4},{6,7},{7,6},{8,9},{9,8},{10,11... | collective-permute-start | bytes 958472 | tf_op jit(solution)/shard_map/ppermute | solution.py:31
  51.6 3.9 %collective-permute-start.18 = (bf16[4,104,768]{2,1,0:T(8,128)(2,1)S(1)}, bf16[4,104,768]{2,1,0:T(8,128)(2,1)S(1)}, u32[]{:S(2)}, u32[]{:S(2)}) collective-permute-start(bf16[4,104,768]{2,1,0:T(8,128)(2,1)S(1)} %pad_maximum_fusion.1.refs_0_), channel_id=1, source_target_pairs={{0,1},{1,0},{2,3},{3,2},{4,5},{5,4},{6,7},{7,6},{8,9},{9,8},{10,11... | collective-permute-start | bytes 1916936 | tf_op jit(solution)/shard_map/ppermute | solution.py:31
  51.7 24.3 %collective-permute-start.25 = (bf16[4,160,768]{2,1,0:T(8,128)(2,1)S(1)}, bf16[4,160,768]{2,1,0:T(8,128)(2,1)S(1)}, u32[]{:S(2)}, u32[]{:S(2)}) collective-permute-start(bf16[4,160,768]{2,1,0:T(8,128)(2,1)S(1)} %pad_maximum_fusion.refs_0_), channel_id=1, source_target_pairs={{0,4},{4,0},{8,12},{12,8},{16,20},{20,16},{24,28},{28,24},{1,5},{5... | collective-permute-start | bytes 2949128 | tf_op jit(solution)/shard_map/ppermute | solution.py:39
  53.2 23.8 %collective-permute-start.24 = (bf16[4,160,768]{2,1,0:T(8,128)(2,1)S(1)}, bf16[4,160,768]{2,1,0:T(8,128)(2,1)S(1)}, u32[]{:S(2)}, u32[]{:S(2)}) collective-permute-start(bf16[4,160,768]{2,1,0:T(8,128)(2,1)S(1)} %pad_maximum_fusion.refs_0_), channel_id=1, source_target_pairs={{0,2},{1,3},{2,0},{3,1},{4,6},{5,7},{6,4},{7,5},{8,10},{9,11},{10,... | collective-permute-start | bytes 2949128 | tf_op jit(solution)/shard_map/ppermute | solution.py:35
  54.8 2.8 %collective-permute-start.19 = (bf16[4,104,768]{2,1,0:T(8,128)(2,1)S(1)}, bf16[4,104,768]{2,1,0:T(8,128)(2,1)S(1)}, u32[]{:S(2)}, u32[]{:S(2)}) collective-permute-start(bf16[4,104,768]{2,1,0:T(8,128)(2,1)S(1)} %collective-permute-done.8.refs_1_), channel_id=1, source_target_pairs={{0,1},{1,0},{2,3},{3,2},{4,5},{5,4},{6,7},{7,6},{8,9},{9,8},{10,11... | collective-permute-start | bytes 1916936 | tf_op jit(solution)/shard_map/ppermute | solution.py:31
  54.9 2.9 %collective-permute-start.20 = (bf16[4,104,768]{2,1,0:T(8,128)(2,1)S(1)}, bf16[4,104,768]{2,1,0:T(8,128)(2,1)S(1)}, u32[]{:S(2)}, u32[]{:S(2)}) collective-permute-start(bf16[4,104,768]{2,1,0:T(8,128)(2,1)S(1)} %collective-permute-done.9.refs_2_), channel_id=1, source_target_pairs={{0,1},{1,0},{2,3},{3,2},{4,5},{5,4},{6,7},{7,6},{8,9},{9,8},{10,11... | collective-permute-start | bytes 1916936 | tf_op jit(solution)/shard_map/ppermute | solution.py:31
  55.5 20.5 %collective-permute-start.26 = (bf16[8,32,768]{2,1,0:T(8,128)(2,1)S(1)}, bf16[8,32,768]{2,1,0:T(8,128)(2,1)S(1)}, u32[]{:S(2)}, u32[]{:S(2)}) collective-permute-start(bf16[8,32,768]{2,1,0:T(8,128)(2,1)S(1)} %pad_maximum_fusion.2), channel_id=1, source_target_pairs={{0,16},{4,20},{8,24},{12,28},{16,0},{20,4},{24,8},{28,12},{1,17},{... | collective-permute-start | bytes 1179656 | tf_op jit(solution)/shard_map/ppermute | solution.py:43
  72.0 7.2 %collective-permute-start.29 = (bf16[256,768]{1,0:T(8,128)(2,1)S(1)}, bf16[256,768]{1,0:T(8,128)(2,1)S(1)}, u32[]{:S(2)}, u32[]{:S(2)}) collective-permute-start(bf16[256,768]{1,0:T(8,128)(2,1)S(1)} %get-tuple-element.194.x0.x), channel_id=1, source_target_pairs={{0,1},{1,0},{2,3},{3,2},{4,5},{5,4},{6,7},{7,6},{8,9},{9,8},{10,11... | collective-permute-start | bytes 1179656 | tf_op jit(solution)/shard_map/ppermute | solution.py:31
  77.1 12.5 %collective-permute-start.28 = (bf16[2,160,768]{2,1,0:T(8,128)(2,1)S(1)}, bf16[2,160,768]{2,1,0:T(8,128)(2,1)S(1)}, u32[]{:S(2)}, u32[]{:S(2)}) collective-permute-start(bf16[2,160,768]{2,1,0:T(8,128)(2,1)S(1)} %slice.107), channel_id=1, source_target_pairs={{0,4},{4,0},{8,12},{12,8},{16,20},{20,16},{24,28},{28,24},{1,5},{5... | collective-permute-start | bytes 1474568 | tf_op jit(solution)/shard_map/ppermute | solution.py:39
  77.7 12.3 %collective-permute-start.27 = (bf16[2,160,768]{2,1,0:T(8,128)(2,1)S(1)}, bf16[2,160,768]{2,1,0:T(8,128)(2,1)S(1)}, u32[]{:S(2)}, u32[]{:S(2)}) collective-permute-start(bf16[2,160,768]{2,1,0:T(8,128)(2,1)S(1)} %slice.106), channel_id=1, source_target_pairs={{0,2},{1,3},{2,0},{3,1},{4,6},{5,7},{6,4},{7,5},{8,10},{9,11},{10,... | collective-permute-start | bytes 1474568 | tf_op jit(solution)/shard_map/ppermute | solution.py:35
  96.5 15.4 %collective-permute-start.33 = (bf16[2,192,768]{2,1,0:T(8,128)(2,1)S(1)}, bf16[2,192,768]{2,1,0:T(8,128)(2,1)S(1)}, u32[]{:S(2)}, u32[]{:S(2)}) collective-permute-start(bf16[2,192,768]{2,1,0:T(8,128)(2,1)S(1)} %get-tuple-element.244), channel_id=1, source_target_pairs={{0,4},{4,0},{8,12},{12,8},{16,20},{20,16},{24,28},{28,24},{1,5},{5... | collective-permute-start | bytes 1769480 | tf_op jit(solution)/shard_map/ppermute | solution.py:39
  98.0 15.1 %collective-permute-start.34 = (bf16[2,192,768]{2,1,0:T(8,128)(2,1)S(1)}, bf16[2,192,768]{2,1,0:T(8,128)(2,1)S(1)}, u32[]{:S(2)}, u32[]{:S(2)}) collective-permute-start(bf16[2,192,768]{2,1,0:T(8,128)(2,1)S(1)} %get-tuple-element.247), channel_id=1, source_target_pairs={{0,2},{1,3},{2,0},{3,1},{4,6},{5,7},{6,4},{7,5},{8,10},{9,11},{10,... | collective-permute-start | bytes 1769480 | tf_op jit(solution)/shard_map/ppermute | solution.py:35
  114.3 15.7 %collective-permute-start.37 = (bf16[4,96,768]{2,1,0:T(8,128)(2,1)S(1)}, bf16[4,96,768]{2,1,0:T(8,128)(2,1)S(1)}, u32[]{:S(2)}, u32[]{:S(2)}) collective-permute-start(bf16[4,96,768]{2,1,0:T(8,128)(2,1)S(1)} %get-tuple-element.267), channel_id=1, source_target_pairs={{0,2},{1,3},{2,0},{3,1},{4,6},{5,7},{6,4},{7,5},{8,10},{9,11},{10,... | collective-permute-start | bytes 1769480 | tf_op jit(solution)/shard_map/ppermute | solution.py:35
  115.9 15.4 %collective-permute-start.38 = (bf16[4,96,768]{2,1,0:T(8,128)(2,1)S(1)}, bf16[4,96,768]{2,1,0:T(8,128)(2,1)S(1)}, u32[]{:S(2)}, u32[]{:S(2)}) collective-permute-start(bf16[4,96,768]{2,1,0:T(8,128)(2,1)S(1)} %get-tuple-element.268), channel_id=1, source_target_pairs={{0,4},{4,0},{8,12},{12,8},{16,20},{20,16},{24,28},{28,24},{1,5},{5... | collective-permute-start | bytes 1769480 | tf_op jit(solution)/shard_map/ppermute | solution.py:39
  125.7 5.6 %collective-permute-start.36 = (bf16[256,768]{1,0:T(8,128)(2,1)S(1)}, bf16[256,768]{1,0:T(8,128)(2,1)S(1)}, u32[]{:S(2)}, u32[]{:S(2)}) collective-permute-start(bf16[256,768]{1,0:T(8,128)(2,1)S(1)} %get-tuple-element.259), channel_id=1, source_target_pairs={{0,1},{1,0},{2,3},{3,2},{4,5},{5,4},{6,7},{7,6},{8,9},{9,8},{10,11... | collective-permute-start | bytes 1179656 | tf_op jit(solution)/shard_map/ppermute | solution.py:31
  131.3 22.3 %collective-permute-start.39 = (bf16[6,96,768]{2,1,0:T(8,128)(2,1)}, bf16[6,96,768]{2,1,0:T(8,128)(2,1)}, u32[]{:S(2)}, u32[]{:S(2)}) collective-permute-start(bf16[6,96,768]{2,1,0:T(8,128)(2,1)} %get-tuple-element.269), channel_id=1, source_target_pairs={{0,2},{1,3},{2,0},{3,1},{4,6},{5,7},{6,4},{7,5},{8,10},{9,11},{10,... | collective-permute-start | bytes 2654216 | tf_op jit(solution)/shard_map/ppermute | solution.py:35
  131.8 21.8 %collective-permute-start.40 = (bf16[6,96,768]{2,1,0:T(8,128)(2,1)}, bf16[6,96,768]{2,1,0:T(8,128)(2,1)}, u32[]{:S(2)}, u32[]{:S(2)}) collective-permute-start(bf16[6,96,768]{2,1,0:T(8,128)(2,1)} %get-tuple-element.270), channel_id=1, source_target_pairs={{0,4},{4,0},{8,12},{12,8},{16,20},{20,16},{24,28},{28,24},{1,5},{5... | collective-permute-start | bytes 2654216 | tf_op jit(solution)/shard_map/ppermute | solution.py:39
  133.3 20.2 %collective-permute-start.41 = (bf16[96,768]{1,0:T(8,128)(2,1)}, bf16[96,768]{1,0:T(8,128)(2,1)S(1)}, u32[]{:S(2)}, u32[]{:S(2)}) collective-permute-start(bf16[96,768]{1,0:T(8,128)(2,1)} %get-tuple-element.274), channel_id=1, source_target_pairs={{0,8},{4,12},{8,0},{12,4},{16,24},{20,28},{24,16},{28,20},{1,9},{5... | collective-permute-start | bytes 442376 | tf_op jit(solution)/shard_map/ppermute | solution.py:43
  134.4 19.2 %collective-permute-start.42 = (bf16[96,768]{1,0:T(8,128)(2,1)}, bf16[96,768]{1,0:T(8,128)(2,1)}, u32[]{:S(2)}, u32[]{:S(2)}) collective-permute-start(bf16[96,768]{1,0:T(8,128)(2,1)} %get-tuple-element.275), channel_id=1, source_target_pairs={{0,16},{4,20},{8,24},{12,28},{16,0},{20,4},{24,8},{28,12},{1,17},{... | collective-permute-start | bytes 442376 | tf_op jit(solution)/shard_map/ppermute | solution.py:43
  136.6 17.0 %collective-permute-start.43 = (bf16[96,768]{1,0:T(8,128)(2,1)}, bf16[96,768]{1,0:T(8,128)(2,1)}, u32[]{:S(2)}, u32[]{:S(2)}) collective-permute-start(bf16[96,768]{1,0:T(8,128)(2,1)} %get-tuple-element.276), channel_id=1, source_target_pairs={{0,24},{4,28},{8,16},{12,20},{16,8},{20,12},{24,0},{28,4},{1,25},{... | collective-permute-start | bytes 442376 | tf_op jit(solution)/shard_map/ppermute | solution.py:43
  138.7 14.9 %all-to-all-start = ((bf16[32,8,128]{2,1,0:T(8,128)(2,1)}), bf16[32,8,128]{2,1,0:T(8,128)(2,1)S(1)}, u32[]{:S(2)}, u32[]{:S(2)}) async-start(bf16[32,8,128]{2,1,0:T(8,128)(2,1)} %shard_map.299), calls=%async_computation | async-start | bytes 131072 | tf_op jit(solution)/shard_map/all_to_all | solution.py:1176
  155.9 17.1 %collective-permute-start.44 = (bf16[4,96,768]{2,1,0:T(8,128)(2,1)S(1)}, bf16[4,96,768]{2,1,0:T(8,128)(2,1)S(1)}, u32[]{:S(2)}, u32[]{:S(2)}) collective-permute-start(bf16[4,96,768]{2,1,0:T(8,128)(2,1)S(1)} %get-tuple-element.286), channel_id=1, source_target_pairs={{0,2},{1,3},{2,0},{3,1},{4,6},{5,7},{6,4},{7,5},{8,10},{9,11},{10,... | collective-permute-start | bytes 1769480 | tf_op jit(solution)/shard_map/ppermute | solution.py:35
  157.4 15.7 %collective-permute-start.45 = (bf16[4,96,768]{2,1,0:T(8,128)(2,1)S(1)}, bf16[4,96,768]{2,1,0:T(8,128)(2,1)S(1)}, u32[]{:S(2)}, u32[]{:S(2)}) collective-permute-start(bf16[4,96,768]{2,1,0:T(8,128)(2,1)S(1)} %get-tuple-element.287), channel_id=1, source_target_pairs={{0,4},{4,0},{8,12},{12,8},{16,20},{20,16},{24,28},{28,24},{1,5},{5... | collective-permute-start | bytes 1769480 | tf_op jit(solution)/shard_map/ppermute | solution.py:39
  158.0 7.5 %collective-permute-start.46 = (bf16[96,768]{1,0:T(8,128)(2,1)}, bf16[96,768]{1,0:T(8,128)(2,1)S(1)}, u32[]{:S(2)}, u32[]{:S(2)}) collective-permute-start(bf16[96,768]{1,0:T(8,128)(2,1)} %get-tuple-element.288), channel_id=1, source_target_pairs={{0,8},{4,12},{8,0},{12,4},{16,24},{20,28},{24,16},{28,20},{1,9},{5... | collective-permute-start | bytes 442376 | tf_op jit(solution)/shard_map/ppermute | solution.py:43
  158.9 14.1 %collective-permute-start.47 = (bf16[96,768]{1,0:T(8,128)(2,1)}, bf16[96,768]{1,0:T(8,128)(2,1)S(1)}, u32[]{:S(2)}, u32[]{:S(2)}) collective-permute-start(bf16[96,768]{1,0:T(8,128)(2,1)} %get-tuple-element.289), channel_id=1, source_target_pairs={{0,16},{4,20},{8,24},{12,28},{16,0},{20,4},{24,8},{28,12},{1,17},{... | collective-permute-start | bytes 442376 | tf_op jit(solution)/shard_map/ppermute | solution.py:43
  161.0 12.0 %collective-permute-start.48 = (bf16[96,768]{1,0:T(8,128)(2,1)}, bf16[96,768]{1,0:T(8,128)(2,1)S(1)}, u32[]{:S(2)}, u32[]{:S(2)}) collective-permute-start(bf16[96,768]{1,0:T(8,128)(2,1)} %get-tuple-element.290), channel_id=1, source_target_pairs={{0,24},{4,28},{8,16},{12,20},{16,8},{20,12},{24,0},{28,4},{1,25},{... | collective-permute-start | bytes 442376 | tf_op jit(solution)/shard_map/ppermute | solution.py:43
  173.3 7.1 %collective-permute-start.49 = (bf16[96,768]{1,0:T(8,128)(2,1)S(1)}, bf16[96,768]{1,0:T(8,128)(2,1)S(1)}, u32[]{:S(2)}, u32[]{:S(2)}) collective-permute-start(bf16[96,768]{1,0:T(8,128)(2,1)S(1)} %get-tuple-element.295), channel_id=1, source_target_pairs={{0,8},{4,12},{8,0},{12,4},{16,24},{20,28},{24,16},{28,20},{1,9},{5... | collective-permute-start | bytes 442376 | tf_op jit(solution)/shard_map/ppermute | solution.py:43
  175.5 12.9 %collective-permute-start.50 = (bf16[96,768]{1,0:T(8,128)(2,1)S(1)}, bf16[96,768]{1,0:T(8,128)(2,1)S(1)}, u32[]{:S(2)}, u32[]{:S(2)}) collective-permute-start(bf16[96,768]{1,0:T(8,128)(2,1)S(1)} %get-tuple-element.296), channel_id=1, source_target_pairs={{0,16},{4,20},{8,24},{12,28},{16,0},{20,4},{24,8},{28,12},{1,17},{... | collective-permute-start | bytes 442376 | tf_op jit(solution)/shard_map/ppermute | solution.py:43
  176.5 11.8 %collective-permute-start.51 = (bf16[96,768]{1,0:T(8,128)(2,1)S(1)}, bf16[96,768]{1,0:T(8,128)(2,1)S(1)}, u32[]{:S(2)}, u32[]{:S(2)}) collective-permute-start(bf16[96,768]{1,0:T(8,128)(2,1)S(1)} %get-tuple-element.297), channel_id=1, source_target_pairs={{0,24},{4,28},{8,16},{12,20},{16,8},{20,12},{24,0},{28,4},{1,25},{... | collective-permute-start | bytes 442376 | tf_op jit(solution)/shard_map/ppermute | solution.py:43
  (27 other events, 232.9 us)
